TPU v7x, 32 devices: a whole 2x2x4 slice. The times are simulated.
32 devices in a mesh: facet: 4 (over x, core), col: 8 (over z, y).
Axes of the slice: x: 2, y: 2, z: 4, core: 2. Of those that a mesh axis runs over, the one named last changes fastest.
Arguments:
- facet_spectra: bfloat16 [2, 4, 2, 512, 8192], P(None, 'facet', None, None, 'col'), may hold values from -6 to 6
- facet_offsets: int32 [4, 2], P('facet'), may hold values from 0 to 65535
- column_index: int32 [2], replicated, may hold values from 0 to 145
- subgrid_offsets: int32 [2, 8], P(None, 'col'), may hold values from 0 to 65528, as said below
- weights: bfloat16 [2, 8, 512, 512], P(None, 'col', 'facet'), may hold values from 0.25 to 4
Outputs:
- subgrids: bfloat16 [2, 8, 2, 512, 512], P(None, 'col', None, 'facet')
- facet_updates: bfloat16 [2, 4, 2, 512, 8192], P(None, 'facet', None, None, 'col')
Inputs may be any that keep to these rules, and one draw needn't show every extreme that they name: `subgrid_offsets`: every offset is a multiple of 8; subgrid s of a column has position p = offset / 8 with (s // 1) * 1024 <= p < (s + 1) * 1024. In every column some subgrid has p exactly at such a lower end, and some subgrid has p at (s + 1) * 1024 - 128 // 2 + 1 or above.
All inputs are finite; a program needn't handle non-finite values.
Results may differ from a plain program's by a relative error of at most 0.015.
Values may be sent and summed in bfloat16 or wider, within the bound.
No kernel may reach another device: no remote copies, remote signals or barrier semaphores. Data moves between devices by JAX's collectives and lax.ppermute only.
A program may use at most 64 MiB of HBM per device.

v0:
```python
import math

import jax
import jax.numpy as jnp
from jax import lax
from jax.sharding import PartitionSpec as P

IMAGE = 65536
XM = 512
WM = 128
XA = 448


TAU = 2.0 * math.pi


def extended(block, sides, width):
    for axis, dim in sides:
        count = lax.axis_size(axis)
        forward = [(i, i + 1) for i in range(count - 1)]
        forward.append((count - 1, 0))
        backward = [(target, source) for source, target in forward]
        low = lax.ppermute(
            lax.slice_in_dim(block, block.shape[dim] - width, None, axis=dim), axis, forward
        )
        high = lax.ppermute(lax.slice_in_dim(block, 0, width, axis=dim), axis, backward)
        block = jnp.concatenate([low, block, high], axis=dim)
    return block


def passed_along(block, axis, distance):
    devices = range(lax.axis_size(axis))
    route = [((i - distance) % len(devices), i) for i in devices]
    return lax.ppermute(block, axis, route)


def modular(first, second, image):
    upper = second // 256
    lower = second % 256
    return (first * upper % (image // 256) * 256 + first * lower) % image


def make_table(facets):
    place = jnp.arange(WM, dtype=jnp.int32)
    cell = jnp.arange(XM, dtype=jnp.int32)
    turns = (place[:, None] - WM // 2) * (cell[None, :] - XM // 2) % XM
    angle = TAU * turns.astype(jnp.float32) / XM
    relative = (place.astype(jnp.float32) + 0.5 - WM / 2.0) / (WM / 2.0)
    taper = (0.3 + 0.7 * (1.0 - relative * relative)) / jnp.sqrt(jnp.float32(WM * facets))
    return (
        (taper[:, None] * jnp.cos(angle)).astype(jnp.bfloat16),
        (taper[:, None] * jnp.sin(angle)).astype(jnp.bfloat16),
    )


def phases(column_pos, offsets, indices, length):
    first = modular(column_pos, offsets[0], IMAGE)
    second = indices * offsets[1] % length
    return TAU * (first.astype(jnp.float32) / IMAGE + second.astype(jnp.float32) / length)


def per_device(facet_spectra, facet_offsets, column_index, subgrid_offsets, weights):
    spectra = facet_spectra[:, 0]
    cols = spectra.shape[0]
    shard = spectra.shape[3]
    half = WM // 2
    facets = lax.axis_size("facet")
    length = shard * lax.axis_size("col")
    here = lax.axis_index("col")
    offsets = facet_offsets[0]
    real_tab, imag_tab = make_table(facets)
    padded = extended(spectra, (("col", 3),), half)
    grids = []
    buffers = []
    for column in range(cols):
        centres = subgrid_offsets[column] // (IMAGE // length)
        starts = centres - here * shard
        indices = (centres[:, None] - half + jnp.arange(WM, dtype=jnp.int32)[None, :]) % length
        column_pos = column_index[column] * XA
        angle = phases(column_pos, offsets, indices, length)
        cosine = jnp.cos(angle)
        sine = jnp.sin(angle)
        windows = jnp.stack([lax.dynamic_slice_in_dim(padded[column], starts[0], WM, 2)], axis=2)
        window = windows.astype(jnp.float32)
        phased_real = (window[0] * cosine + window[1] * sine).astype(jnp.bfloat16)
        phased_imag = (window[1] * cosine - window[0] * sine).astype(jnp.bfloat16)
        phased = jnp.stack([phased_real, phased_imag]).astype(jnp.float32)
        summed = lax.psum_scatter(
            phased.astype(jnp.bfloat16), "facet", scatter_dimension=1, tiled=True
        ).astype(jnp.float32)
        real_hi = real_tab.astype(jnp.float32)
        imag_hi = imag_tab.astype(jnp.float32)
        grid_real = jnp.einsum(
            "xsm,ml->sxl", summed[0], real_hi, precision=lax.Precision.HIGHEST
        ) - jnp.einsum("xsm,ml->sxl", summed[1], imag_hi, precision=lax.Precision.HIGHEST)
        grid_imag = jnp.einsum(
            "xsm,ml->sxl", summed[0], imag_hi, precision=lax.Precision.HIGHEST
        ) + jnp.einsum("xsm,ml->sxl", summed[1], real_hi, precision=lax.Precision.HIGHEST)
        grid = jnp.stack([grid_real, grid_imag], axis=1).astype(jnp.bfloat16)
        grids.append(grid)
        scaled = (grid.astype(jnp.float32) * weights[column].astype(jnp.float32)[:, None]).astype(
            jnp.bfloat16
        )
        back_real = jnp.einsum(
            "sxl,ml->sxm", scaled[:, 0], real_tab, preferred_element_type=jnp.float32
        ) + jnp.einsum("sxl,ml->sxm", scaled[:, 1], imag_tab, preferred_element_type=jnp.float32)
        back_imag = jnp.einsum(
            "sxl,ml->sxm", scaled[:, 1], real_tab, preferred_element_type=jnp.float32
        ) - jnp.einsum("sxl,ml->sxm", scaled[:, 0], imag_tab, preferred_element_type=jnp.float32)
        projected = lax.all_gather(
            jnp.stack([back_real, back_imag], axis=1), "facet", axis=2, tiled=True
        )
        upd_real = projected[:, 0] * cosine[:, None, :] - projected[:, 1] * sine[:, None, :]
        upd_imag = projected[:, 1] * cosine[:, None, :] + projected[:, 0] * sine[:, None, :]
        buffer = jnp.zeros((2, XM, shard + WM), jnp.float32)
        update = jnp.stack([upd_real[0], upd_imag[0]])
        buffer = lax.dynamic_update_slice_in_dim(buffer, update, starts[0], 2)
        buffers.append(buffer)
    stacked = jnp.stack(buffers)
    lower_part = stacked[..., :half]
    upper_part = stacked[..., shard + half :]
    middle = stacked[..., half : shard + half]
    from_below = passed_along(upper_part.astype(jnp.bfloat16), "col", 1).astype(upper_part.dtype)
    from_above = passed_along(lower_part.astype(jnp.bfloat16), "col", -1).astype(lower_part.dtype)
    middle = middle.at[..., :half].add(from_below)
    middle = middle.at[..., shard - half :].add(from_above)
    return (jnp.stack(grids), middle.astype(jnp.bfloat16)[:, None])


def solution(mesh):
    in_specs = (
        P(None, "facet", None, None, "col"),
        P("facet", None),
        P(),
        P(None, "col"),
        P(None, "col", "facet", None),
    )
    out_specs = (P(None, "col", None, "facet", None), P(None, "facet", None, None, "col"))
    return jax.shard_map(
        per_device, mesh=mesh, in_specs=in_specs, out_specs=out_specs, check_vma=False
    )
```

profile of v0, /device:TPU:0, one launch (start us, length us, event | category | flops | bytes accessed | tf_op | source)
XLA Modules:
  0.0 192.7 jit_solution(12361966203086080229)
XLA Ops:
  8.6 6.1 %collective-permute-start.1 = (bf16[2,2,512,64]{3,2,1,0:T(8,128)(2,1)S(1)}, bf16[2,2,512,64]{3,2,1,0:T(8,128)(2,1)S(1)}, u32[]{:S(2)}, u32[]{:S(2)}) collective-permute-start(bf16[2,2,512,64]{3,2,1,0:T(8,128)(2,1)S(1)} %get-tuple-element.32), channel_id=1, source_target_pairs={{1,0},{2,1},{3,2},{4,3},{5,4},{6,5},{7,6},{0,7},{9,8},{10,9},{11,1... | collective-permute-start | bytes 786440 | tf_op jit(solution)/shard_map/ppermute | solution.py:26
  30.4 4.5 %collective-permute-done.1 = bf16[2,2,512,64]{3,2,1,0:T(8,128)(2,1)S(1)} collective-permute-done((bf16[2,2,512,64]{3,2,1,0:T(8,128)(2,1)S(1)}, bf16[2,2,512,64]{3,2,1,0:T(8,128)(2,1)S(1)}, u32[]{:S(2)}, u32[]{:S(2)}) %collective-permute-start.1) | collective-permute-done | bytes 262176 | tf_op jit(solution)/shard_map/ppermute | solution.py:26
  35.0 9.2 %concatenate.43 = bf16[2,2,512,1152]{3,2,1,0:T(8,128)(2,1)} concatenate(bf16[2,2,512,64]{3,2,1,0:T(8,128)(2,1)S(1)} %collective-permute-done, bf16[2,2,512,1024]{3,2,1,0:T(8,128)(2,1)} %bitcast.143, bf16[2,2,512,64]{3,2,1,0:T(8,128)(2,1)S(1)} %collective-permute-done.1), dimensions={3} | concatenate | bytes 9437184 | tf_op jit(solution)/shard_map/concatenate | solution.py:27
  44.3 2.7 %fusion.106 = (bf16[1,2,512,1152]{3,2,1,0:T(8,128)(2,1)S(1)}, bf16[1,2,512,1152]{3,2,1,0:T(8,128)(2,1)S(1)}) fusion(bf16[2,2,512,1152]{3,2,1,0:T(8,128)(2,1)} %concatenate.43), kind=kLoop, calls=%fused_computation.180 | loop fusion | bytes 9437184 | tf_op jit(solution)/shard_map/slice | solution.py:83
  49.2 20.5 %reduce-scatter.5.cloned.1.call-done = bf16[2,128,1,128]{3,1,2,0:T(8,128)(2,1)} async-done(((bf16[2,512,1,128]{3,1,2,0:T(8,128)(2,1)}), bf16[2,128,1,128]{3,1,2,0:T(8,128)(2,1)}) %reduce-scatter.5.cloned.1.call-update) | async-done | bytes 65552 | tf_op jit(solution)/shard_map/reduce_scatter | solution.py:88
  69.8 2.0 %fusion.21 = f32[512,128]{1,0:T(8,128)S(1)} fusion(s32[512]{0:T(512)S(1)} %iota_add_fusion, s32[128]{0:T(128)S(1)} %iota_add_fusion.1, f32[128]{0:T(128)S(1)} %add_multiply_fusion, bf16[2,128,1,128]{3,1,2,0:T(8,128)(2,1)} %reduce-scatter.5.cloned.1.call-done), kind=kOutput, calls=%fused_computation.76 | convolution fusion | flops 17825792 | bytes 297984 | tf_op jit(solution)/shard_map/xsm,ml->sxl/dot_general | solution.py:96
  75.7 2.0 %fusion.4 = bf16[512,128]{1,0:T(8,128)(2,1)S(1)} fusion(f32[512,128]{1,0:T(8,128)S(1)} %fusion.19, s32[512]{0:T(512)S(1)} %iota_add_fusion, s32[128]{0:T(128)S(1)} %iota_add_fusion.1, f32[128]{0:T(128)S(1)} %add_multiply_fusion, bf16[2,128,1,128]{3,1,2,0:T(8,128)(2,1)} %reduce-scatter.5.cloned.1.call-done), kind=kOutput, calls=%fused_computation.14 | convolution fusion | flops 17956864 | bytes 429056 | tf_op jit(solution)/shard_map/xsm,ml->sxl/dot_general | solution.py:95
  80.1 12.7 %reduce-scatter.3.cloned.1.call-done = bf16[2,128,1,128]{3,1,2,0:T(8,128)(2,1)} async-done(((bf16[2,512,1,128]{3,1,2,0:T(8,128)(2,1)}), bf16[2,128,1,128]{3,1,2,0:T(8,128)(2,1)}) %reduce-scatter.3.cloned.1.call-update) | async-done | bytes 65552 | tf_op jit(solution)/shard_map/reduce_scatter | solution.py:88
  92.9 2.0 %fusion.22 = f32[512,128]{1,0:T(8,128)S(1)} fusion(s32[512]{0:T(512)S(1)} %iota_add_fusion, s32[128]{0:T(128)S(1)} %iota_add_fusion.1, f32[128]{0:T(128)S(1)} %add_multiply_fusion, bf16[2,128,1,128]{3,1,2,0:T(8,128)(2,1)} %reduce-scatter.3.cloned.1.call-done), kind=kOutput, calls=%fused_computation.77 | convolution fusion | flops 17825792 | bytes 297984 | tf_op jit(solution)/shard_map/xsm,ml->sxl/dot_general | solution.py:96
  96.8 2.0 %fusion.3 = bf16[512,128]{1,0:T(8,128)(2,1)S(1)} fusion(f32[512,128]{1,0:T(8,128)S(1)} %fusion.22, s32[512]{0:T(512)S(1)} %iota_add_fusion, s32[128]{0:T(128)S(1)} %iota_add_fusion.1, f32[128]{0:T(128)S(1)} %add_multiply_fusion, bf16[2,128,1,128]{3,1,2,0:T(8,128)(2,1)} %reduce-scatter.3.cloned.1.call-done), kind=kOutput, calls=%fused_computation.13 | convolution fusion | flops 17956864 | bytes 429056 | tf_op jit(solution)/shard_map/xsm,ml->sxl/dot_general | solution.py:98
  98.8 2.0 %fusion.2 = bf16[512,128]{1,0:T(8,128)(2,1)S(1)} fusion(f32[512,128]{1,0:T(8,128)S(1)} %fusion.20, s32[512]{0:T(512)S(1)} %iota_add_fusion, s32[128]{0:T(128)S(1)} %iota_add_fusion.1, f32[128]{0:T(128)S(1)} %add_multiply_fusion, bf16[2,128,1,128]{3,1,2,0:T(8,128)(2,1)} %reduce-scatter.3.cloned.1.call-done), kind=kOutput, calls=%fused_computation.12 | convolution fusion | flops 17956864 | bytes 429056 | tf_op jit(solution)/shard_map/xsm,ml->sxl/dot_general | solution.py:95
  109.3 6.6 %all_gather.6 = f32[1,2,512,128]{3,2,1,0:T(8,128)S(1)} all-gather(f32[1,2,128,128]{3,2,1,0:T(8,128)S(1)} %pad_maximum_fusion.3), channel_id=1, replica_groups=mesh['facet'=4,'col'=8] {'facet'}, dimensions={2}, use_global_device_ids=true | all-gather | bytes 655360 | tf_op jit(solution)/shard_map/all_gather | solution.py:110
  116.0 7.3 %all_gather.7 = f32[1,2,512,128]{3,2,1,0:T(8,128)S(1)} all-gather(f32[1,2,128,128]{3,2,1,0:T(8,128)S(1)} %pad_maximum_fusion.4), channel_id=1, replica_groups=mesh['facet'=4,'col'=8] {'facet'}, dimensions={2}, use_global_device_ids=true | all-gather | bytes 655360 | tf_op jit(solution)/shard_map/all_gather | solution.py:110
  123.4 2.4 %stack.91.clone = f32[1,2,512,1152]{3,2,1,0:T(8,128)} broadcast(f32[]{:T(128)} %constant.242.clone.1), dimensions={} | broadcast | bytes 4718596 | tf_op jit(solution)/shard_map/stack | solution.py:119
  125.8 3.8 %dynamic_update_slice.8 = f32[1,2,512,1152]{3,2,1,0:T(8,128)} dynamic-update-slice(f32[1,2,512,1152]{3,2,1,0:T(8,128)} %stack.91.clone, f32[1,2,512,128]{3,2,1,0:T(8,128)S(1)} %maximum_bitcast_fusion, s32[]{:T(128)} %constant.216.clone.1, s32[]{:T(128)} %constant.216.clone.1, s32[]{:T(128)} %constant.216.clone.1, s32[]{:T(128)S(6)} %select_n.142) | dynamic-update-slice | bytes 1048580 | tf_op jit(solution)/shard_map/dynamic_update_slice | solution.py:117
  129.6 2.5 %stack.91.clone.1 = f32[1,2,512,1152]{3,2,1,0:T(8,128)} broadcast(f32[]{:T(128)} %constant.242.clone.1), dimensions={} | broadcast | bytes 4718596 | tf_op jit(solution)/shard_map/stack | solution.py:119
  132.1 3.6 %dynamic_update_slice.9 = f32[1,2,512,1152]{3,2,1,0:T(8,128)} dynamic-update-slice(f32[1,2,512,1152]{3,2,1,0:T(8,128)} %stack.91.clone.1, f32[1,2,512,128]{3,2,1,0:T(8,128)S(1)} %maximum_bitcast_fusion.1, s32[]{:T(128)} %constant.216.clone.1, s32[]{:T(128)} %constant.216.clone.1, s32[]{:T(128)} %constant.216.clone.1, s32[]{:T(128)S(6)} %select_n.150) | dynamic-update-slice | bytes 1048580 | tf_op jit(solution)/shard_map/dynamic_update_slice | solution.py:117
  135.7 4.6 %fusion = bf16[2,2,512,1152]{3,2,1,0:T(8,128)(2,1)S(1)} fusion(f32[1,2,512,1152]{3,2,1,0:T(8,128)} %dynamic_update_slice.9, f32[1,2,512,1152]{3,2,1,0:T(8,128)} %dynamic_update_slice.8), kind=kLoop, calls=%fused_computation.5 | loop fusion | flops 2359296 | bytes 14155776 | tf_op jit(solution)/shard_map/convert.3
  140.5 4.3 %collective-permute-start.3 = (bf16[2,2,512,64]{3,2,1,0:T(8,128)(2,1)S(1)}, bf16[2,2,512,64]{3,2,1,0:T(8,128)(2,1)S(1)}, u32[]{:S(2)}, u32[]{:S(2)}) collective-permute-start(bf16[2,2,512,64]{3,2,1,0:T(8,128)(2,1)S(1)} %get-tuple-element.28), channel_id=1, source_target_pairs={{1,0},{2,1},{3,2},{4,3},{5,4},{6,5},{7,6},{0,7},{9,8},{10,9},{11,1... | collective-permute-start | bytes 786440 | tf_op jit(solution)/shard_map/ppermute | solution.py:34
  144.9 4.9 %fusion.1 = f32[2,2,512,1024]{3,2,1,0:T(8,128)} fusion(f32[1,2,512,1152]{3,2,1,0:T(8,128)S(1)} %bitcast.141, f32[1,2,512,1152]{3,2,1,0:T(8,128)S(1)} %copy-done), kind=kLoop, calls=%fused_computation.6 | loop fusion | flops 2097152 | bytes 17825792 | tf_op jit(solution)/shard_map/stack | solution.py:119
  149.7 16.6 %collective-permute-done.2 = bf16[2,2,512,64]{3,2,1,0:T(8,128)(2,1)S(1)} collective-permute-done((bf16[2,2,512,64]{3,2,1,0:T(8,128)(2,1)S(1)}, bf16[2,2,512,64]{3,2,1,0:T(8,128)(2,1)S(1)}, u32[]{:S(2)}, u32[]{:S(2)}) %collective-permute-start.2) | collective-permute-done | bytes 262176 | tf_op jit(solution)/shard_map/ppermute | solution.py:34
  166.7 5.8 %scatter-add.6 = f32[2,2,512,1024]{3,2,1,0:T(8,128)} dynamic-update-slice(f32[2,2,512,1024]{3,2,1,0:T(8,128)} %fusion.1, f32[2,2,512,64]{3,2,1,0:T(8,128)S(1)} %fusion.11, s32[]{:T(128)} %constant.216.clone.1, s32[]{:T(128)} %constant.216.clone.1, s32[]{:T(128)} %constant.216.clone.1, s32[]{:T(128)} %constant.216.clone.1) | dynamic-update-slice | bytes 1048580 | tf_op jit(solution)/shard_map/scatter-add | solution.py:125
  174.0 5.8 %scatter-add.9 = f32[2,2,512,1024]{3,2,1,0:T(8,128)} dynamic-update-slice(f32[2,2,512,1024]{3,2,1,0:T(8,128)} %scatter-add.6, f32[2,2,512,64]{3,2,1,0:T(8,128)S(1)} %slice_add_fusion, s32[]{:T(128)} %constant.216.clone.1, s32[]{:T(128)} %constant.216.clone.1, s32[]{:T(128)} %constant.216.clone.1, s32[]{:T(128)} %constant.243.clone.1) | dynamic-update-slice | bytes 1048580 | tf_op jit(solution)/shard_map/scatter-add | solution.py:126
  179.8 6.1 %convert_bitcast_fusion = bf16[2,1,2,512,1024]{4,3,2,1,0:T(8,128)(2,1)} fusion(f32[2,2,512,1024]{3,2,1,0:T(8,128)} %scatter-add.9), kind=kLoop, calls=%fused_computation.7 | loop fusion | flops 2097152 | bytes 12582912 | tf_op jit(solution)/shard_map/broadcast_in_dim | solution.py:127
  (56 shorter events, 29.4 us)
Async XLA Ops:
  7.2 62.6 %reduce-scatter.5.cloned.1.call-start = ((), (), s32[]{:S(2)}) async-start(), calls=%async_computation.3 | async-start | bytes 327680 | tf_op jit(solution)/shard_map/reduce_scatter | solution.py:88
  8.6 26.2 %collective-permute-start.1 = (bf16[2,2,512,64]{3,2,1,0:T(8,128)(2,1)S(1)}, bf16[2,2,512,64]{3,2,1,0:T(8,128)(2,1)S(1)}, u32[]{:S(2)}, u32[]{:S(2)}) collective-permute-start(bf16[2,2,512,64]{3,2,1,0:T(8,128)(2,1)S(1)} %get-tuple-element.32), channel_id=1, source_target_pairs={{1,0},{2,1},{3,2},{4,3},{5,4},{6,5},{7,6},{0,7},{9,8},{10,9},{11,1... | collective-permute-start | bytes 786440 | tf_op jit(solution)/shard_map/ppermute | solution.py:26
  14.7 20.3 %collective-permute-start = (bf16[2,2,512,64]{3,2,1,0:T(8,128)(2,1)S(1)}, bf16[2,2,512,64]{3,2,1,0:T(8,128)(2,1)S(1)}, u32[]{:S(2)}, u32[]{:S(2)}) collective-permute-start(bf16[2,2,512,64]{3,2,1,0:T(8,128)(2,1)S(1)} %get-tuple-element.33), channel_id=1, source_target_pairs={{0,1},{1,2},{2,3},{3,4},{4,5},{5,6},{6,7},{7,0},{8,9},{9,10},{10,1... | collective-permute-start | bytes 786440 | tf_op jit(solution)/shard_map/ppermute | solution.py:23
  48.1 44.8 %reduce-scatter.3.cloned.1.call-start = ((), (), s32[]{:S(2)}) async-start(), calls=%async_computation.2 | async-start | bytes 327680 | tf_op jit(solution)/shard_map/reduce_scatter | solution.py:88
  132.1 12.7 %slice-start = ((s8[4718592]{0:T(1024)(128)(4,1)}), s8[524288]{0:T(1024)(128)(4,1)S(1)}, s32[]{:S(2)}) async-start(s8[4718592]{0:T(1024)(128)(4,1)} %bitcast.140), calls=%async_computation.4 | async-start | bytes 1048576
  135.7 9.2 %copy-start = (f32[1,2,512,1152]{3,2,1,0:T(8,128)S(1)}, f32[1,2,512,1152]{3,2,1,0:T(8,128)}, u32[]{:S(2)}) copy-start(f32[1,2,512,1152]{3,2,1,0:T(8,128)} %dynamic_update_slice.9) | copy-start | bytes 14155780
  135.7 9.2 %slice-start.1 = ((s8[4718592]{0:T(1024)(128)(4,1)}), s8[4194304]{0:T(1024)(128)(4,1)S(1)}, s32[]{:S(2)}) async-start(s8[4718592]{0:T(1024)(128)(4,1)} %bitcast.140), calls=%async_computation.5 | async-start | bytes 8388608
  140.5 31.9 %collective-permute-start.3 = (bf16[2,2,512,64]{3,2,1,0:T(8,128)(2,1)S(1)}, bf16[2,2,512,64]{3,2,1,0:T(8,128)(2,1)S(1)}, u32[]{:S(2)}, u32[]{:S(2)}) collective-permute-start(bf16[2,2,512,64]{3,2,1,0:T(8,128)(2,1)S(1)} %get-tuple-element.28), channel_id=1, source_target_pairs={{1,0},{2,1},{3,2},{4,3},{5,4},{6,5},{7,6},{0,7},{9,8},{10,9},{11,1... | collective-permute-start | bytes 786440 | tf_op jit(solution)/shard_map/ppermute | solution.py:34
  144.9 21.5 %collective-permute-start.2 = (bf16[2,2,512,64]{3,2,1,0:T(8,128)(2,1)S(1)}, bf16[2,2,512,64]{3,2,1,0:T(8,128)(2,1)S(1)}, u32[]{:S(2)}, u32[]{:S(2)}) collective-permute-start(bf16[2,2,512,64]{3,2,1,0:T(8,128)(2,1)S(1)} %get-tuple-element.29), channel_id=1, source_target_pairs={{7,0},{0,1},{1,2},{2,3},{3,4},{4,5},{5,6},{6,7},{15,8},{8,9},{9,10... | collective-permute-start | bytes 786440 | tf_op jit(solution)/shard_map/ppermute | solution.py:34
Sparse Core Ops, SparseCore 0:
  48.2 21.5 reduce-scatter.4
  72.8 20.0 reduce-scatter.2
where the time goes:
time: 194 us; the launch traced here: 193 us
  waiting for transfers between devices  54.5 us (28%)
  local copies, waits for them, and re-layouts  42.8 us (22%)
  matrix products  25.5 us (13%)
  between operations  23.5 us (12%)
  other arithmetic  22 us (11%)
  blocking collectives  13.8 us (7%)
  starting transfers between devices  10.5 us (5%)
    reduce_scatter x2, waiting for transfers between devices, per_device(): lax.psum_scatter(phased.astype(jnp.bfloat16), 'facet', scatter_dimension=...  33.3 us
    ppermute x2, waiting for transfers between devices, passed_along(): return lax.ppermute(block, axis, route)  16.6 us
    all_gather x2, blocking collectives, per_device(): lax.all_gather(jnp.stack([back_real, back_imag], axis=1), 'facet', axis=2...  13.8 us
    concatenate x1, local copies, waits for them, and re-layouts, extended(): block = jnp.concatenate([low, block, high], axis=dim)  9.25 us
    dynamic_update_slice x2, local copies, waits for them, and re-layouts, per_device(): buffer = lax.dynamic_update_slice_in_dim(buffer, update, starts[0], 2)  7.37 us
    ppermute x1, starting transfers between devices, extended(): lax.ppermute(lax.slice_in_dim(block, 0, width, axis=dim), axis, backward)  6.09 us
    broadcast_in_dim x1, other arithmetic, per_device(): return (jnp.stack(grids), middle.astype(jnp.bfloat16)[:, None])  6.06 us
    scatter-add x1, local copies, waits for them, and re-layouts, per_device(): middle = middle.at[..., shard - half:].add(from_above)  5.83 us
  transfers between devices with their start and end apart: 6, of which 5 were waited for; matrix products, arithmetic and copies ran while one was open for 15% of the time, Pallas kernels for 0%

commit v1 on v0

v1 whole, which is shorter than its diff:
```python
import functools
import math

import jax
import jax.numpy as jnp
from jax import lax
from jax.experimental import pallas as pl
from jax.experimental.pallas import tpu as pltpu
from jax.sharding import PartitionSpec as P

IMAGE = 65536
XM = 512
WM = 128
XA = 448
LANES = 128
HALF = WM // 2

TAU = 2.0 * math.pi

VMEM = pl.BlockSpec(memory_space=pltpu.VMEM)
SMEM = pl.BlockSpec(memory_space=pltpu.SMEM)
ANY = pl.BlockSpec(memory_space=pl.ANY)


def make_table(facets):
    place = jnp.arange(WM, dtype=jnp.int32)
    cell = jnp.arange(XM, dtype=jnp.int32)
    turns = (place[:, None] - WM // 2) * (cell[None, :] - XM // 2) % XM
    angle = TAU * turns.astype(jnp.float32) / XM
    relative = (place.astype(jnp.float32) + 0.5 - WM / 2.0) / (WM / 2.0)
    taper = (0.3 + 0.7 * (1.0 - relative * relative)) / jnp.sqrt(jnp.float32(WM * facets))
    return (
        (taper[:, None] * jnp.cos(angle)).astype(jnp.bfloat16),
        (taper[:, None] * jnp.sin(angle)).astype(jnp.bfloat16),
    )


def remainder(value, modulus):
    if modulus & (modulus - 1) == 0:
        return value & (modulus - 1)
    return lax.rem(value, jnp.int32(modulus))


def modular(first, second, image):
    upper = second // 256
    lower = remainder(second, 256)
    return remainder(remainder(first * upper, image // 256) * 256 + first * lower, image)


def place_of(subgrid_offset, here, shard, length):
    start = subgrid_offset // (IMAGE // length) - here * shard - HALF + LANES
    return lax.div(start, jnp.int32(LANES)) - 1, remainder(start, LANES)


def lanes_of(shape):
    return lax.broadcasted_iota(jnp.int32, shape, len(shape) - 1)


def spectrum_kernel(
    cols, facets, length, offsets, column, subgrid, spectra, send, keep, turn, buf, sems
):
    shard = spectra.shape[4]
    tiles = shard // LANES
    block = XM // facets
    here = lax.axis_index("col")
    facet = lax.axis_index("facet")
    copies = []
    places = []
    for c in range(cols):
        tile, lane = place_of(subgrid[c, 0], here, shard, length)
        places.append((tile, lane))
        low = jnp.maximum(tile, 0)
        high = jnp.minimum(tile + 1, tiles - 1)
        for slot, which in enumerate((low, high, 0, tiles - 1)):
            at = which * LANES
            if not isinstance(at, int):
                at = pl.multiple_of(at, LANES)
            copy = pltpu.make_async_copy(
                spectra.at[c, 0, :, :, pl.ds(at, LANES)], buf.at[c, slot], sems.at[c, slot]
            )
            copy.start()
            copies.append(copy)
    lanes = lanes_of((1, LANES))
    base = here * shard
    for c in range(cols):
        tile, lane = places[c]
        first = modular(column[c] * XA, offsets[0, 0], IMAGE).astype(jnp.float32)
        at = base + lanes + jnp.where(lanes >= lane, tile, tile + 1) * LANES
        at = remainder(at + length, length)
        edge = base + lanes + jnp.where(lanes < HALF, 0, shard - LANES)
        for kind, index in enumerate((at, edge)):
            second = remainder(index * offsets[0, 1], length)
            angle = TAU * (first / IMAGE + second.astype(jnp.float32) / length)
            row = (c * 2 + kind) * 2
            turn[row : row + 1, :] = jnp.cos(angle)
            turn[row + 1 : row + 2, :] = jnp.sin(angle)
    for c in range(cols):
        tile, lane = places[c]
        for slot in range(4):
            copies[c * 4 + slot].wait()
        from_low = jnp.logical_and(lanes >= lane, tile >= 0)
        from_high = jnp.logical_and(lanes < lane, tile + 1 < tiles)
        for s in range(facets):
            rows = pl.ds(pl.multiple_of((facet ^ s) * block, block), block)
            target = send if s % 2 else keep
            parts = []
            for part in range(2):
                zero = jnp.zeros((block, LANES), jnp.float32)
                parts.append(
                    jnp.where(from_low, buf[c, 0, part, rows, :].astype(jnp.float32), zero)
                    + jnp.where(from_high, buf[c, 1, part, rows, :].astype(jnp.float32), zero)
                )
            row = c * 4
            cosine = turn[row : row + 1, :]
            sine = turn[row + 1 : row + 2, :]
            target[0, s // 2, c, 0] = (parts[0] * cosine + parts[1] * sine).astype(jnp.bfloat16)
            target[0, s // 2, c, 1] = (parts[1] * cosine - parts[0] * sine).astype(jnp.bfloat16)
            cosine = turn[row + 2 : row + 3, :]
            sine = turn[row + 3 : row + 4, :]
            parts = []
            for part in range(2):
                parts.append(
                    jnp.where(
                        lanes < HALF,
                        buf[c, 2, part, rows, :].astype(jnp.float32),
                        buf[c, 3, part, rows, :].astype(jnp.float32),
                    )
                )
            real = parts[0] * cosine + parts[1] * sine
            imag = parts[1] * cosine - parts[0] * sine
            real_turned = pltpu.roll(real, HALF, 1)
            imag_turned = pltpu.roll(imag, HALF, 1)
            target[1, s // 2, c, 0] = jnp.where(lanes < HALF, real, imag_turned).astype(
                jnp.bfloat16
            )
            target[1, s // 2, c, 1] = jnp.where(lanes < HALF, real_turned, imag).astype(
                jnp.bfloat16
            )


def subgrid_kernel(
    cols,
    length,
    shard,
    subgrid,
    main,
    from_prev,
    from_next,
    table,
    weights,
    grids,
    back,
    to_prev,
    to_next,
    stack,
    scaled,
):
    tiles = shard // LANES
    block = main.shape[2]
    here = lax.axis_index("col")
    lanes = lanes_of((1, LANES))
    for c in range(cols):
        tile, lane = place_of(subgrid[c, 0], here, shard, length)
        low = jnp.logical_and(lanes >= lane, tile < 0)
        high = jnp.logical_and(lanes < lane, tile + 1 >= tiles)
        prev = from_prev[c].astype(jnp.float32)
        nxt = from_next[c].astype(jnp.float32)
        shift = remainder(LANES - lane, LANES)
        zero = jnp.zeros((block, LANES), jnp.float32)
        real = main[c, 0].astype(jnp.float32)
        real = real + jnp.where(low, pltpu.roll(prev, HALF, 1), zero)
        real = real + jnp.where(high, nxt, zero)
        imag = main[c, 1].astype(jnp.float32)
        imag = imag + jnp.where(low, prev, zero)
        imag = imag + jnp.where(high, pltpu.roll(nxt, HALF, 1), zero)
        rows = slice(c * block, (c + 1) * block)
        stack[rows, :WM] = pltpu.roll(real, shift, 1).astype(jnp.bfloat16)
        stack[rows, WM:] = pltpu.roll(imag, shift, 1).astype(jnp.bfloat16)
    for part in range(2):
        span = slice(part * XM, (part + 1) * XM)
        product = jnp.dot(stack[...], table[:, span], preferred_element_type=jnp.float32)
        rounded = product.astype(jnp.bfloat16)
        for c in range(cols):
            rows = slice(c * block, (c + 1) * block)
            piece = rounded[rows]
            grids[c, 0, part] = piece
            scaled[rows, span] = (
                piece.astype(jnp.float32) * weights[c, 0].astype(jnp.float32)
            ).astype(jnp.bfloat16)
    result = lax.dot_general(
        scaled[...],
        table[...],
        (((1,), (1,)), ((), ())),
        preferred_element_type=jnp.float32,
    )
    for c in range(cols):
        tile, lane = place_of(subgrid[c, 0], here, shard, length)
        rows = slice(c * block, (c + 1) * block)
        low = jnp.logical_and(lanes >= lane, tile < 0)
        high = jnp.logical_and(lanes < lane, tile + 1 >= tiles)
        zero = jnp.zeros((block, LANES), jnp.float32)
        real = pltpu.roll(result[rows, :WM], lane, 1)
        imag = pltpu.roll(result[rows, WM:], lane, 1)
        back[c, 0] = real.astype(jnp.bfloat16)
        back[c, 1] = imag.astype(jnp.bfloat16)
        real_low = jnp.where(low, real, zero)
        imag_low = jnp.where(low, imag, zero)
        real_high = jnp.where(high, real, zero)
        imag_high = jnp.where(high, imag, zero)
        to_prev[c] = (pltpu.roll(real_low, HALF, 1) + imag_low).astype(jnp.bfloat16)
        to_next[c] = (real_high + pltpu.roll(imag_high, HALF, 1)).astype(jnp.bfloat16)


def update_kernel(
    cols, facets, length, subgrid, turn, even, odd, even_edge, odd_edge, out
):
    shard = out.shape[4]
    tiles = shard // LANES
    block = XM // facets
    here = lax.axis_index("col")
    facet = lax.axis_index("facet")
    lanes = lanes_of((1, LANES))
    c = pl.program_id(0)
    tile, lane = place_of(subgrid[c, 0], here, shard, length)
    out[...] = jnp.zeros(out.shape, jnp.bfloat16)
    low_at = pl.ds(pl.multiple_of(jnp.maximum(tile, 0) * LANES, LANES), LANES)
    high_at = pl.ds(pl.multiple_of(jnp.minimum(tile + 1, tiles - 1) * LANES, LANES), LANES)
    row = c * 4
    cosine = turn[pl.ds(row, 1), :]
    sine = turn[pl.ds(row + 1, 1), :]
    edge_cosine = turn[pl.ds(row + 2, 1), :]
    edge_sine = turn[pl.ds(row + 3, 1), :]
    is_low = lanes >= lane
    is_left = lanes < HALF
    first_low = jnp.logical_and(is_low, tile == 0)
    first_high = jnp.logical_and(jnp.logical_not(is_low), tile == -1)
    last_low = jnp.logical_and(is_low, tile == tiles - 1)
    last_high = jnp.logical_and(jnp.logical_not(is_low), tile == tiles - 2)
    in_first = jnp.logical_or(first_low, first_high)
    in_last = jnp.logical_or(last_low, last_high)
    for s in range(facets):
        source = odd if s % 2 else even
        edges = odd_edge if s % 2 else even_edge
        rows = pl.ds(pl.multiple_of((facet ^ s) * block, block), block)
        zero = jnp.zeros((block, LANES), jnp.float32)
        real = source[s // 2, c, 0].astype(jnp.float32)
        imag = source[s // 2, c, 1].astype(jnp.float32)
        whole = (real * cosine - imag * sine, imag * cosine + real * sine)
        prev = edges[s // 2, 0, c].astype(jnp.float32)
        nxt = edges[s // 2, 1, c].astype(jnp.float32)
        real = jnp.where(is_left, prev, pltpu.roll(nxt, HALF, 1))
        imag = jnp.where(is_left, pltpu.roll(prev, HALF, 1), nxt)
        ends = (
            real * edge_cosine - imag * edge_sine,
            imag * edge_cosine + real * edge_sine,
        )
        for part in range(2):
            value = whole[part]
            end = ends[part]
            out[0, 0, part, rows, low_at] = jnp.where(is_low, value, zero).astype(jnp.bfloat16)
            out[0, 0, part, rows, high_at] = jnp.where(is_low, zero, value).astype(jnp.bfloat16)
            out[0, 0, part, rows, :LANES] = (
                jnp.where(is_left, end, zero) + jnp.where(in_first, value, zero)
            ).astype(jnp.bfloat16)
            out[0, 0, part, rows, shard - LANES :] = (
                jnp.where(is_left, zero, end) + jnp.where(in_last, value, zero)
            ).astype(jnp.bfloat16)


def swapped(block, bit):
    facets = lax.axis_size("facet")
    return lax.ppermute(block, "facet", [(i, i ^ bit) for i in range(facets)])


def shifted(block, distance):
    count = lax.axis_size("col")
    return lax.ppermute(block, "col", [(i, (i + distance) % count) for i in range(count)])


def added(kept, received):
    return (kept.astype(jnp.float32) + received.astype(jnp.float32)).astype(jnp.bfloat16)


def reduced(blocks, facets):
    bit = 2
    while bit < facets:
        kept, sent = blocks[0::2], blocks[1::2]
        blocks = added(kept, swapped(sent, bit))
        bit *= 2
    return blocks[0]


def gathered(block, facets):
    blocks = block[None]
    bit = facets // 2
    while bit > 1:
        received = swapped(blocks, bit)
        blocks = jnp.stack([blocks, received], axis=1).reshape((-1,) + blocks.shape[1:])
        bit //= 2
    return blocks, swapped(blocks, 1)


def per_device(facet_spectra, facet_offsets, column_index, subgrid_offsets, weights):
    cols = facet_spectra.shape[0]
    shard = facet_spectra.shape[4]
    facets = lax.axis_size("facet")
    length = shard * lax.axis_size("col")
    block = XM // facets
    bf16 = jnp.bfloat16

    pieces = jax.ShapeDtypeStruct((2, facets // 2, cols, 2, block, LANES), bf16)
    send, keep, turn = pl.pallas_call(
        functools.partial(spectrum_kernel, cols, facets, length),
        out_shape=(pieces, pieces, jax.ShapeDtypeStruct((cols * 4, LANES), jnp.float32)),
        in_specs=[SMEM, SMEM, SMEM, ANY],
        out_specs=(VMEM, VMEM, VMEM),
        scratch_shapes=[
            pltpu.VMEM((cols, 4, 2, XM, LANES), bf16),
            pltpu.SemaphoreType.DMA((cols, 4)),
        ],
        name="spectrum",
    )(facet_offsets, column_index, subgrid_offsets, facet_spectra)

    real_tab, imag_tab = make_table(facets)
    table = jnp.concatenate(
        [
            jnp.concatenate([real_tab, imag_tab], axis=1),
            jnp.concatenate([-imag_tab, real_tab], axis=1),
        ],
        axis=0,
    )

    summed = added(keep, swapped(send, 1))
    edges = reduced(summed[1], facets)
    main = reduced(summed[0], facets)
    from_next = shifted(edges[:, 0], -1)
    from_prev = shifted(edges[:, 1], 1)

    edge = jax.ShapeDtypeStruct((cols, block, LANES), bf16)
    grids, back, to_prev, to_next = pl.pallas_call(
        functools.partial(subgrid_kernel, cols, length, shard),
        out_shape=(
            jax.ShapeDtypeStruct((cols, 1, 2, block, XM), bf16),
            jax.ShapeDtypeStruct((cols, 2, block, LANES), bf16),
            edge,
            edge,
        ),
        in_specs=[SMEM, VMEM, VMEM, VMEM, VMEM, VMEM],
        out_specs=(VMEM, VMEM, VMEM, VMEM),
        scratch_shapes=[
            pltpu.VMEM((cols * block, 2 * WM), bf16),
            pltpu.VMEM((cols * block, 2 * XM), bf16),
        ],
        name="subgrid",
    )(subgrid_offsets, main, from_prev, from_next, table, weights)

    came_prev = shifted(to_next, 1)
    came_next = shifted(to_prev, -1)
    even, odd = gathered(back, facets)
    even_edge, odd_edge = gathered(jnp.stack([came_prev, came_next]), facets)

    def whole(array):
        rank = array.ndim
        return pl.BlockSpec(array.shape, lambda i: (0,) * rank)

    updates = pl.pallas_call(
        functools.partial(update_kernel, cols, facets, length),
        grid=(cols,),
        out_shape=jax.ShapeDtypeStruct((cols, 1, 2, XM, shard), bf16),
        in_specs=[SMEM, whole(turn), whole(even), whole(odd), whole(even_edge), whole(odd_edge)],
        out_specs=pl.BlockSpec((1, 1, 2, XM, shard), lambda i: (i, 0, 0, 0, 0)),
        name="update",
    )(subgrid_offsets, turn, even, odd, even_edge, odd_edge)
    return grids, updates


def solution(mesh):
    in_specs = (
        P(None, "facet", None, None, "col"),
        P("facet", None),
        P(),
        P(None, "col"),
        P(None, "col", "facet", None),
    )
    out_specs = (P(None, "col", None, "facet", None), P(None, "facet", None, None, "col"))
    return jax.shard_map(
        per_device, mesh=mesh, in_specs=in_specs, out_specs=out_specs, check_vma=False
    )
```

time: 194 us -> 53.6 us (0.28)
  local copies, waits for them, and re-layouts: 42.8 us -> 4.4 us
  waiting for transfers between devices: 54.5 us -> 16.1 us
  matrix products: 25.5 us -> 0 us
  between operations: 23.5 us -> 0.75 us
  other arithmetic: 22 us -> 5.42 us
  blocking collectives: 13.8 us -> 0 us
  Pallas kernels: 0 us -> 10.3 us
  starting transfers between devices: 10.5 us -> 16.3 us
    reduce_scatter x2 -> x0, waiting for transfers between devices: 33.3 us -> none  [per_device(): lax.psum_scatter(phased.astype(jnp.bfloat16), 'facet', scatter_dimension=...]
    dot_general x16 -> x0, matrix products: 25.5 us -> none  [the longest x2 3.96 us: per_device(): jnp.einsum('xsm,ml->sxl', summed[1], imag_hi, precision=lax.Precision.HIG...]
    all_gather x2 -> x0, blocking collectives: 13.8 us -> none  [per_device(): lax.all_gather(jnp.stack([back_real, back_imag], axis=1), 'facet', axis=2...]
    scatter-add x2 -> x0, local copies, waits for them, and re-layouts: 11.6 us -> none  [the longest x1 5.83 us: per_device(): middle = middle.at[..., shard - half:].add(from_above)]
    another operation x9 -> x1, other arithmetic: 11 us -> 0.02 us  [gathered(): jnp.stack([blocks, received], axis=1).reshape((-1,) + blocks.shape[1:])]
    pallas_call x0 -> x3, Pallas kernels: none -> 10.3 us  [the longest x1 3.89 us: per_device(): pl.pallas_call(functools.partial(update_kernel, cols, facets, length), gr...]
    concatenate x1 -> x0, local copies, waits for them, and re-layouts: 9.25 us -> none  [extended(): block = jnp.concatenate([low, block, high], axis=dim)]
    slice x6 -> x1, local copies, waits for them, and re-layouts: 8.42 us -> 0.02 us  [reduced(): kept, sent = (blocks[0::2], blocks[1::2])]
  transfers between devices with their start and end apart: 6 -> 11, of which waited for: 5 -> 10; matrix products, arithmetic and copies ran while one was open for 15% -> 9% of each run, Pallas kernels for 0% -> 0%
where the time goes in v1:
time: 53.6 us; the launch traced here: 53.2 us
  starting transfers between devices  16.3 us (30%)
  waiting for transfers between devices  16.1 us (30%)
  Pallas kernels  10.3 us (19%)
  other arithmetic  5.42 us (10%)
  local copies, waits for them, and re-layouts  4.4 us (8%)
  between operations  0.75 us (1%)
    ppermute x7, waiting for transfers between devices, swapped(): return lax.ppermute(block, 'facet', [(i, i ^ bit) for i in range(facets)])  9.67 us
    ppermute x4, starting transfers between devices, shifted(): lax.ppermute(block, 'col', [(i, (i + distance) % count) for i in range(co...  9.53 us
    ppermute x7, starting transfers between devices, swapped(): return lax.ppermute(block, 'facet', [(i, i ^ bit) for i in range(facets)])  6.74 us
    ppermute x4, waiting for transfers between devices, shifted(): lax.ppermute(block, 'col', [(i, (i + distance) % count) for i in range(co...  6.41 us
    pallas_call x1, Pallas kernels, per_device(): pl.pallas_call(functools.partial(update_kernel, cols, facets, length), gr...  3.89 us
    pallas_call x1, Pallas kernels, per_device(): pl.pallas_call(functools.partial(spectrum_kernel, cols, facets, length),...  3.7 us
    pallas_call x1, Pallas kernels, per_device(): pl.pallas_call(functools.partial(subgrid_kernel, cols, length, shard), ou...  2.71 us
    unnamed x13, local copies, waits for them, and re-layouts  2.63 us
  transfers between devices with their start and end apart: 11, of which 10 were waited for; matrix products, arithmetic and copies ran while one was open for 9% of the time, Pallas kernels for 0%

profile of v1, /device:TPU:0, one launch (start us, length us, event | category | flops | bytes accessed | tf_op | source)
XLA Modules:
  0.0 53.2 jit_solution(4605365351846391518)
XLA Ops:
  0.6 1.3 %copy.10.subgrid = s32[2,1]{1,0:T(2,128)} copy(s32[2,1]{0,1:T(1,128)} %param.8) | data formatting | bytes 16 | tf_op args[3]
  1.9 3.7 %spectrum.1 = (bf16[2,2,2,2,128,128]{5,4,3,2,1,0:T(8,128)(2,1)}, bf16[2,2,2,2,128,128]{5,4,3,2,1,0:T(8,128)(2,1)}, f32[8,128]{1,0:T(8,128)}) custom-call(s32[1,2]{1,0:T(1,128)} %offsets.1, s32[2]{0:T(128)} %column.1, s32[2,1]{1,0:T(2,128)} %copy.10.subgrid, bf16[2,1,2,512,1024]{4,3,2,1,0:T(8,128)(2,1)} %spectra.1), custom_call_target="tpu_custom_call" | custom-call | tf_op jit(solution)/shard_map/spectrum/pallas_call | solution.py:312
  5.6 1.1 %copy.9 = bf16[2,2,2,2,128,128]{5,4,2,3,1,0:T(8,128)(2,1)S(1)} copy(bf16[2,2,2,2,128,128]{5,4,3,2,1,0:T(8,128)(2,1)} %get-tuple-element.10) | data formatting | bytes 1048576 | tf_op jit(solution)/shard_map/spectrum/pallas_call | solution.py:312
  7.3 1.3 %multiply_convert_fusion = (bf16[128,512]{1,0:T(8,128)(2,1)S(1)}, bf16[128,512]{1,0:T(8,128)(2,1)S(1)}) fusion(s32[512]{0:T(512)S(1)} %iota_add_fusion, s32[128]{0:T(128)S(1)} %iota_add_fusion.1, f32[128]{0:T(128)S(1)} %add_multiply_fusion), kind=kLoop, calls=%fused_computation.16 | loop fusion | flops 1179648 | bytes 265216 | tf_op jit(solution)/shard_map/convert_element_type | solution.py:34
  8.8 1.2 %add_convert_fusion = bf16[2,2,2,2,128,128]{5,4,2,3,1,0:T(8,128)(2,1)S(1)} fusion(bf16[2,2,2,2,128,128]{5,4,2,3,1,0:T(8,128)(2,1)S(1)} %collective-permute-done, bf16[2,2,2,2,128,128]{5,4,3,2,1,0:T(8,128)(2,1)} %get-tuple-element.9), kind=kLoop, calls=%fused_computation | loop fusion | flops 1048576 | bytes 1572864 | tf_op jit(solution)/shard_map/convert_element_type | solution.py:281
  10.0 2.9 %collective-permute-start.2 = (bf16[1,2,2,128,128]{4,3,1,2,0:T(8,128)(2,1)S(1)}, bf16[1,2,2,128,128]{4,3,1,2,0:T(8,128)(2,1)S(1)}, u32[]{:S(2)}, u32[]{:S(2)}) collective-permute-start(bf16[1,2,2,128,128]{4,3,1,2,0:T(8,128)(2,1)S(1)} %get-tuple-element.18), channel_id=1, source_target_pairs={{0,16},{8,24},{16,0},{24,8},{1,17},{9,25},{17,1},{25,9},{2,18},{10... | collective-permute-start | bytes 393224 | tf_op jit(solution)/shard_map/ppermute | solution.py:272
  13.0 1.1 %fusion.9 = bf16[128,512]{1,0:T(8,128)(2,1)S(1)} fusion(s32[512]{0:T(512)S(1)} %iota_add_fusion, s32[128]{0:T(128)S(1)} %iota_add_fusion.1, f32[128]{0:T(128)S(1)} %add_multiply_fusion), kind=kLoop, calls=%fused_computation.30 | loop fusion | flops 1245184 | bytes 134144 | tf_op jit(solution)/shard_map/neg | solution.py:328
  14.1 3.2 %collective-permute-done.2 = bf16[1,2,2,128,128]{4,3,1,2,0:T(8,128)(2,1)S(1)} collective-permute-done((bf16[1,2,2,128,128]{4,3,1,2,0:T(8,128)(2,1)S(1)}, bf16[1,2,2,128,128]{4,3,1,2,0:T(8,128)(2,1)S(1)}, u32[]{:S(2)}, u32[]{:S(2)}) %collective-permute-start.2) | collective-permute-done | bytes 131104 | tf_op jit(solution)/shard_map/ppermute | solution.py:272
  17.3 2.3 %collective-permute-done.1 = bf16[1,2,2,128,128]{4,3,1,2,0:T(8,128)(2,1)S(1)} collective-permute-done((bf16[1,2,2,128,128]{4,3,1,2,0:T(8,128)(2,1)S(1)}, bf16[1,2,2,128,128]{4,3,1,2,0:T(8,128)(2,1)S(1)}, u32[]{:S(2)}, u32[]{:S(2)}) %collective-permute-start.1) | collective-permute-done | bytes 131104 | tf_op jit(solution)/shard_map/ppermute | solution.py:272
  19.7 4.8 %collective-permute-start.4 = (bf16[2,128,128]{2,1,0:T(8,128)(2,1)S(1)}, bf16[2,128,128]{2,1,0:T(8,128)(2,1)S(1)}, u32[]{:S(2)}, u32[]{:S(2)}) collective-permute-start(bf16[2,128,128]{2,1,0:T(8,128)(2,1)S(1)} %get-tuple-element.22), channel_id=1, source_target_pairs={{0,7},{1,0},{2,1},{3,2},{4,3},{5,4},{6,5},{7,6},{8,15},{9,8},{10,9... | collective-permute-start | bytes 196616 | tf_op jit(solution)/shard_map/ppermute | solution.py:277
  24.5 0.8 %maximum_maximum_fusion.table = bf16[256,1024]{1,0:T(8,128)(2,1)} fusion(bf16[128,512]{1,0:T(8,128)(2,1)S(1)} %get-tuple-element.25, bf16[128,512]{1,0:T(8,128)(2,1)S(1)} %fusion.9, bf16[128,512]{1,0:T(8,128)(2,1)S(1)} %get-tuple-element.24), kind=kLoop, calls=%fused_computation.1 | loop fusion | flops 2097152 | bytes 917504 | tf_op jit(solution)/shard_map/concatenate | solution.py:325
  25.3 0.7 %copy.11.main = bf16[2,2,128,128]{3,2,1,0:T(8,128)(2,1)} copy(bf16[2,2,128,128]{3,2,0,1:T(8,128)(2,1)S(1)} %get-tuple-element.17) | data formatting | bytes 262144 | tf_op jit(solution)/shard_map/squeeze | solution.py:290
  26.4 5.1 %collective-permute-done.3.from_prev = bf16[2,128,128]{2,1,0:T(8,128)(2,1)S(1)} collective-permute-done((bf16[2,128,128]{2,1,0:T(8,128)(2,1)S(1)}, bf16[2,128,128]{2,1,0:T(8,128)(2,1)S(1)}, u32[]{:S(2)}, u32[]{:S(2)}) %collective-permute-start.3) | collective-permute-done | bytes 65568 | tf_op jit(solution)/shard_map/ppermute | solution.py:277
  32.0 2.7 %subgrid.4 = (bf16[2,1,2,128,512]{4,3,2,1,0:T(8,128)(2,1)}, bf16[2,2,128,128]{3,2,1,0:T(8,128)(2,1)}, bf16[2,128,128]{2,1,0:T(8,128)(2,1)}, bf16[2,128,128]{2,1,0:T(8,128)(2,1)}) custom-call(s32[2,1]{1,0:T(2,128)} %copy.10.subgrid, bf16[2,2,128,128]{3,2,1,0:T(8,128)(2,1)} %copy.11.main, bf16[2,128,128]{2,1,0:T(8,128)(2,1)} %copy-done.5, ...), custom_call_target="tpu_custom_call" | custom-call | tf_op jit(solution)/shard_map/subgrid/pallas_call | solution.py:340
  34.8 4.7 %collective-permute-start.8 = (bf16[2,128,128]{2,1,0:T(8,128)(2,1)}, bf16[2,128,128]{2,1,0:T(8,128)(2,1)S(1)}, u32[]{:S(2)}, u32[]{:S(2)}) collective-permute-start(bf16[2,128,128]{2,1,0:T(8,128)(2,1)} %get-tuple-element.15), channel_id=1, source_target_pairs={{0,7},{1,0},{2,1},{3,2},{4,3},{5,4},{6,5},{7,6},{8,15},{9,8},{10,9... | collective-permute-start | bytes 196616 | tf_op jit(solution)/shard_map/ppermute | solution.py:277
  39.5 1.5 %collective-permute-start.5 = (bf16[1,2,2,128,128]{4,3,2,1,0:T(8,128)(2,1)}, bf16[1,2,2,128,128]{4,3,2,1,0:T(8,128)(2,1)S(1)}, u32[]{:S(2)}, u32[]{:S(2)}) collective-permute-start(bf16[1,2,2,128,128]{4,3,2,1,0:T(8,128)(2,1)} %bitcast.36), channel_id=1, source_target_pairs={{0,16},{8,24},{16,0},{24,8},{1,17},{9,25},{17,1},{25,9},{2,18},{10... | collective-permute-start | bytes 393224 | tf_op jit(solution)/shard_map/ppermute | solution.py:272
  41.0 1.0 %collective-permute-done.7 = bf16[2,128,128]{2,1,0:T(8,128)(2,1)S(1)} collective-permute-done((bf16[2,128,128]{2,1,0:T(8,128)(2,1)}, bf16[2,128,128]{2,1,0:T(8,128)(2,1)S(1)}, u32[]{:S(2)}, u32[]{:S(2)}) %collective-permute-start.7) | collective-permute-done | bytes 65568 | tf_op jit(solution)/shard_map/ppermute | solution.py:277
  42.0 1.6 %collective-permute-start.9 = (bf16[1,2,2,128,128]{4,3,2,1,0:T(8,128)(2,1)S(1)}, bf16[1,2,2,128,128]{4,3,2,1,0:T(8,128)(2,1)S(1)}, u32[]{:S(2)}, u32[]{:S(2)}) collective-permute-start(bf16[1,2,2,128,128]{4,3,2,1,0:T(8,128)(2,1)S(1)} %get-tuple-element.21), channel_id=1, source_target_pairs={{0,16},{8,24},{16,0},{24,8},{1,17},{9,25},{17,1},{25,9},{2,18},{10... | collective-permute-start | bytes 393224 | tf_op jit(solution)/shard_map/ppermute | solution.py:272
  43.5 1.1 %collective-permute-done.5 = bf16[1,2,2,128,128]{4,3,2,1,0:T(8,128)(2,1)S(1)} collective-permute-done((bf16[1,2,2,128,128]{4,3,2,1,0:T(8,128)(2,1)}, bf16[1,2,2,128,128]{4,3,2,1,0:T(8,128)(2,1)S(1)}, u32[]{:S(2)}, u32[]{:S(2)}) %collective-permute-start.5) | collective-permute-done | bytes 131104 | tf_op jit(solution)/shard_map/ppermute | solution.py:272
  44.7 0.9 %maximum_bitcast_fusion.even = bf16[2,2,2,128,128]{4,3,2,1,0:T(8,128)(2,1)S(1)} fusion(bf16[1,1,2,2,128,128]{5,4,3,2,1,0:T(8,128)(2,1)S(1)} %bitcast.38, bf16[1,1,2,2,128,128]{5,4,3,2,1,0:T(8,128)(2,1)} %bitcast.37), kind=kLoop, calls=%fused_computation.10 | loop fusion | flops 131072 | bytes 524288 | tf_op jit(solution)/shard_map/reshape | solution.py:298
  45.7 1.3 %collective-permute-done.9 = bf16[1,2,2,128,128]{4,3,2,1,0:T(8,128)(2,1)S(1)} collective-permute-done((bf16[1,2,2,128,128]{4,3,2,1,0:T(8,128)(2,1)S(1)}, bf16[1,2,2,128,128]{4,3,2,1,0:T(8,128)(2,1)S(1)}, u32[]{:S(2)}, u32[]{:S(2)}) %collective-permute-start.9) | collective-permute-done | bytes 131104 | tf_op jit(solution)/shard_map/ppermute | solution.py:272
  47.2 1.4 %collective-permute-done.10.odd_edge = bf16[2,2,2,128,128]{4,3,2,1,0:T(8,128)(2,1)S(1)} collective-permute-done((bf16[2,2,2,128,128]{4,3,2,1,0:T(8,128)(2,1)S(1)}, bf16[2,2,2,128,128]{4,3,2,1,0:T(8,128)(2,1)S(1)}, u32[]{:S(2)}, u32[]{:S(2)}) %collective-permute-start.10) | collective-permute-done | bytes 262176 | tf_op jit(solution)/shard_map/ppermute | solution.py:272
  48.6 0.7 %copy-done.3 = bf16[2,2,2,128,128]{4,3,2,1,0:T(8,128)(2,1)} copy-done((bf16[2,2,2,128,128]{4,3,2,1,0:T(8,128)(2,1)}, bf16[2,2,2,128,128]{4,3,2,1,0:T(8,128)(2,1)S(1)}, u32[]{:S(2)}) %copy-start.3) | copy-done | bytes 262168
  49.3 3.9 %update.1 = bf16[2,1,2,512,1024]{4,3,2,1,0:T(8,128)(2,1)} custom-call(s32[2,1]{1,0:T(2,128)} %copy.10.subgrid, f32[8,128]{1,0:T(8,128)} %get-tuple-element.12.turn, bf16[2,2,2,128,128]{4,3,2,1,0:T(8,128)(2,1)} %copy-done, bf16[2,2,2,128,128]{4,3,2,1,0:T(8,128)(2,1)} %copy-done.2, bf16[2,2,2,128,128]{4,3,2,1,0:T(8,128)(2,1)} %copy-done.1, ...), custom_call_target="tpu_custom_call" | custom-call | tf_op jit(solution)/shard_map/update/pallas_call | solution.py:366
  (29 shorter events, 2.3 us)
Async XLA Ops:
  6.7 2.1 %collective-permute-start = (bf16[2,2,2,2,128,128]{5,4,2,3,1,0:T(8,128)(2,1)S(1)}, bf16[2,2,2,2,128,128]{5,4,2,3,1,0:T(8,128)(2,1)S(1)}, u32[]{:S(2)}, u32[]{:S(2)}) collective-permute-start(bf16[2,2,2,2,128,128]{5,4,2,3,1,0:T(8,128)(2,1)S(1)} %copy.9), channel_id=1, source_target_pairs={{0,8},{8,0},{16,24},{24,16},{1,9},{9,1},{17,25},{25,17},{2,10},{10... | collective-permute-start | bytes 1572872 | tf_op jit(solution)/shard_map/ppermute | solution.py:272
  10.0 7.3 %collective-permute-start.2 = (bf16[1,2,2,128,128]{4,3,1,2,0:T(8,128)(2,1)S(1)}, bf16[1,2,2,128,128]{4,3,1,2,0:T(8,128)(2,1)S(1)}, u32[]{:S(2)}, u32[]{:S(2)}) collective-permute-start(bf16[1,2,2,128,128]{4,3,1,2,0:T(8,128)(2,1)S(1)} %get-tuple-element.18), channel_id=1, source_target_pairs={{0,16},{8,24},{16,0},{24,8},{1,17},{9,25},{17,1},{25,9},{2,18},{10... | collective-permute-start | bytes 393224 | tf_op jit(solution)/shard_map/ppermute | solution.py:272
  13.0 6.6 %collective-permute-start.1 = (bf16[1,2,2,128,128]{4,3,1,2,0:T(8,128)(2,1)S(1)}, bf16[1,2,2,128,128]{4,3,1,2,0:T(8,128)(2,1)S(1)}, u32[]{:S(2)}, u32[]{:S(2)}) collective-permute-start(bf16[1,2,2,128,128]{4,3,1,2,0:T(8,128)(2,1)S(1)} %get-tuple-element.19), channel_id=1, source_target_pairs={{0,16},{8,24},{16,0},{24,8},{1,17},{9,25},{17,1},{25,9},{2,18},{10... | collective-permute-start | bytes 393224 | tf_op jit(solution)/shard_map/ppermute | solution.py:272
  19.7 6.7 %collective-permute-start.4 = (bf16[2,128,128]{2,1,0:T(8,128)(2,1)S(1)}, bf16[2,128,128]{2,1,0:T(8,128)(2,1)S(1)}, u32[]{:S(2)}, u32[]{:S(2)}) collective-permute-start(bf16[2,128,128]{2,1,0:T(8,128)(2,1)S(1)} %get-tuple-element.22), channel_id=1, source_target_pairs={{0,7},{1,0},{2,1},{3,2},{4,3},{5,4},{6,5},{7,6},{8,15},{9,8},{10,9... | collective-permute-start | bytes 196616 | tf_op jit(solution)/shard_map/ppermute | solution.py:277
  24.5 7.0 %collective-permute-start.3 = (bf16[2,128,128]{2,1,0:T(8,128)(2,1)S(1)}, bf16[2,128,128]{2,1,0:T(8,128)(2,1)S(1)}, u32[]{:S(2)}, u32[]{:S(2)}) collective-permute-start(bf16[2,128,128]{2,1,0:T(8,128)(2,1)S(1)} %get-tuple-element.23), channel_id=1, source_target_pairs={{0,1},{1,2},{2,3},{3,4},{4,5},{5,6},{6,7},{7,0},{8,9},{9,10},{10,1... | collective-permute-start | bytes 196616 | tf_op jit(solution)/shard_map/ppermute | solution.py:277
  26.4 5.1 %copy-start.4 = (bf16[2,128,128]{2,1,0:T(8,128)(2,1)}, bf16[2,128,128]{2,1,0:T(8,128)(2,1)S(1)}, u32[]{:S(2)}) copy-start(bf16[2,128,128]{2,1,0:T(8,128)(2,1)S(1)} %collective-permute-done.4.from_next) | copy-start | bytes 196612
  31.4 0.6 %copy-start.5 = (bf16[2,128,128]{2,1,0:T(8,128)(2,1)}, bf16[2,128,128]{2,1,0:T(8,128)(2,1)S(1)}, u32[]{:S(2)}) copy-start(bf16[2,128,128]{2,1,0:T(8,128)(2,1)S(1)} %collective-permute-done.3.from_prev) | copy-start | bytes 196612
  34.8 7.2 %collective-permute-start.7 = (bf16[2,128,128]{2,1,0:T(8,128)(2,1)}, bf16[2,128,128]{2,1,0:T(8,128)(2,1)S(1)}, u32[]{:S(2)}, u32[]{:S(2)}) collective-permute-start(bf16[2,128,128]{2,1,0:T(8,128)(2,1)} %get-tuple-element.14), channel_id=1, source_target_pairs={{0,1},{1,2},{2,3},{3,4},{4,5},{5,6},{6,7},{7,0},{8,9},{9,10},{10,1... | collective-permute-start | bytes 196616 | tf_op jit(solution)/shard_map/ppermute | solution.py:277
  34.8 7.2 %collective-permute-start.8 = (bf16[2,128,128]{2,1,0:T(8,128)(2,1)}, bf16[2,128,128]{2,1,0:T(8,128)(2,1)S(1)}, u32[]{:S(2)}, u32[]{:S(2)}) collective-permute-start(bf16[2,128,128]{2,1,0:T(8,128)(2,1)} %get-tuple-element.15), channel_id=1, source_target_pairs={{0,7},{1,0},{2,1},{3,2},{4,3},{5,4},{6,5},{7,6},{8,15},{9,8},{10,9... | collective-permute-start | bytes 196616 | tf_op jit(solution)/shard_map/ppermute | solution.py:277
  39.5 5.2 %collective-permute-start.5 = (bf16[1,2,2,128,128]{4,3,2,1,0:T(8,128)(2,1)}, bf16[1,2,2,128,128]{4,3,2,1,0:T(8,128)(2,1)S(1)}, u32[]{:S(2)}, u32[]{:S(2)}) collective-permute-start(bf16[1,2,2,128,128]{4,3,2,1,0:T(8,128)(2,1)} %bitcast.36), channel_id=1, source_target_pairs={{0,16},{8,24},{16,0},{24,8},{1,17},{9,25},{17,1},{25,9},{2,18},{10... | collective-permute-start | bytes 393224 | tf_op jit(solution)/shard_map/ppermute | solution.py:272
  42.0 5.0 %collective-permute-start.9 = (bf16[1,2,2,128,128]{4,3,2,1,0:T(8,128)(2,1)S(1)}, bf16[1,2,2,128,128]{4,3,2,1,0:T(8,128)(2,1)S(1)}, u32[]{:S(2)}, u32[]{:S(2)}) collective-permute-start(bf16[1,2,2,128,128]{4,3,2,1,0:T(8,128)(2,1)S(1)} %get-tuple-element.21), channel_id=1, source_target_pairs={{0,16},{8,24},{16,0},{24,8},{1,17},{9,25},{17,1},{25,9},{2,18},{10... | collective-permute-start | bytes 393224 | tf_op jit(solution)/shard_map/ppermute | solution.py:272
  45.6 3.0 %copy-start = (bf16[2,2,2,128,128]{4,3,2,1,0:T(8,128)(2,1)}, bf16[2,2,2,128,128]{4,3,2,1,0:T(8,128)(2,1)S(1)}, u32[]{:S(2)}) copy-start(bf16[2,2,2,128,128]{4,3,2,1,0:T(8,128)(2,1)S(1)} %maximum_bitcast_fusion.even) | copy-start | bytes 786436
  45.6 1.6 %collective-permute-start.6 = (bf16[2,2,2,128,128]{4,3,2,1,0:T(8,128)(2,1)S(1)}, bf16[2,2,2,128,128]{4,3,2,1,0:T(8,128)(2,1)S(1)}, u32[]{:S(2)}, u32[]{:S(2)}) collective-permute-start(bf16[2,2,2,128,128]{4,3,2,1,0:T(8,128)(2,1)S(1)} %maximum_bitcast_fusion.even), channel_id=1, source_target_pairs={{0,8},{8,0},{16,24},{24,16},{1,9},{9,1},{17,25},{25,17},{2,10},{10... | collective-permute-start | bytes 786440 | tf_op jit(solution)/shard_map/ppermute | solution.py:272
  47.0 1.6 %copy-start.1 = (bf16[2,2,2,128,128]{4,3,2,1,0:T(8,128)(2,1)}, bf16[2,2,2,128,128]{4,3,2,1,0:T(8,128)(2,1)S(1)}, u32[]{:S(2)}) copy-start(bf16[2,2,2,128,128]{4,3,2,1,0:T(8,128)(2,1)S(1)} %maximum_bitcast_fusion.1.even_edge) | copy-start | bytes 786436
  47.0 1.6 %collective-permute-start.10 = (bf16[2,2,2,128,128]{4,3,2,1,0:T(8,128)(2,1)S(1)}, bf16[2,2,2,128,128]{4,3,2,1,0:T(8,128)(2,1)S(1)}, u32[]{:S(2)}, u32[]{:S(2)}) collective-permute-start(bf16[2,2,2,128,128]{4,3,2,1,0:T(8,128)(2,1)S(1)} %maximum_bitcast_fusion.1.even_edge), channel_id=1, source_target_pairs={{0,8},{8,0},{16,24},{24,16},{1,9},{9,1},{17,25},{25,17},{2,10},{10... | collective-permute-start | bytes 786440 | tf_op jit(solution)/shard_map/ppermute | solution.py:272
  47.2 1.4 %copy-start.2 = (bf16[2,2,2,128,128]{4,3,2,1,0:T(8,128)(2,1)}, bf16[2,2,2,128,128]{4,3,2,1,0:T(8,128)(2,1)S(1)}, u32[]{:S(2)}) copy-start(bf16[2,2,2,128,128]{4,3,2,1,0:T(8,128)(2,1)S(1)} %collective-permute-done.6.odd) | copy-start | bytes 786436
  48.6 0.7 %copy-start.3 = (bf16[2,2,2,128,128]{4,3,2,1,0:T(8,128)(2,1)}, bf16[2,2,2,128,128]{4,3,2,1,0:T(8,128)(2,1)S(1)}, u32[]{:S(2)}) copy-start(bf16[2,2,2,128,128]{4,3,2,1,0:T(8,128)(2,1)S(1)} %collective-permute-done.10.odd_edge) | copy-start | bytes 786436

commit v2 on v1

v2 whole, which is shorter than its diff:
```python
import functools
import math

import jax
import jax.numpy as jnp
from jax import lax
from jax.experimental import pallas as pl
from jax.experimental.pallas import tpu as pltpu
from jax.sharding import PartitionSpec as P


IMAGE = 65536
XM = 512
WM = 128
XA = 448
LANES = 128
HALF = WM // 2

TAU = 2.0 * math.pi
BF16 = jnp.bfloat16
F32 = jnp.float32

VMEM = pl.BlockSpec(memory_space=pltpu.VMEM)
SMEM = pl.BlockSpec(memory_space=pltpu.SMEM)
HBM = pl.BlockSpec(memory_space=pltpu.HBM)


def make_table(facets, zero):
    place = jnp.arange(WM, dtype=jnp.int32) + zero
    cell = jnp.arange(XM, dtype=jnp.int32)
    turns = (place[:, None] - WM // 2) * (cell[None, :] - XM // 2) % XM
    angle = TAU * turns.astype(F32) / XM
    relative = (place.astype(F32) + 0.5 - WM / 2.0) / (WM / 2.0)
    taper = (0.3 + 0.7 * (1.0 - relative * relative)) / jnp.sqrt(F32(WM * facets))
    return (
        (taper[:, None] * jnp.cos(angle)).astype(BF16),
        (taper[:, None] * jnp.sin(angle)).astype(BF16),
    )


def remainder(value, modulus):
    if modulus & (modulus - 1) == 0:
        return value & (modulus - 1)
    return lax.rem(value, jnp.int32(modulus))


def modular(first, second, image):
    upper = second // 256
    lower = remainder(second, 256)
    return remainder(remainder(first * upper, image // 256) * 256 + first * lower, image)


def place_of(subgrid_offset, here, shard, length):
    start = subgrid_offset // (IMAGE // length) - here * shard - HALF + LANES
    return lax.div(start, jnp.int32(LANES)) - 1, remainder(start, LANES)


def lanes_of(shape):
    return lax.broadcasted_iota(jnp.int32, shape, len(shape) - 1)


def turns_of(turn, index, firsts, second, length):
    rows = lax.broadcasted_iota(jnp.int32, (8, LANES), 0)
    first = jnp.zeros((8, LANES), F32)
    for c, value in enumerate(firsts):
        first = jnp.where(rows == c, value.astype(F32), first)
    steps = remainder(index * second, length).astype(F32)
    angle = TAU * (first / IMAGE + steps / length)
    turn[0:8, :] = jnp.cos(angle)
    turn[8:16, :] = jnp.sin(angle)


def firsts_of(cols, offsets, column):
    return [modular(column[c] * XA, offsets[0, 0], IMAGE) for c in range(cols)]


def edge_kernel(cols, facets, length, offsets, column, spectra, send, keep, turn, buf, sems):
    shard = spectra.shape[4]
    block = XM // facets
    here = lax.axis_index("col")
    facet = lax.axis_index("facet")
    copies = []
    for c in range(cols):
        for slot, at in enumerate((0, shard - LANES)):
            copy = pltpu.make_async_copy(
                spectra.at[c, 0, :, :, pl.ds(at, LANES)], buf.at[c, slot], sems.at[c, slot]
            )
            copy.start()
            copies.append(copy)
    lanes = lanes_of((8, LANES))
    index = here * shard + lanes + jnp.where(lanes < HALF, 0, shard - LANES)
    turns_of(turn, index, firsts_of(cols, offsets, column), offsets[0, 1], length)
    left = lanes_of((1, LANES)) < HALF
    for c in range(cols):
        copies[c * 2].wait()
        copies[c * 2 + 1].wait()
        cosine = turn[c : c + 1, :]
        sine = turn[8 + c : 9 + c, :]
        for s in range(facets):
            rows = pl.ds(pl.multiple_of((facet ^ s) * block, block), block)
            target = send if s % 2 else keep
            parts = [
                jnp.where(
                    left,
                    buf[c, 0, part, rows, :].astype(F32),
                    buf[c, 1, part, rows, :].astype(F32),
                )
                for part in range(2)
            ]
            real = parts[0] * cosine + parts[1] * sine
            imag = parts[1] * cosine - parts[0] * sine
            low = jnp.where(left, real, pltpu.roll(imag, HALF, 1))
            high = jnp.where(left, pltpu.roll(real, HALF, 1), imag)
            target[0, s // 2, c] = low.astype(BF16)
            target[1, s // 2, c] = high.astype(BF16)


def main_kernel(
    cols, facets, length, offsets, column, subgrid, spectra, after, send, keep, turn, buf, sems
):
    del after
    shard = spectra.shape[4]
    tiles = shard // LANES
    block = XM // facets
    here = lax.axis_index("col")
    facet = lax.axis_index("facet")
    copies = []
    places = []
    for c in range(cols):
        tile, lane = place_of(subgrid[0, c], here, shard, length)
        places.append((tile, lane))
        low = jnp.maximum(tile, 0)
        high = jnp.minimum(tile + 1, tiles - 1)
        for slot, which in enumerate((low, high)):
            at = pl.multiple_of(which * LANES, LANES)
            copy = pltpu.make_async_copy(
                spectra.at[c, 0, :, :, pl.ds(at, LANES)], buf.at[c, slot], sems.at[c, slot]
            )
            copy.start()
            copies.append(copy)
    lanes = lanes_of((8, LANES))
    rows = lax.broadcasted_iota(jnp.int32, (8, LANES), 0)
    index = jnp.zeros((8, LANES), jnp.int32)
    for c in range(cols):
        tile, lane = places[c]
        at = here * shard + lanes + jnp.where(lanes >= lane, tile, tile + 1) * LANES
        index = jnp.where(rows == c, remainder(at + length, length), index)
    turns_of(turn, index, firsts_of(cols, offsets, column), offsets[0, 1], length)
    lanes = lanes_of((1, LANES))
    for c in range(cols):
        tile, lane = places[c]
        copies[c * 2].wait()
        copies[c * 2 + 1].wait()
        from_low = jnp.logical_and(lanes >= lane, tile >= 0)
        from_high = jnp.logical_and(lanes < lane, tile + 1 < tiles)
        zero = jnp.zeros((1, LANES), F32)
        cosine = turn[c : c + 1, :]
        sine = turn[8 + c : 9 + c, :]
        for s in range(facets):
            rows = pl.ds(pl.multiple_of((facet ^ s) * block, block), block)
            target = send if s % 2 else keep
            parts = [
                jnp.where(
                    from_low,
                    buf[c, 0, part, rows, :].astype(F32),
                    jnp.where(from_high, buf[c, 1, part, rows, :].astype(F32), zero),
                )
                for part in range(2)
            ]
            target[0, s // 2, c] = (parts[0] * cosine + parts[1] * sine).astype(BF16)
            target[1, s // 2, c] = (parts[1] * cosine - parts[0] * sine).astype(BF16)


def subgrid_kernel(
    cols,
    length,
    shard,
    subgrid,
    kept,
    received,
    from_prev,
    from_next,
    table,
    weights,
    grids,
    back,
    to_prev,
    to_next,
    stack,
    scaled,
):
    tiles = shard // LANES
    block = kept.shape[3]
    here = lax.axis_index("col")
    lanes = lanes_of((1, LANES))
    zero = jnp.zeros((1, LANES), F32)
    for c in range(cols):
        tile, lane = place_of(subgrid[0, c], here, shard, length)
        low = jnp.logical_and(lanes >= lane, tile < 0)
        high = jnp.logical_and(lanes < lane, tile + 1 >= tiles)
        prev = from_prev[0, c].astype(F32)
        nxt = from_next[0, c].astype(F32)
        shift = remainder(LANES - lane, LANES)
        real = kept[0, 0, c].astype(F32) + received[0, 0, c].astype(F32)
        real = real + jnp.where(low, pltpu.roll(prev, HALF, 1), jnp.where(high, nxt, zero))
        imag = kept[1, 0, c].astype(F32) + received[1, 0, c].astype(F32)
        imag = imag + jnp.where(low, prev, jnp.where(high, pltpu.roll(nxt, HALF, 1), zero))
        rows = slice(c * block, (c + 1) * block)
        stack[rows, :WM] = pltpu.roll(real, shift, 1).astype(BF16)
        stack[rows, WM:] = pltpu.roll(imag, shift, 1).astype(BF16)
    for part in range(2):
        span = slice(part * XM, (part + 1) * XM)
        product = jnp.dot(stack[...], table[:, span], preferred_element_type=F32)
        rounded = product.astype(BF16)
        for c in range(cols):
            rows = slice(c * block, (c + 1) * block)
            piece = rounded[rows]
            grids[c, 0, part] = piece
            scaled[rows, span] = (piece.astype(F32) * weights[c, 0].astype(F32)).astype(BF16)
    result = lax.dot_general(
        scaled[...],
        table[...],
        (((1,), (1,)), ((), ())),
        preferred_element_type=F32,
    )
    for c in range(cols):
        tile, lane = place_of(subgrid[0, c], here, shard, length)
        rows = slice(c * block, (c + 1) * block)
        low = jnp.logical_and(lanes >= lane, tile < 0)
        high = jnp.logical_and(lanes < lane, tile + 1 >= tiles)
        real = pltpu.roll(result[rows, :WM], lane, 1)
        imag = pltpu.roll(result[rows, WM:], lane, 1)
        back[0, 0, c] = real.astype(BF16)
        back[1, 0, c] = imag.astype(BF16)
        real_low = jnp.where(low, real, zero)
        imag_low = jnp.where(low, imag, zero)
        real_high = jnp.where(high, real, zero)
        imag_high = jnp.where(high, imag, zero)
        to_prev[0, c] = (pltpu.roll(real_low, HALF, 1) + imag_low).astype(BF16)
        to_next[0, c] = (real_high + pltpu.roll(imag_high, HALF, 1)).astype(BF16)


def phased(source, s, c, cosine, sine):
    real = source[0, s // 2, c].astype(F32)
    imag = source[1, s // 2, c].astype(F32)
    return real * cosine - imag * sine, imag * cosine + real * sine


def update_kernel(facets, length, subgrid, turn, even, odd, out):
    shard = out.shape[4]
    tiles = shard // LANES
    block = XM // facets
    here = lax.axis_index("col")
    facet = lax.axis_index("facet")
    lanes = lanes_of((1, LANES))
    zero = jnp.zeros((1, LANES), F32)
    c = pl.program_id(0)
    tile, lane = place_of(subgrid[0, c], here, shard, length)
    out[...] = jnp.zeros(out.shape, BF16)
    low_at = pl.ds(pl.multiple_of(jnp.maximum(tile, 0) * LANES, LANES), LANES)
    high_at = pl.ds(pl.multiple_of(jnp.minimum(tile + 1, tiles - 1) * LANES, LANES), LANES)
    cosine = turn[pl.ds(c, 1), :]
    sine = turn[pl.ds(8 + c, 1), :]
    is_low = lanes >= lane
    for s in range(facets):
        rows = pl.ds(pl.multiple_of((facet ^ s) * block, block), block)
        whole = phased(odd if s % 2 else even, s, c, cosine, sine)
        for part in range(2):
            value = whole[part]
            out[0, 0, part, rows, low_at] = jnp.where(is_low, value, zero).astype(BF16)
            out[0, 0, part, rows, high_at] = jnp.where(is_low, zero, value).astype(BF16)


def end_kernel(
    cols,
    facets,
    length,
    subgrid,
    turn,
    edge_turn,
    even,
    odd,
    even_edge,
    odd_edge,
    whole,
    out,
    buf,
    sems,
):
    shard = out.shape[4]
    tiles = shard // LANES
    block = XM // facets
    here = lax.axis_index("col")
    facet = lax.axis_index("facet")
    lanes = lanes_of((1, LANES))
    left = lanes < HALF
    zero = jnp.zeros((1, LANES), F32)
    copies = []
    for c in range(cols):
        tile, lane = place_of(subgrid[0, c], here, shard, length)
        cosine = turn[c : c + 1, :]
        sine = turn[8 + c : 9 + c, :]
        edge_cosine = edge_turn[c : c + 1, :]
        edge_sine = edge_turn[8 + c : 9 + c, :]
        at = jnp.where(lanes >= lane, tile, tile + 1)
        in_first = at == 0
        in_last = at == tiles - 1
        for s in range(facets):
            rows = pl.ds(pl.multiple_of((facet ^ s) * block, block), block)
            values = phased(odd if s % 2 else even, s, c, cosine, sine)
            edges = odd_edge if s % 2 else even_edge
            prev = edges[0, s // 2, c].astype(F32)
            nxt = edges[1, s // 2, c].astype(F32)
            real = jnp.where(left, prev, pltpu.roll(nxt, HALF, 1))
            imag = jnp.where(left, pltpu.roll(prev, HALF, 1), nxt)
            ends = (
                real * edge_cosine - imag * edge_sine,
                imag * edge_cosine + real * edge_sine,
            )
            for part in range(2):
                value = values[part]
                end = ends[part]
                buf[c, 0, part, rows, :] = (
                    jnp.where(left, end, zero) + jnp.where(in_first, value, zero)
                ).astype(BF16)
                buf[c, 1, part, rows, :] = (
                    jnp.where(left, zero, end) + jnp.where(in_last, value, zero)
                ).astype(BF16)
        for slot, start in enumerate((0, shard - LANES)):
            copy = pltpu.make_async_copy(
                buf.at[c, slot], out.at[c, 0, :, :, pl.ds(start, LANES)], sems.at[c, slot]
            )
            copy.start()
            copies.append(copy)
    for copy in copies:
        copy.wait()


def swapped(block, bit):
    facets = lax.axis_size("facet")
    return lax.ppermute(block, "facet", [(i, i ^ bit) for i in range(facets)])


def shifted(block, distance):
    count = lax.axis_size("col")
    return lax.ppermute(block, "col", [(i, (i + distance) % count) for i in range(count)])


def added(kept, received):
    return (kept.astype(F32) + received.astype(F32)).astype(BF16)


def reduced(kept, sent, facets):
    received = swapped(sent, 1)
    bit = 2
    while bit < facets:
        blocks = added(kept, received)
        kept, sent = blocks[:, 0::2], blocks[:, 1::2]
        received = swapped(sent, bit)
        bit *= 2
    return kept, received


def gathered(blocks, facets):
    bit = facets // 2
    while bit > 1:
        received = swapped(blocks, bit)
        shape = (blocks.shape[0], -1) + blocks.shape[2:]
        blocks = jnp.stack([blocks, received], axis=2).reshape(shape)
        bit //= 2
    return blocks, swapped(blocks, 1)


def params(mib):
    return pltpu.CompilerParams(vmem_limit_bytes=mib * 1024 * 1024)


def computed(facet_spectra, facet_offsets, column_index, subgrid_offsets, weights):
    cols = facet_spectra.shape[0]
    shard = facet_spectra.shape[4]
    facets = lax.axis_size("facet")
    length = shard * lax.axis_size("col")
    block = XM // facets
    facet_spectra, facet_offsets, column_index, places = (
        pltpu.with_memory_space_constraint(array, pltpu.HBM)
        for array in (facet_spectra, facet_offsets, column_index, subgrid_offsets.T)
    )

    pieces = jax.ShapeDtypeStruct((2, facets // 2, cols, block, LANES), BF16)
    turns = jax.ShapeDtypeStruct((16, LANES), F32)
    scratch = [pltpu.VMEM((cols, 2, 2, XM, LANES), BF16), pltpu.SemaphoreType.DMA((cols, 2))]
    edge_send, edge_keep, edge_turn = pl.pallas_call(
        functools.partial(edge_kernel, cols, facets, length),
        out_shape=(pieces, pieces, turns),
        in_specs=[SMEM, SMEM, HBM],
        out_specs=(VMEM, VMEM, VMEM),
        scratch_shapes=scratch,
        compiler_params=params(12),
        name="edge",
    )(facet_offsets, column_index, facet_spectra)
    main_send, main_keep, turn = pl.pallas_call(
        functools.partial(main_kernel, cols, facets, length),
        out_shape=(pieces, pieces, turns),
        in_specs=[SMEM, SMEM, SMEM, HBM, VMEM],
        out_specs=(VMEM, VMEM, VMEM),
        scratch_shapes=scratch,
        compiler_params=params(12),
        name="main",
    )(facet_offsets, column_index, places, facet_spectra, edge_turn)

    edges = added(*reduced(edge_keep, edge_send, facets))
    main_kept, main_received = reduced(main_keep, main_send, facets)
    from_prev = shifted(edges[1], 1)
    from_next = shifted(edges[0], -1)

    real_tab, imag_tab = make_table(facets, 0)
    table = jnp.concatenate(
        [
            jnp.concatenate([real_tab, imag_tab], axis=1),
            jnp.concatenate([-imag_tab, real_tab], axis=1),
        ],
        axis=0,
    )

    edge = jax.ShapeDtypeStruct((1, cols, block, LANES), BF16)
    grids, back, to_prev, to_next = pl.pallas_call(
        functools.partial(subgrid_kernel, cols, length, shard),
        out_shape=(
            jax.ShapeDtypeStruct((cols, 1, 2, block, XM), BF16),
            jax.ShapeDtypeStruct((2, 1, cols, block, LANES), BF16),
            edge,
            edge,
        ),
        in_specs=[SMEM] + [VMEM] * 6,
        out_specs=(VMEM, VMEM, VMEM, VMEM),
        scratch_shapes=[
            pltpu.VMEM((cols * block, 2 * WM), BF16),
            pltpu.VMEM((cols * block, 2 * XM), BF16),
        ],
        compiler_params=params(12),
        name="subgrid",
    )(places, main_kept, main_received, from_prev, from_next, table, weights)

    came_prev = shifted(to_next, 1)
    came_next = shifted(to_prev, -1)
    even, odd = gathered(back, facets)
    even_edge, odd_edge = gathered(jnp.stack([came_prev, came_next]), facets)

    def all_of(array):
        rank = array.ndim
        return pl.BlockSpec(array.shape, lambda i: (0,) * rank)

    updates = pl.pallas_call(
        functools.partial(update_kernel, facets, length),
        grid=(cols,),
        out_shape=jax.ShapeDtypeStruct((cols, 1, 2, XM, shard), BF16),
        in_specs=[SMEM, all_of(turn), all_of(even), all_of(odd)],
        out_specs=pl.BlockSpec((1, 1, 2, XM, shard), lambda i: (i, 0, 0, 0, 0)),
        compiler_params=params(16),
        name="update",
    )(places, turn, even, odd)
    updates = pl.pallas_call(
        functools.partial(end_kernel, cols, facets, length),
        out_shape=jax.ShapeDtypeStruct((cols, 1, 2, XM, shard), BF16),
        in_specs=[SMEM] + [VMEM] * 6 + [HBM],
        out_specs=HBM,
        scratch_shapes=scratch,
        input_output_aliases={7: 0},
        compiler_params=params(12),
        name="end",
    )(places, turn, edge_turn, even, odd, even_edge, odd_edge, updates)
    return grids, updates


def solution(mesh):
    in_specs = (
        P(None, "facet", None, None, "col"),
        P("facet", None),
        P(),
        P(None, "col"),
        P(None, "col", "facet", None),
    )
    out_specs = (P(None, "col", None, "facet", None), P(None, "facet", None, None, "col"))
    return jax.shard_map(
        computed, mesh=mesh, in_specs=in_specs, out_specs=out_specs, check_vma=False
    )
```

time: 53.6 us -> 47.4 us (0.88)
  local copies, waits for them, and re-layouts: 4.4 us -> 0.04 us
  other arithmetic: 5.42 us -> 2.65 us
  Pallas kernels: 10.3 us -> 11.7 us
  waiting for transfers between devices: 16.1 us -> 15.2 us
  starting transfers between devices: 16.3 us -> 16.9 us
    unnamed x13 -> x2, local copies, waits for them, and re-layouts: 2.63 us -> 0.01 us
    ppermute x7 -> x8, waiting for transfers between devices: 9.67 us -> 7.53 us  [swapped(): return lax.ppermute(block, 'facet', [(i, i ^ bit) for i in range(facets)])]
    pallas_call x3 -> x5, Pallas kernels: 10.3 us -> 11.7 us  [the longest x1 2.99 us: computed(): pl.pallas_call(functools.partial(update_kernel, facets, length), grid=(co...]
    ppermute x4, waiting for transfers between devices: 6.41 us -> 7.65 us  [shifted(): lax.ppermute(block, 'col', [(i, (i + distance) % count) for i in range(co...]
    pallas_call x1 -> x0, local copies, waits for them, and re-layouts: 1.08 us -> none  [per_device(): pl.pallas_call(functools.partial(spectrum_kernel, cols, facets, length),...]
    convert_element_type x2 -> x4, other arithmetic: 2.45 us -> 1.45 us  [the longest x1 1.27 us: make_table(): (taper[:, None] * jnp.sin(angle)).astype(BF16)]
    reshape x2, other arithmetic: 0.96 us -> 0.05 us  [gathered(): blocks = jnp.stack([blocks, received], axis=2).reshape(shape)]
    concatenate x1, other arithmetic: 0.84 us -> 0.04 us  [computed(): jnp.concatenate([jnp.concatenate([real_tab, imag_tab], axis=1), jnp.conca...]
  transfers between devices with their start and end apart: 11 -> 12, of which waited for: 10 -> 6; matrix products, arithmetic and copies ran while one was open for 9% -> 6% of each run, Pallas kernels for 0% -> 11%
where the time goes in v2:
time: 47.4 us; the launch traced here: 47.2 us
  starting transfers between devices  16.9 us (36%)
  waiting for transfers between devices  15.2 us (32%)
  Pallas kernels  11.7 us (25%)
  other arithmetic  2.65 us (6%)
  between operations  0.77 us (2%)
    ppermute x4, starting transfers between devices, shifted(): lax.ppermute(block, 'col', [(i, (i + distance) % count) for i in range(co...  9.9 us
    ppermute x4, waiting for transfers between devices, shifted(): lax.ppermute(block, 'col', [(i, (i + distance) % count) for i in range(co...  7.65 us
    ppermute x8, waiting for transfers between devices, swapped(): return lax.ppermute(block, 'facet', [(i, i ^ bit) for i in range(facets)])  7.53 us
    ppermute x8, starting transfers between devices, swapped(): return lax.ppermute(block, 'facet', [(i, i ^ bit) for i in range(facets)])  6.95 us
    pallas_call x1, Pallas kernels, computed(): pl.pallas_call(functools.partial(update_kernel, facets, length), grid=(co...  2.99 us
    pallas_call x1, Pallas kernels, computed(): pl.pallas_call(functools.partial(subgrid_kernel, cols, length, shard), ou...  2.26 us
    pallas_call x1, Pallas kernels, computed(): pl.pallas_call(functools.partial(main_kernel, cols, facets, length), out_...  2.21 us
    pallas_call x1, Pallas kernels, computed(): pl.pallas_call(functools.partial(end_kernel, cols, facets, length), out_s...  2.13 us
  transfers between devices with their start and end apart: 12, of which 6 were waited for; matrix products, arithmetic and copies ran while one was open for 6% of the time, Pallas kernels for 11%

profile of v2, /device:TPU:0, one launch (start us, length us, event | category | flops | bytes accessed | tf_op | source)
XLA Modules:
  0.0 47.2 jit_solution(6663066775653449342)
XLA Ops:
  0.6 2.1 %edge.1 = (bf16[2,2,2,128,128]{4,3,2,1,0:T(8,128)(2,1)S(1)}, bf16[2,2,2,128,128]{4,3,2,1,0:T(8,128)(2,1)S(1)}, f32[16,128]{1,0:T(8,128)S(1)}) custom-call(s32[1,2]{1,0:T(1,128)} %offsets.3, s32[2]{0:T(128)} %column.3, bf16[2,1,2,512,1024]{4,3,2,1,0:T(8,128)(2,1)} %spectra.3), custom_call_target="tpu_custom_call" | custom-call | tf_op jit(solution)/shard_map/edge/pallas_call | solution.py:392
  2.8 0.6 %collective-permute-start.2 = (bf16[2,2,2,128,128]{4,3,2,1,0:T(8,128)(2,1)S(1)}, bf16[2,2,2,128,128]{4,3,2,1,0:T(8,128)(2,1)S(1)}, u32[]{:S(2)}, u32[]{:S(2)}) collective-permute-start(bf16[2,2,2,128,128]{4,3,2,1,0:T(8,128)(2,1)S(1)} %get-tuple-element.16), channel_id=1, source_target_pairs={{0,8},{8,0},{16,24},{24,16},{1,9},{9,1},{17,25},{25,17},{2,10},{10... | collective-permute-start | bytes 786440 | tf_op jit(solution)/shard_map/ppermute | solution.py:341
  3.3 2.2 %main.1 = (bf16[2,2,2,128,128]{4,3,2,1,0:T(8,128)(2,1)S(1)}, bf16[2,2,2,128,128]{4,3,2,1,0:T(8,128)(2,1)S(1)}, f32[16,128]{1,0:T(8,128)S(1)}) custom-call(s32[1,2]{1,0:T(1,128)} %offsets.3, s32[2]{0:T(128)} %column.3, s32[1,2]{1,0:T(1,128)} %bitcast.25, bf16[2,1,2,512,1024]{4,3,2,1,0:T(8,128)(2,1)} %spectra.3, f32[16,128]{1,0:T(8,128)S(1)} %get-tuple-element.12.after.edge_turn), custom_call_target="tpu_custom_call" | custom-call | tf_op jit(solution)/shard_map/main/pallas_call | solution.py:401
  5.5 0.1 collective-permute-start
  5.7 1.3 %multiply_convert_fusion = (bf16[128,512]{1,0:T(8,128)(2,1)S(1)}, bf16[128,512]{1,0:T(8,128)(2,1)S(1)}) fusion(s32[512]{0:T(512)S(1)} %iota_add_fusion, s32[128]{0:T(128)S(1)} %iota_add_fusion.1, f32[128]{0:T(128)S(1)} %add_multiply_fusion), kind=kLoop, calls=%fused_computation.13 | loop fusion | flops 1179648 | bytes 265216 | tf_op jit(solution)/shard_map/convert_element_type | solution.py:37
  6.9 1.1 %fusion.3 = bf16[128,512]{1,0:T(8,128)(2,1)S(1)} fusion(s32[512]{0:T(512)S(1)} %iota_add_fusion, s32[128]{0:T(128)S(1)} %iota_add_fusion.1, f32[128]{0:T(128)S(1)} %add_multiply_fusion), kind=kLoop, calls=%fused_computation.20 | loop fusion | flops 1245184 | bytes 134144 | tf_op jit(solution)/shard_map/neg | solution.py:420
  8.0 0.1 add_convert_fusion
  8.1 3.0 %collective-permute-start.3 = (bf16[2,1,2,128,128]{4,3,2,1,0:T(8,128)(2,1)S(1)}, bf16[2,1,2,128,128]{4,3,2,1,0:T(8,128)(2,1)S(1)}, u32[]{:S(2)}, u32[]{:S(2)}) collective-permute-start(bf16[2,1,2,128,128]{4,3,2,1,0:T(8,128)(2,1)S(1)} %slice.31), channel_id=1, source_target_pairs={{0,16},{8,24},{16,0},{24,8},{1,17},{9,25},{17,1},{25,9},{2,18},{10... | collective-permute-start | bytes 393224 | tf_op jit(solution)/shard_map/ppermute | solution.py:341
  11.1 0.1 add_convert_fusion.1
  11.2 0.1 collective-permute-start.1
  11.3 4.2 %collective-permute-done.3 = bf16[2,1,2,128,128]{4,3,2,1,0:T(8,128)(2,1)S(1)} collective-permute-done((bf16[2,1,2,128,128]{4,3,2,1,0:T(8,128)(2,1)S(1)}, bf16[2,1,2,128,128]{4,3,2,1,0:T(8,128)(2,1)S(1)}, u32[]{:S(2)}, u32[]{:S(2)}) %collective-permute-start.3) | collective-permute-done | bytes 131104 | tf_op jit(solution)/shard_map/ppermute | solution.py:341
  15.5 5.2 %collective-permute-start.5 = (bf16[1,2,128,128]{3,2,1,0:T(8,128)(2,1)S(1)}, bf16[1,2,128,128]{3,2,1,0:T(8,128)(2,1)S(1)}, u32[]{:S(2)}, u32[]{:S(2)}) collective-permute-start(bf16[1,2,128,128]{3,2,1,0:T(8,128)(2,1)S(1)} %get-tuple-element.26), channel_id=1, source_target_pairs={{0,7},{1,0},{2,1},{3,2},{4,3},{5,4},{6,5},{7,6},{8,15},{9,8},{10,9... | collective-permute-start | bytes 196616 | tf_op jit(solution)/shard_map/ppermute | solution.py:346
  20.8 1.8 %collective-permute-done.5.from_next = bf16[1,2,128,128]{3,2,1,0:T(8,128)(2,1)S(1)} collective-permute-done((bf16[1,2,128,128]{3,2,1,0:T(8,128)(2,1)S(1)}, bf16[1,2,128,128]{3,2,1,0:T(8,128)(2,1)S(1)}, u32[]{:S(2)}, u32[]{:S(2)}) %collective-permute-start.5) | collective-permute-done | bytes 65568 | tf_op jit(solution)/shard_map/ppermute | solution.py:346
  22.6 5.1 %collective-permute-done.4.from_prev = bf16[1,2,128,128]{3,2,1,0:T(8,128)(2,1)S(1)} collective-permute-done((bf16[1,2,128,128]{3,2,1,0:T(8,128)(2,1)S(1)}, bf16[1,2,128,128]{3,2,1,0:T(8,128)(2,1)S(1)}, u32[]{:S(2)}, u32[]{:S(2)}) %collective-permute-start.4) | collective-permute-done | bytes 65568 | tf_op jit(solution)/shard_map/ppermute | solution.py:346
  27.7 2.3 %subgrid.1 = (bf16[2,1,2,128,512]{4,3,2,1,0:T(8,128)(2,1)}, bf16[2,1,2,128,128]{4,3,2,1,0:T(8,128)(2,1)S(1)}, bf16[1,2,128,128]{3,2,1,0:T(8,128)(2,1)S(1)}, bf16[1,2,128,128]{3,2,1,0:T(8,128)(2,1)S(1)}) custom-call(s32[1,2]{1,0:T(1,128)} %bitcast.26, bf16[2,1,2,128,128]{4,3,2,1,0:T(8,128)(2,1)S(1)} %get-tuple-element.23.kept, ...), custom_call_target="tpu_custom_call" | custom-call | tf_op jit(solution)/shard_map/subgrid/pallas_call | solution.py:426
  29.9 4.7 %collective-permute-start.9 = (bf16[1,2,128,128]{3,2,1,0:T(8,128)(2,1)S(1)}, bf16[1,2,128,128]{3,2,1,0:T(8,128)(2,1)S(1)}, u32[]{:S(2)}, u32[]{:S(2)}) collective-permute-start(bf16[1,2,128,128]{3,2,1,0:T(8,128)(2,1)S(1)} %get-tuple-element.21), channel_id=1, source_target_pairs={{0,7},{1,0},{2,1},{3,2},{4,3},{5,4},{6,5},{7,6},{8,15},{9,8},{10,9... | collective-permute-start | bytes 196616 | tf_op jit(solution)/shard_map/ppermute | solution.py:346
  34.7 1.5 %collective-permute-start.6 = (bf16[2,1,2,128,128]{4,3,2,0,1:T(8,128)(2,1)S(1)}, bf16[2,1,2,128,128]{4,3,2,0,1:T(8,128)(2,1)S(1)}, u32[]{:S(2)}, u32[]{:S(2)}) collective-permute-start(bf16[2,1,2,128,128]{4,3,2,0,1:T(8,128)(2,1)S(1)} %bitcast.19), channel_id=1, source_target_pairs={{0,16},{8,24},{16,0},{24,8},{1,17},{9,25},{17,1},{25,9},{2,18},{10... | collective-permute-start | bytes 393224 | tf_op jit(solution)/shard_map/ppermute | solution.py:341
  36.2 0.7 %collective-permute-done.8 = bf16[1,2,128,128]{3,2,1,0:T(8,128)(2,1)S(1)} collective-permute-done((bf16[1,2,128,128]{3,2,1,0:T(8,128)(2,1)S(1)}, bf16[1,2,128,128]{3,2,1,0:T(8,128)(2,1)S(1)}, u32[]{:S(2)}, u32[]{:S(2)}) %collective-permute-start.8) | collective-permute-done | bytes 65568 | tf_op jit(solution)/shard_map/ppermute | solution.py:346
  36.9 1.6 %collective-permute-start.10 = (bf16[2,1,2,128,128]{4,3,2,0,1:T(8,128)(2,1)S(1)}, bf16[2,1,2,128,128]{4,3,2,0,1:T(8,128)(2,1)S(1)}, u32[]{:S(2)}, u32[]{:S(2)}) collective-permute-start(bf16[2,1,2,128,128]{4,3,2,0,1:T(8,128)(2,1)S(1)} %get-tuple-element.25), channel_id=1, source_target_pairs={{0,16},{8,24},{16,0},{24,8},{1,17},{9,25},{17,1},{25,9},{2,18},{10... | collective-permute-start | bytes 393224 | tf_op jit(solution)/shard_map/ppermute | solution.py:341
  38.5 1.1 %collective-permute-done.6 = bf16[2,1,2,128,128]{4,3,2,0,1:T(8,128)(2,1)S(1)} collective-permute-done((bf16[2,1,2,128,128]{4,3,2,0,1:T(8,128)(2,1)S(1)}, bf16[2,1,2,128,128]{4,3,2,0,1:T(8,128)(2,1)S(1)}, u32[]{:S(2)}, u32[]{:S(2)}) %collective-permute-start.6) | collective-permute-done | bytes 131104 | tf_op jit(solution)/shard_map/ppermute | solution.py:341
  39.7 0.1 collective-permute-start.7
  39.7 2.2 %collective-permute-done.10 = bf16[2,1,2,128,128]{4,3,2,0,1:T(8,128)(2,1)S(1)} collective-permute-done((bf16[2,1,2,128,128]{4,3,2,0,1:T(8,128)(2,1)S(1)}, bf16[2,1,2,128,128]{4,3,2,0,1:T(8,128)(2,1)S(1)}, u32[]{:S(2)}, u32[]{:S(2)}) %collective-permute-start.10) | collective-permute-done | bytes 131104 | tf_op jit(solution)/shard_map/ppermute | solution.py:341
  42.1 3.0 %update.1.whole = bf16[2,1,2,512,1024]{4,3,2,1,0:T(8,128)(2,1)} custom-call(s32[1,2]{1,0:T(1,128)} %bitcast.27, f32[16,128]{1,0:T(8,128)S(1)} %get-tuple-element.18.turn, bf16[2,2,2,128,128]{4,3,2,1,0:T(8,128)(2,1)S(1)} %maximum_bitcast_fusion.even, bf16[2,2,2,128,128]{4,3,2,1,0:T(8,128)(2,1)S(1)} %collective-permute-done.7.odd), custom_call_target="tpu_custom_call" | custom-call | tf_op jit(solution)/shard_map/update/pallas_call | solution.py:453
  45.1 2.1 %end.1 = bf16[2,1,2,512,1024]{4,3,2,1,0:T(8,128)(2,1)} custom-call(s32[1,2]{1,0:T(1,128)} %bitcast.28, f32[16,128]{1,0:T(8,128)S(1)} %get-tuple-element.18.turn, f32[16,128]{1,0:T(8,128)S(1)} %get-tuple-element.12.after.edge_turn, bf16[2,2,2,128,128]{4,3,2,1,0:T(8,128)(2,1)S(1)} %maximum_bitcast_fusion.even, ...), custom_call_target="tpu_custom_call", output_to_operand_aliasing={{}: (7, {})} | custom-call | tf_op jit(solution)/shard_map/end/pallas_call | solution.py:462
  (22 shorter events, 0.3 us)
Async XLA Ops:
  2.8 5.2 %collective-permute-start.2 = (bf16[2,2,2,128,128]{4,3,2,1,0:T(8,128)(2,1)S(1)}, bf16[2,2,2,128,128]{4,3,2,1,0:T(8,128)(2,1)S(1)}, u32[]{:S(2)}, u32[]{:S(2)}) collective-permute-start(bf16[2,2,2,128,128]{4,3,2,1,0:T(8,128)(2,1)S(1)} %get-tuple-element.16), channel_id=1, source_target_pairs={{0,8},{8,0},{16,24},{24,16},{1,9},{9,1},{17,25},{25,17},{2,10},{10... | collective-permute-start | bytes 786440 | tf_op jit(solution)/shard_map/ppermute | solution.py:341
  3.3 24.4 %copy-start = (bf16[2,1,128,512]{3,2,1,0:T(8,128)(2,1)S(1)}, bf16[2,1,128,512]{3,2,1,0:T(8,128)(2,1)}, u32[]{:S(2)}) copy-start(bf16[2,1,128,512]{3,2,1,0:T(8,128)(2,1)} %weights.1) | copy-start | bytes 786436
  5.5 5.6 %collective-permute-start = (bf16[2,2,2,128,128]{4,3,2,1,0:T(8,128)(2,1)S(1)}, bf16[2,2,2,128,128]{4,3,2,1,0:T(8,128)(2,1)S(1)}, u32[]{:S(2)}, u32[]{:S(2)}) collective-permute-start(bf16[2,2,2,128,128]{4,3,2,1,0:T(8,128)(2,1)S(1)} %get-tuple-element.14), channel_id=1, source_target_pairs={{0,8},{8,0},{16,24},{24,16},{1,9},{9,1},{17,25},{25,17},{2,10},{10... | collective-permute-start | bytes 786440 | tf_op jit(solution)/shard_map/ppermute | solution.py:341
  8.1 7.4 %collective-permute-start.3 = (bf16[2,1,2,128,128]{4,3,2,1,0:T(8,128)(2,1)S(1)}, bf16[2,1,2,128,128]{4,3,2,1,0:T(8,128)(2,1)S(1)}, u32[]{:S(2)}, u32[]{:S(2)}) collective-permute-start(bf16[2,1,2,128,128]{4,3,2,1,0:T(8,128)(2,1)S(1)} %slice.31), channel_id=1, source_target_pairs={{0,16},{8,24},{16,0},{24,8},{1,17},{9,25},{17,1},{25,9},{2,18},{10... | collective-permute-start | bytes 393224 | tf_op jit(solution)/shard_map/ppermute | solution.py:341
  11.2 9.5 %collective-permute-start.1 = (bf16[2,1,2,128,128]{4,3,2,1,0:T(8,128)(2,1)S(1)}, bf16[2,1,2,128,128]{4,3,2,1,0:T(8,128)(2,1)S(1)}, u32[]{:S(2)}, u32[]{:S(2)}) collective-permute-start(bf16[2,1,2,128,128]{4,3,2,1,0:T(8,128)(2,1)S(1)} %get-tuple-element.22), channel_id=1, source_target_pairs={{0,16},{8,24},{16,0},{24,8},{1,17},{9,25},{17,1},{25,9},{2,18},{10... | collective-permute-start | bytes 393224 | tf_op jit(solution)/shard_map/ppermute | solution.py:341
  15.5 7.1 %collective-permute-start.5 = (bf16[1,2,128,128]{3,2,1,0:T(8,128)(2,1)S(1)}, bf16[1,2,128,128]{3,2,1,0:T(8,128)(2,1)S(1)}, u32[]{:S(2)}, u32[]{:S(2)}) collective-permute-start(bf16[1,2,128,128]{3,2,1,0:T(8,128)(2,1)S(1)} %get-tuple-element.26), channel_id=1, source_target_pairs={{0,7},{1,0},{2,1},{3,2},{4,3},{5,4},{6,5},{7,6},{8,15},{9,8},{10,9... | collective-permute-start | bytes 196616 | tf_op jit(solution)/shard_map/ppermute | solution.py:346
  20.7 7.0 %collective-permute-start.4 = (bf16[1,2,128,128]{3,2,1,0:T(8,128)(2,1)S(1)}, bf16[1,2,128,128]{3,2,1,0:T(8,128)(2,1)S(1)}, u32[]{:S(2)}, u32[]{:S(2)}) collective-permute-start(bf16[1,2,128,128]{3,2,1,0:T(8,128)(2,1)S(1)} %get-tuple-element.27), channel_id=1, source_target_pairs={{0,1},{1,2},{2,3},{3,4},{4,5},{5,6},{6,7},{7,0},{8,9},{9,10},{10,1... | collective-permute-start | bytes 196616 | tf_op jit(solution)/shard_map/ppermute | solution.py:346
  29.9 7.0 %collective-permute-start.8 = (bf16[1,2,128,128]{3,2,1,0:T(8,128)(2,1)S(1)}, bf16[1,2,128,128]{3,2,1,0:T(8,128)(2,1)S(1)}, u32[]{:S(2)}, u32[]{:S(2)}) collective-permute-start(bf16[1,2,128,128]{3,2,1,0:T(8,128)(2,1)S(1)} %get-tuple-element.20), channel_id=1, source_target_pairs={{0,1},{1,2},{2,3},{3,4},{4,5},{5,6},{6,7},{7,0},{8,9},{9,10},{10,1... | collective-permute-start | bytes 196616 | tf_op jit(solution)/shard_map/ppermute | solution.py:346
  29.9 7.0 %collective-permute-start.9 = (bf16[1,2,128,128]{3,2,1,0:T(8,128)(2,1)S(1)}, bf16[1,2,128,128]{3,2,1,0:T(8,128)(2,1)S(1)}, u32[]{:S(2)}, u32[]{:S(2)}) collective-permute-start(bf16[1,2,128,128]{3,2,1,0:T(8,128)(2,1)S(1)} %get-tuple-element.21), channel_id=1, source_target_pairs={{0,7},{1,0},{2,1},{3,2},{4,3},{5,4},{6,5},{7,6},{8,15},{9,8},{10,9... | collective-permute-start | bytes 196616 | tf_op jit(solution)/shard_map/ppermute | solution.py:346
  34.7 5.0 %collective-permute-start.6 = (bf16[2,1,2,128,128]{4,3,2,0,1:T(8,128)(2,1)S(1)}, bf16[2,1,2,128,128]{4,3,2,0,1:T(8,128)(2,1)S(1)}, u32[]{:S(2)}, u32[]{:S(2)}) collective-permute-start(bf16[2,1,2,128,128]{4,3,2,0,1:T(8,128)(2,1)S(1)} %bitcast.19), channel_id=1, source_target_pairs={{0,16},{8,24},{16,0},{24,8},{1,17},{9,25},{17,1},{25,9},{2,18},{10... | collective-permute-start | bytes 393224 | tf_op jit(solution)/shard_map/ppermute | solution.py:341
  36.9 5.0 %collective-permute-start.10 = (bf16[2,1,2,128,128]{4,3,2,0,1:T(8,128)(2,1)S(1)}, bf16[2,1,2,128,128]{4,3,2,0,1:T(8,128)(2,1)S(1)}, u32[]{:S(2)}, u32[]{:S(2)}) collective-permute-start(bf16[2,1,2,128,128]{4,3,2,0,1:T(8,128)(2,1)S(1)} %get-tuple-element.25), channel_id=1, source_target_pairs={{0,16},{8,24},{16,0},{24,8},{1,17},{9,25},{17,1},{25,9},{2,18},{10... | collective-permute-start | bytes 393224 | tf_op jit(solution)/shard_map/ppermute | solution.py:341
  39.7 2.4 %collective-permute-start.7 = (bf16[2,2,2,128,128]{4,3,2,1,0:T(8,128)(2,1)S(1)}, bf16[2,2,2,128,128]{4,3,2,1,0:T(8,128)(2,1)S(1)}, u32[]{:S(2)}, u32[]{:S(2)}) collective-permute-start(bf16[2,2,2,128,128]{4,3,2,1,0:T(8,128)(2,1)S(1)} %maximum_bitcast_fusion.even), channel_id=1, source_target_pairs={{0,8},{8,0},{16,24},{24,16},{1,9},{9,1},{17,25},{25,17},{2,10},{10... | collective-permute-start | bytes 786440 | tf_op jit(solution)/shard_map/ppermute | solution.py:341
  42.0 3.1 %collective-permute-start.11 = (bf16[2,2,2,128,128]{4,3,2,1,0:T(8,128)(2,1)S(1)}, bf16[2,2,2,128,128]{4,3,2,1,0:T(8,128)(2,1)S(1)}, u32[]{:S(2)}, u32[]{:S(2)}) collective-permute-start(bf16[2,2,2,128,128]{4,3,2,1,0:T(8,128)(2,1)S(1)} %maximum_bitcast_fusion.1.even_edge), channel_id=1, source_target_pairs={{0,8},{8,0},{16,24},{24,16},{1,9},{9,1},{17,25},{25,17},{2,10},{10... | collective-permute-start | bytes 786440 | tf_op jit(solution)/shard_map/ppermute | solution.py:341

commit v3 on v2

v3 whole, which is shorter than its diff:
```python
import functools
import math

import jax
import jax.numpy as jnp
from jax import lax
from jax.experimental import pallas as pl
from jax.experimental.pallas import tpu as pltpu
from jax.sharding import PartitionSpec as P


IMAGE = 65536
XM = 512
WM = 128
XA = 448
LANES = 128
HALF = WM // 2

TAU = 2.0 * math.pi
BF16 = jnp.bfloat16
F32 = jnp.float32

VMEM = pl.BlockSpec(memory_space=pltpu.VMEM)
SMEM = pl.BlockSpec(memory_space=pltpu.SMEM)
HBM = pl.BlockSpec(memory_space=pltpu.HBM)


def remainder(value, modulus):
    if modulus & (modulus - 1) == 0:
        return value & (modulus - 1)
    return lax.rem(value, jnp.int32(modulus))


def modular(first, second, image):
    upper = second // 256
    lower = remainder(second, 256)
    return remainder(remainder(first * upper, image // 256) * 256 + first * lower, image)


def place_of(subgrid_offset, here, shard, length):
    start = subgrid_offset // (IMAGE // length) - here * shard - HALF + LANES
    return lax.div(start, jnp.int32(LANES)) - 1, remainder(start, LANES)


def lanes_of(shape):
    return lax.broadcasted_iota(jnp.int32, shape, len(shape) - 1)


def turns_of(turn, index, firsts, second, length):
    rows = lax.broadcasted_iota(jnp.int32, (8, LANES), 0)
    first = jnp.zeros((8, LANES), F32)
    for c, value in enumerate(firsts):
        first = jnp.where(rows == c, value.astype(F32), first)
    steps = remainder(index * second, length).astype(F32)
    angle = TAU * (first / IMAGE + steps / length)
    turn[0:8, :] = jnp.cos(angle)
    turn[8:16, :] = jnp.sin(angle)


def firsts_of(cols, offsets, column):
    return [modular(column[c] * XA, offsets[0, 0], IMAGE) for c in range(cols)]


def rows_of(facet, s, block):
    return pl.ds(pl.multiple_of((facet ^ s) * block, block), block)


def fetched(spectra, buf, sems, c, s, rows, places):
    copies = []
    for slot, at in enumerate(places):
        copy = pltpu.make_async_copy(
            spectra.at[c, 0, :, rows, pl.ds(at, LANES)],
            buf.at[c, slot, :, rows, :],
            sems.at[c, slot, s],
        )
        copy.start()
        copies.append(copy)
    return copies


def turned(parts, cosine, sine):
    return parts[0] * cosine + parts[1] * sine, parts[1] * cosine - parts[0] * sine


def edge_kernel(
    cols, facets, length, offsets, column, spectra, send, keep, turn, buf, sems, own, held, small
):
    shard = spectra.shape[4]
    block = XM // facets
    here = lax.axis_index("col")
    facet = lax.axis_index("facet")
    scalars = [
        pltpu.make_async_copy(offsets, own, small.at[0]),
        pltpu.make_async_copy(column, held, small.at[1]),
    ]
    for copy in scalars:
        copy.start()
    copies = {}
    order = [s for s in range(facets) if s % 2] + [s for s in range(facets) if s % 2 == 0]
    for c in range(cols):
        for s in order:
            rows = rows_of(facet, s, block)
            copies[c, s] = fetched(spectra, buf, sems, c, s, rows, (0, shard - LANES))
    for copy in scalars:
        copy.wait()
    lanes = lanes_of((8, LANES))
    index = here * shard + lanes + jnp.where(lanes < HALF, 0, shard - LANES)
    turns_of(turn, index, firsts_of(cols, own, held), own[0, 1], length)
    left = lanes_of((1, LANES)) < HALF
    for c in range(cols):
        cosine = turn[c : c + 1, :]
        sine = turn[8 + c : 9 + c, :]
        for s in order:
            for copy in copies[c, s]:
                copy.wait()
            rows = rows_of(facet, s, block)
            target = send if s % 2 else keep
            parts = [
                jnp.where(
                    left,
                    buf[c, 0, part, rows, :].astype(F32),
                    buf[c, 1, part, rows, :].astype(F32),
                )
                for part in range(2)
            ]
            real, imag = turned(parts, cosine, sine)
            low = jnp.where(left, real, pltpu.roll(imag, HALF, 1))
            high = jnp.where(left, pltpu.roll(real, HALF, 1), imag)
            target[0, s // 2, c] = low.astype(BF16)
            target[1, s // 2, c] = high.astype(BF16)


def main_kernel(
    cols, facets, length, offsets, column, subgrid, spectra, after, send, keep, turn, buf, sems
):
    del after
    shard = spectra.shape[4]
    tiles = shard // LANES
    block = XM // facets
    here = lax.axis_index("col")
    facet = lax.axis_index("facet")
    copies = {}
    places = []
    for c in range(cols):
        tile, lane = place_of(subgrid[0, c], here, shard, length)
        places.append((tile, lane))
        low = pl.multiple_of(jnp.maximum(tile, 0) * LANES, LANES)
        high = pl.multiple_of(jnp.minimum(tile + 1, tiles - 1) * LANES, LANES)
        for s in range(facets):
            rows = rows_of(facet, s, block)
            copies[c, s] = fetched(spectra, buf, sems, c, s, rows, (low, high))
    lanes = lanes_of((8, LANES))
    rows = lax.broadcasted_iota(jnp.int32, (8, LANES), 0)
    held = jnp.zeros((8, LANES), jnp.int32)
    begins = jnp.zeros((8, LANES), jnp.int32)
    for c in range(cols):
        tile, lane = places[c]
        held = jnp.where(rows == c, jnp.where(lanes >= lane, tile, tile + 1), held)
        begins = jnp.where(rows == c, lane, begins)
    index = remainder(here * shard + lanes + held * LANES + length, length)
    turns_of(turn, index, firsts_of(cols, offsets, column), offsets[0, 1], length)
    turn[16:24, :] = held.astype(F32)
    turn[24:32, :] = begins.astype(F32)
    lanes = lanes_of((1, LANES))
    zero = jnp.zeros((1, LANES), F32)
    for c in range(cols):
        tile, lane = places[c]
        from_low = jnp.logical_and(lanes >= lane, tile >= 0)
        from_high = jnp.logical_and(lanes < lane, tile + 1 < tiles)
        cosine = turn[c : c + 1, :]
        sine = turn[8 + c : 9 + c, :]
        for s in range(facets):
            for copy in copies[c, s]:
                copy.wait()
            rows = rows_of(facet, s, block)
            target = send if s % 2 else keep
            parts = [
                jnp.where(
                    from_low,
                    buf[c, 0, part, rows, :].astype(F32),
                    jnp.where(from_high, buf[c, 1, part, rows, :].astype(F32), zero),
                )
                for part in range(2)
            ]
            real, imag = turned(parts, cosine, sine)
            target[0, s // 2, c] = real.astype(BF16)
            target[1, s // 2, c] = imag.astype(BF16)


def table_kernel(facets, after, table):
    del after
    place = lax.broadcasted_iota(jnp.int32, (WM, LANES), 0)
    cell = lanes_of((WM, LANES))
    angle = TAU * remainder((place - HALF) * cell + HALF * XM, XM).astype(F32) / XM
    relative = (place.astype(F32) + 0.5 - WM / 2.0) / (WM / 2.0)
    taper = (0.3 + 0.7 * (1.0 - relative * relative)) / jnp.sqrt(
        jnp.full((1, LANES), WM * facets, F32)
    )
    cosine = taper * jnp.cos(angle)
    sine = taper * jnp.sin(angle)
    for tile in range(XM // LANES):
        first = tile * LANES - XM // 2
        quarter = remainder((place - HALF) * (first * 4 // XM) + HALF * 4, 4)
        odd = remainder(quarter, 2) == 1
        real = jnp.where(odd, sine, cosine)
        imag = jnp.where(odd, cosine, sine)
        real = jnp.where(jnp.logical_or(quarter == 1, quarter == 2), -real, real).astype(BF16)
        imag = jnp.where(quarter >= 2, -imag, imag)
        span = slice(tile * LANES, (tile + 1) * LANES)
        other = slice(XM + tile * LANES, XM + (tile + 1) * LANES)
        table[:WM, span] = real
        table[WM:, other] = real
        table[:WM, other] = imag.astype(BF16)
        table[WM:, span] = (-imag).astype(BF16)


def zero_kernel(after, out, buf, sems):
    del after
    cols, _, _, height, _ = out.shape
    block = buf.shape[0]
    buf[...] = jnp.zeros(buf.shape, BF16)
    copies = []
    for c in range(cols):
        for part in range(2):
            for i in range(height // block):
                rows = pl.ds(i * block, block)
                copies.append(
                    pltpu.make_async_copy(buf, out.at[c, 0, part, rows, :], sems.at[c, part, i])
                )
    for copy in copies:
        copy.start()
    for copy in copies:
        copy.wait()


def subgrid_kernel(
    cols,
    shard,
    turn,
    kept,
    received,
    from_prev,
    from_next,
    table,
    weights,
    grids,
    back,
    to_prev,
    to_next,
    stack,
    scaled,
    stage,
    sems,
):
    tiles = shard // LANES
    block = kept.shape[3]
    zero = jnp.zeros((1, LANES), F32)
    begins = [jnp.max(turn[24 + c : 25 + c, :].astype(jnp.int32)) for c in range(cols)]
    for c in range(cols):
        held = turn[16 + c : 17 + c, :]
        low = held < 0
        high = held > tiles - 1
        prev = from_prev[0, c].astype(F32)
        nxt = from_next[0, c].astype(F32)
        shift = remainder(LANES - begins[c], LANES)
        real = kept[0, 0, c].astype(F32) + received[0, 0, c].astype(F32)
        real = real + jnp.where(low, pltpu.roll(prev, HALF, 1), jnp.where(high, nxt, zero))
        imag = kept[1, 0, c].astype(F32) + received[1, 0, c].astype(F32)
        imag = imag + jnp.where(low, prev, jnp.where(high, pltpu.roll(nxt, HALF, 1), zero))
        rows = slice(c * block, (c + 1) * block)
        stack[rows, :WM] = pltpu.roll(real, shift, 1).astype(BF16)
        stack[rows, WM:] = pltpu.roll(imag, shift, 1).astype(BF16)
    copies = []
    for part in range(2):
        span = slice(part * XM, (part + 1) * XM)
        product = jnp.dot(stack[...], table[:, span], preferred_element_type=F32)
        rounded = product.astype(BF16)
        for c in range(cols):
            rows = slice(c * block, (c + 1) * block)
            piece = rounded[rows]
            stage[c, part] = piece
            scaled[rows, span] = (piece.astype(F32) * weights[c, 0].astype(F32)).astype(BF16)
        copy = pltpu.make_async_copy(stage.at[:, part], grids.at[:, 0, part], sems.at[part])
        copy.start()
        copies.append(copy)
    result = lax.dot_general(
        scaled[...],
        table[...],
        (((1,), (1,)), ((), ())),
        preferred_element_type=F32,
    )
    for c in range(cols):
        held = turn[16 + c : 17 + c, :]
        rows = slice(c * block, (c + 1) * block)
        low = held < 0
        high = held > tiles - 1
        real = pltpu.roll(result[rows, :WM], begins[c], 1)
        imag = pltpu.roll(result[rows, WM:], begins[c], 1)
        back[0, 0, c] = real.astype(BF16)
        back[1, 0, c] = imag.astype(BF16)
        real_low = jnp.where(low, real, zero)
        imag_low = jnp.where(low, imag, zero)
        real_high = jnp.where(high, real, zero)
        imag_high = jnp.where(high, imag, zero)
        to_prev[0, c] = (pltpu.roll(real_low, HALF, 1) + imag_low).astype(BF16)
        to_next[0, c] = (real_high + pltpu.roll(imag_high, HALF, 1)).astype(BF16)
    for copy in copies:
        copy.wait()


def phased(source, s, c, cosine, sine):
    real = source[0, s // 2, c].astype(F32)
    imag = source[1, s // 2, c].astype(F32)
    return real * cosine - imag * sine, imag * cosine + real * sine


def window_kernel(cols, facets, length, subgrid, turn, even, odd, whole, out, buf, sems):
    shard = out.shape[4]
    tiles = shard // LANES
    block = XM // facets
    here = lax.axis_index("col")
    facet = lax.axis_index("facet")
    lanes = lanes_of((1, LANES))
    zero = jnp.zeros((1, LANES), F32)
    copies = []
    for c in range(cols):
        tile, lane = place_of(subgrid[0, c], here, shard, length)
        cosine = turn[c : c + 1, :]
        sine = turn[8 + c : 9 + c, :]
        is_low = lanes >= lane
        for s in range(facets):
            rows = rows_of(facet, s, block)
            values = phased(odd if s % 2 else even, s, c, cosine, sine)
            for part in range(2):
                buf[c, 0, part, rows, :] = jnp.where(is_low, values[part], zero).astype(BF16)
                buf[c, 1, part, rows, :] = jnp.where(is_low, zero, values[part]).astype(BF16)
        for slot in range(2):
            which = tile + slot
            at = pl.multiple_of(jnp.clip(which, 0, tiles - 1) * LANES, LANES)
            copy = pltpu.make_async_copy(
                buf.at[c, slot], out.at[c, 0, :, :, pl.ds(at, LANES)], sems.at[c, slot]
            )
            inside = jnp.logical_and(which > 0, which < tiles - 1)
            pl.when(inside)(copy.start)
            copies.append((inside, copy))
    for inside, copy in copies:
        pl.when(inside)(copy.wait)


def end_kernel(
    cols, facets, turn, edge_turn, even, odd, even_edge, odd_edge, whole, out, buf, sems
):
    shard = out.shape[4]
    tiles = shard // LANES
    block = XM // facets
    facet = lax.axis_index("facet")
    left = lanes_of((1, LANES)) < HALF
    zero = jnp.zeros((1, LANES), F32)
    copies = []
    for c in range(cols):
        cosine = turn[c : c + 1, :]
        sine = turn[8 + c : 9 + c, :]
        edge_cosine = edge_turn[c : c + 1, :]
        edge_sine = edge_turn[8 + c : 9 + c, :]
        held = turn[16 + c : 17 + c, :]
        in_first = held == 0
        in_last = held == tiles - 1
        for s in range(facets):
            rows = rows_of(facet, s, block)
            values = phased(odd if s % 2 else even, s, c, cosine, sine)
            edges = odd_edge if s % 2 else even_edge
            prev = edges[0, s // 2, c].astype(F32)
            nxt = edges[1, s // 2, c].astype(F32)
            real = jnp.where(left, prev, pltpu.roll(nxt, HALF, 1))
            imag = jnp.where(left, pltpu.roll(prev, HALF, 1), nxt)
            ends = (
                real * edge_cosine - imag * edge_sine,
                imag * edge_cosine + real * edge_sine,
            )
            for part in range(2):
                value = values[part]
                end = ends[part]
                buf[c, 0, part, rows, :] = (
                    jnp.where(left, end, zero) + jnp.where(in_first, value, zero)
                ).astype(BF16)
                buf[c, 1, part, rows, :] = (
                    jnp.where(left, zero, end) + jnp.where(in_last, value, zero)
                ).astype(BF16)
            for slot, start in enumerate((0, shard - LANES)):
                copy = pltpu.make_async_copy(
                    buf.at[c, slot, :, rows, :],
                    out.at[c, 0, :, rows, pl.ds(start, LANES)],
                    sems.at[c, slot, s],
                )
                copy.start()
                copies.append(copy)
    for copy in copies:
        copy.wait()


def swapped(block, bit):
    facets = lax.axis_size("facet")
    return lax.ppermute(block, "facet", [(i, i ^ bit) for i in range(facets)])


def shifted(block, distance):
    count = lax.axis_size("col")
    return lax.ppermute(block, "col", [(i, (i + distance) % count) for i in range(count)])


def added(kept, received):
    return (kept.astype(F32) + received.astype(F32)).astype(BF16)


def reduced(kept, sent, facets):
    received = swapped(sent, 1)
    bit = 2
    while bit < facets:
        blocks = added(kept, received)
        kept, sent = blocks[:, 0::2], blocks[:, 1::2]
        received = swapped(sent, bit)
        bit *= 2
    return kept, received


def gathered(blocks, facets):
    bit = facets // 2
    while bit > 1:
        received = swapped(blocks, bit)
        shape = (blocks.shape[0], -1) + blocks.shape[2:]
        blocks = jnp.stack([blocks, received], axis=2).reshape(shape)
        bit //= 2
    return blocks, swapped(blocks, 1)


def params(mib):
    return pltpu.CompilerParams(vmem_limit_bytes=mib * 1024 * 1024)


def computed(facet_spectra, facet_offsets, column_index, subgrid_offsets, weights):
    cols = facet_spectra.shape[0]
    shard = facet_spectra.shape[4]
    facets = lax.axis_size("facet")
    length = shard * lax.axis_size("col")
    block = XM // facets
    facet_spectra, facet_offsets, column_index, places = (
        pltpu.with_memory_space_constraint(array, pltpu.HBM)
        for array in (facet_spectra, facet_offsets, column_index, subgrid_offsets.T)
    )

    pieces = jax.ShapeDtypeStruct((2, facets // 2, cols, block, LANES), BF16)
    tile_pair = pltpu.VMEM((cols, 2, 2, XM, LANES), BF16)
    pair_sems = pltpu.SemaphoreType.DMA((cols, 2, facets))
    edge_send, edge_keep, edge_turn = pl.pallas_call(
        functools.partial(edge_kernel, cols, facets, length),
        out_shape=(pieces, pieces, jax.ShapeDtypeStruct((16, LANES), F32)),
        in_specs=[HBM, HBM, HBM],
        out_specs=(VMEM, VMEM, VMEM),
        scratch_shapes=[
            tile_pair,
            pair_sems,
            pltpu.SMEM(facet_offsets.shape, jnp.int32),
            pltpu.SMEM(column_index.shape, jnp.int32),
            pltpu.SemaphoreType.DMA((2,)),
        ],
        compiler_params=params(12),
        name="edge",
    )(facet_offsets, column_index, facet_spectra)
    edges = added(*reduced(edge_keep, edge_send, facets))

    main_send, main_keep, turn = pl.pallas_call(
        functools.partial(main_kernel, cols, facets, length),
        out_shape=(pieces, pieces, jax.ShapeDtypeStruct((32, LANES), F32)),
        in_specs=[SMEM, SMEM, SMEM, HBM, VMEM],
        out_specs=(VMEM, VMEM, VMEM),
        scratch_shapes=[tile_pair, pair_sems],
        compiler_params=params(12),
        name="main",
    )(facet_offsets, column_index, places, facet_spectra, edge_turn)
    main_kept, main_received = reduced(main_keep, main_send, facets)
    from_prev = shifted(edges[1], 1)
    from_next = shifted(edges[0], -1)

    table = pl.pallas_call(
        functools.partial(table_kernel, facets),
        out_shape=jax.ShapeDtypeStruct((2 * WM, 2 * XM), BF16),
        in_specs=[VMEM],
        out_specs=VMEM,
        compiler_params=params(12),
        name="table",
    )(edge_turn)
    shape = jax.ShapeDtypeStruct((cols, 1, 2, XM, shard), BF16)
    updates = pl.pallas_call(
        zero_kernel,
        out_shape=shape,
        in_specs=[VMEM],
        out_specs=HBM,
        scratch_shapes=[
            pltpu.VMEM((LANES, shard), BF16),
            pltpu.SemaphoreType.DMA((cols, 2, XM // LANES)),
        ],
        compiler_params=params(12),
        name="zero",
    )(turn)

    edge = jax.ShapeDtypeStruct((1, cols, block, LANES), BF16)
    grids, back, to_prev, to_next = pl.pallas_call(
        functools.partial(subgrid_kernel, cols, shard),
        out_shape=(
            jax.ShapeDtypeStruct((cols, 1, 2, block, XM), BF16),
            jax.ShapeDtypeStruct((2, 1, cols, block, LANES), BF16),
            edge,
            edge,
        ),
        in_specs=[VMEM] * 7,
        out_specs=(HBM, VMEM, VMEM, VMEM),
        scratch_shapes=[
            pltpu.VMEM((cols * block, 2 * WM), BF16),
            pltpu.VMEM((cols * block, 2 * XM), BF16),
            pltpu.VMEM((cols, 2, block, XM), BF16),
            pltpu.SemaphoreType.DMA((2,)),
        ],
        compiler_params=params(12),
        name="subgrid",
    )(turn, main_kept, main_received, from_prev, from_next, table, weights)

    came_prev = shifted(to_next, 1)
    came_next = shifted(to_prev, -1)
    even, odd = gathered(back, facets)
    even_edge, odd_edge = gathered(jnp.stack([came_prev, came_next]), facets)

    updates = pl.pallas_call(
        functools.partial(window_kernel, cols, facets, length),
        out_shape=shape,
        in_specs=[SMEM, VMEM, VMEM, VMEM, HBM],
        out_specs=HBM,
        scratch_shapes=[tile_pair, pltpu.SemaphoreType.DMA((cols, 2))],
        input_output_aliases={4: 0},
        compiler_params=params(12),
        name="window",
    )(places, turn, even, odd, updates)
    updates = pl.pallas_call(
        functools.partial(end_kernel, cols, facets),
        out_shape=shape,
        in_specs=[VMEM] * 6 + [HBM],
        out_specs=HBM,
        scratch_shapes=[tile_pair, pair_sems],
        input_output_aliases={6: 0},
        compiler_params=params(12),
        name="end",
    )(turn, edge_turn, even, odd, even_edge, odd_edge, updates)
    return grids, updates


def solution(mesh):
    in_specs = (
        P(None, "facet", None, None, "col"),
        P("facet", None),
        P(),
        P(None, "col"),
        P(None, "col", "facet", None),
    )
    out_specs = (P(None, "col", None, "facet", None), P(None, "facet", None, None, "col"))
    return jax.shard_map(
        computed, mesh=mesh, in_specs=in_specs, out_specs=out_specs, check_vma=False
    )
```

time: 47.4 us -> 44.8 us (0.945)
  other arithmetic: 2.65 us -> 0.26 us
  waiting for transfers between devices: 15.2 us -> 13.8 us
  starting transfers between devices: 16.9 us -> 17.8 us
    convert_element_type x1 -> x0, other arithmetic: 1.27 us -> none  [make_table(): (taper[:, None] * jnp.sin(angle)).astype(BF16)]
    neg x1 -> x0, other arithmetic: 1.06 us -> none  [computed(): -imag_tab]
    ppermute x8, starting transfers between devices: 6.95 us -> 7.92 us  [swapped(): return lax.ppermute(block, 'facet', [(i, i ^ bit) for i in range(facets)])]
    ppermute x8, waiting for transfers between devices: 7.53 us -> 6.56 us  [swapped(): return lax.ppermute(block, 'facet', [(i, i ^ bit) for i in range(facets)])]
    pallas_call x3 -> x5, Pallas kernels: 7.38 us -> 7.76 us  [the longest x1 2.15 us: computed(): pl.pallas_call(zero_kernel, out_shape=shape, in_specs=[VMEM], out_specs=H...]
  transfers between devices with their start and end apart: 12 -> 12, of which waited for: 6 -> 6; matrix products, arithmetic and copies ran while one was open for 6% -> 1% of each run, Pallas kernels for 11% -> 14%
where the time goes in v3:
time: 44.8 us; the launch traced here: 44.6 us
  starting transfers between devices  17.8 us (40%)
  waiting for transfers between devices  13.8 us (31%)
  Pallas kernels  11.8 us (26%)
  between operations  0.79 us (2%)
    ppermute x4, starting transfers between devices, shifted(): lax.ppermute(block, 'col', [(i, (i + distance) % count) for i in range(co...  9.91 us
    ppermute x8, starting transfers between devices, swapped(): return lax.ppermute(block, 'facet', [(i, i ^ bit) for i in range(facets)])  7.92 us
    ppermute x4, waiting for transfers between devices, shifted(): lax.ppermute(block, 'col', [(i, (i + distance) % count) for i in range(co...  7.26 us
    ppermute x8, waiting for transfers between devices, swapped(): return lax.ppermute(block, 'facet', [(i, i ^ bit) for i in range(facets)])  6.56 us
    pallas_call x1, Pallas kernels, computed(): pl.pallas_call(functools.partial(main_kernel, cols, facets, length), out_...  2.16 us
    pallas_call x1, Pallas kernels, computed(): pl.pallas_call(zero_kernel, out_shape=shape, in_specs=[VMEM], out_specs=H...  2.15 us
    pallas_call x1, Pallas kernels, computed(): pl.pallas_call(functools.partial(edge_kernel, cols, facets, length), out_...  1.89 us
    pallas_call x1, Pallas kernels, computed(): pl.pallas_call(functools.partial(end_kernel, cols, facets), out_shape=sha...  1.83 us
  transfers between devices with their start and end apart: 12, of which 6 were waited for; matrix products, arithmetic and copies ran while one was open for 1% of the time, Pallas kernels for 14%

profile of v3, /device:TPU:0, one launch (start us, length us, event | category | flops | bytes accessed | tf_op | source)
XLA Modules:
  0.0 44.6 jit_solution(13593848648552931709)
XLA Ops:
  0.6 1.9 %edge.1 = (bf16[2,2,2,128,128]{4,3,2,1,0:T(8,128)(2,1)S(1)}, bf16[2,2,2,128,128]{4,3,2,1,0:T(8,128)(2,1)S(1)}, f32[16,128]{1,0:T(8,128)S(1)}) custom-call(s32[1,2]{1,0:T(1,128)} %offsets.3, s32[2]{0:T(128)} %column.3, bf16[2,1,2,512,1024]{4,3,2,1,0:T(8,128)(2,1)} %spectra.3), custom_call_target="tpu_custom_call" | custom-call | tf_op jit(solution)/shard_map/edge/pallas_call | solution.py:454
  2.5 0.6 %collective-permute-start.2 = (bf16[2,2,2,128,128]{4,3,2,1,0:T(8,128)(2,1)S(1)}, bf16[2,2,2,128,128]{4,3,2,1,0:T(8,128)(2,1)S(1)}, u32[]{:S(2)}, u32[]{:S(2)}) collective-permute-start(bf16[2,2,2,128,128]{4,3,2,1,0:T(8,128)(2,1)S(1)} %get-tuple-element.17), channel_id=1, source_target_pairs={{0,8},{8,0},{16,24},{24,16},{1,9},{9,1},{17,25},{25,17},{2,10},{10... | collective-permute-start | bytes 786440 | tf_op jit(solution)/shard_map/ppermute | solution.py:403
  3.1 2.2 %main.1 = (bf16[2,2,2,128,128]{4,3,2,1,0:T(8,128)(2,1)S(1)}, bf16[2,2,2,128,128]{4,3,2,1,0:T(8,128)(2,1)S(1)}, f32[32,128]{1,0:T(8,128)S(1)}) custom-call(s32[1,2]{1,0:T(1,128)} %offsets.3, s32[2]{0:T(128)} %column.3, s32[1,2]{1,0:T(1,128)} %bitcast.25, bf16[2,1,2,512,1024]{4,3,2,1,0:T(8,128)(2,1)} %spectra.3, f32[16,128]{1,0:T(8,128)S(1)} %get-tuple-element.12.after.edge_turn), custom_call_target="tpu_custom_call" | custom-call | tf_op jit(solution)/shard_map/main/pallas_call | solution.py:471
  5.3 0.1 collective-permute-start
  5.4 0.1 add_convert_fusion
  5.5 3.0 %collective-permute-start.3 = (bf16[2,1,2,128,128]{4,3,2,1,0:T(8,128)(2,1)S(1)}, bf16[2,1,2,128,128]{4,3,2,1,0:T(8,128)(2,1)S(1)}, u32[]{:S(2)}, u32[]{:S(2)}) collective-permute-start(bf16[2,1,2,128,128]{4,3,2,1,0:T(8,128)(2,1)S(1)} %slice.31), channel_id=1, source_target_pairs={{0,16},{8,24},{16,0},{24,8},{1,17},{9,25},{17,1},{25,9},{2,18},{10... | collective-permute-start | bytes 393224 | tf_op jit(solution)/shard_map/ppermute | solution.py:403
  8.5 0.1 add_convert_fusion.1
  8.6 1.1 %collective-permute-start.1 = (bf16[2,1,2,128,128]{4,3,2,1,0:T(8,128)(2,1)S(1)}, bf16[2,1,2,128,128]{4,3,2,1,0:T(8,128)(2,1)S(1)}, u32[]{:S(2)}, u32[]{:S(2)}) collective-permute-start(bf16[2,1,2,128,128]{4,3,2,1,0:T(8,128)(2,1)S(1)} %get-tuple-element.22), channel_id=1, source_target_pairs={{0,16},{8,24},{16,0},{24,8},{1,17},{9,25},{17,1},{25,9},{2,18},{10... | collective-permute-start | bytes 393224 | tf_op jit(solution)/shard_map/ppermute | solution.py:403
  9.7 3.2 %collective-permute-done.3 = bf16[2,1,2,128,128]{4,3,2,1,0:T(8,128)(2,1)S(1)} collective-permute-done((bf16[2,1,2,128,128]{4,3,2,1,0:T(8,128)(2,1)S(1)}, bf16[2,1,2,128,128]{4,3,2,1,0:T(8,128)(2,1)S(1)}, u32[]{:S(2)}, u32[]{:S(2)}) %collective-permute-start.3) | collective-permute-done | bytes 131104 | tf_op jit(solution)/shard_map/ppermute | solution.py:403
  12.9 5.1 %collective-permute-start.5 = (bf16[1,2,128,128]{3,2,1,0:T(8,128)(2,1)S(1)}, bf16[1,2,128,128]{3,2,1,0:T(8,128)(2,1)S(1)}, u32[]{:S(2)}, u32[]{:S(2)}) collective-permute-start(bf16[1,2,128,128]{3,2,1,0:T(8,128)(2,1)S(1)} %get-tuple-element.26), channel_id=1, source_target_pairs={{0,7},{1,0},{2,1},{3,2},{4,3},{5,4},{6,5},{7,6},{8,15},{9,8},{10,9... | collective-permute-start | bytes 196616 | tf_op jit(solution)/shard_map/ppermute | solution.py:408
  18.0 0.4 table.1
  18.5 1.5 %collective-permute-done.5.from_next = bf16[1,2,128,128]{3,2,1,0:T(8,128)(2,1)S(1)} collective-permute-done((bf16[1,2,128,128]{3,2,1,0:T(8,128)(2,1)S(1)}, bf16[1,2,128,128]{3,2,1,0:T(8,128)(2,1)S(1)}, u32[]{:S(2)}, u32[]{:S(2)}) %collective-permute-start.5) | collective-permute-done | bytes 65568 | tf_op jit(solution)/shard_map/ppermute | solution.py:408
  19.9 5.1 %collective-permute-done.4.from_prev = bf16[1,2,128,128]{3,2,1,0:T(8,128)(2,1)S(1)} collective-permute-done((bf16[1,2,128,128]{3,2,1,0:T(8,128)(2,1)S(1)}, bf16[1,2,128,128]{3,2,1,0:T(8,128)(2,1)S(1)}, u32[]{:S(2)}, u32[]{:S(2)}) %collective-permute-start.4) | collective-permute-done | bytes 65568 | tf_op jit(solution)/shard_map/ppermute | solution.py:408
  25.0 1.7 %subgrid.1 = (bf16[2,1,2,128,512]{4,3,2,1,0:T(8,128)(2,1)}, bf16[2,1,2,128,128]{4,3,2,1,0:T(8,128)(2,1)S(1)}, bf16[1,2,128,128]{3,2,1,0:T(8,128)(2,1)S(1)}, bf16[1,2,128,128]{3,2,1,0:T(8,128)(2,1)S(1)}) custom-call(f32[32,128]{1,0:T(8,128)S(1)} %get-tuple-element.13.turn.after, bf16[2,1,2,128,128]{4,3,2,1,0:T(8,128)(2,1)S(1)} %get-tuple-element.23.kept, ...), custom_call_target="tpu_custom_call" | custom-call | tf_op jit(solution)/shard_map/subgrid/pallas_call | solution.py:507
  26.7 4.7 %collective-permute-start.9 = (bf16[1,2,128,128]{3,2,1,0:T(8,128)(2,1)S(1)}, bf16[1,2,128,128]{3,2,1,0:T(8,128)(2,1)S(1)}, u32[]{:S(2)}, u32[]{:S(2)}) collective-permute-start(bf16[1,2,128,128]{3,2,1,0:T(8,128)(2,1)S(1)} %get-tuple-element.21), channel_id=1, source_target_pairs={{0,7},{1,0},{2,1},{3,2},{4,3},{5,4},{6,5},{7,6},{8,15},{9,8},{10,9... | collective-permute-start | bytes 196616 | tf_op jit(solution)/shard_map/ppermute | solution.py:408
  31.4 1.5 %collective-permute-start.6 = (bf16[2,1,2,128,128]{4,3,2,0,1:T(8,128)(2,1)S(1)}, bf16[2,1,2,128,128]{4,3,2,0,1:T(8,128)(2,1)S(1)}, u32[]{:S(2)}, u32[]{:S(2)}) collective-permute-start(bf16[2,1,2,128,128]{4,3,2,0,1:T(8,128)(2,1)S(1)} %bitcast.19), channel_id=1, source_target_pairs={{0,16},{8,24},{16,0},{24,8},{1,17},{9,25},{17,1},{25,9},{2,18},{10... | collective-permute-start | bytes 393224 | tf_op jit(solution)/shard_map/ppermute | solution.py:403
  32.9 0.7 %collective-permute-done.8 = bf16[1,2,128,128]{3,2,1,0:T(8,128)(2,1)S(1)} collective-permute-done((bf16[1,2,128,128]{3,2,1,0:T(8,128)(2,1)S(1)}, bf16[1,2,128,128]{3,2,1,0:T(8,128)(2,1)S(1)}, u32[]{:S(2)}, u32[]{:S(2)}) %collective-permute-start.8) | collective-permute-done | bytes 65568 | tf_op jit(solution)/shard_map/ppermute | solution.py:408
  33.7 1.6 %collective-permute-start.10 = (bf16[2,1,2,128,128]{4,3,2,0,1:T(8,128)(2,1)S(1)}, bf16[2,1,2,128,128]{4,3,2,0,1:T(8,128)(2,1)S(1)}, u32[]{:S(2)}, u32[]{:S(2)}) collective-permute-start(bf16[2,1,2,128,128]{4,3,2,0,1:T(8,128)(2,1)S(1)} %get-tuple-element.25), channel_id=1, source_target_pairs={{0,16},{8,24},{16,0},{24,8},{1,17},{9,25},{17,1},{25,9},{2,18},{10... | collective-permute-start | bytes 393224 | tf_op jit(solution)/shard_map/ppermute | solution.py:403
  35.3 1.1 %collective-permute-done.6 = bf16[2,1,2,128,128]{4,3,2,0,1:T(8,128)(2,1)S(1)} collective-permute-done((bf16[2,1,2,128,128]{4,3,2,0,1:T(8,128)(2,1)S(1)}, bf16[2,1,2,128,128]{4,3,2,0,1:T(8,128)(2,1)S(1)}, u32[]{:S(2)}, u32[]{:S(2)}) %collective-permute-start.6) | collective-permute-done | bytes 131104 | tf_op jit(solution)/shard_map/ppermute | solution.py:403
  36.4 0.1 collective-permute-start.7
  36.5 2.2 %collective-permute-done.10 = bf16[2,1,2,128,128]{4,3,2,0,1:T(8,128)(2,1)S(1)} collective-permute-done((bf16[2,1,2,128,128]{4,3,2,0,1:T(8,128)(2,1)S(1)}, bf16[2,1,2,128,128]{4,3,2,0,1:T(8,128)(2,1)S(1)}, u32[]{:S(2)}, u32[]{:S(2)}) %collective-permute-start.10) | collective-permute-done | bytes 131104 | tf_op jit(solution)/shard_map/ppermute | solution.py:403
  38.9 2.2 %zero.1.whole = bf16[2,1,2,512,1024]{4,3,2,1,0:T(8,128)(2,1)} custom-call(f32[32,128]{1,0:T(8,128)S(1)} %get-tuple-element.13.turn.after), custom_call_target="tpu_custom_call" | custom-call | tf_op jit(solution)/shard_map/zero/pallas_call | solution.py:493
  41.0 1.7 %window.1.whole = bf16[2,1,2,512,1024]{4,3,2,1,0:T(8,128)(2,1)} custom-call(s32[1,2]{1,0:T(1,128)} %bitcast.26, f32[32,128]{1,0:T(8,128)S(1)} %get-tuple-element.13.turn.after, bf16[2,2,2,128,128]{4,3,2,1,0:T(8,128)(2,1)S(1)} %maximum_bitcast_fusion.even, ...), custom_call_target="tpu_custom_call", output_to_operand_aliasing={{}: (4, {})} | custom-call | tf_op jit(solution)/shard_map/window/pallas_call | solution.py:532
  42.7 1.8 %end.1 = bf16[2,1,2,512,1024]{4,3,2,1,0:T(8,128)(2,1)} custom-call(f32[32,128]{1,0:T(8,128)S(1)} %get-tuple-element.13.turn.after, f32[16,128]{1,0:T(8,128)S(1)} %get-tuple-element.12.after.edge_turn, bf16[2,2,2,128,128]{4,3,2,1,0:T(8,128)(2,1)S(1)} %maximum_bitcast_fusion.even, ...), custom_call_target="tpu_custom_call", output_to_operand_aliasing={{}: (6, {})} | custom-call | tf_op jit(solution)/shard_map/end/pallas_call | solution.py:542
  (18 shorter events, 0.3 us)
Async XLA Ops:
  2.5 22.5 %copy-start = (bf16[2,1,128,512]{3,2,1,0:T(8,128)(2,1)S(1)}, bf16[2,1,128,512]{3,2,1,0:T(8,128)(2,1)}, u32[]{:S(2)}) copy-start(bf16[2,1,128,512]{3,2,1,0:T(8,128)(2,1)} %weights.1) | copy-start | bytes 786436
  2.5 2.8 %collective-permute-start.2 = (bf16[2,2,2,128,128]{4,3,2,1,0:T(8,128)(2,1)S(1)}, bf16[2,2,2,128,128]{4,3,2,1,0:T(8,128)(2,1)S(1)}, u32[]{:S(2)}, u32[]{:S(2)}) collective-permute-start(bf16[2,2,2,128,128]{4,3,2,1,0:T(8,128)(2,1)S(1)} %get-tuple-element.17), channel_id=1, source_target_pairs={{0,8},{8,0},{16,24},{24,16},{1,9},{9,1},{17,25},{25,17},{2,10},{10... | collective-permute-start | bytes 786440 | tf_op jit(solution)/shard_map/ppermute | solution.py:403
  5.3 3.2 %collective-permute-start = (bf16[2,2,2,128,128]{4,3,2,1,0:T(8,128)(2,1)S(1)}, bf16[2,2,2,128,128]{4,3,2,1,0:T(8,128)(2,1)S(1)}, u32[]{:S(2)}, u32[]{:S(2)}) collective-permute-start(bf16[2,2,2,128,128]{4,3,2,1,0:T(8,128)(2,1)S(1)} %get-tuple-element.15), channel_id=1, source_target_pairs={{0,8},{8,0},{16,24},{24,16},{1,9},{9,1},{17,25},{25,17},{2,10},{10... | collective-permute-start | bytes 786440 | tf_op jit(solution)/shard_map/ppermute | solution.py:403
  5.5 7.4 %collective-permute-start.3 = (bf16[2,1,2,128,128]{4,3,2,1,0:T(8,128)(2,1)S(1)}, bf16[2,1,2,128,128]{4,3,2,1,0:T(8,128)(2,1)S(1)}, u32[]{:S(2)}, u32[]{:S(2)}) collective-permute-start(bf16[2,1,2,128,128]{4,3,2,1,0:T(8,128)(2,1)S(1)} %slice.31), channel_id=1, source_target_pairs={{0,16},{8,24},{16,0},{24,8},{1,17},{9,25},{17,1},{25,9},{2,18},{10... | collective-permute-start | bytes 393224 | tf_op jit(solution)/shard_map/ppermute | solution.py:403
  8.6 9.9 %collective-permute-start.1 = (bf16[2,1,2,128,128]{4,3,2,1,0:T(8,128)(2,1)S(1)}, bf16[2,1,2,128,128]{4,3,2,1,0:T(8,128)(2,1)S(1)}, u32[]{:S(2)}, u32[]{:S(2)}) collective-permute-start(bf16[2,1,2,128,128]{4,3,2,1,0:T(8,128)(2,1)S(1)} %get-tuple-element.22), channel_id=1, source_target_pairs={{0,16},{8,24},{16,0},{24,8},{1,17},{9,25},{17,1},{25,9},{2,18},{10... | collective-permute-start | bytes 393224 | tf_op jit(solution)/shard_map/ppermute | solution.py:403
  12.9 7.0 %collective-permute-start.5 = (bf16[1,2,128,128]{3,2,1,0:T(8,128)(2,1)S(1)}, bf16[1,2,128,128]{3,2,1,0:T(8,128)(2,1)S(1)}, u32[]{:S(2)}, u32[]{:S(2)}) collective-permute-start(bf16[1,2,128,128]{3,2,1,0:T(8,128)(2,1)S(1)} %get-tuple-element.26), channel_id=1, source_target_pairs={{0,7},{1,0},{2,1},{3,2},{4,3},{5,4},{6,5},{7,6},{8,15},{9,8},{10,9... | collective-permute-start | bytes 196616 | tf_op jit(solution)/shard_map/ppermute | solution.py:408
  18.0 7.0 %collective-permute-start.4 = (bf16[1,2,128,128]{3,2,1,0:T(8,128)(2,1)S(1)}, bf16[1,2,128,128]{3,2,1,0:T(8,128)(2,1)S(1)}, u32[]{:S(2)}, u32[]{:S(2)}) collective-permute-start(bf16[1,2,128,128]{3,2,1,0:T(8,128)(2,1)S(1)} %get-tuple-element.27), channel_id=1, source_target_pairs={{0,1},{1,2},{2,3},{3,4},{4,5},{5,6},{6,7},{7,0},{8,9},{9,10},{10,1... | collective-permute-start | bytes 196616 | tf_op jit(solution)/shard_map/ppermute | solution.py:408
  26.7 7.0 %collective-permute-start.8 = (bf16[1,2,128,128]{3,2,1,0:T(8,128)(2,1)S(1)}, bf16[1,2,128,128]{3,2,1,0:T(8,128)(2,1)S(1)}, u32[]{:S(2)}, u32[]{:S(2)}) collective-permute-start(bf16[1,2,128,128]{3,2,1,0:T(8,128)(2,1)S(1)} %get-tuple-element.20), channel_id=1, source_target_pairs={{0,1},{1,2},{2,3},{3,4},{4,5},{5,6},{6,7},{7,0},{8,9},{9,10},{10,1... | collective-permute-start | bytes 196616 | tf_op jit(solution)/shard_map/ppermute | solution.py:408
  26.7 7.0 %collective-permute-start.9 = (bf16[1,2,128,128]{3,2,1,0:T(8,128)(2,1)S(1)}, bf16[1,2,128,128]{3,2,1,0:T(8,128)(2,1)S(1)}, u32[]{:S(2)}, u32[]{:S(2)}) collective-permute-start(bf16[1,2,128,128]{3,2,1,0:T(8,128)(2,1)S(1)} %get-tuple-element.21), channel_id=1, source_target_pairs={{0,7},{1,0},{2,1},{3,2},{4,3},{5,4},{6,5},{7,6},{8,15},{9,8},{10,9... | collective-permute-start | bytes 196616 | tf_op jit(solution)/shard_map/ppermute | solution.py:408
  31.4 5.0 %collective-permute-start.6 = (bf16[2,1,2,128,128]{4,3,2,0,1:T(8,128)(2,1)S(1)}, bf16[2,1,2,128,128]{4,3,2,0,1:T(8,128)(2,1)S(1)}, u32[]{:S(2)}, u32[]{:S(2)}) collective-permute-start(bf16[2,1,2,128,128]{4,3,2,0,1:T(8,128)(2,1)S(1)} %bitcast.19), channel_id=1, source_target_pairs={{0,16},{8,24},{16,0},{24,8},{1,17},{9,25},{17,1},{25,9},{2,18},{10... | collective-permute-start | bytes 393224 | tf_op jit(solution)/shard_map/ppermute | solution.py:403
  33.7 5.0 %collective-permute-start.10 = (bf16[2,1,2,128,128]{4,3,2,0,1:T(8,128)(2,1)S(1)}, bf16[2,1,2,128,128]{4,3,2,0,1:T(8,128)(2,1)S(1)}, u32[]{:S(2)}, u32[]{:S(2)}) collective-permute-start(bf16[2,1,2,128,128]{4,3,2,0,1:T(8,128)(2,1)S(1)} %get-tuple-element.25), channel_id=1, source_target_pairs={{0,16},{8,24},{16,0},{24,8},{1,17},{9,25},{17,1},{25,9},{2,18},{10... | collective-permute-start | bytes 393224 | tf_op jit(solution)/shard_map/ppermute | solution.py:403
  36.4 4.6 %collective-permute-start.7 = (bf16[2,2,2,128,128]{4,3,2,1,0:T(8,128)(2,1)S(1)}, bf16[2,2,2,128,128]{4,3,2,1,0:T(8,128)(2,1)S(1)}, u32[]{:S(2)}, u32[]{:S(2)}) collective-permute-start(bf16[2,2,2,128,128]{4,3,2,1,0:T(8,128)(2,1)S(1)} %maximum_bitcast_fusion.even), channel_id=1, source_target_pairs={{0,8},{8,0},{16,24},{24,16},{1,9},{9,1},{17,25},{25,17},{2,10},{10... | collective-permute-start | bytes 786440 | tf_op jit(solution)/shard_map/ppermute | solution.py:403
  38.8 4.0 %collective-permute-start.11 = (bf16[2,2,2,128,128]{4,3,2,1,0:T(8,128)(2,1)S(1)}, bf16[2,2,2,128,128]{4,3,2,1,0:T(8,128)(2,1)S(1)}, u32[]{:S(2)}, u32[]{:S(2)}) collective-permute-start(bf16[2,2,2,128,128]{4,3,2,1,0:T(8,128)(2,1)S(1)} %maximum_bitcast_fusion.1.even_edge), channel_id=1, source_target_pairs={{0,8},{8,0},{16,24},{24,16},{1,9},{9,1},{17,25},{25,17},{2,10},{10... | collective-permute-start | bytes 786440 | tf_op jit(solution)/shard_map/ppermute | solution.py:403

commit v4 on v3

--- a/solution.py
+++ b/solution.py
@@ -82,30 +82,13 @@
     return parts[0] * cosine + parts[1] * sine, parts[1] * cosine - parts[0] * sine
 
 
-def edge_kernel(
-    cols, facets, length, offsets, column, spectra, send, keep, turn, buf, sems, own, held, small
-):
-    shard = spectra.shape[4]
-    block = XM // facets
-    here = lax.axis_index("col")
-    facet = lax.axis_index("facet")
-    scalars = [
-        pltpu.make_async_copy(offsets, own, small.at[0]),
-        pltpu.make_async_copy(column, held, small.at[1]),
-    ]
-    for copy in scalars:
-        copy.start()
-    copies = {}
-    order = [s for s in range(facets) if s % 2] + [s for s in range(facets) if s % 2 == 0]
-    for c in range(cols):
-        for s in order:
-            rows = rows_of(facet, s, block)
-            copies[c, s] = fetched(spectra, buf, sems, c, s, rows, (0, shard - LANES))
-    for copy in scalars:
-        copy.wait()
-    lanes = lanes_of((8, LANES))
-    index = here * shard + lanes + jnp.where(lanes < HALF, 0, shard - LANES)
-    turns_of(turn, index, firsts_of(cols, own, held), own[0, 1], length)
+def places_of(turn, cols):
+    tiles = [jnp.min(turn[16 + c : 17 + c, :]).astype(jnp.int32) for c in range(cols)]
+    lanes = [jnp.max(turn[24 + c : 25 + c, :]).astype(jnp.int32) for c in range(cols)]
+    return tiles, lanes
+
+
+def edges_of(target, buf, copies, turn, order, cols, block, facet):
     left = lanes_of((1, LANES)) < HALF
     for c in range(cols):
         cosine = turn[c : c + 1, :]
@@ -114,7 +97,6 @@
             for copy in copies[c, s]:
                 copy.wait()
             rows = rows_of(facet, s, block)
-            target = send if s % 2 else keep
             parts = [
                 jnp.where(
                     left,
@@ -130,45 +112,107 @@
             target[1, s // 2, c] = high.astype(BF16)
 
 
-def main_kernel(
-    cols, facets, length, offsets, column, subgrid, spectra, after, send, keep, turn, buf, sems
+def edge_kernel(
+    cols, facets, length, offsets, column, spectra, send, turn, buf, sems, own, held, small
 ):
+    shard = spectra.shape[4]
+    block = XM // facets
+    here = lax.axis_index("col")
+    facet = lax.axis_index("facet")
+    scalars = [
+        pltpu.make_async_copy(offsets, own, small.at[0]),
+        pltpu.make_async_copy(column, held, small.at[1]),
+    ]
+    for copy in scalars:
+        copy.start()
+    copies = {}
+    order = range(1, facets, 2)
+    for c in range(cols):
+        for s in order:
+            rows = rows_of(facet, s, block)
+            copies[c, s] = fetched(spectra, buf, sems, c, s, rows, (0, shard - LANES))
+    for copy in scalars:
+        copy.wait()
+    lanes = lanes_of((8, LANES))
+    index = here * shard + lanes + jnp.where(lanes < HALF, 0, shard - LANES)
+    turns_of(turn, index, firsts_of(cols, own, held), own[0, 1], length)
+    edges_of(send, buf, copies, turn, order, cols, block, facet)
+
+
+def hold_kernel(
+    cols,
+    facets,
+    length,
+    offsets,
+    column,
+    subgrid,
+    spectra,
+    edge_turn,
+    keep,
+    turn,
+    buf,
+    sems,
+    own,
+    held,
+    spots,
+    small,
+):
+    shard = spectra.shape[4]
+    block = XM // facets
+    here = lax.axis_index("col")
+    facet = lax.axis_index("facet")
+    scalars = [
+        pltpu.make_async_copy(offsets, own, small.at[0]),
+        pltpu.make_async_copy(column, held, small.at[1]),
+        pltpu.make_async_copy(subgrid, spots, small.at[2]),
+    ]
+    for copy in scalars:
+        copy.start()
+    copies = {}
+    order = range(0, facets, 2)
+    for c in range(cols):
+        for s in order:
+            rows = rows_of(facet, s, block)
+            copies[c, s] = fetched(spectra, buf, sems, c, s, rows, (0, shard - LANES))
+    for copy in scalars:
+        copy.wait()
+    lanes = lanes_of((8, LANES))
+    rows = lax.broadcasted_iota(jnp.int32, (8, LANES), 0)
+    tile_at = jnp.zeros((8, LANES), jnp.int32)
+    begins = jnp.zeros((8, LANES), jnp.int32)
+    for c in range(cols):
+        tile, lane = place_of(spots[0, c], here, shard, length)
+        tile_at = jnp.where(rows == c, jnp.where(lanes >= lane, tile, tile + 1), tile_at)
+        begins = jnp.where(rows == c, lane, begins)
+    index = remainder(here * shard + lanes + tile_at * LANES + length, length)
+    turns_of(turn, index, firsts_of(cols, own, held), own[0, 1], length)
+    turn[16:24, :] = tile_at.astype(F32)
+    turn[24:32, :] = begins.astype(F32)
+    edges_of(keep, buf, copies, edge_turn, order, cols, block, facet)
+
+
+def main_kernel(cols, facets, spectra, turn, after, send, keep, buf, sems):
     del after
     shard = spectra.shape[4]
     tiles = shard // LANES
     block = XM // facets
-    here = lax.axis_index("col")
     facet = lax.axis_index("facet")
     copies = {}
-    places = []
-    for c in range(cols):
-        tile, lane = place_of(subgrid[0, c], here, shard, length)
-        places.append((tile, lane))
+    first_tiles, _ = places_of(turn, cols)
+    for c in range(cols):
+        tile = first_tiles[c]
         low = pl.multiple_of(jnp.maximum(tile, 0) * LANES, LANES)
         high = pl.multiple_of(jnp.minimum(tile + 1, tiles - 1) * LANES, LANES)
         for s in range(facets):
             rows = rows_of(facet, s, block)
             copies[c, s] = fetched(spectra, buf, sems, c, s, rows, (low, high))
-    lanes = lanes_of((8, LANES))
-    rows = lax.broadcasted_iota(jnp.int32, (8, LANES), 0)
-    held = jnp.zeros((8, LANES), jnp.int32)
-    begins = jnp.zeros((8, LANES), jnp.int32)
-    for c in range(cols):
-        tile, lane = places[c]
-        held = jnp.where(rows == c, jnp.where(lanes >= lane, tile, tile + 1), held)
-        begins = jnp.where(rows == c, lane, begins)
-    index = remainder(here * shard + lanes + held * LANES + length, length)
-    turns_of(turn, index, firsts_of(cols, offsets, column), offsets[0, 1], length)
-    turn[16:24, :] = held.astype(F32)
-    turn[24:32, :] = begins.astype(F32)
-    lanes = lanes_of((1, LANES))
     zero = jnp.zeros((1, LANES), F32)
     for c in range(cols):
-        tile, lane = places[c]
-        from_low = jnp.logical_and(lanes >= lane, tile >= 0)
-        from_high = jnp.logical_and(lanes < lane, tile + 1 < tiles)
-        cosine = turn[c : c + 1, :]
-        sine = turn[8 + c : 9 + c, :]
+        tile_at = turn[16 + c : 17 + c, :]
+        is_low = lanes_of((1, LANES)).astype(F32) >= turn[24 + c : 25 + c, :]
+        inside = jnp.logical_and(tile_at >= 0, tile_at <= tiles - 1)
+        cosine = jnp.where(inside, turn[c : c + 1, :], zero)
+        sine = jnp.where(inside, turn[8 + c : 9 + c, :], zero)
         for s in range(facets):
             for copy in copies[c, s]:
                 copy.wait()
@@ -176,9 +220,9 @@
             target = send if s % 2 else keep
             parts = [
                 jnp.where(
-                    from_low,
+                    is_low,
                     buf[c, 0, part, rows, :].astype(F32),
-                    jnp.where(from_high, buf[c, 1, part, rows, :].astype(F32), zero),
+                    buf[c, 1, part, rows, :].astype(F32),
                 )
                 for part in range(2)
             ]
@@ -255,7 +299,7 @@
     tiles = shard // LANES
     block = kept.shape[3]
     zero = jnp.zeros((1, LANES), F32)
-    begins = [jnp.max(turn[24 + c : 25 + c, :].astype(jnp.int32)) for c in range(cols)]
+    _, begins = places_of(turn, cols)
     for c in range(cols):
         held = turn[16 + c : 17 + c, :]
         low = held < 0
@@ -314,20 +358,18 @@
     return real * cosine - imag * sine, imag * cosine + real * sine
 
 
-def window_kernel(cols, facets, length, subgrid, turn, even, odd, whole, out, buf, sems):
+def window_kernel(cols, facets, turn, even, odd, whole, out, buf, sems):
     shard = out.shape[4]
     tiles = shard // LANES
     block = XM // facets
-    here = lax.axis_index("col")
     facet = lax.axis_index("facet")
-    lanes = lanes_of((1, LANES))
     zero = jnp.zeros((1, LANES), F32)
+    first_tiles, _ = places_of(turn, cols)
     copies = []
     for c in range(cols):
-        tile, lane = place_of(subgrid[0, c], here, shard, length)
         cosine = turn[c : c + 1, :]
         sine = turn[8 + c : 9 + c, :]
-        is_low = lanes >= lane
+        is_low = lanes_of((1, LANES)).astype(F32) >= turn[24 + c : 25 + c, :]
         for s in range(facets):
             rows = rows_of(facet, s, block)
             values = phased(odd if s % 2 else even, s, c, cosine, sine)
@@ -335,7 +377,7 @@
                 buf[c, 0, part, rows, :] = jnp.where(is_low, values[part], zero).astype(BF16)
                 buf[c, 1, part, rows, :] = jnp.where(is_low, zero, values[part]).astype(BF16)
         for slot in range(2):
-            which = tile + slot
+            which = first_tiles[c] + slot
             at = pl.multiple_of(jnp.clip(which, 0, tiles - 1) * LANES, LANES)
             copy = pltpu.make_async_copy(
                 buf.at[c, slot], out.at[c, 0, :, :, pl.ds(at, LANES)], sems.at[c, slot]
@@ -347,9 +389,7 @@
         pl.when(inside)(copy.wait)
 
 
-def end_kernel(
-    cols, facets, turn, edge_turn, even, odd, even_edge, odd_edge, whole, out, buf, sems
-):
+def end_kernel(cols, facets, odd, turn, edge_turn, main, edges, whole, out, buf, sems):
     shard = out.shape[4]
     tiles = shard // LANES
     block = XM // facets
@@ -362,13 +402,12 @@
         sine = turn[8 + c : 9 + c, :]
         edge_cosine = edge_turn[c : c + 1, :]
         edge_sine = edge_turn[8 + c : 9 + c, :]
-        held = turn[16 + c : 17 + c, :]
-        in_first = held == 0
-        in_last = held == tiles - 1
-        for s in range(facets):
+        tile_at = turn[16 + c : 17 + c, :]
+        in_first = tile_at == 0
+        in_last = tile_at == tiles - 1
+        for s in range(odd, facets, 2):
             rows = rows_of(facet, s, block)
-            values = phased(odd if s % 2 else even, s, c, cosine, sine)
-            edges = odd_edge if s % 2 else even_edge
+            values = phased(main, s, c, cosine, sine)
             prev = edges[0, s // 2, c].astype(F32)
             nxt = edges[1, s // 2, c].astype(F32)
             real = jnp.where(left, prev, pltpu.roll(nxt, HALF, 1))
@@ -380,17 +419,17 @@
             for part in range(2):
                 value = values[part]
                 end = ends[part]
-                buf[c, 0, part, rows, :] = (
+                buf[c, 0, part, s // 2] = (
                     jnp.where(left, end, zero) + jnp.where(in_first, value, zero)
                 ).astype(BF16)
-                buf[c, 1, part, rows, :] = (
+                buf[c, 1, part, s // 2] = (
                     jnp.where(left, zero, end) + jnp.where(in_last, value, zero)
                 ).astype(BF16)
             for slot, start in enumerate((0, shard - LANES)):
                 copy = pltpu.make_async_copy(
-                    buf.at[c, slot, :, rows, :],
+                    buf.at[c, slot, :, s // 2],
                     out.at[c, 0, :, rows, pl.ds(start, LANES)],
-                    sems.at[c, slot, s],
+                    sems.at[c, slot, s // 2],
                 )
                 copy.start()
                 copies.append(copy)
@@ -451,32 +490,46 @@
     pieces = jax.ShapeDtypeStruct((2, facets // 2, cols, block, LANES), BF16)
     tile_pair = pltpu.VMEM((cols, 2, 2, XM, LANES), BF16)
     pair_sems = pltpu.SemaphoreType.DMA((cols, 2, facets))
-    edge_send, edge_keep, edge_turn = pl.pallas_call(
+    whole_scalars = [
+        pltpu.SMEM(facet_offsets.shape, jnp.int32),
+        pltpu.SMEM(column_index.shape, jnp.int32),
+    ]
+    edge_send, edge_turn = pl.pallas_call(
         functools.partial(edge_kernel, cols, facets, length),
-        out_shape=(pieces, pieces, jax.ShapeDtypeStruct((16, LANES), F32)),
+        out_shape=(pieces, jax.ShapeDtypeStruct((16, LANES), F32)),
         in_specs=[HBM, HBM, HBM],
-        out_specs=(VMEM, VMEM, VMEM),
+        out_specs=(VMEM, VMEM),
+        scratch_shapes=[tile_pair, pair_sems, *whole_scalars, pltpu.SemaphoreType.DMA((2,))],
+        compiler_params=params(12),
+        name="edge",
+    )(facet_offsets, column_index, facet_spectra)
+    edge_keep, turn = pl.pallas_call(
+        functools.partial(hold_kernel, cols, facets, length),
+        out_shape=(pieces, jax.ShapeDtypeStruct((32, LANES), F32)),
+        in_specs=[HBM, HBM, HBM, HBM, VMEM],
+        out_specs=(VMEM, VMEM),
         scratch_shapes=[
             tile_pair,
             pair_sems,
-            pltpu.SMEM(facet_offsets.shape, jnp.int32),
-            pltpu.SMEM(column_index.shape, jnp.int32),
-            pltpu.SemaphoreType.DMA((2,)),
+            *whole_scalars,
+            pltpu.SMEM(places.shape, jnp.int32),
+            pltpu.SemaphoreType.DMA((3,)),
         ],
         compiler_params=params(12),
-        name="edge",
-    )(facet_offsets, column_index, facet_spectra)
-    edges = added(*reduced(edge_keep, edge_send, facets))
-
-    main_send, main_keep, turn = pl.pallas_call(
-        functools.partial(main_kernel, cols, facets, length),
-        out_shape=(pieces, pieces, jax.ShapeDtypeStruct((32, LANES), F32)),
-        in_specs=[SMEM, SMEM, SMEM, HBM, VMEM],
-        out_specs=(VMEM, VMEM, VMEM),
+        name="hold",
+    )(facet_offsets, column_index, places, facet_spectra, edge_turn)
+    pair = reduced(edge_keep, edge_send, facets)
+    edges = added(*pair)
+
+    main_send, main_keep = pl.pallas_call(
+        functools.partial(main_kernel, cols, facets),
+        out_shape=(pieces, pieces),
+        in_specs=[HBM, VMEM, VMEM],
+        out_specs=(VMEM, VMEM),
         scratch_shapes=[tile_pair, pair_sems],
         compiler_params=params(12),
         name="main",
-    )(facet_offsets, column_index, places, facet_spectra, edge_turn)
+    )(facet_spectra, turn, edge_turn)
     main_kept, main_received = reduced(main_keep, main_send, facets)
     from_prev = shifted(edges[1], 1)
     from_next = shifted(edges[0], -1)
@@ -530,25 +583,29 @@
     even_edge, odd_edge = gathered(jnp.stack([came_prev, came_next]), facets)
 
     updates = pl.pallas_call(
-        functools.partial(window_kernel, cols, facets, length),
+        functools.partial(window_kernel, cols, facets),
         out_shape=shape,
-        in_specs=[SMEM, VMEM, VMEM, VMEM, HBM],
+        in_specs=[VMEM, VMEM, VMEM, HBM],
         out_specs=HBM,
         scratch_shapes=[tile_pair, pltpu.SemaphoreType.DMA((cols, 2))],
-        input_output_aliases={4: 0},
+        input_output_aliases={3: 0},
         compiler_params=params(12),
         name="window",
-    )(places, turn, even, odd, updates)
-    updates = pl.pallas_call(
-        functools.partial(end_kernel, cols, facets),
-        out_shape=shape,
-        in_specs=[VMEM] * 6 + [HBM],
-        out_specs=HBM,
-        scratch_shapes=[tile_pair, pair_sems],
-        input_output_aliases={6: 0},
-        compiler_params=params(12),
-        name="end",
-    )(turn, edge_turn, even, odd, even_edge, odd_edge, updates)
+    )(turn, even, odd, updates)
+    halves = ((0, even, even_edge), (1, odd, odd_edge))
+    for half, main, ends in halves:
+        updates = pl.pallas_call(
+            functools.partial(end_kernel, cols, facets, half),
+            out_shape=shape,
+            in_specs=[VMEM] * 4 + [HBM],
+            out_specs=HBM,
+            scratch_shapes=[
+                pltpu.VMEM((cols, 2, 2, facets // 2, block, LANES), BF16),
+                pltpu.SemaphoreType.DMA((cols, 2, facets // 2)),
+            ],
+            input_output_aliases={4: 0},
+            compiler_params=params(12),
+        )(turn, edge_turn, main, ends, updates)
     return grids, updates
 
 

time: 44.8 us -> 40.6 us (0.906)
  waiting for transfers between devices: 13.8 us -> 8.79 us
    ppermute x4, waiting for transfers between devices: 7.26 us -> 2.33 us  [shifted(): lax.ppermute(block, 'col', [(i, (i + distance) % count) for i in range(co...]
    pallas_call x3 -> x5, Pallas kernels: 5.69 us -> 6.62 us  [the longest x2 2.48 us: computed(): pl.pallas_call(functools.partial(end_kernel, cols, facets, half), out_sha...]
  transfers between devices with their start and end apart: 12 -> 12, of which waited for: 6 -> 5; matrix products, arithmetic and copies ran while one was open for 1% -> 1% of each run, Pallas kernels for 14% -> 20%
where the time goes in v4:
time: 40.6 us; the launch traced here: 40.4 us
  starting transfers between devices  18.2 us (45%)
  Pallas kernels  12.2 us (30%)
  waiting for transfers between devices  8.79 us (22%)
  between operations  0.8 us (2%)
    ppermute x4, starting transfers between devices, shifted(): lax.ppermute(block, 'col', [(i, (i + distance) % count) for i in range(co...  10.1 us
    ppermute x8, starting transfers between devices, swapped(): return lax.ppermute(block, 'facet', [(i, i ^ bit) for i in range(facets)])  8.12 us
    ppermute x8, waiting for transfers between devices, swapped(): return lax.ppermute(block, 'facet', [(i, i ^ bit) for i in range(facets)])  6.46 us
    pallas_call x2, Pallas kernels, computed(): pl.pallas_call(functools.partial(end_kernel, cols, facets, half), out_sha...  2.48 us
    ppermute x4, waiting for transfers between devices, shifted(): lax.ppermute(block, 'col', [(i, (i + distance) % count) for i in range(co...  2.33 us
    pallas_call x1, Pallas kernels, computed(): pl.pallas_call(zero_kernel, out_shape=shape, in_specs=[VMEM], out_specs=H...  2.15 us
    pallas_call x1, Pallas kernels, computed(): pl.pallas_call(functools.partial(main_kernel, cols, facets), out_shape=(p...  1.58 us
    pallas_call x1, Pallas kernels, computed(): pl.pallas_call(functools.partial(subgrid_kernel, cols, shard), out_shape=...  1.57 us
  transfers between devices with their start and end apart: 12, of which 5 were waited for; matrix products, arithmetic and copies ran while one was open for 1% of the time, Pallas kernels for 20%

profile of v4, /device:TPU:0, one launch (start us, length us, event | category | flops | bytes accessed | tf_op | source)
XLA Modules:
  0.0 40.4 jit_solution(13110817318783352424)
XLA Ops:
  0.6 1.5 %edge.1 = (bf16[2,2,2,128,128]{4,3,2,1,0:T(8,128)(2,1)S(1)}, f32[16,128]{1,0:T(8,128)S(1)}) custom-call(s32[1,2]{1,0:T(1,128)} %offsets.3, s32[2]{0:T(128)} %column.3, bf16[2,1,2,512,1024]{4,3,2,1,0:T(8,128)(2,1)} %spectra.5), custom_call_target="tpu_custom_call" | custom-call | tf_op jit(solution)/shard_map/edge/pallas_call | solution.py:497
  2.1 0.6 %collective-permute-start.2 = (bf16[2,2,2,128,128]{4,3,2,1,0:T(8,128)(2,1)S(1)}, bf16[2,2,2,128,128]{4,3,2,1,0:T(8,128)(2,1)S(1)}, u32[]{:S(2)}, u32[]{:S(2)}) collective-permute-start(bf16[2,2,2,128,128]{4,3,2,1,0:T(8,128)(2,1)S(1)} %get-tuple-element.17), channel_id=1, source_target_pairs={{0,8},{8,0},{16,24},{24,16},{1,9},{9,1},{17,25},{25,17},{2,10},{10... | collective-permute-start | bytes 786440 | tf_op jit(solution)/shard_map/ppermute | solution.py:442
  2.7 1.5 %hold.1 = (bf16[2,2,2,128,128]{4,3,2,1,0:T(8,128)(2,1)S(1)}, f32[32,128]{1,0:T(8,128)S(1)}) custom-call(s32[1,2]{1,0:T(1,128)} %offsets.3, s32[2]{0:T(128)} %column.3, s32[1,2]{1,0:T(1,128)} %bitcast.25, bf16[2,1,2,512,1024]{4,3,2,1,0:T(8,128)(2,1)} %spectra.5, f32[16,128]{1,0:T(8,128)S(1)} %get-tuple-element.12.edge_turn.after), custom_call_target="tpu_custom_call" | custom-call | tf_op jit(solution)/shard_map/hold/pallas_call | solution.py:506
  4.2 1.6 %main.1 = (bf16[2,2,2,128,128]{4,3,2,1,0:T(8,128)(2,1)S(1)}, bf16[2,2,2,128,128]{4,3,2,1,0:T(8,128)(2,1)S(1)}) custom-call(bf16[2,1,2,512,1024]{4,3,2,1,0:T(8,128)(2,1)} %spectra.5, f32[32,128]{1,0:T(8,128)S(1)} %get-tuple-element.13.turn.after, f32[16,128]{1,0:T(8,128)S(1)} %get-tuple-element.12.edge_turn.after), custom_call_target="tpu_custom_call" | custom-call | tf_op jit(solution)/shard_map/main/pallas_call | solution.py:524
  5.7 0.1 collective-permute-start
  5.9 3.0 %collective-permute-start.3 = (bf16[2,1,2,128,128]{4,3,2,1,0:T(8,128)(2,1)S(1)}, bf16[2,1,2,128,128]{4,3,2,1,0:T(8,128)(2,1)S(1)}, u32[]{:S(2)}, u32[]{:S(2)}) collective-permute-start(bf16[2,1,2,128,128]{4,3,2,1,0:T(8,128)(2,1)S(1)} %slice.31), channel_id=1, source_target_pairs={{0,16},{8,24},{16,0},{24,8},{1,17},{9,25},{17,1},{25,9},{2,18},{10... | collective-permute-start | bytes 393224 | tf_op jit(solution)/shard_map/ppermute | solution.py:442
  9.1 1.1 %collective-permute-start.1 = (bf16[2,1,2,128,128]{4,3,2,1,0:T(8,128)(2,1)S(1)}, bf16[2,1,2,128,128]{4,3,2,1,0:T(8,128)(2,1)S(1)}, u32[]{:S(2)}, u32[]{:S(2)}) collective-permute-start(bf16[2,1,2,128,128]{4,3,2,1,0:T(8,128)(2,1)S(1)} %get-tuple-element.22), channel_id=1, source_target_pairs={{0,16},{8,24},{16,0},{24,8},{1,17},{9,25},{17,1},{25,9},{2,18},{10... | collective-permute-start | bytes 393224 | tf_op jit(solution)/shard_map/ppermute | solution.py:442
  10.1 3.2 %collective-permute-done.3 = bf16[2,1,2,128,128]{4,3,2,1,0:T(8,128)(2,1)S(1)} collective-permute-done((bf16[2,1,2,128,128]{4,3,2,1,0:T(8,128)(2,1)S(1)}, bf16[2,1,2,128,128]{4,3,2,1,0:T(8,128)(2,1)S(1)}, u32[]{:S(2)}, u32[]{:S(2)}) %collective-permute-start.3) | collective-permute-done | bytes 131104 | tf_op jit(solution)/shard_map/ppermute | solution.py:442
  13.4 2.1 %collective-permute-start.4 = (bf16[1,2,128,128]{3,2,1,0:T(8,128)(2,1)S(1)}, bf16[1,2,128,128]{3,2,1,0:T(8,128)(2,1)S(1)}, u32[]{:S(2)}, u32[]{:S(2)}) collective-permute-start(bf16[1,2,128,128]{3,2,1,0:T(8,128)(2,1)S(1)} %get-tuple-element.27), channel_id=1, source_target_pairs={{0,1},{1,2},{2,3},{3,4},{4,5},{5,6},{6,7},{7,0},{8,9},{9,10},{10,1... | collective-permute-start | bytes 196616 | tf_op jit(solution)/shard_map/ppermute | solution.py:447
  15.5 3.1 %collective-permute-start.5 = (bf16[1,2,128,128]{3,2,1,0:T(8,128)(2,1)S(1)}, bf16[1,2,128,128]{3,2,1,0:T(8,128)(2,1)S(1)}, u32[]{:S(2)}, u32[]{:S(2)}) collective-permute-start(bf16[1,2,128,128]{3,2,1,0:T(8,128)(2,1)S(1)} %get-tuple-element.26), channel_id=1, source_target_pairs={{0,7},{1,0},{2,1},{3,2},{4,3},{5,4},{6,5},{7,6},{8,15},{9,8},{10,9... | collective-permute-start | bytes 196616 | tf_op jit(solution)/shard_map/ppermute | solution.py:447
  18.6 0.4 %table.1 = bf16[256,1024]{1,0:T(8,128)(2,1)S(1)} custom-call(f32[16,128]{1,0:T(8,128)S(1)} %get-tuple-element.12.edge_turn.after), custom_call_target="tpu_custom_call" | custom-call | tf_op jit(solution)/shard_map/table/pallas_call | solution.py:537
  19.0 1.7 %collective-permute-done.4.from_prev = bf16[1,2,128,128]{3,2,1,0:T(8,128)(2,1)S(1)} collective-permute-done((bf16[1,2,128,128]{3,2,1,0:T(8,128)(2,1)S(1)}, bf16[1,2,128,128]{3,2,1,0:T(8,128)(2,1)S(1)}, u32[]{:S(2)}, u32[]{:S(2)}) %collective-permute-start.4) | collective-permute-done | bytes 65568 | tf_op jit(solution)/shard_map/ppermute | solution.py:447
  20.8 1.6 %subgrid.1 = (bf16[2,1,2,128,512]{4,3,2,1,0:T(8,128)(2,1)}, bf16[2,1,2,128,128]{4,3,2,1,0:T(8,128)(2,1)S(1)}, bf16[1,2,128,128]{3,2,1,0:T(8,128)(2,1)S(1)}, bf16[1,2,128,128]{3,2,1,0:T(8,128)(2,1)S(1)}) custom-call(f32[32,128]{1,0:T(8,128)S(1)} %get-tuple-element.13.turn.after, bf16[2,1,2,128,128]{4,3,2,1,0:T(8,128)(2,1)S(1)} %get-tuple-element.23.kept, ...), custom_call_target="tpu_custom_call" | custom-call | tf_op jit(solution)/shard_map/subgrid/pallas_call | solution.py:560
  22.3 1.4 %collective-permute-start.8 = (bf16[1,2,128,128]{3,2,1,0:T(8,128)(2,1)S(1)}, bf16[1,2,128,128]{3,2,1,0:T(8,128)(2,1)S(1)}, u32[]{:S(2)}, u32[]{:S(2)}) collective-permute-start(bf16[1,2,128,128]{3,2,1,0:T(8,128)(2,1)S(1)} %get-tuple-element.20), channel_id=1, source_target_pairs={{0,1},{1,2},{2,3},{3,4},{4,5},{5,6},{6,7},{7,0},{8,9},{9,10},{10,1... | collective-permute-start | bytes 196616 | tf_op jit(solution)/shard_map/ppermute | solution.py:447
  23.8 3.4 %collective-permute-start.9 = (bf16[1,2,128,128]{3,2,1,0:T(8,128)(2,1)S(1)}, bf16[1,2,128,128]{3,2,1,0:T(8,128)(2,1)S(1)}, u32[]{:S(2)}, u32[]{:S(2)}) collective-permute-start(bf16[1,2,128,128]{3,2,1,0:T(8,128)(2,1)S(1)} %get-tuple-element.21), channel_id=1, source_target_pairs={{0,7},{1,0},{2,1},{3,2},{4,3},{5,4},{6,5},{7,6},{8,15},{9,8},{10,9... | collective-permute-start | bytes 196616 | tf_op jit(solution)/shard_map/ppermute | solution.py:447
  27.2 1.6 %collective-permute-start.6 = (bf16[2,1,2,128,128]{4,3,2,0,1:T(8,128)(2,1)S(1)}, bf16[2,1,2,128,128]{4,3,2,0,1:T(8,128)(2,1)S(1)}, u32[]{:S(2)}, u32[]{:S(2)}) collective-permute-start(bf16[2,1,2,128,128]{4,3,2,0,1:T(8,128)(2,1)S(1)} %bitcast.19), channel_id=1, source_target_pairs={{0,16},{8,24},{16,0},{24,8},{1,17},{9,25},{17,1},{25,9},{2,18},{10... | collective-permute-start | bytes 393224 | tf_op jit(solution)/shard_map/ppermute | solution.py:442
  28.8 0.6 %collective-permute-done.8 = bf16[1,2,128,128]{3,2,1,0:T(8,128)(2,1)S(1)} collective-permute-done((bf16[1,2,128,128]{3,2,1,0:T(8,128)(2,1)S(1)}, bf16[1,2,128,128]{3,2,1,0:T(8,128)(2,1)S(1)}, u32[]{:S(2)}, u32[]{:S(2)}) %collective-permute-start.8) | collective-permute-done | bytes 65568 | tf_op jit(solution)/shard_map/ppermute | solution.py:447
  29.4 1.7 %collective-permute-start.10 = (bf16[2,1,2,128,128]{4,3,2,0,1:T(8,128)(2,1)S(1)}, bf16[2,1,2,128,128]{4,3,2,0,1:T(8,128)(2,1)S(1)}, u32[]{:S(2)}, u32[]{:S(2)}) collective-permute-start(bf16[2,1,2,128,128]{4,3,2,0,1:T(8,128)(2,1)S(1)} %get-tuple-element.25), channel_id=1, source_target_pairs={{0,16},{8,24},{16,0},{24,8},{1,17},{9,25},{17,1},{25,9},{2,18},{10... | collective-permute-start | bytes 393224 | tf_op jit(solution)/shard_map/ppermute | solution.py:442
  31.1 1.1 %collective-permute-done.6 = bf16[2,1,2,128,128]{4,3,2,0,1:T(8,128)(2,1)S(1)} collective-permute-done((bf16[2,1,2,128,128]{4,3,2,0,1:T(8,128)(2,1)S(1)}, bf16[2,1,2,128,128]{4,3,2,0,1:T(8,128)(2,1)S(1)}, u32[]{:S(2)}, u32[]{:S(2)}) %collective-permute-start.6) | collective-permute-done | bytes 131104 | tf_op jit(solution)/shard_map/ppermute | solution.py:442
  32.3 2.2 %collective-permute-done.10 = bf16[2,1,2,128,128]{4,3,2,0,1:T(8,128)(2,1)S(1)} collective-permute-done((bf16[2,1,2,128,128]{4,3,2,0,1:T(8,128)(2,1)S(1)}, bf16[2,1,2,128,128]{4,3,2,0,1:T(8,128)(2,1)S(1)}, u32[]{:S(2)}, u32[]{:S(2)}) %collective-permute-start.10) | collective-permute-done | bytes 131104 | tf_op jit(solution)/shard_map/ppermute | solution.py:442
  34.6 2.2 %zero.1.whole = bf16[2,1,2,512,1024]{4,3,2,1,0:T(8,128)(2,1)} custom-call(f32[32,128]{1,0:T(8,128)S(1)} %get-tuple-element.13.turn.after), custom_call_target="tpu_custom_call" | custom-call | tf_op jit(solution)/shard_map/zero/pallas_call | solution.py:546
  36.7 1.1 %window.1.whole = bf16[2,1,2,512,1024]{4,3,2,1,0:T(8,128)(2,1)} custom-call(f32[32,128]{1,0:T(8,128)S(1)} %get-tuple-element.13.turn.after, bf16[2,2,2,128,128]{4,3,2,1,0:T(8,128)(2,1)S(1)} %maximum_bitcast_fusion.even.main, bf16[2,2,2,128,128]{4,3,2,1,0:T(8,128)(2,1)S(1)} %collective-permute-done.7.odd.main, ...), custom_call_target="tpu_custom_call", output_to_operand_aliasing={{}: (3, {})} | custom-call | tf_op jit(solution)/shard_map/window/pallas_call | solution.py:585
  37.9 1.2 %shard_map.68.whole = bf16[2,1,2,512,1024]{4,3,2,1,0:T(8,128)(2,1)} custom-call(f32[32,128]{1,0:T(8,128)S(1)} %get-tuple-element.13.turn.after, f32[16,128]{1,0:T(8,128)S(1)} %get-tuple-element.12.edge_turn.after, bf16[2,2,2,128,128]{4,3,2,1,0:T(8,128)(2,1)S(1)} %maximum_bitcast_fusion.even.main, ...), custom_call_target="tpu_custom_call", output_to_operand_aliasing={{}: (4, {})} | custom-call | tf_op jit(solution)/shard_map/pallas_call | solution.py:597
  39.1 1.2 %shard_map.69 = bf16[2,1,2,512,1024]{4,3,2,1,0:T(8,128)(2,1)} custom-call(f32[32,128]{1,0:T(8,128)S(1)} %get-tuple-element.13.turn.after, f32[16,128]{1,0:T(8,128)S(1)} %get-tuple-element.12.edge_turn.after, bf16[2,2,2,128,128]{4,3,2,1,0:T(8,128)(2,1)S(1)} %collective-permute-done.7.odd.main, ...), custom_call_target="tpu_custom_call", output_to_operand_aliasing={{}: (4, {})} | custom-call | tf_op jit(solution)/shard_map/pallas_call | solution.py:597
  (20 shorter events, 0.5 us)
Async XLA Ops:
  2.1 3.7 %collective-permute-start.2 = (bf16[2,2,2,128,128]{4,3,2,1,0:T(8,128)(2,1)S(1)}, bf16[2,2,2,128,128]{4,3,2,1,0:T(8,128)(2,1)S(1)}, u32[]{:S(2)}, u32[]{:S(2)}) collective-permute-start(bf16[2,2,2,128,128]{4,3,2,1,0:T(8,128)(2,1)S(1)} %get-tuple-element.17), channel_id=1, source_target_pairs={{0,8},{8,0},{16,24},{24,16},{1,9},{9,1},{17,25},{25,17},{2,10},{10... | collective-permute-start | bytes 786440 | tf_op jit(solution)/shard_map/ppermute | solution.py:442
  4.1 16.6 %copy-start = (bf16[2,1,128,512]{3,2,1,0:T(8,128)(2,1)S(1)}, bf16[2,1,128,512]{3,2,1,0:T(8,128)(2,1)}, u32[]{:S(2)}) copy-start(bf16[2,1,128,512]{3,2,1,0:T(8,128)(2,1)} %weights.1) | copy-start | bytes 786436
  5.7 3.2 %collective-permute-start = (bf16[2,2,2,128,128]{4,3,2,1,0:T(8,128)(2,1)S(1)}, bf16[2,2,2,128,128]{4,3,2,1,0:T(8,128)(2,1)S(1)}, u32[]{:S(2)}, u32[]{:S(2)}) collective-permute-start(bf16[2,2,2,128,128]{4,3,2,1,0:T(8,128)(2,1)S(1)} %get-tuple-element.15), channel_id=1, source_target_pairs={{0,8},{8,0},{16,24},{24,16},{1,9},{9,1},{17,25},{25,17},{2,10},{10... | collective-permute-start | bytes 786440 | tf_op jit(solution)/shard_map/ppermute | solution.py:442
  5.9 7.4 %collective-permute-start.3 = (bf16[2,1,2,128,128]{4,3,2,1,0:T(8,128)(2,1)S(1)}, bf16[2,1,2,128,128]{4,3,2,1,0:T(8,128)(2,1)S(1)}, u32[]{:S(2)}, u32[]{:S(2)}) collective-permute-start(bf16[2,1,2,128,128]{4,3,2,1,0:T(8,128)(2,1)S(1)} %slice.31), channel_id=1, source_target_pairs={{0,16},{8,24},{16,0},{24,8},{1,17},{9,25},{17,1},{25,9},{2,18},{10... | collective-permute-start | bytes 393224 | tf_op jit(solution)/shard_map/ppermute | solution.py:442
  9.1 9.9 %collective-permute-start.1 = (bf16[2,1,2,128,128]{4,3,2,1,0:T(8,128)(2,1)S(1)}, bf16[2,1,2,128,128]{4,3,2,1,0:T(8,128)(2,1)S(1)}, u32[]{:S(2)}, u32[]{:S(2)}) collective-permute-start(bf16[2,1,2,128,128]{4,3,2,1,0:T(8,128)(2,1)S(1)} %get-tuple-element.22), channel_id=1, source_target_pairs={{0,16},{8,24},{16,0},{24,8},{1,17},{9,25},{17,1},{25,9},{2,18},{10... | collective-permute-start | bytes 393224 | tf_op jit(solution)/shard_map/ppermute | solution.py:442
  13.4 7.4 %collective-permute-start.4 = (bf16[1,2,128,128]{3,2,1,0:T(8,128)(2,1)S(1)}, bf16[1,2,128,128]{3,2,1,0:T(8,128)(2,1)S(1)}, u32[]{:S(2)}, u32[]{:S(2)}) collective-permute-start(bf16[1,2,128,128]{3,2,1,0:T(8,128)(2,1)S(1)} %get-tuple-element.27), channel_id=1, source_target_pairs={{0,1},{1,2},{2,3},{3,4},{4,5},{5,6},{6,7},{7,0},{8,9},{9,10},{10,1... | collective-permute-start | bytes 196616 | tf_op jit(solution)/shard_map/ppermute | solution.py:447
  15.5 5.3 %collective-permute-start.5 = (bf16[1,2,128,128]{3,2,1,0:T(8,128)(2,1)S(1)}, bf16[1,2,128,128]{3,2,1,0:T(8,128)(2,1)S(1)}, u32[]{:S(2)}, u32[]{:S(2)}) collective-permute-start(bf16[1,2,128,128]{3,2,1,0:T(8,128)(2,1)S(1)} %get-tuple-element.26), channel_id=1, source_target_pairs={{0,7},{1,0},{2,1},{3,2},{4,3},{5,4},{6,5},{7,6},{8,15},{9,8},{10,9... | collective-permute-start | bytes 196616 | tf_op jit(solution)/shard_map/ppermute | solution.py:447
  22.3 7.1 %collective-permute-start.8 = (bf16[1,2,128,128]{3,2,1,0:T(8,128)(2,1)S(1)}, bf16[1,2,128,128]{3,2,1,0:T(8,128)(2,1)S(1)}, u32[]{:S(2)}, u32[]{:S(2)}) collective-permute-start(bf16[1,2,128,128]{3,2,1,0:T(8,128)(2,1)S(1)} %get-tuple-element.20), channel_id=1, source_target_pairs={{0,1},{1,2},{2,3},{3,4},{4,5},{5,6},{6,7},{7,0},{8,9},{9,10},{10,1... | collective-permute-start | bytes 196616 | tf_op jit(solution)/shard_map/ppermute | solution.py:447
  23.8 5.6 %collective-permute-start.9 = (bf16[1,2,128,128]{3,2,1,0:T(8,128)(2,1)S(1)}, bf16[1,2,128,128]{3,2,1,0:T(8,128)(2,1)S(1)}, u32[]{:S(2)}, u32[]{:S(2)}) collective-permute-start(bf16[1,2,128,128]{3,2,1,0:T(8,128)(2,1)S(1)} %get-tuple-element.21), channel_id=1, source_target_pairs={{0,7},{1,0},{2,1},{3,2},{4,3},{5,4},{6,5},{7,6},{8,15},{9,8},{10,9... | collective-permute-start | bytes 196616 | tf_op jit(solution)/shard_map/ppermute | solution.py:447
  27.2 5.0 %collective-permute-start.6 = (bf16[2,1,2,128,128]{4,3,2,0,1:T(8,128)(2,1)S(1)}, bf16[2,1,2,128,128]{4,3,2,0,1:T(8,128)(2,1)S(1)}, u32[]{:S(2)}, u32[]{:S(2)}) collective-permute-start(bf16[2,1,2,128,128]{4,3,2,0,1:T(8,128)(2,1)S(1)} %bitcast.19), channel_id=1, source_target_pairs={{0,16},{8,24},{16,0},{24,8},{1,17},{9,25},{17,1},{25,9},{2,18},{10... | collective-permute-start | bytes 393224 | tf_op jit(solution)/shard_map/ppermute | solution.py:442
  29.4 5.0 %collective-permute-start.10 = (bf16[2,1,2,128,128]{4,3,2,0,1:T(8,128)(2,1)S(1)}, bf16[2,1,2,128,128]{4,3,2,0,1:T(8,128)(2,1)S(1)}, u32[]{:S(2)}, u32[]{:S(2)}) collective-permute-start(bf16[2,1,2,128,128]{4,3,2,0,1:T(8,128)(2,1)S(1)} %get-tuple-element.25), channel_id=1, source_target_pairs={{0,16},{8,24},{16,0},{24,8},{1,17},{9,25},{17,1},{25,9},{2,18},{10... | collective-permute-start | bytes 393224 | tf_op jit(solution)/shard_map/ppermute | solution.py:442
  32.2 4.5 %collective-permute-start.7 = (bf16[2,2,2,128,128]{4,3,2,1,0:T(8,128)(2,1)S(1)}, bf16[2,2,2,128,128]{4,3,2,1,0:T(8,128)(2,1)S(1)}, u32[]{:S(2)}, u32[]{:S(2)}) collective-permute-start(bf16[2,2,2,128,128]{4,3,2,1,0:T(8,128)(2,1)S(1)} %maximum_bitcast_fusion.even.main), channel_id=1, source_target_pairs={{0,8},{8,0},{16,24},{24,16},{1,9},{9,1},{17,25},{25,17},{2,10},{10... | collective-permute-start | bytes 786440 | tf_op jit(solution)/shard_map/ppermute | solution.py:442
  34.5 4.6 %collective-permute-start.11 = (bf16[2,2,2,128,128]{4,3,2,1,0:T(8,128)(2,1)S(1)}, bf16[2,2,2,128,128]{4,3,2,1,0:T(8,128)(2,1)S(1)}, u32[]{:S(2)}, u32[]{:S(2)}) collective-permute-start(bf16[2,2,2,128,128]{4,3,2,1,0:T(8,128)(2,1)S(1)} %maximum_bitcast_fusion.1.edges), channel_id=1, source_target_pairs={{0,8},{8,0},{16,24},{24,16},{1,9},{9,1},{17,25},{25,17},{2,10},{10... | collective-permute-start | bytes 786440 | tf_op jit(solution)/shard_map/ppermute | solution.py:442

commit v5 on v4

--- a/solution.py
+++ b/solution.py
@@ -352,64 +352,55 @@
         copy.wait()
 
 
-def phased(source, s, c, cosine, sine):
-    real = source[0, s // 2, c].astype(F32)
-    imag = source[1, s // 2, c].astype(F32)
-    return real * cosine - imag * sine, imag * cosine + real * sine
-
-
-def window_kernel(cols, facets, turn, even, odd, whole, out, buf, sems):
+def windows_of(main, half, base, turn, out, buf, sems, tiles, cols, facets, facet):
+    block = XM // facets
+    zero = jnp.zeros((1, LANES), F32)
+    first_tiles, _ = places_of(turn, cols)
+    copies = []
+    for c in range(cols):
+        cosine = turn[c : c + 1, :]
+        sine = turn[8 + c : 9 + c, :]
+        is_low = lanes_of((1, LANES)).astype(F32) >= turn[24 + c : 25 + c, :]
+        for i in range(facets // 2):
+            rows = rows_of(facet, 2 * i + half, block)
+            real = main[0, i, c].astype(F32)
+            imag = main[1, i, c].astype(F32)
+            values = (real * cosine - imag * sine, imag * cosine + real * sine)
+            for part in range(2):
+                base[part, i, c] = values[part]
+                buf[c, 0, part, i] = jnp.where(is_low, values[part], zero).astype(BF16)
+                buf[c, 1, part, i] = jnp.where(is_low, zero, values[part]).astype(BF16)
+            for slot in range(2):
+                which = first_tiles[c] + slot
+                at = pl.multiple_of(jnp.clip(which, 0, tiles - 1) * LANES, LANES)
+                copy = pltpu.make_async_copy(
+                    buf.at[c, slot, :, i],
+                    out.at[c, 0, :, rows, pl.ds(at, LANES)],
+                    sems.at[c, slot, i],
+                )
+                inside = jnp.logical_and(which > 0, which < tiles - 1)
+                pl.when(inside)(copy.start)
+                copies.append((inside, copy))
+    return copies
+
+
+def ends_of(edges, half, base, turn, edge_turn, out, buf, sems, cols, facets, facet):
     shard = out.shape[4]
     tiles = shard // LANES
     block = XM // facets
-    facet = lax.axis_index("facet")
-    zero = jnp.zeros((1, LANES), F32)
-    first_tiles, _ = places_of(turn, cols)
-    copies = []
-    for c in range(cols):
-        cosine = turn[c : c + 1, :]
-        sine = turn[8 + c : 9 + c, :]
-        is_low = lanes_of((1, LANES)).astype(F32) >= turn[24 + c : 25 + c, :]
-        for s in range(facets):
-            rows = rows_of(facet, s, block)
-            values = phased(odd if s % 2 else even, s, c, cosine, sine)
-            for part in range(2):
-                buf[c, 0, part, rows, :] = jnp.where(is_low, values[part], zero).astype(BF16)
-                buf[c, 1, part, rows, :] = jnp.where(is_low, zero, values[part]).astype(BF16)
-        for slot in range(2):
-            which = first_tiles[c] + slot
-            at = pl.multiple_of(jnp.clip(which, 0, tiles - 1) * LANES, LANES)
-            copy = pltpu.make_async_copy(
-                buf.at[c, slot], out.at[c, 0, :, :, pl.ds(at, LANES)], sems.at[c, slot]
-            )
-            inside = jnp.logical_and(which > 0, which < tiles - 1)
-            pl.when(inside)(copy.start)
-            copies.append((inside, copy))
-    for inside, copy in copies:
-        pl.when(inside)(copy.wait)
-
-
-def end_kernel(cols, facets, odd, turn, edge_turn, main, edges, whole, out, buf, sems):
-    shard = out.shape[4]
-    tiles = shard // LANES
-    block = XM // facets
-    facet = lax.axis_index("facet")
     left = lanes_of((1, LANES)) < HALF
     zero = jnp.zeros((1, LANES), F32)
     copies = []
     for c in range(cols):
-        cosine = turn[c : c + 1, :]
-        sine = turn[8 + c : 9 + c, :]
         edge_cosine = edge_turn[c : c + 1, :]
         edge_sine = edge_turn[8 + c : 9 + c, :]
         tile_at = turn[16 + c : 17 + c, :]
         in_first = tile_at == 0
         in_last = tile_at == tiles - 1
-        for s in range(odd, facets, 2):
-            rows = rows_of(facet, s, block)
-            values = phased(main, s, c, cosine, sine)
-            prev = edges[0, s // 2, c].astype(F32)
-            nxt = edges[1, s // 2, c].astype(F32)
+        for i in range(facets // 2):
+            rows = rows_of(facet, 2 * i + half, block)
+            prev = edges[0, i, c].astype(F32)
+            nxt = edges[1, i, c].astype(F32)
             real = jnp.where(left, prev, pltpu.roll(nxt, HALF, 1))
             imag = jnp.where(left, pltpu.roll(prev, HALF, 1), nxt)
             ends = (
@@ -417,24 +408,67 @@
                 imag * edge_cosine + real * edge_sine,
             )
             for part in range(2):
-                value = values[part]
+                value = base[part, i, c]
                 end = ends[part]
-                buf[c, 0, part, s // 2] = (
+                buf[c, 0, part, i] = (
                     jnp.where(left, end, zero) + jnp.where(in_first, value, zero)
                 ).astype(BF16)
-                buf[c, 1, part, s // 2] = (
+                buf[c, 1, part, i] = (
                     jnp.where(left, zero, end) + jnp.where(in_last, value, zero)
                 ).astype(BF16)
             for slot, start in enumerate((0, shard - LANES)):
                 copy = pltpu.make_async_copy(
-                    buf.at[c, slot, :, s // 2],
+                    buf.at[c, slot, :, i],
                     out.at[c, 0, :, rows, pl.ds(start, LANES)],
-                    sems.at[c, slot, s // 2],
+                    sems.at[c, slot, i],
                 )
                 copy.start()
                 copies.append(copy)
-    for copy in copies:
+    return copies
+
+
+def finish(windows, ends):
+    for inside, copy in windows:
+        pl.when(inside)(copy.wait)
+    for copy in ends:
         copy.wait()
+
+
+def window_kernel(cols, facets, turn, even, whole, out, base, buf, sems):
+    facet = lax.axis_index("facet")
+    tiles = out.shape[4] // LANES
+    finish(windows_of(even, 0, base, turn, out, buf, sems, tiles, cols, facets, facet), ())
+
+
+def middle_kernel(
+    cols,
+    facets,
+    turn,
+    edge_turn,
+    odd,
+    even_edge,
+    even_base,
+    whole,
+    out,
+    base,
+    buf,
+    sems,
+    end_buf,
+    end_sems,
+):
+    facet = lax.axis_index("facet")
+    tiles = out.shape[4] // LANES
+    windows = windows_of(odd, 1, base, turn, out, buf, sems, tiles, cols, facets, facet)
+    ends = ends_of(
+        even_edge, 0, even_base, turn, edge_turn, out, end_buf, end_sems, cols, facets, facet
+    )
+    finish(windows, ends)
+
+
+def end_kernel(cols, facets, turn, edge_turn, odd_edge, odd_base, whole, out, buf, sems):
+    facet = lax.axis_index("facet")
+    ends = ends_of(odd_edge, 1, odd_base, turn, edge_turn, out, buf, sems, cols, facets, facet)
+    finish((), ends)
 
 
 def swapped(block, bit):
@@ -582,30 +616,41 @@
     even, odd = gathered(back, facets)
     even_edge, odd_edge = gathered(jnp.stack([came_prev, came_next]), facets)
 
+    base = jax.ShapeDtypeStruct((2, facets // 2, cols, block, LANES), F32)
+    tile_half = [
+        pltpu.VMEM((cols, 2, 2, facets // 2, block, LANES), BF16),
+        pltpu.SemaphoreType.DMA((cols, 2, facets // 2)),
+    ]
+    updates, even_base = pl.pallas_call(
+        functools.partial(window_kernel, cols, facets),
+        out_shape=(shape, base),
+        in_specs=[VMEM, VMEM, HBM],
+        out_specs=(HBM, VMEM),
+        scratch_shapes=tile_half,
+        input_output_aliases={2: 0},
+        compiler_params=params(12),
+        name="window",
+    )(turn, even, updates)
+    updates, odd_base = pl.pallas_call(
+        functools.partial(middle_kernel, cols, facets),
+        out_shape=(shape, base),
+        in_specs=[VMEM] * 5 + [HBM],
+        out_specs=(HBM, VMEM),
+        scratch_shapes=tile_half * 2,
+        input_output_aliases={5: 0},
+        compiler_params=params(12),
+        name="middle",
+    )(turn, edge_turn, odd, even_edge, even_base, updates)
     updates = pl.pallas_call(
-        functools.partial(window_kernel, cols, facets),
+        functools.partial(end_kernel, cols, facets),
         out_shape=shape,
-        in_specs=[VMEM, VMEM, VMEM, HBM],
+        in_specs=[VMEM] * 4 + [HBM],
         out_specs=HBM,
-        scratch_shapes=[tile_pair, pltpu.SemaphoreType.DMA((cols, 2))],
-        input_output_aliases={3: 0},
-        compiler_params=params(12),
-        name="window",
-    )(turn, even, odd, updates)
-    halves = ((0, even, even_edge), (1, odd, odd_edge))
-    for half, main, ends in halves:
-        updates = pl.pallas_call(
-            functools.partial(end_kernel, cols, facets, half),
-            out_shape=shape,
-            in_specs=[VMEM] * 4 + [HBM],
-            out_specs=HBM,
-            scratch_shapes=[
-                pltpu.VMEM((cols, 2, 2, facets // 2, block, LANES), BF16),
-                pltpu.SemaphoreType.DMA((cols, 2, facets // 2)),
-            ],
-            input_output_aliases={4: 0},
-            compiler_params=params(12),
-        )(turn, edge_turn, main, ends, updates)
+        scratch_shapes=tile_half,
+        input_output_aliases={4: 0},
+        compiler_params=params(12),
+        name="end",
+    )(turn, edge_turn, odd_edge, odd_base, updates)
     return grids, updates
 
 

time: 40.6 us -> 40.9 us (level)
  no operation moved by 1% of the time
where the time goes in v5:
time: 40.9 us; the launch traced here: 40.6 us
  starting transfers between devices  18.2 us (44%)
  Pallas kernels  12.5 us (31%)
  waiting for transfers between devices  8.8 us (22%)
  between operations  0.8 us (2%)
    ppermute x4, starting transfers between devices, shifted(): lax.ppermute(block, 'col', [(i, (i + distance) % count) for i in range(co...  10.1 us
    ppermute x8, starting transfers between devices, swapped(): return lax.ppermute(block, 'facet', [(i, i ^ bit) for i in range(facets)])  8.12 us
    ppermute x8, waiting for transfers between devices, swapped(): return lax.ppermute(block, 'facet', [(i, i ^ bit) for i in range(facets)])  6.46 us
    ppermute x4, waiting for transfers between devices, shifted(): lax.ppermute(block, 'col', [(i, (i + distance) % count) for i in range(co...  2.33 us
    pallas_call x1, Pallas kernels, computed(): pl.pallas_call(zero_kernel, out_shape=shape, in_specs=[VMEM], out_specs=H...  2.15 us
    pallas_call x1, Pallas kernels, computed(): pl.pallas_call(functools.partial(middle_kernel, cols, facets), out_shape=...  1.59 us
    pallas_call x1, Pallas kernels, computed(): pl.pallas_call(functools.partial(main_kernel, cols, facets), out_shape=(p...  1.58 us
    pallas_call x1, Pallas kernels, computed(): pl.pallas_call(functools.partial(subgrid_kernel, cols, shard), out_shape=...  1.57 us
  transfers between devices with their start and end apart: 12, of which 5 were waited for; matrix products, arithmetic and copies ran while one was open for 1% of the time, Pallas kernels for 20%

profile of v5, /device:TPU:0, one launch (start us, length us, event | category | flops | bytes accessed | tf_op | source)
XLA Modules:
  0.0 40.6 jit_solution(13685613365301201560)
XLA Ops:
  0.6 1.5 %edge.1 = (bf16[2,2,2,128,128]{4,3,2,1,0:T(8,128)(2,1)S(1)}, f32[16,128]{1,0:T(8,128)S(1)}) custom-call(s32[1,2]{1,0:T(1,128)} %offsets.3, s32[2]{0:T(128)} %column.3, bf16[2,1,2,512,1024]{4,3,2,1,0:T(8,128)(2,1)} %spectra.5), custom_call_target="tpu_custom_call" | custom-call | tf_op jit(solution)/shard_map/edge/pallas_call | solution.py:531
  2.1 0.6 %collective-permute-start.2 = (bf16[2,2,2,128,128]{4,3,2,1,0:T(8,128)(2,1)S(1)}, bf16[2,2,2,128,128]{4,3,2,1,0:T(8,128)(2,1)S(1)}, u32[]{:S(2)}, u32[]{:S(2)}) collective-permute-start(bf16[2,2,2,128,128]{4,3,2,1,0:T(8,128)(2,1)S(1)} %get-tuple-element.21), channel_id=1, source_target_pairs={{0,8},{8,0},{16,24},{24,16},{1,9},{9,1},{17,25},{25,17},{2,10},{10... | collective-permute-start | bytes 786440 | tf_op jit(solution)/shard_map/ppermute | solution.py:476
  2.7 1.5 %hold.1 = (bf16[2,2,2,128,128]{4,3,2,1,0:T(8,128)(2,1)S(1)}, f32[32,128]{1,0:T(8,128)S(1)}) custom-call(s32[1,2]{1,0:T(1,128)} %offsets.3, s32[2]{0:T(128)} %column.3, s32[1,2]{1,0:T(1,128)} %bitcast.25, bf16[2,1,2,512,1024]{4,3,2,1,0:T(8,128)(2,1)} %spectra.5, f32[16,128]{1,0:T(8,128)S(1)} %get-tuple-element.16.edge_turn.after), custom_call_target="tpu_custom_call" | custom-call | tf_op jit(solution)/shard_map/hold/pallas_call | solution.py:540
  4.2 1.6 %main.1 = (bf16[2,2,2,128,128]{4,3,2,1,0:T(8,128)(2,1)S(1)}, bf16[2,2,2,128,128]{4,3,2,1,0:T(8,128)(2,1)S(1)}) custom-call(bf16[2,1,2,512,1024]{4,3,2,1,0:T(8,128)(2,1)} %spectra.5, f32[32,128]{1,0:T(8,128)S(1)} %get-tuple-element.17.turn.after, f32[16,128]{1,0:T(8,128)S(1)} %get-tuple-element.16.edge_turn.after), custom_call_target="tpu_custom_call" | custom-call | tf_op jit(solution)/shard_map/main/pallas_call | solution.py:558
  5.7 0.1 collective-permute-start
  5.9 3.0 %collective-permute-start.3 = (bf16[2,1,2,128,128]{4,3,2,1,0:T(8,128)(2,1)S(1)}, bf16[2,1,2,128,128]{4,3,2,1,0:T(8,128)(2,1)S(1)}, u32[]{:S(2)}, u32[]{:S(2)}) collective-permute-start(bf16[2,1,2,128,128]{4,3,2,1,0:T(8,128)(2,1)S(1)} %slice.31), channel_id=1, source_target_pairs={{0,16},{8,24},{16,0},{24,8},{1,17},{9,25},{17,1},{25,9},{2,18},{10... | collective-permute-start | bytes 393224 | tf_op jit(solution)/shard_map/ppermute | solution.py:476
  9.1 1.1 %collective-permute-start.1 = (bf16[2,1,2,128,128]{4,3,2,1,0:T(8,128)(2,1)S(1)}, bf16[2,1,2,128,128]{4,3,2,1,0:T(8,128)(2,1)S(1)}, u32[]{:S(2)}, u32[]{:S(2)}) collective-permute-start(bf16[2,1,2,128,128]{4,3,2,1,0:T(8,128)(2,1)S(1)} %get-tuple-element.30), channel_id=1, source_target_pairs={{0,16},{8,24},{16,0},{24,8},{1,17},{9,25},{17,1},{25,9},{2,18},{10... | collective-permute-start | bytes 393224 | tf_op jit(solution)/shard_map/ppermute | solution.py:476
  10.1 3.2 %collective-permute-done.3 = bf16[2,1,2,128,128]{4,3,2,1,0:T(8,128)(2,1)S(1)} collective-permute-done((bf16[2,1,2,128,128]{4,3,2,1,0:T(8,128)(2,1)S(1)}, bf16[2,1,2,128,128]{4,3,2,1,0:T(8,128)(2,1)S(1)}, u32[]{:S(2)}, u32[]{:S(2)}) %collective-permute-start.3) | collective-permute-done | bytes 131104 | tf_op jit(solution)/shard_map/ppermute | solution.py:476
  13.4 2.1 %collective-permute-start.4 = (bf16[1,2,128,128]{3,2,1,0:T(8,128)(2,1)S(1)}, bf16[1,2,128,128]{3,2,1,0:T(8,128)(2,1)S(1)}, u32[]{:S(2)}, u32[]{:S(2)}) collective-permute-start(bf16[1,2,128,128]{3,2,1,0:T(8,128)(2,1)S(1)} %get-tuple-element.35), channel_id=1, source_target_pairs={{0,1},{1,2},{2,3},{3,4},{4,5},{5,6},{6,7},{7,0},{8,9},{9,10},{10,1... | collective-permute-start | bytes 196616 | tf_op jit(solution)/shard_map/ppermute | solution.py:481
  15.5 3.1 %collective-permute-start.5 = (bf16[1,2,128,128]{3,2,1,0:T(8,128)(2,1)S(1)}, bf16[1,2,128,128]{3,2,1,0:T(8,128)(2,1)S(1)}, u32[]{:S(2)}, u32[]{:S(2)}) collective-permute-start(bf16[1,2,128,128]{3,2,1,0:T(8,128)(2,1)S(1)} %get-tuple-element.34), channel_id=1, source_target_pairs={{0,7},{1,0},{2,1},{3,2},{4,3},{5,4},{6,5},{7,6},{8,15},{9,8},{10,9... | collective-permute-start | bytes 196616 | tf_op jit(solution)/shard_map/ppermute | solution.py:481
  18.6 0.4 %table.1 = bf16[256,1024]{1,0:T(8,128)(2,1)S(1)} custom-call(f32[16,128]{1,0:T(8,128)S(1)} %get-tuple-element.16.edge_turn.after), custom_call_target="tpu_custom_call" | custom-call | tf_op jit(solution)/shard_map/table/pallas_call | solution.py:571
  19.0 1.7 %collective-permute-done.4.from_prev = bf16[1,2,128,128]{3,2,1,0:T(8,128)(2,1)S(1)} collective-permute-done((bf16[1,2,128,128]{3,2,1,0:T(8,128)(2,1)S(1)}, bf16[1,2,128,128]{3,2,1,0:T(8,128)(2,1)S(1)}, u32[]{:S(2)}, u32[]{:S(2)}) %collective-permute-start.4) | collective-permute-done | bytes 65568 | tf_op jit(solution)/shard_map/ppermute | solution.py:481
  20.8 1.6 %subgrid.1 = (bf16[2,1,2,128,512]{4,3,2,1,0:T(8,128)(2,1)}, bf16[2,1,2,128,128]{4,3,2,1,0:T(8,128)(2,1)S(1)}, bf16[1,2,128,128]{3,2,1,0:T(8,128)(2,1)S(1)}, bf16[1,2,128,128]{3,2,1,0:T(8,128)(2,1)S(1)}) custom-call(f32[32,128]{1,0:T(8,128)S(1)} %get-tuple-element.17.turn.after, bf16[2,1,2,128,128]{4,3,2,1,0:T(8,128)(2,1)S(1)} %get-tuple-element.31.kept, ...), custom_call_target="tpu_custom_call" | custom-call | tf_op jit(solution)/shard_map/subgrid/pallas_call | solution.py:594
  22.3 1.4 %collective-permute-start.6 = (bf16[1,2,128,128]{3,2,1,0:T(8,128)(2,1)S(1)}, bf16[1,2,128,128]{3,2,1,0:T(8,128)(2,1)S(1)}, u32[]{:S(2)}, u32[]{:S(2)}) collective-permute-start(bf16[1,2,128,128]{3,2,1,0:T(8,128)(2,1)S(1)} %get-tuple-element.23), channel_id=1, source_target_pairs={{0,1},{1,2},{2,3},{3,4},{4,5},{5,6},{6,7},{7,0},{8,9},{9,10},{10,1... | collective-permute-start | bytes 196616 | tf_op jit(solution)/shard_map/ppermute | solution.py:481
  23.8 3.4 %collective-permute-start.7 = (bf16[1,2,128,128]{3,2,1,0:T(8,128)(2,1)S(1)}, bf16[1,2,128,128]{3,2,1,0:T(8,128)(2,1)S(1)}, u32[]{:S(2)}, u32[]{:S(2)}) collective-permute-start(bf16[1,2,128,128]{3,2,1,0:T(8,128)(2,1)S(1)} %get-tuple-element.24), channel_id=1, source_target_pairs={{0,7},{1,0},{2,1},{3,2},{4,3},{5,4},{6,5},{7,6},{8,15},{9,8},{10,9... | collective-permute-start | bytes 196616 | tf_op jit(solution)/shard_map/ppermute | solution.py:481
  27.2 1.6 %collective-permute-start.10 = (bf16[2,1,2,128,128]{4,3,2,0,1:T(8,128)(2,1)S(1)}, bf16[2,1,2,128,128]{4,3,2,0,1:T(8,128)(2,1)S(1)}, u32[]{:S(2)}, u32[]{:S(2)}) collective-permute-start(bf16[2,1,2,128,128]{4,3,2,0,1:T(8,128)(2,1)S(1)} %bitcast.19), channel_id=1, source_target_pairs={{0,16},{8,24},{16,0},{24,8},{1,17},{9,25},{17,1},{25,9},{2,18},{10... | collective-permute-start | bytes 393224 | tf_op jit(solution)/shard_map/ppermute | solution.py:476
  28.8 0.6 %collective-permute-done.6 = bf16[1,2,128,128]{3,2,1,0:T(8,128)(2,1)S(1)} collective-permute-done((bf16[1,2,128,128]{3,2,1,0:T(8,128)(2,1)S(1)}, bf16[1,2,128,128]{3,2,1,0:T(8,128)(2,1)S(1)}, u32[]{:S(2)}, u32[]{:S(2)}) %collective-permute-start.6) | collective-permute-done | bytes 65568 | tf_op jit(solution)/shard_map/ppermute | solution.py:481
  29.4 1.7 %collective-permute-start.8 = (bf16[2,1,2,128,128]{4,3,2,0,1:T(8,128)(2,1)S(1)}, bf16[2,1,2,128,128]{4,3,2,0,1:T(8,128)(2,1)S(1)}, u32[]{:S(2)}, u32[]{:S(2)}) collective-permute-start(bf16[2,1,2,128,128]{4,3,2,0,1:T(8,128)(2,1)S(1)} %get-tuple-element.33), channel_id=1, source_target_pairs={{0,16},{8,24},{16,0},{24,8},{1,17},{9,25},{17,1},{25,9},{2,18},{10... | collective-permute-start | bytes 393224 | tf_op jit(solution)/shard_map/ppermute | solution.py:476
  31.1 1.1 %collective-permute-done.10 = bf16[2,1,2,128,128]{4,3,2,0,1:T(8,128)(2,1)S(1)} collective-permute-done((bf16[2,1,2,128,128]{4,3,2,0,1:T(8,128)(2,1)S(1)}, bf16[2,1,2,128,128]{4,3,2,0,1:T(8,128)(2,1)S(1)}, u32[]{:S(2)}, u32[]{:S(2)}) %collective-permute-start.10) | collective-permute-done | bytes 131104 | tf_op jit(solution)/shard_map/ppermute | solution.py:476
  32.3 2.2 %collective-permute-done.8 = bf16[2,1,2,128,128]{4,3,2,0,1:T(8,128)(2,1)S(1)} collective-permute-done((bf16[2,1,2,128,128]{4,3,2,0,1:T(8,128)(2,1)S(1)}, bf16[2,1,2,128,128]{4,3,2,0,1:T(8,128)(2,1)S(1)}, u32[]{:S(2)}, u32[]{:S(2)}) %collective-permute-start.8) | collective-permute-done | bytes 131104 | tf_op jit(solution)/shard_map/ppermute | solution.py:476
  34.6 2.2 %zero.1.whole = bf16[2,1,2,512,1024]{4,3,2,1,0:T(8,128)(2,1)} custom-call(f32[32,128]{1,0:T(8,128)S(1)} %get-tuple-element.17.turn.after), custom_call_target="tpu_custom_call" | custom-call | tf_op jit(solution)/shard_map/zero/pallas_call | solution.py:580
  36.7 1.0 %window.1 = (bf16[2,1,2,512,1024]{4,3,2,1,0:T(8,128)(2,1)}, f32[2,2,2,128,128]{4,3,2,1,0:T(8,128)S(1)}) custom-call(f32[32,128]{1,0:T(8,128)S(1)} %get-tuple-element.17.turn.after, bf16[2,2,2,128,128]{4,3,2,1,0:T(8,128)(2,1)S(1)} %maximum_bitcast_fusion.1.even, bf16[2,1,2,512,1024]{4,3,2,1,0:T(8,128)(2,1)} %zero.1.whole), custom_call_target="tpu_custom_call", output_to_operand_aliasing={{0}: (2, {})} | custom-call | tf_op jit(solution)/shard_map/window/pallas_call | solution.py:624
  37.7 1.6 %middle.1 = (bf16[2,1,2,512,1024]{4,3,2,1,0:T(8,128)(2,1)}, f32[2,2,2,128,128]{4,3,2,1,0:T(8,128)S(1)}) custom-call(f32[32,128]{1,0:T(8,128)S(1)} %get-tuple-element.17.turn.after, f32[16,128]{1,0:T(8,128)S(1)} %get-tuple-element.16.edge_turn.after, bf16[2,2,2,128,128]{4,3,2,1,0:T(8,128)(2,1)S(1)} %collective-permute-done.11.odd, ...), custom_call_target="tpu_custom_call", output_to_operand_aliasing={{0}: (5, {})} | custom-call | tf_op jit(solution)/shard_map/middle/pallas_call | solution.py:634
  39.4 1.2 %end.1 = bf16[2,1,2,512,1024]{4,3,2,1,0:T(8,128)(2,1)} custom-call(f32[32,128]{1,0:T(8,128)S(1)} %get-tuple-element.17.turn.after, f32[16,128]{1,0:T(8,128)S(1)} %get-tuple-element.16.edge_turn.after, bf16[2,2,2,128,128]{4,3,2,1,0:T(8,128)(2,1)S(1)} %collective-permute-done.9.odd_edge, ...), custom_call_target="tpu_custom_call", output_to_operand_aliasing={{}: (4, {})} | custom-call | tf_op jit(solution)/shard_map/end/pallas_call | solution.py:644
  (20 shorter events, 0.5 us)
Async XLA Ops:
  2.1 3.7 %collective-permute-start.2 = (bf16[2,2,2,128,128]{4,3,2,1,0:T(8,128)(2,1)S(1)}, bf16[2,2,2,128,128]{4,3,2,1,0:T(8,128)(2,1)S(1)}, u32[]{:S(2)}, u32[]{:S(2)}) collective-permute-start(bf16[2,2,2,128,128]{4,3,2,1,0:T(8,128)(2,1)S(1)} %get-tuple-element.21), channel_id=1, source_target_pairs={{0,8},{8,0},{16,24},{24,16},{1,9},{9,1},{17,25},{25,17},{2,10},{10... | collective-permute-start | bytes 786440 | tf_op jit(solution)/shard_map/ppermute | solution.py:476
  4.1 16.6 %copy-start = (bf16[2,1,128,512]{3,2,1,0:T(8,128)(2,1)S(1)}, bf16[2,1,128,512]{3,2,1,0:T(8,128)(2,1)}, u32[]{:S(2)}) copy-start(bf16[2,1,128,512]{3,2,1,0:T(8,128)(2,1)} %weights.1) | copy-start | bytes 786436
  5.7 3.2 %collective-permute-start = (bf16[2,2,2,128,128]{4,3,2,1,0:T(8,128)(2,1)S(1)}, bf16[2,2,2,128,128]{4,3,2,1,0:T(8,128)(2,1)S(1)}, u32[]{:S(2)}, u32[]{:S(2)}) collective-permute-start(bf16[2,2,2,128,128]{4,3,2,1,0:T(8,128)(2,1)S(1)} %get-tuple-element.19), channel_id=1, source_target_pairs={{0,8},{8,0},{16,24},{24,16},{1,9},{9,1},{17,25},{25,17},{2,10},{10... | collective-permute-start | bytes 786440 | tf_op jit(solution)/shard_map/ppermute | solution.py:476
  5.9 7.4 %collective-permute-start.3 = (bf16[2,1,2,128,128]{4,3,2,1,0:T(8,128)(2,1)S(1)}, bf16[2,1,2,128,128]{4,3,2,1,0:T(8,128)(2,1)S(1)}, u32[]{:S(2)}, u32[]{:S(2)}) collective-permute-start(bf16[2,1,2,128,128]{4,3,2,1,0:T(8,128)(2,1)S(1)} %slice.31), channel_id=1, source_target_pairs={{0,16},{8,24},{16,0},{24,8},{1,17},{9,25},{17,1},{25,9},{2,18},{10... | collective-permute-start | bytes 393224 | tf_op jit(solution)/shard_map/ppermute | solution.py:476
  9.1 9.9 %collective-permute-start.1 = (bf16[2,1,2,128,128]{4,3,2,1,0:T(8,128)(2,1)S(1)}, bf16[2,1,2,128,128]{4,3,2,1,0:T(8,128)(2,1)S(1)}, u32[]{:S(2)}, u32[]{:S(2)}) collective-permute-start(bf16[2,1,2,128,128]{4,3,2,1,0:T(8,128)(2,1)S(1)} %get-tuple-element.30), channel_id=1, source_target_pairs={{0,16},{8,24},{16,0},{24,8},{1,17},{9,25},{17,1},{25,9},{2,18},{10... | collective-permute-start | bytes 393224 | tf_op jit(solution)/shard_map/ppermute | solution.py:476
  13.4 7.4 %collective-permute-start.4 = (bf16[1,2,128,128]{3,2,1,0:T(8,128)(2,1)S(1)}, bf16[1,2,128,128]{3,2,1,0:T(8,128)(2,1)S(1)}, u32[]{:S(2)}, u32[]{:S(2)}) collective-permute-start(bf16[1,2,128,128]{3,2,1,0:T(8,128)(2,1)S(1)} %get-tuple-element.35), channel_id=1, source_target_pairs={{0,1},{1,2},{2,3},{3,4},{4,5},{5,6},{6,7},{7,0},{8,9},{9,10},{10,1... | collective-permute-start | bytes 196616 | tf_op jit(solution)/shard_map/ppermute | solution.py:481
  15.5 5.3 %collective-permute-start.5 = (bf16[1,2,128,128]{3,2,1,0:T(8,128)(2,1)S(1)}, bf16[1,2,128,128]{3,2,1,0:T(8,128)(2,1)S(1)}, u32[]{:S(2)}, u32[]{:S(2)}) collective-permute-start(bf16[1,2,128,128]{3,2,1,0:T(8,128)(2,1)S(1)} %get-tuple-element.34), channel_id=1, source_target_pairs={{0,7},{1,0},{2,1},{3,2},{4,3},{5,4},{6,5},{7,6},{8,15},{9,8},{10,9... | collective-permute-start | bytes 196616 | tf_op jit(solution)/shard_map/ppermute | solution.py:481
  22.3 7.1 %collective-permute-start.6 = (bf16[1,2,128,128]{3,2,1,0:T(8,128)(2,1)S(1)}, bf16[1,2,128,128]{3,2,1,0:T(8,128)(2,1)S(1)}, u32[]{:S(2)}, u32[]{:S(2)}) collective-permute-start(bf16[1,2,128,128]{3,2,1,0:T(8,128)(2,1)S(1)} %get-tuple-element.23), channel_id=1, source_target_pairs={{0,1},{1,2},{2,3},{3,4},{4,5},{5,6},{6,7},{7,0},{8,9},{9,10},{10,1... | collective-permute-start | bytes 196616 | tf_op jit(solution)/shard_map/ppermute | solution.py:481
  23.8 5.6 %collective-permute-start.7 = (bf16[1,2,128,128]{3,2,1,0:T(8,128)(2,1)S(1)}, bf16[1,2,128,128]{3,2,1,0:T(8,128)(2,1)S(1)}, u32[]{:S(2)}, u32[]{:S(2)}) collective-permute-start(bf16[1,2,128,128]{3,2,1,0:T(8,128)(2,1)S(1)} %get-tuple-element.24), channel_id=1, source_target_pairs={{0,7},{1,0},{2,1},{3,2},{4,3},{5,4},{6,5},{7,6},{8,15},{9,8},{10,9... | collective-permute-start | bytes 196616 | tf_op jit(solution)/shard_map/ppermute | solution.py:481
  27.2 5.0 %collective-permute-start.10 = (bf16[2,1,2,128,128]{4,3,2,0,1:T(8,128)(2,1)S(1)}, bf16[2,1,2,128,128]{4,3,2,0,1:T(8,128)(2,1)S(1)}, u32[]{:S(2)}, u32[]{:S(2)}) collective-permute-start(bf16[2,1,2,128,128]{4,3,2,0,1:T(8,128)(2,1)S(1)} %bitcast.19), channel_id=1, source_target_pairs={{0,16},{8,24},{16,0},{24,8},{1,17},{9,25},{17,1},{25,9},{2,18},{10... | collective-permute-start | bytes 393224 | tf_op jit(solution)/shard_map/ppermute | solution.py:476
  29.4 5.0 %collective-permute-start.8 = (bf16[2,1,2,128,128]{4,3,2,0,1:T(8,128)(2,1)S(1)}, bf16[2,1,2,128,128]{4,3,2,0,1:T(8,128)(2,1)S(1)}, u32[]{:S(2)}, u32[]{:S(2)}) collective-permute-start(bf16[2,1,2,128,128]{4,3,2,0,1:T(8,128)(2,1)S(1)} %get-tuple-element.33), channel_id=1, source_target_pairs={{0,16},{8,24},{16,0},{24,8},{1,17},{9,25},{17,1},{25,9},{2,18},{10... | collective-permute-start | bytes 393224 | tf_op jit(solution)/shard_map/ppermute | solution.py:476
  32.2 5.5 %collective-permute-start.11 = (bf16[2,2,2,128,128]{4,3,2,1,0:T(8,128)(2,1)S(1)}, bf16[2,2,2,128,128]{4,3,2,1,0:T(8,128)(2,1)S(1)}, u32[]{:S(2)}, u32[]{:S(2)}) collective-permute-start(bf16[2,2,2,128,128]{4,3,2,1,0:T(8,128)(2,1)S(1)} %maximum_bitcast_fusion.1.even), channel_id=1, source_target_pairs={{0,8},{8,0},{16,24},{24,16},{1,9},{9,1},{17,25},{25,17},{2,10},{10... | collective-permute-start | bytes 786440 | tf_op jit(solution)/shard_map/ppermute | solution.py:476
  34.5 4.9 %collective-permute-start.9 = (bf16[2,2,2,128,128]{4,3,2,1,0:T(8,128)(2,1)S(1)}, bf16[2,2,2,128,128]{4,3,2,1,0:T(8,128)(2,1)S(1)}, u32[]{:S(2)}, u32[]{:S(2)}) collective-permute-start(bf16[2,2,2,128,128]{4,3,2,1,0:T(8,128)(2,1)S(1)} %maximum_bitcast_fusion.even_edge), channel_id=1, source_target_pairs={{0,8},{8,0},{16,24},{24,16},{1,9},{9,1},{17,25},{25,17},{2,10},{10... | collective-permute-start | bytes 786440 | tf_op jit(solution)/shard_map/ppermute | solution.py:476

commit v6 on v5

--- a/solution.py
+++ b/solution.py
@@ -293,8 +293,6 @@
     to_next,
     stack,
     scaled,
-    stage,
-    sems,
 ):
     tiles = shard // LANES
     block = kept.shape[3]
@@ -314,7 +312,6 @@
         rows = slice(c * block, (c + 1) * block)
         stack[rows, :WM] = pltpu.roll(real, shift, 1).astype(BF16)
         stack[rows, WM:] = pltpu.roll(imag, shift, 1).astype(BF16)
-    copies = []
     for part in range(2):
         span = slice(part * XM, (part + 1) * XM)
         product = jnp.dot(stack[...], table[:, span], preferred_element_type=F32)
@@ -322,11 +319,8 @@
         for c in range(cols):
             rows = slice(c * block, (c + 1) * block)
             piece = rounded[rows]
-            stage[c, part] = piece
+            grids[c, 0, part] = piece
             scaled[rows, span] = (piece.astype(F32) * weights[c, 0].astype(F32)).astype(BF16)
-        copy = pltpu.make_async_copy(stage.at[:, part], grids.at[:, 0, part], sems.at[part])
-        copy.start()
-        copies.append(copy)
     result = lax.dot_general(
         scaled[...],
         table[...],
@@ -348,8 +342,6 @@
         imag_high = jnp.where(high, imag, zero)
         to_prev[0, c] = (pltpu.roll(real_low, HALF, 1) + imag_low).astype(BF16)
         to_next[0, c] = (real_high + pltpu.roll(imag_high, HALF, 1)).astype(BF16)
-    for copy in copies:
-        copy.wait()
 
 
 def windows_of(main, half, base, turn, out, buf, sems, tiles, cols, facets, facet):
@@ -434,10 +426,15 @@
         copy.wait()
 
 
-def window_kernel(cols, facets, turn, even, whole, out, base, buf, sems):
+def window_kernel(
+    cols, facets, turn, even, held, whole, out, base, grids, buf, sems, grid_sem
+):
     facet = lax.axis_index("facet")
     tiles = out.shape[4] // LANES
-    finish(windows_of(even, 0, base, turn, out, buf, sems, tiles, cols, facets, facet), ())
+    store = pltpu.make_async_copy(held, grids, grid_sem)
+    store.start()
+    windows = windows_of(even, 0, base, turn, out, buf, sems, tiles, cols, facets, facet)
+    finish(windows, (store,))
 
 
 def middle_kernel(
@@ -591,21 +588,20 @@
     )(turn)
 
     edge = jax.ShapeDtypeStruct((1, cols, block, LANES), BF16)
-    grids, back, to_prev, to_next = pl.pallas_call(
+    grid_shape = jax.ShapeDtypeStruct((cols, 1, 2, block, XM), BF16)
+    held, back, to_prev, to_next = pl.pallas_call(
         functools.partial(subgrid_kernel, cols, shard),
         out_shape=(
-            jax.ShapeDtypeStruct((cols, 1, 2, block, XM), BF16),
+            grid_shape,
             jax.ShapeDtypeStruct((2, 1, cols, block, LANES), BF16),
             edge,
             edge,
         ),
         in_specs=[VMEM] * 7,
-        out_specs=(HBM, VMEM, VMEM, VMEM),
+        out_specs=(VMEM, VMEM, VMEM, VMEM),
         scratch_shapes=[
             pltpu.VMEM((cols * block, 2 * WM), BF16),
             pltpu.VMEM((cols * block, 2 * XM), BF16),
-            pltpu.VMEM((cols, 2, block, XM), BF16),
-            pltpu.SemaphoreType.DMA((2,)),
         ],
         compiler_params=params(12),
         name="subgrid",
@@ -621,16 +617,16 @@
         pltpu.VMEM((cols, 2, 2, facets // 2, block, LANES), BF16),
         pltpu.SemaphoreType.DMA((cols, 2, facets // 2)),
     ]
-    updates, even_base = pl.pallas_call(
+    updates, even_base, grids = pl.pallas_call(
         functools.partial(window_kernel, cols, facets),
-        out_shape=(shape, base),
-        in_specs=[VMEM, VMEM, HBM],
-        out_specs=(HBM, VMEM),
-        scratch_shapes=tile_half,
-        input_output_aliases={2: 0},
+        out_shape=(shape, base, grid_shape),
+        in_specs=[VMEM, VMEM, VMEM, HBM],
+        out_specs=(HBM, VMEM, HBM),
+        scratch_shapes=[*tile_half, pltpu.SemaphoreType.DMA(())],
+        input_output_aliases={3: 0},
         compiler_params=params(12),
         name="window",
-    )(turn, even, updates)
+    )(turn, even, held, updates)
     updates, odd_base = pl.pallas_call(
         functools.partial(middle_kernel, cols, facets),
         out_shape=(shape, base),

time: 40.9 us -> 40.2 us (0.983)
  Pallas kernels: 12.5 us -> 11.8 us
    pallas_call x1, Pallas kernels: 1.57 us -> 0.91 us  [computed(): pl.pallas_call(functools.partial(subgrid_kernel, cols, shard), out_shape=...]
  transfers between devices with their start and end apart: 12 -> 12, of which waited for: 5 -> 5; matrix products, arithmetic and copies ran while one was open for 1% -> 1% of each run, Pallas kernels for 20% -> 21%
where the time goes in v6:
time: 40.2 us; the launch traced here: 39.9 us
  starting transfers between devices  18.2 us (45%)
  Pallas kernels  11.8 us (29%)
  waiting for transfers between devices  8.77 us (22%)
  between operations  0.79 us (2%)
    ppermute x4, starting transfers between devices, shifted(): lax.ppermute(block, 'col', [(i, (i + distance) % count) for i in range(co...  10.1 us
    ppermute x8, starting transfers between devices, swapped(): return lax.ppermute(block, 'facet', [(i, i ^ bit) for i in range(facets)])  8.14 us
    ppermute x8, waiting for transfers between devices, swapped(): return lax.ppermute(block, 'facet', [(i, i ^ bit) for i in range(facets)])  6.45 us
    ppermute x4, waiting for transfers between devices, shifted(): lax.ppermute(block, 'col', [(i, (i + distance) % count) for i in range(co...  2.32 us
    pallas_call x1, Pallas kernels, computed(): pl.pallas_call(zero_kernel, out_shape=shape, in_specs=[VMEM], out_specs=H...  2.15 us
    pallas_call x1, Pallas kernels, computed(): pl.pallas_call(functools.partial(middle_kernel, cols, facets), out_shape=...  1.59 us
    pallas_call x1, Pallas kernels, computed(): pl.pallas_call(functools.partial(main_kernel, cols, facets), out_shape=(p...  1.58 us
    pallas_call x1, Pallas kernels, computed(): pl.pallas_call(functools.partial(edge_kernel, cols, facets, length), out_...  1.47 us
  transfers between devices with their start and end apart: 12, of which 5 were waited for; matrix products, arithmetic and copies ran while one was open for 1% of the time, Pallas kernels for 21%

profile of v6, /device:TPU:0, one launch (start us, length us, event | category | flops | bytes accessed | tf_op | source)
XLA Modules:
  0.0 39.9 jit_solution(9074772435188666314)
XLA Ops:
  0.6 1.5 %edge.1 = (bf16[2,2,2,128,128]{4,3,2,1,0:T(8,128)(2,1)S(1)}, f32[16,128]{1,0:T(8,128)S(1)}) custom-call(s32[1,2]{1,0:T(1,128)} %offsets.3, s32[2]{0:T(128)} %column.3, bf16[2,1,2,512,1024]{4,3,2,1,0:T(8,128)(2,1)} %spectra.5), custom_call_target="tpu_custom_call" | custom-call | tf_op jit(solution)/shard_map/edge/pallas_call | solution.py:528
  2.1 0.6 %collective-permute-start.2 = (bf16[2,2,2,128,128]{4,3,2,1,0:T(8,128)(2,1)S(1)}, bf16[2,2,2,128,128]{4,3,2,1,0:T(8,128)(2,1)S(1)}, u32[]{:S(2)}, u32[]{:S(2)}) collective-permute-start(bf16[2,2,2,128,128]{4,3,2,1,0:T(8,128)(2,1)S(1)} %get-tuple-element.22), channel_id=1, source_target_pairs={{0,8},{8,0},{16,24},{24,16},{1,9},{9,1},{17,25},{25,17},{2,10},{10... | collective-permute-start | bytes 786440 | tf_op jit(solution)/shard_map/ppermute | solution.py:473
  2.7 1.5 %hold.1 = (bf16[2,2,2,128,128]{4,3,2,1,0:T(8,128)(2,1)S(1)}, f32[32,128]{1,0:T(8,128)S(1)}) custom-call(s32[1,2]{1,0:T(1,128)} %offsets.3, s32[2]{0:T(128)} %column.3, s32[1,2]{1,0:T(1,128)} %bitcast.25, bf16[2,1,2,512,1024]{4,3,2,1,0:T(8,128)(2,1)} %spectra.5, f32[16,128]{1,0:T(8,128)S(1)} %get-tuple-element.17.edge_turn.after), custom_call_target="tpu_custom_call" | custom-call | tf_op jit(solution)/shard_map/hold/pallas_call | solution.py:537
  4.2 1.6 %main.1 = (bf16[2,2,2,128,128]{4,3,2,1,0:T(8,128)(2,1)S(1)}, bf16[2,2,2,128,128]{4,3,2,1,0:T(8,128)(2,1)S(1)}) custom-call(bf16[2,1,2,512,1024]{4,3,2,1,0:T(8,128)(2,1)} %spectra.5, f32[32,128]{1,0:T(8,128)S(1)} %get-tuple-element.18.turn.after, f32[16,128]{1,0:T(8,128)S(1)} %get-tuple-element.17.edge_turn.after), custom_call_target="tpu_custom_call" | custom-call | tf_op jit(solution)/shard_map/main/pallas_call | solution.py:555
  5.7 0.1 collective-permute-start
  5.9 3.0 %collective-permute-start.3 = (bf16[2,1,2,128,128]{4,3,2,1,0:T(8,128)(2,1)S(1)}, bf16[2,1,2,128,128]{4,3,2,1,0:T(8,128)(2,1)S(1)}, u32[]{:S(2)}, u32[]{:S(2)}) collective-permute-start(bf16[2,1,2,128,128]{4,3,2,1,0:T(8,128)(2,1)S(1)} %slice.31), channel_id=1, source_target_pairs={{0,16},{8,24},{16,0},{24,8},{1,17},{9,25},{17,1},{25,9},{2,18},{10... | collective-permute-start | bytes 393224 | tf_op jit(solution)/shard_map/ppermute | solution.py:473
  9.1 1.1 %collective-permute-start.1 = (bf16[2,1,2,128,128]{4,3,2,1,0:T(8,128)(2,1)S(1)}, bf16[2,1,2,128,128]{4,3,2,1,0:T(8,128)(2,1)S(1)}, u32[]{:S(2)}, u32[]{:S(2)}) collective-permute-start(bf16[2,1,2,128,128]{4,3,2,1,0:T(8,128)(2,1)S(1)} %get-tuple-element.32), channel_id=1, source_target_pairs={{0,16},{8,24},{16,0},{24,8},{1,17},{9,25},{17,1},{25,9},{2,18},{10... | collective-permute-start | bytes 393224 | tf_op jit(solution)/shard_map/ppermute | solution.py:473
  10.1 3.2 %collective-permute-done.3 = bf16[2,1,2,128,128]{4,3,2,1,0:T(8,128)(2,1)S(1)} collective-permute-done((bf16[2,1,2,128,128]{4,3,2,1,0:T(8,128)(2,1)S(1)}, bf16[2,1,2,128,128]{4,3,2,1,0:T(8,128)(2,1)S(1)}, u32[]{:S(2)}, u32[]{:S(2)}) %collective-permute-start.3) | collective-permute-done | bytes 131104 | tf_op jit(solution)/shard_map/ppermute | solution.py:473
  13.4 2.1 %collective-permute-start.4 = (bf16[1,2,128,128]{3,2,1,0:T(8,128)(2,1)S(1)}, bf16[1,2,128,128]{3,2,1,0:T(8,128)(2,1)S(1)}, u32[]{:S(2)}, u32[]{:S(2)}) collective-permute-start(bf16[1,2,128,128]{3,2,1,0:T(8,128)(2,1)S(1)} %get-tuple-element.37), channel_id=1, source_target_pairs={{0,1},{1,2},{2,3},{3,4},{4,5},{5,6},{6,7},{7,0},{8,9},{9,10},{10,1... | collective-permute-start | bytes 196616 | tf_op jit(solution)/shard_map/ppermute | solution.py:478
  15.5 3.1 %collective-permute-start.5 = (bf16[1,2,128,128]{3,2,1,0:T(8,128)(2,1)S(1)}, bf16[1,2,128,128]{3,2,1,0:T(8,128)(2,1)S(1)}, u32[]{:S(2)}, u32[]{:S(2)}) collective-permute-start(bf16[1,2,128,128]{3,2,1,0:T(8,128)(2,1)S(1)} %get-tuple-element.36), channel_id=1, source_target_pairs={{0,7},{1,0},{2,1},{3,2},{4,3},{5,4},{6,5},{7,6},{8,15},{9,8},{10,9... | collective-permute-start | bytes 196616 | tf_op jit(solution)/shard_map/ppermute | solution.py:478
  18.6 0.4 %table.1 = bf16[256,1024]{1,0:T(8,128)(2,1)S(1)} custom-call(f32[16,128]{1,0:T(8,128)S(1)} %get-tuple-element.17.edge_turn.after), custom_call_target="tpu_custom_call" | custom-call | tf_op jit(solution)/shard_map/table/pallas_call | solution.py:568
  19.0 1.7 %collective-permute-done.4.from_prev = bf16[1,2,128,128]{3,2,1,0:T(8,128)(2,1)S(1)} collective-permute-done((bf16[1,2,128,128]{3,2,1,0:T(8,128)(2,1)S(1)}, bf16[1,2,128,128]{3,2,1,0:T(8,128)(2,1)S(1)}, u32[]{:S(2)}, u32[]{:S(2)}) %collective-permute-start.4) | collective-permute-done | bytes 65568 | tf_op jit(solution)/shard_map/ppermute | solution.py:478
  20.8 0.9 %subgrid.1 = (bf16[2,1,2,128,512]{4,3,2,1,0:T(8,128)(2,1)S(1)}, bf16[2,1,2,128,128]{4,3,2,1,0:T(8,128)(2,1)S(1)}, bf16[1,2,128,128]{3,2,1,0:T(8,128)(2,1)S(1)}, bf16[1,2,128,128]{3,2,1,0:T(8,128)(2,1)S(1)}) custom-call(f32[32,128]{1,0:T(8,128)S(1)} %get-tuple-element.18.turn.after, bf16[2,1,2,128,128]{4,3,2,1,0:T(8,128)(2,1)S(1)} %get-tuple-element.33.kept, ...), custom_call_target="tpu_custom_call" | custom-call | tf_op jit(solution)/shard_map/subgrid/pallas_call | solution.py:592
  21.7 1.5 %collective-permute-start.7 = (bf16[1,2,128,128]{3,2,1,0:T(8,128)(2,1)S(1)}, bf16[1,2,128,128]{3,2,1,0:T(8,128)(2,1)S(1)}, u32[]{:S(2)}, u32[]{:S(2)}) collective-permute-start(bf16[1,2,128,128]{3,2,1,0:T(8,128)(2,1)S(1)} %get-tuple-element.26), channel_id=1, source_target_pairs={{0,1},{1,2},{2,3},{3,4},{4,5},{5,6},{6,7},{7,0},{8,9},{9,10},{10,1... | collective-permute-start | bytes 196616 | tf_op jit(solution)/shard_map/ppermute | solution.py:478
  23.1 3.4 %collective-permute-start.8 = (bf16[1,2,128,128]{3,2,1,0:T(8,128)(2,1)S(1)}, bf16[1,2,128,128]{3,2,1,0:T(8,128)(2,1)S(1)}, u32[]{:S(2)}, u32[]{:S(2)}) collective-permute-start(bf16[1,2,128,128]{3,2,1,0:T(8,128)(2,1)S(1)} %get-tuple-element.27), channel_id=1, source_target_pairs={{0,7},{1,0},{2,1},{3,2},{4,3},{5,4},{6,5},{7,6},{8,15},{9,8},{10,9... | collective-permute-start | bytes 196616 | tf_op jit(solution)/shard_map/ppermute | solution.py:478
  26.6 1.6 %collective-permute-start.6 = (bf16[2,1,2,128,128]{4,3,2,0,1:T(8,128)(2,1)S(1)}, bf16[2,1,2,128,128]{4,3,2,0,1:T(8,128)(2,1)S(1)}, u32[]{:S(2)}, u32[]{:S(2)}) collective-permute-start(bf16[2,1,2,128,128]{4,3,2,0,1:T(8,128)(2,1)S(1)} %bitcast.19), channel_id=1, source_target_pairs={{0,16},{8,24},{16,0},{24,8},{1,17},{9,25},{17,1},{25,9},{2,18},{10... | collective-permute-start | bytes 393224 | tf_op jit(solution)/shard_map/ppermute | solution.py:473
  28.2 0.6 %collective-permute-done.7 = bf16[1,2,128,128]{3,2,1,0:T(8,128)(2,1)S(1)} collective-permute-done((bf16[1,2,128,128]{3,2,1,0:T(8,128)(2,1)S(1)}, bf16[1,2,128,128]{3,2,1,0:T(8,128)(2,1)S(1)}, u32[]{:S(2)}, u32[]{:S(2)}) %collective-permute-start.7) | collective-permute-done | bytes 65568 | tf_op jit(solution)/shard_map/ppermute | solution.py:478
  28.8 1.7 %collective-permute-start.9 = (bf16[2,1,2,128,128]{4,3,2,0,1:T(8,128)(2,1)S(1)}, bf16[2,1,2,128,128]{4,3,2,0,1:T(8,128)(2,1)S(1)}, u32[]{:S(2)}, u32[]{:S(2)}) collective-permute-start(bf16[2,1,2,128,128]{4,3,2,0,1:T(8,128)(2,1)S(1)} %get-tuple-element.35), channel_id=1, source_target_pairs={{0,16},{8,24},{16,0},{24,8},{1,17},{9,25},{17,1},{25,9},{2,18},{10... | collective-permute-start | bytes 393224 | tf_op jit(solution)/shard_map/ppermute | solution.py:473
  30.4 1.1 %collective-permute-done.6 = bf16[2,1,2,128,128]{4,3,2,0,1:T(8,128)(2,1)S(1)} collective-permute-done((bf16[2,1,2,128,128]{4,3,2,0,1:T(8,128)(2,1)S(1)}, bf16[2,1,2,128,128]{4,3,2,0,1:T(8,128)(2,1)S(1)}, u32[]{:S(2)}, u32[]{:S(2)}) %collective-permute-start.6) | collective-permute-done | bytes 131104 | tf_op jit(solution)/shard_map/ppermute | solution.py:473
  31.6 2.2 %collective-permute-done.9 = bf16[2,1,2,128,128]{4,3,2,0,1:T(8,128)(2,1)S(1)} collective-permute-done((bf16[2,1,2,128,128]{4,3,2,0,1:T(8,128)(2,1)S(1)}, bf16[2,1,2,128,128]{4,3,2,0,1:T(8,128)(2,1)S(1)}, u32[]{:S(2)}, u32[]{:S(2)}) %collective-permute-start.9) | collective-permute-done | bytes 131104 | tf_op jit(solution)/shard_map/ppermute | solution.py:473
  33.9 2.2 %zero.1.whole = bf16[2,1,2,512,1024]{4,3,2,1,0:T(8,128)(2,1)} custom-call(f32[32,128]{1,0:T(8,128)S(1)} %get-tuple-element.18.turn.after), custom_call_target="tpu_custom_call" | custom-call | tf_op jit(solution)/shard_map/zero/pallas_call | solution.py:577
  36.1 1.0 %window.1 = (bf16[2,1,2,512,1024]{4,3,2,1,0:T(8,128)(2,1)}, f32[2,2,2,128,128]{4,3,2,1,0:T(8,128)S(1)}, bf16[2,1,2,128,512]{4,3,2,1,0:T(8,128)(2,1)}) custom-call(f32[32,128]{1,0:T(8,128)S(1)} %get-tuple-element.18.turn.after, bf16[2,2,2,128,128]{4,3,2,1,0:T(8,128)(2,1)S(1)} %maximum_bitcast_fusion.even, ...), custom_call_target="tpu_custom_call", output_to_operand_aliasing={{0}: (3, {})} | custom-call | tf_op jit(solution)/shard_map/window/pallas_call | solution.py:620
  37.1 1.6 %middle.1 = (bf16[2,1,2,512,1024]{4,3,2,1,0:T(8,128)(2,1)}, f32[2,2,2,128,128]{4,3,2,1,0:T(8,128)S(1)}) custom-call(f32[32,128]{1,0:T(8,128)S(1)} %get-tuple-element.18.turn.after, f32[16,128]{1,0:T(8,128)S(1)} %get-tuple-element.17.edge_turn.after, bf16[2,2,2,128,128]{4,3,2,1,0:T(8,128)(2,1)S(1)} %collective-permute-done.11.odd, ...), custom_call_target="tpu_custom_call", output_to_operand_aliasing={{0}: (5, {})} | custom-call | tf_op jit(solution)/shard_map/middle/pallas_call | solution.py:630
  38.7 1.2 %end.1 = bf16[2,1,2,512,1024]{4,3,2,1,0:T(8,128)(2,1)} custom-call(f32[32,128]{1,0:T(8,128)S(1)} %get-tuple-element.18.turn.after, f32[16,128]{1,0:T(8,128)S(1)} %get-tuple-element.17.edge_turn.after, bf16[2,2,2,128,128]{4,3,2,1,0:T(8,128)(2,1)S(1)} %collective-permute-done.10.odd_edge, ...), custom_call_target="tpu_custom_call", output_to_operand_aliasing={{}: (4, {})} | custom-call | tf_op jit(solution)/shard_map/end/pallas_call | solution.py:640
  (20 shorter events, 0.5 us)
Async XLA Ops:
  2.1 3.7 %collective-permute-start.2 = (bf16[2,2,2,128,128]{4,3,2,1,0:T(8,128)(2,1)S(1)}, bf16[2,2,2,128,128]{4,3,2,1,0:T(8,128)(2,1)S(1)}, u32[]{:S(2)}, u32[]{:S(2)}) collective-permute-start(bf16[2,2,2,128,128]{4,3,2,1,0:T(8,128)(2,1)S(1)} %get-tuple-element.22), channel_id=1, source_target_pairs={{0,8},{8,0},{16,24},{24,16},{1,9},{9,1},{17,25},{25,17},{2,10},{10... | collective-permute-start | bytes 786440 | tf_op jit(solution)/shard_map/ppermute | solution.py:473
  4.1 16.6 %copy-start = (bf16[2,1,128,512]{3,2,1,0:T(8,128)(2,1)S(1)}, bf16[2,1,128,512]{3,2,1,0:T(8,128)(2,1)}, u32[]{:S(2)}) copy-start(bf16[2,1,128,512]{3,2,1,0:T(8,128)(2,1)} %weights.1) | copy-start | bytes 786436
  5.7 3.2 %collective-permute-start = (bf16[2,2,2,128,128]{4,3,2,1,0:T(8,128)(2,1)S(1)}, bf16[2,2,2,128,128]{4,3,2,1,0:T(8,128)(2,1)S(1)}, u32[]{:S(2)}, u32[]{:S(2)}) collective-permute-start(bf16[2,2,2,128,128]{4,3,2,1,0:T(8,128)(2,1)S(1)} %get-tuple-element.20), channel_id=1, source_target_pairs={{0,8},{8,0},{16,24},{24,16},{1,9},{9,1},{17,25},{25,17},{2,10},{10... | collective-permute-start | bytes 786440 | tf_op jit(solution)/shard_map/ppermute | solution.py:473
  5.9 7.4 %collective-permute-start.3 = (bf16[2,1,2,128,128]{4,3,2,1,0:T(8,128)(2,1)S(1)}, bf16[2,1,2,128,128]{4,3,2,1,0:T(8,128)(2,1)S(1)}, u32[]{:S(2)}, u32[]{:S(2)}) collective-permute-start(bf16[2,1,2,128,128]{4,3,2,1,0:T(8,128)(2,1)S(1)} %slice.31), channel_id=1, source_target_pairs={{0,16},{8,24},{16,0},{24,8},{1,17},{9,25},{17,1},{25,9},{2,18},{10... | collective-permute-start | bytes 393224 | tf_op jit(solution)/shard_map/ppermute | solution.py:473
  9.1 9.9 %collective-permute-start.1 = (bf16[2,1,2,128,128]{4,3,2,1,0:T(8,128)(2,1)S(1)}, bf16[2,1,2,128,128]{4,3,2,1,0:T(8,128)(2,1)S(1)}, u32[]{:S(2)}, u32[]{:S(2)}) collective-permute-start(bf16[2,1,2,128,128]{4,3,2,1,0:T(8,128)(2,1)S(1)} %get-tuple-element.32), channel_id=1, source_target_pairs={{0,16},{8,24},{16,0},{24,8},{1,17},{9,25},{17,1},{25,9},{2,18},{10... | collective-permute-start | bytes 393224 | tf_op jit(solution)/shard_map/ppermute | solution.py:473
  13.4 7.4 %collective-permute-start.4 = (bf16[1,2,128,128]{3,2,1,0:T(8,128)(2,1)S(1)}, bf16[1,2,128,128]{3,2,1,0:T(8,128)(2,1)S(1)}, u32[]{:S(2)}, u32[]{:S(2)}) collective-permute-start(bf16[1,2,128,128]{3,2,1,0:T(8,128)(2,1)S(1)} %get-tuple-element.37), channel_id=1, source_target_pairs={{0,1},{1,2},{2,3},{3,4},{4,5},{5,6},{6,7},{7,0},{8,9},{9,10},{10,1... | collective-permute-start | bytes 196616 | tf_op jit(solution)/shard_map/ppermute | solution.py:478
  15.5 5.3 %collective-permute-start.5 = (bf16[1,2,128,128]{3,2,1,0:T(8,128)(2,1)S(1)}, bf16[1,2,128,128]{3,2,1,0:T(8,128)(2,1)S(1)}, u32[]{:S(2)}, u32[]{:S(2)}) collective-permute-start(bf16[1,2,128,128]{3,2,1,0:T(8,128)(2,1)S(1)} %get-tuple-element.36), channel_id=1, source_target_pairs={{0,7},{1,0},{2,1},{3,2},{4,3},{5,4},{6,5},{7,6},{8,15},{9,8},{10,9... | collective-permute-start | bytes 196616 | tf_op jit(solution)/shard_map/ppermute | solution.py:478
  21.7 7.1 %collective-permute-start.7 = (bf16[1,2,128,128]{3,2,1,0:T(8,128)(2,1)S(1)}, bf16[1,2,128,128]{3,2,1,0:T(8,128)(2,1)S(1)}, u32[]{:S(2)}, u32[]{:S(2)}) collective-permute-start(bf16[1,2,128,128]{3,2,1,0:T(8,128)(2,1)S(1)} %get-tuple-element.26), channel_id=1, source_target_pairs={{0,1},{1,2},{2,3},{3,4},{4,5},{5,6},{6,7},{7,0},{8,9},{9,10},{10,1... | collective-permute-start | bytes 196616 | tf_op jit(solution)/shard_map/ppermute | solution.py:478
  23.1 5.6 %collective-permute-start.8 = (bf16[1,2,128,128]{3,2,1,0:T(8,128)(2,1)S(1)}, bf16[1,2,128,128]{3,2,1,0:T(8,128)(2,1)S(1)}, u32[]{:S(2)}, u32[]{:S(2)}) collective-permute-start(bf16[1,2,128,128]{3,2,1,0:T(8,128)(2,1)S(1)} %get-tuple-element.27), channel_id=1, source_target_pairs={{0,7},{1,0},{2,1},{3,2},{4,3},{5,4},{6,5},{7,6},{8,15},{9,8},{10,9... | collective-permute-start | bytes 196616 | tf_op jit(solution)/shard_map/ppermute | solution.py:478
  26.6 5.0 %collective-permute-start.6 = (bf16[2,1,2,128,128]{4,3,2,0,1:T(8,128)(2,1)S(1)}, bf16[2,1,2,128,128]{4,3,2,0,1:T(8,128)(2,1)S(1)}, u32[]{:S(2)}, u32[]{:S(2)}) collective-permute-start(bf16[2,1,2,128,128]{4,3,2,0,1:T(8,128)(2,1)S(1)} %bitcast.19), channel_id=1, source_target_pairs={{0,16},{8,24},{16,0},{24,8},{1,17},{9,25},{17,1},{25,9},{2,18},{10... | collective-permute-start | bytes 393224 | tf_op jit(solution)/shard_map/ppermute | solution.py:473
  28.8 5.0 %collective-permute-start.9 = (bf16[2,1,2,128,128]{4,3,2,0,1:T(8,128)(2,1)S(1)}, bf16[2,1,2,128,128]{4,3,2,0,1:T(8,128)(2,1)S(1)}, u32[]{:S(2)}, u32[]{:S(2)}) collective-permute-start(bf16[2,1,2,128,128]{4,3,2,0,1:T(8,128)(2,1)S(1)} %get-tuple-element.35), channel_id=1, source_target_pairs={{0,16},{8,24},{16,0},{24,8},{1,17},{9,25},{17,1},{25,9},{2,18},{10... | collective-permute-start | bytes 393224 | tf_op jit(solution)/shard_map/ppermute | solution.py:473
  31.6 5.5 %collective-permute-start.11 = (bf16[2,2,2,128,128]{4,3,2,1,0:T(8,128)(2,1)S(1)}, bf16[2,2,2,128,128]{4,3,2,1,0:T(8,128)(2,1)S(1)}, u32[]{:S(2)}, u32[]{:S(2)}) collective-permute-start(bf16[2,2,2,128,128]{4,3,2,1,0:T(8,128)(2,1)S(1)} %maximum_bitcast_fusion.even), channel_id=1, source_target_pairs={{0,8},{8,0},{16,24},{24,16},{1,9},{9,1},{17,25},{25,17},{2,10},{10... | collective-permute-start | bytes 786440 | tf_op jit(solution)/shard_map/ppermute | solution.py:473
  33.8 4.9 %collective-permute-start.10 = (bf16[2,2,2,128,128]{4,3,2,1,0:T(8,128)(2,1)S(1)}, bf16[2,2,2,128,128]{4,3,2,1,0:T(8,128)(2,1)S(1)}, u32[]{:S(2)}, u32[]{:S(2)}) collective-permute-start(bf16[2,2,2,128,128]{4,3,2,1,0:T(8,128)(2,1)S(1)} %maximum_bitcast_fusion.1.even_edge), channel_id=1, source_target_pairs={{0,8},{8,0},{16,24},{24,16},{1,9},{9,1},{17,25},{25,17},{2,10},{10... | collective-permute-start | bytes 786440 | tf_op jit(solution)/shard_map/ppermute | solution.py:473

commit v7 on v6

--- a/solution.py
+++ b/solution.py
@@ -344,31 +344,37 @@
         to_next[0, c] = (real_high + pltpu.roll(imag_high, HALF, 1)).astype(BF16)
 
 
-def windows_of(main, half, base, turn, out, buf, sems, tiles, cols, facets, facet):
-    block = XM // facets
+def window_of(main, i, c, turn):
+    cosine = turn[c : c + 1, :]
+    sine = turn[8 + c : 9 + c, :]
+    real = main[0, i, c].astype(F32)
+    imag = main[1, i, c].astype(F32)
+    return real * cosine - imag * sine, imag * cosine + real * sine
+
+
+def windows_of(mains, slots, base, turn, out, buf, sems, cols, block):
+    tiles = out.shape[4] // LANES
+    facet = lax.axis_index("facet")
     zero = jnp.zeros((1, LANES), F32)
     first_tiles, _ = places_of(turn, cols)
     copies = []
     for c in range(cols):
-        cosine = turn[c : c + 1, :]
-        sine = turn[8 + c : 9 + c, :]
         is_low = lanes_of((1, LANES)).astype(F32) >= turn[24 + c : 25 + c, :]
-        for i in range(facets // 2):
-            rows = rows_of(facet, 2 * i + half, block)
-            real = main[0, i, c].astype(F32)
-            imag = main[1, i, c].astype(F32)
-            values = (real * cosine - imag * sine, imag * cosine + real * sine)
+        for i, slot in enumerate(slots):
+            rows = rows_of(facet, slot, block)
+            main, at_main = mains[i]
+            values = window_of(main, at_main, c, turn)
             for part in range(2):
                 base[part, i, c] = values[part]
                 buf[c, 0, part, i] = jnp.where(is_low, values[part], zero).astype(BF16)
                 buf[c, 1, part, i] = jnp.where(is_low, zero, values[part]).astype(BF16)
-            for slot in range(2):
-                which = first_tiles[c] + slot
+            for side in range(2):
+                which = first_tiles[c] + side
                 at = pl.multiple_of(jnp.clip(which, 0, tiles - 1) * LANES, LANES)
                 copy = pltpu.make_async_copy(
-                    buf.at[c, slot, :, i],
+                    buf.at[c, side, :, i],
                     out.at[c, 0, :, rows, pl.ds(at, LANES)],
-                    sems.at[c, slot, i],
+                    sems.at[c, side, i],
                 )
                 inside = jnp.logical_and(which > 0, which < tiles - 1)
                 pl.when(inside)(copy.start)
@@ -376,10 +382,10 @@
     return copies
 
 
-def ends_of(edges, half, base, turn, edge_turn, out, buf, sems, cols, facets, facet):
+def ends_of(edges, slots, base, turn, edge_turn, out, buf, sems, cols, block):
     shard = out.shape[4]
     tiles = shard // LANES
-    block = XM // facets
+    facet = lax.axis_index("facet")
     left = lanes_of((1, LANES)) < HALF
     zero = jnp.zeros((1, LANES), F32)
     copies = []
@@ -389,10 +395,11 @@
         tile_at = turn[16 + c : 17 + c, :]
         in_first = tile_at == 0
         in_last = tile_at == tiles - 1
-        for i in range(facets // 2):
-            rows = rows_of(facet, 2 * i + half, block)
-            prev = edges[0, i, c].astype(F32)
-            nxt = edges[1, i, c].astype(F32)
+        for i, slot in enumerate(slots):
+            rows = rows_of(facet, slot, block)
+            edge, at_edge = edges[i]
+            prev = edge[0, at_edge, c].astype(F32)
+            nxt = edge[1, at_edge, c].astype(F32)
             real = jnp.where(left, prev, pltpu.roll(nxt, HALF, 1))
             imag = jnp.where(left, pltpu.roll(prev, HALF, 1), nxt)
             ends = (
@@ -408,11 +415,11 @@
                 buf[c, 1, part, i] = (
                     jnp.where(left, zero, end) + jnp.where(in_last, value, zero)
                 ).astype(BF16)
-            for slot, start in enumerate((0, shard - LANES)):
+            for side, start in enumerate((0, shard - LANES)):
                 copy = pltpu.make_async_copy(
-                    buf.at[c, slot, :, i],
+                    buf.at[c, side, :, i],
                     out.at[c, 0, :, rows, pl.ds(start, LANES)],
-                    sems.at[c, slot, i],
+                    sems.at[c, side, i],
                 )
                 copy.start()
                 copies.append(copy)
@@ -426,25 +433,48 @@
         copy.wait()
 
 
-def window_kernel(
-    cols, facets, turn, even, held, whole, out, base, grids, buf, sems, grid_sem
+def each(array, count):
+    return [(array, i) for i in range(count)]
+
+
+def early_kernel(
+    cols,
+    turn,
+    edge_turn,
+    own,
+    near,
+    own_edge,
+    held,
+    whole,
+    out,
+    grids,
+    near_base,
+    base,
+    buf,
+    sems,
+    end_buf,
+    end_sems,
+    grid_sem,
 ):
-    facet = lax.axis_index("facet")
-    tiles = out.shape[4] // LANES
+    block = own.shape[3]
     store = pltpu.make_async_copy(held, grids, grid_sem)
     store.start()
-    windows = windows_of(even, 0, base, turn, out, buf, sems, tiles, cols, facets, facet)
-    finish(windows, (store,))
-
-
-def middle_kernel(
+    first = buf.at[:, :, :, 0:1], sems.at[:, :, 0:1]
+    second = buf.at[:, :, :, 1:2], sems.at[:, :, 1:2]
+    windows = windows_of(((own, 0),), (0,), base, turn, out, *first, cols, block)
+    ends = ends_of(((own_edge, 0),), (0,), base, turn, edge_turn, out, end_buf, end_sems, cols, block)
+    windows += windows_of(((near, 0),), (1,), near_base, turn, out, *second, cols, block)
+    finish(windows, (*ends, store))
+
+
+def window_kernel(
     cols,
-    facets,
+    slots,
     turn,
     edge_turn,
-    odd,
-    even_edge,
-    even_base,
+    main,
+    near_edge,
+    near_base,
     whole,
     out,
     base,
@@ -453,19 +483,53 @@
     end_buf,
     end_sems,
 ):
-    facet = lax.axis_index("facet")
-    tiles = out.shape[4] // LANES
-    windows = windows_of(odd, 1, base, turn, out, buf, sems, tiles, cols, facets, facet)
+    block = main.shape[3]
+    mains = each(main, len(slots))
+    windows = windows_of(mains, slots, base, turn, out, buf, sems, cols, block)
+    edges = ((near_edge, 0),)
+    ends = ends_of(edges, (1,), near_base, turn, edge_turn, out, end_buf, end_sems, cols, block)
+    finish(windows, ends)
+
+
+def middle_kernel(
+    cols,
+    slots,
+    end_slots,
+    turn,
+    edge_turn,
+    main,
+    edge,
+    edge_base,
+    whole,
+    out,
+    base,
+    buf,
+    sems,
+    end_buf,
+    end_sems,
+):
+    block = main.shape[3]
+    count = len(slots)
+    windows = windows_of(each(main, count), slots, base, turn, out, buf, sems, cols, block)
     ends = ends_of(
-        even_edge, 0, even_base, turn, edge_turn, out, end_buf, end_sems, cols, facets, facet
+        each(edge, count),
+        end_slots,
+        edge_base,
+        turn,
+        edge_turn,
+        out,
+        end_buf,
+        end_sems,
+        cols,
+        block,
     )
     finish(windows, ends)
 
 
-def end_kernel(cols, facets, turn, edge_turn, odd_edge, odd_base, whole, out, buf, sems):
-    facet = lax.axis_index("facet")
-    ends = ends_of(odd_edge, 1, odd_base, turn, edge_turn, out, buf, sems, cols, facets, facet)
-    finish((), ends)
+def end_kernel(cols, slots, turn, edge_turn, edge, base, whole, out, buf, sems):
+    block = edge.shape[3]
+    edges = each(edge, len(slots))
+    finish((), ends_of(edges, slots, base, turn, edge_turn, out, buf, sems, cols, block))
 
 
 def swapped(block, bit):
@@ -495,12 +559,16 @@
 
 def gathered(blocks, facets):
     bit = facets // 2
-    while bit > 1:
+    while bit > 2:
         received = swapped(blocks, bit)
         shape = (blocks.shape[0], -1) + blocks.shape[2:]
         blocks = jnp.stack([blocks, received], axis=2).reshape(shape)
         bit //= 2
-    return blocks, swapped(blocks, 1)
+    received = swapped(blocks, bit)
+    if blocks.shape[1] == 1:
+        return received
+    shape = (blocks.shape[0], -1) + blocks.shape[2:]
+    return jnp.stack([blocks, received], axis=2).reshape(shape)[:, 1:]
 
 
 def params(mib):
@@ -609,44 +677,69 @@
 
     came_prev = shifted(to_next, 1)
     came_next = shifted(to_prev, -1)
-    even, odd = gathered(back, facets)
-    even_edge, odd_edge = gathered(jnp.stack([came_prev, came_next]), facets)
-
-    base = jax.ShapeDtypeStruct((2, facets // 2, cols, block, LANES), F32)
-    tile_half = [
-        pltpu.VMEM((cols, 2, 2, facets // 2, block, LANES), BF16),
-        pltpu.SemaphoreType.DMA((cols, 2, facets // 2)),
-    ]
-    updates, even_base, grids = pl.pallas_call(
-        functools.partial(window_kernel, cols, facets),
-        out_shape=(shape, base, grid_shape),
-        in_specs=[VMEM, VMEM, VMEM, HBM],
-        out_specs=(HBM, VMEM, HBM),
-        scratch_shapes=[*tile_half, pltpu.SemaphoreType.DMA(())],
-        input_output_aliases={3: 0},
-        compiler_params=params(12),
-        name="window",
-    )(turn, even, held, updates)
-    updates, odd_base = pl.pallas_call(
-        functools.partial(middle_kernel, cols, facets),
+    near = swapped(back, 1)
+    rest = gathered(back, facets)
+    far = swapped(rest, 1)
+    came = jnp.stack([came_prev, came_next])
+    near_edge = swapped(came, 1)
+    rest_edge = gathered(came, facets)
+    far_edge = swapped(rest_edge, 1)
+    evens = tuple(range(2, facets, 2))
+    odds = tuple(range(3, facets, 2))
+
+    def tiles_for(count):
+        return [
+            pltpu.VMEM((cols, 2, 2, count, block, LANES), BF16),
+            pltpu.SemaphoreType.DMA((cols, 2, count)),
+        ]
+
+    base = jax.ShapeDtypeStruct((2, len(evens), cols, block, LANES), F32)
+    single = jax.ShapeDtypeStruct((2, 1, cols, block, LANES), F32)
+    updates, grids, near_base = pl.pallas_call(
+        functools.partial(early_kernel, cols),
+        out_shape=(shape, grid_shape, single),
+        in_specs=[VMEM] * 6 + [HBM],
+        out_specs=(HBM, HBM, VMEM),
+        scratch_shapes=[
+            pltpu.VMEM(single.shape, F32),
+            *tiles_for(2),
+            *tiles_for(1),
+            pltpu.SemaphoreType.DMA(()),
+        ],
+        input_output_aliases={6: 0},
+        compiler_params=params(12),
+        name="early",
+    )(turn, edge_turn, back, near, came, held, updates)
+    updates, rest_base = pl.pallas_call(
+        functools.partial(window_kernel, cols, evens),
         out_shape=(shape, base),
         in_specs=[VMEM] * 5 + [HBM],
         out_specs=(HBM, VMEM),
-        scratch_shapes=tile_half * 2,
+        scratch_shapes=[*tiles_for(len(evens)), *tiles_for(1)],
         input_output_aliases={5: 0},
         compiler_params=params(12),
+        name="window",
+    )(turn, edge_turn, rest, near_edge, near_base, updates)
+    updates, far_base = pl.pallas_call(
+        functools.partial(middle_kernel, cols, odds, evens),
+        out_shape=(shape, base),
+        in_specs=[VMEM] * 5 + [HBM],
+        out_specs=(HBM, VMEM),
+        scratch_shapes=tiles_for(len(evens)) * 2,
+        input_output_aliases={5: 0},
+        compiler_params=params(12),
         name="middle",
-    )(turn, edge_turn, odd, even_edge, even_base, updates)
+    )(turn, edge_turn, far, rest_edge, rest_base, updates)
     updates = pl.pallas_call(
-        functools.partial(end_kernel, cols, facets),
+        functools.partial(end_kernel, cols, odds),
         out_shape=shape,
         in_specs=[VMEM] * 4 + [HBM],
         out_specs=HBM,
-        scratch_shapes=tile_half,
+        scratch_shapes=tiles_for(len(odds)),
         input_output_aliases={4: 0},
         compiler_params=params(12),
         name="end",
-    )(turn, edge_turn, odd_edge, odd_base, updates)
+    )(turn, edge_turn, far_edge, far_base, updates)
     return grids, updates
 
 

time: 40.2 us -> 41 us (1.020)
  Pallas kernels: 11.8 us -> 12.7 us
    pallas_call x3 -> x4, Pallas kernels: 3.84 us -> 4.67 us  [the longest x1 1.39 us: computed(): pl.pallas_call(functools.partial(early_kernel, cols), out_shape=(shape, g...]
    ppermute x8 -> x10, waiting for transfers between devices: 6.45 us -> 6.06 us  [swapped(): return lax.ppermute(block, 'facet', [(i, i ^ bit) for i in range(facets)])]
    ppermute x8 -> x10, starting transfers between devices: 8.14 us -> 8.49 us  [swapped(): return lax.ppermute(block, 'facet', [(i, i ^ bit) for i in range(facets)])]
  transfers between devices with their start and end apart: 12 -> 14, of which waited for: 5 -> 5; matrix products, arithmetic and copies ran while one was open for 1% -> 1% of each run, Pallas kernels for 21% -> 23%
where the time goes in v7:
time: 41 us; the launch traced here: 40.7 us
  starting transfers between devices  18.6 us (45%)
  Pallas kernels  12.7 us (31%)
  waiting for transfers between devices  8.39 us (20%)
  between operations  0.8 us (2%)
    ppermute x4, starting transfers between devices, shifted(): lax.ppermute(block, 'col', [(i, (i + distance) % count) for i in range(co...  10.1 us
    ppermute x10, starting transfers between devices, swapped(): return lax.ppermute(block, 'facet', [(i, i ^ bit) for i in range(facets)])  8.49 us
    ppermute x10, waiting for transfers between devices, swapped(): return lax.ppermute(block, 'facet', [(i, i ^ bit) for i in range(facets)])  6.06 us
    ppermute x4, waiting for transfers between devices, shifted(): lax.ppermute(block, 'col', [(i, (i + distance) % count) for i in range(co...  2.33 us
    pallas_call x1, Pallas kernels, computed(): pl.pallas_call(zero_kernel, out_shape=shape, in_specs=[VMEM], out_specs=H...  2.15 us
    pallas_call x1, Pallas kernels, computed(): pl.pallas_call(functools.partial(main_kernel, cols, facets), out_shape=(p...  1.58 us
    pallas_call x1, Pallas kernels, computed(): pl.pallas_call(functools.partial(edge_kernel, cols, facets, length), out_...  1.47 us
    pallas_call x1, Pallas kernels, computed(): pl.pallas_call(functools.partial(hold_kernel, cols, facets, length), out_...  1.46 us
  transfers between devices with their start and end apart: 14, of which 5 were waited for; matrix products, arithmetic and copies ran while one was open for 1% of the time, Pallas kernels for 23%

profile of v7, /device:TPU:0, one launch (start us, length us, event | category | flops | bytes accessed | tf_op | source)
XLA Modules:
  0.0 40.7 jit_solution(16995929733416282228)
XLA Ops:
  0.6 1.5 %edge.1 = (bf16[2,2,2,128,128]{4,3,2,1,0:T(8,128)(2,1)S(1)}, f32[16,128]{1,0:T(8,128)S(1)}) custom-call(s32[1,2]{1,0:T(1,128)} %offsets.3, s32[2]{0:T(128)} %column.3, bf16[2,1,2,512,1024]{4,3,2,1,0:T(8,128)(2,1)} %spectra.5), custom_call_target="tpu_custom_call" | custom-call | tf_op jit(solution)/shard_map/edge/pallas_call | solution.py:596
  2.1 0.6 %collective-permute-start.2 = (bf16[2,2,2,128,128]{4,3,2,1,0:T(8,128)(2,1)S(1)}, bf16[2,2,2,128,128]{4,3,2,1,0:T(8,128)(2,1)S(1)}, u32[]{:S(2)}, u32[]{:S(2)}) collective-permute-start(bf16[2,2,2,128,128]{4,3,2,1,0:T(8,128)(2,1)S(1)} %get-tuple-element.24), channel_id=1, source_target_pairs={{0,8},{8,0},{16,24},{24,16},{1,9},{9,1},{17,25},{25,17},{2,10},{10... | collective-permute-start | bytes 786440 | tf_op jit(solution)/shard_map/ppermute | solution.py:537
  2.7 1.5 %hold.1 = (bf16[2,2,2,128,128]{4,3,2,1,0:T(8,128)(2,1)S(1)}, f32[32,128]{1,0:T(8,128)S(1)}) custom-call(s32[1,2]{1,0:T(1,128)} %offsets.3, s32[2]{0:T(128)} %column.3, s32[1,2]{1,0:T(1,128)} %bitcast.9, bf16[2,1,2,512,1024]{4,3,2,1,0:T(8,128)(2,1)} %spectra.5, f32[16,128]{1,0:T(8,128)S(1)} %get-tuple-element.19.edge_turn.after), custom_call_target="tpu_custom_call" | custom-call | tf_op jit(solution)/shard_map/hold/pallas_call | solution.py:605
  4.2 1.6 %main.1 = (bf16[2,2,2,128,128]{4,3,2,1,0:T(8,128)(2,1)S(1)}, bf16[2,2,2,128,128]{4,3,2,1,0:T(8,128)(2,1)S(1)}) custom-call(bf16[2,1,2,512,1024]{4,3,2,1,0:T(8,128)(2,1)} %spectra.5, f32[32,128]{1,0:T(8,128)S(1)} %get-tuple-element.20.turn.after, f32[16,128]{1,0:T(8,128)S(1)} %get-tuple-element.19.edge_turn.after), custom_call_target="tpu_custom_call" | custom-call | tf_op jit(solution)/shard_map/main/pallas_call | solution.py:623
  5.9 3.0 %collective-permute-start.3 = (bf16[2,1,2,128,128]{4,3,2,1,0:T(8,128)(2,1)S(1)}, bf16[2,1,2,128,128]{4,3,2,1,0:T(8,128)(2,1)S(1)}, u32[]{:S(2)}, u32[]{:S(2)}) collective-permute-start(bf16[2,1,2,128,128]{4,3,2,1,0:T(8,128)(2,1)S(1)} %slice.31), channel_id=1, source_target_pairs={{0,16},{8,24},{16,0},{24,8},{1,17},{9,25},{17,1},{25,9},{2,18},{10... | collective-permute-start | bytes 393224 | tf_op jit(solution)/shard_map/ppermute | solution.py:537
  9.1 1.1 %collective-permute-start.1 = (bf16[2,1,2,128,128]{4,3,2,1,0:T(8,128)(2,1)S(1)}, bf16[2,1,2,128,128]{4,3,2,1,0:T(8,128)(2,1)S(1)}, u32[]{:S(2)}, u32[]{:S(2)}) collective-permute-start(bf16[2,1,2,128,128]{4,3,2,1,0:T(8,128)(2,1)S(1)} %get-tuple-element.36), channel_id=1, source_target_pairs={{0,16},{8,24},{16,0},{24,8},{1,17},{9,25},{17,1},{25,9},{2,18},{10... | collective-permute-start | bytes 393224 | tf_op jit(solution)/shard_map/ppermute | solution.py:537
  10.1 3.2 %collective-permute-done.3 = bf16[2,1,2,128,128]{4,3,2,1,0:T(8,128)(2,1)S(1)} collective-permute-done((bf16[2,1,2,128,128]{4,3,2,1,0:T(8,128)(2,1)S(1)}, bf16[2,1,2,128,128]{4,3,2,1,0:T(8,128)(2,1)S(1)}, u32[]{:S(2)}, u32[]{:S(2)}) %collective-permute-start.3) | collective-permute-done | bytes 131104 | tf_op jit(solution)/shard_map/ppermute | solution.py:537
  13.4 2.1 %collective-permute-start.4 = (bf16[1,2,128,128]{3,2,1,0:T(8,128)(2,1)S(1)}, bf16[1,2,128,128]{3,2,1,0:T(8,128)(2,1)S(1)}, u32[]{:S(2)}, u32[]{:S(2)}) collective-permute-start(bf16[1,2,128,128]{3,2,1,0:T(8,128)(2,1)S(1)} %get-tuple-element.39), channel_id=1, source_target_pairs={{0,1},{1,2},{2,3},{3,4},{4,5},{5,6},{6,7},{7,0},{8,9},{9,10},{10,1... | collective-permute-start | bytes 196616 | tf_op jit(solution)/shard_map/ppermute | solution.py:542
  15.5 3.1 %collective-permute-start.5 = (bf16[1,2,128,128]{3,2,1,0:T(8,128)(2,1)S(1)}, bf16[1,2,128,128]{3,2,1,0:T(8,128)(2,1)S(1)}, u32[]{:S(2)}, u32[]{:S(2)}) collective-permute-start(bf16[1,2,128,128]{3,2,1,0:T(8,128)(2,1)S(1)} %get-tuple-element.38), channel_id=1, source_target_pairs={{0,7},{1,0},{2,1},{3,2},{4,3},{5,4},{6,5},{7,6},{8,15},{9,8},{10,9... | collective-permute-start | bytes 196616 | tf_op jit(solution)/shard_map/ppermute | solution.py:542
  19.0 1.7 %collective-permute-done.4.from_prev = bf16[1,2,128,128]{3,2,1,0:T(8,128)(2,1)S(1)} collective-permute-done((bf16[1,2,128,128]{3,2,1,0:T(8,128)(2,1)S(1)}, bf16[1,2,128,128]{3,2,1,0:T(8,128)(2,1)S(1)}, u32[]{:S(2)}, u32[]{:S(2)}) %collective-permute-start.4) | collective-permute-done | bytes 65568 | tf_op jit(solution)/shard_map/ppermute | solution.py:542
  20.8 0.9 %subgrid.1 = (bf16[2,1,2,128,512]{4,3,2,1,0:T(8,128)(2,1)S(1)}, bf16[2,1,2,128,128]{4,3,2,1,0:T(8,128)(2,1)S(1)}, bf16[1,2,128,128]{3,2,1,0:T(8,128)(2,1)S(1)}, bf16[1,2,128,128]{3,2,1,0:T(8,128)(2,1)S(1)}) custom-call(f32[32,128]{1,0:T(8,128)S(1)} %get-tuple-element.20.turn.after, bf16[2,1,2,128,128]{4,3,2,1,0:T(8,128)(2,1)S(1)} %get-tuple-element.37.kept, ...), custom_call_target="tpu_custom_call" | custom-call | tf_op jit(solution)/shard_map/subgrid/pallas_call | solution.py:660
  21.7 1.5 %collective-permute-start.7 = (bf16[1,2,128,128]{3,2,1,0:T(8,128)(2,1)S(1)}, bf16[1,2,128,128]{3,2,1,0:T(8,128)(2,1)S(1)}, u32[]{:S(2)}, u32[]{:S(2)}) collective-permute-start(bf16[1,2,128,128]{3,2,1,0:T(8,128)(2,1)S(1)} %get-tuple-element.26), channel_id=1, source_target_pairs={{0,1},{1,2},{2,3},{3,4},{4,5},{5,6},{6,7},{7,0},{8,9},{9,10},{10,1... | collective-permute-start | bytes 196616 | tf_op jit(solution)/shard_map/ppermute | solution.py:542
  23.1 3.4 %collective-permute-start.8 = (bf16[1,2,128,128]{3,2,1,0:T(8,128)(2,1)S(1)}, bf16[1,2,128,128]{3,2,1,0:T(8,128)(2,1)S(1)}, u32[]{:S(2)}, u32[]{:S(2)}) collective-permute-start(bf16[1,2,128,128]{3,2,1,0:T(8,128)(2,1)S(1)} %get-tuple-element.27), channel_id=1, source_target_pairs={{0,7},{1,0},{2,1},{3,2},{4,3},{5,4},{6,5},{7,6},{8,15},{9,8},{10,9... | collective-permute-start | bytes 196616 | tf_op jit(solution)/shard_map/ppermute | solution.py:542
  26.6 1.6 %collective-permute-start.11 = (bf16[2,1,2,128,128]{4,3,2,1,0:T(8,128)(2,1)S(1)}, bf16[2,1,2,128,128]{4,3,2,1,0:T(8,128)(2,1)S(1)}, u32[]{:S(2)}, u32[]{:S(2)}) collective-permute-start(bf16[2,1,2,128,128]{4,3,2,1,0:T(8,128)(2,1)S(1)} %get-tuple-element.25.own), channel_id=1, source_target_pairs={{0,16},{8,24},{16,0},{24,8},{1,17},{9,25},{17,1},{25,9},{2,18},{10... | collective-permute-start | bytes 393224 | tf_op jit(solution)/shard_map/ppermute | solution.py:537
  28.2 0.6 %collective-permute-done.7 = bf16[1,2,128,128]{3,2,1,0:T(8,128)(2,1)S(1)} collective-permute-done((bf16[1,2,128,128]{3,2,1,0:T(8,128)(2,1)S(1)}, bf16[1,2,128,128]{3,2,1,0:T(8,128)(2,1)S(1)}, u32[]{:S(2)}, u32[]{:S(2)}) %collective-permute-start.7) | collective-permute-done | bytes 65568 | tf_op jit(solution)/shard_map/ppermute | solution.py:542
  28.8 1.7 %collective-permute-start.9 = (bf16[2,1,2,128,128]{4,3,2,1,0:T(8,128)(2,1)S(1)}, bf16[2,1,2,128,128]{4,3,2,1,0:T(8,128)(2,1)S(1)}, u32[]{:S(2)}, u32[]{:S(2)}) collective-permute-start(bf16[2,1,2,128,128]{4,3,2,1,0:T(8,128)(2,1)S(1)} %pad_maximum_fusion.own_edge), channel_id=1, source_target_pairs={{0,16},{8,24},{16,0},{24,8},{1,17},{9,25},{17,1},{25,9},{2,18},{10... | collective-permute-start | bytes 393224 | tf_op jit(solution)/shard_map/ppermute | solution.py:537
  30.4 0.5 %collective-permute-start.13 = (bf16[2,1,2,128,128]{4,3,2,1,0:T(8,128)(2,1)S(1)}, bf16[2,1,2,128,128]{4,3,2,1,0:T(8,128)(2,1)S(1)}, u32[]{:S(2)}, u32[]{:S(2)}) collective-permute-start(bf16[2,1,2,128,128]{4,3,2,1,0:T(8,128)(2,1)S(1)} %pad_maximum_fusion.own_edge), channel_id=1, source_target_pairs={{0,8},{8,0},{16,24},{24,16},{1,9},{9,1},{17,25},{25,17},{2,10},{10... | collective-permute-start | bytes 393224 | tf_op jit(solution)/shard_map/ppermute | solution.py:537
  30.9 0.6 %collective-permute-done.11.main = bf16[2,1,2,128,128]{4,3,2,1,0:T(8,128)(2,1)S(1)} collective-permute-done((bf16[2,1,2,128,128]{4,3,2,1,0:T(8,128)(2,1)S(1)}, bf16[2,1,2,128,128]{4,3,2,1,0:T(8,128)(2,1)S(1)}, u32[]{:S(2)}, u32[]{:S(2)}) %collective-permute-start.11) | collective-permute-done | bytes 131104 | tf_op jit(solution)/shard_map/ppermute | solution.py:537
  31.5 2.3 %collective-permute-done.9.edge = bf16[2,1,2,128,128]{4,3,2,1,0:T(8,128)(2,1)S(1)} collective-permute-done((bf16[2,1,2,128,128]{4,3,2,1,0:T(8,128)(2,1)S(1)}, bf16[2,1,2,128,128]{4,3,2,1,0:T(8,128)(2,1)S(1)}, u32[]{:S(2)}, u32[]{:S(2)}) %collective-permute-start.9) | collective-permute-done | bytes 131104 | tf_op jit(solution)/shard_map/ppermute | solution.py:537
  33.8 2.1 %zero.1.whole = bf16[2,1,2,512,1024]{4,3,2,1,0:T(8,128)(2,1)} custom-call(f32[32,128]{1,0:T(8,128)S(1)} %get-tuple-element.20.turn.after), custom_call_target="tpu_custom_call" | custom-call | tf_op jit(solution)/shard_map/zero/pallas_call | solution.py:645
  36.0 1.4 %early.1 = (bf16[2,1,2,512,1024]{4,3,2,1,0:T(8,128)(2,1)}, bf16[2,1,2,128,512]{4,3,2,1,0:T(8,128)(2,1)}, f32[2,1,2,128,128]{4,3,2,1,0:T(8,128)S(1)}) custom-call(f32[32,128]{1,0:T(8,128)S(1)} %get-tuple-element.20.turn.after, f32[16,128]{1,0:T(8,128)S(1)} %get-tuple-element.19.edge_turn.after, ...), custom_call_target="tpu_custom_call", output_to_operand_aliasing={{0}: (6, {})} | custom-call | tf_op jit(solution)/shard_map/early/pallas_call | solution.py:698
  37.4 1.2 %window.1 = (bf16[2,1,2,512,1024]{4,3,2,1,0:T(8,128)(2,1)}, f32[2,1,2,128,128]{4,3,2,1,0:T(8,128)S(1)}) custom-call(f32[32,128]{1,0:T(8,128)S(1)} %get-tuple-element.20.turn.after, f32[16,128]{1,0:T(8,128)S(1)} %get-tuple-element.19.edge_turn.after, bf16[2,1,2,128,128]{4,3,2,1,0:T(8,128)(2,1)S(1)} %collective-permute-done.11.main, ...), custom_call_target="tpu_custom_call", output_to_operand_aliasing={{0}: (5, {})} | custom-call | tf_op jit(solution)/shard_map/window/pallas_call | solution.py:713
  38.6 1.2 %middle.1 = (bf16[2,1,2,512,1024]{4,3,2,1,0:T(8,128)(2,1)}, f32[2,1,2,128,128]{4,3,2,1,0:T(8,128)S(1)}) custom-call(f32[32,128]{1,0:T(8,128)S(1)} %get-tuple-element.20.turn.after, f32[16,128]{1,0:T(8,128)S(1)} %get-tuple-element.19.edge_turn.after, bf16[2,1,2,128,128]{4,3,2,1,0:T(8,128)(2,1)S(1)} %collective-permute-done.12.main, ...), custom_call_target="tpu_custom_call", output_to_operand_aliasing={{0}: (5, {})} | custom-call | tf_op jit(solution)/shard_map/middle/pallas_call | solution.py:723
  39.7 0.9 %end.1 = bf16[2,1,2,512,1024]{4,3,2,1,0:T(8,128)(2,1)} custom-call(f32[32,128]{1,0:T(8,128)S(1)} %get-tuple-element.20.turn.after, f32[16,128]{1,0:T(8,128)S(1)} %get-tuple-element.19.edge_turn.after, bf16[2,1,2,128,128]{4,3,2,1,0:T(8,128)(2,1)S(1)} %collective-permute-done.10.edge, ...), custom_call_target="tpu_custom_call", output_to_operand_aliasing={{}: (4, {})} | custom-call | tf_op jit(solution)/shard_map/end/pallas_call | solution.py:733
  (23 shorter events, 0.8 us)
Async XLA Ops:
  2.1 3.7 %collective-permute-start.2 = (bf16[2,2,2,128,128]{4,3,2,1,0:T(8,128)(2,1)S(1)}, bf16[2,2,2,128,128]{4,3,2,1,0:T(8,128)(2,1)S(1)}, u32[]{:S(2)}, u32[]{:S(2)}) collective-permute-start(bf16[2,2,2,128,128]{4,3,2,1,0:T(8,128)(2,1)S(1)} %get-tuple-element.24), channel_id=1, source_target_pairs={{0,8},{8,0},{16,24},{24,16},{1,9},{9,1},{17,25},{25,17},{2,10},{10... | collective-permute-start | bytes 786440 | tf_op jit(solution)/shard_map/ppermute | solution.py:537
  4.1 16.6 %copy-start = (bf16[2,1,128,512]{3,2,1,0:T(8,128)(2,1)S(1)}, bf16[2,1,128,512]{3,2,1,0:T(8,128)(2,1)}, u32[]{:S(2)}) copy-start(bf16[2,1,128,512]{3,2,1,0:T(8,128)(2,1)} %weights.1) | copy-start | bytes 786436
  5.7 3.2 %collective-permute-start = (bf16[2,2,2,128,128]{4,3,2,1,0:T(8,128)(2,1)S(1)}, bf16[2,2,2,128,128]{4,3,2,1,0:T(8,128)(2,1)S(1)}, u32[]{:S(2)}, u32[]{:S(2)}) collective-permute-start(bf16[2,2,2,128,128]{4,3,2,1,0:T(8,128)(2,1)S(1)} %get-tuple-element.22), channel_id=1, source_target_pairs={{0,8},{8,0},{16,24},{24,16},{1,9},{9,1},{17,25},{25,17},{2,10},{10... | collective-permute-start | bytes 786440 | tf_op jit(solution)/shard_map/ppermute | solution.py:537
  5.9 7.4 %collective-permute-start.3 = (bf16[2,1,2,128,128]{4,3,2,1,0:T(8,128)(2,1)S(1)}, bf16[2,1,2,128,128]{4,3,2,1,0:T(8,128)(2,1)S(1)}, u32[]{:S(2)}, u32[]{:S(2)}) collective-permute-start(bf16[2,1,2,128,128]{4,3,2,1,0:T(8,128)(2,1)S(1)} %slice.31), channel_id=1, source_target_pairs={{0,16},{8,24},{16,0},{24,8},{1,17},{9,25},{17,1},{25,9},{2,18},{10... | collective-permute-start | bytes 393224 | tf_op jit(solution)/shard_map/ppermute | solution.py:537
  9.1 9.9 %collective-permute-start.1 = (bf16[2,1,2,128,128]{4,3,2,1,0:T(8,128)(2,1)S(1)}, bf16[2,1,2,128,128]{4,3,2,1,0:T(8,128)(2,1)S(1)}, u32[]{:S(2)}, u32[]{:S(2)}) collective-permute-start(bf16[2,1,2,128,128]{4,3,2,1,0:T(8,128)(2,1)S(1)} %get-tuple-element.36), channel_id=1, source_target_pairs={{0,16},{8,24},{16,0},{24,8},{1,17},{9,25},{17,1},{25,9},{2,18},{10... | collective-permute-start | bytes 393224 | tf_op jit(solution)/shard_map/ppermute | solution.py:537
  13.4 7.4 %collective-permute-start.4 = (bf16[1,2,128,128]{3,2,1,0:T(8,128)(2,1)S(1)}, bf16[1,2,128,128]{3,2,1,0:T(8,128)(2,1)S(1)}, u32[]{:S(2)}, u32[]{:S(2)}) collective-permute-start(bf16[1,2,128,128]{3,2,1,0:T(8,128)(2,1)S(1)} %get-tuple-element.39), channel_id=1, source_target_pairs={{0,1},{1,2},{2,3},{3,4},{4,5},{5,6},{6,7},{7,0},{8,9},{9,10},{10,1... | collective-permute-start | bytes 196616 | tf_op jit(solution)/shard_map/ppermute | solution.py:542
  15.5 5.3 %collective-permute-start.5 = (bf16[1,2,128,128]{3,2,1,0:T(8,128)(2,1)S(1)}, bf16[1,2,128,128]{3,2,1,0:T(8,128)(2,1)S(1)}, u32[]{:S(2)}, u32[]{:S(2)}) collective-permute-start(bf16[1,2,128,128]{3,2,1,0:T(8,128)(2,1)S(1)} %get-tuple-element.38), channel_id=1, source_target_pairs={{0,7},{1,0},{2,1},{3,2},{4,3},{5,4},{6,5},{7,6},{8,15},{9,8},{10,9... | collective-permute-start | bytes 196616 | tf_op jit(solution)/shard_map/ppermute | solution.py:542
  21.7 7.1 %collective-permute-start.7 = (bf16[1,2,128,128]{3,2,1,0:T(8,128)(2,1)S(1)}, bf16[1,2,128,128]{3,2,1,0:T(8,128)(2,1)S(1)}, u32[]{:S(2)}, u32[]{:S(2)}) collective-permute-start(bf16[1,2,128,128]{3,2,1,0:T(8,128)(2,1)S(1)} %get-tuple-element.26), channel_id=1, source_target_pairs={{0,1},{1,2},{2,3},{3,4},{4,5},{5,6},{6,7},{7,0},{8,9},{9,10},{10,1... | collective-permute-start | bytes 196616 | tf_op jit(solution)/shard_map/ppermute | solution.py:542
  23.1 5.6 %collective-permute-start.8 = (bf16[1,2,128,128]{3,2,1,0:T(8,128)(2,1)S(1)}, bf16[1,2,128,128]{3,2,1,0:T(8,128)(2,1)S(1)}, u32[]{:S(2)}, u32[]{:S(2)}) collective-permute-start(bf16[1,2,128,128]{3,2,1,0:T(8,128)(2,1)S(1)} %get-tuple-element.27), channel_id=1, source_target_pairs={{0,7},{1,0},{2,1},{3,2},{4,3},{5,4},{6,5},{7,6},{8,15},{9,8},{10,9... | collective-permute-start | bytes 196616 | tf_op jit(solution)/shard_map/ppermute | solution.py:542
  26.6 5.0 %collective-permute-start.11 = (bf16[2,1,2,128,128]{4,3,2,1,0:T(8,128)(2,1)S(1)}, bf16[2,1,2,128,128]{4,3,2,1,0:T(8,128)(2,1)S(1)}, u32[]{:S(2)}, u32[]{:S(2)}) collective-permute-start(bf16[2,1,2,128,128]{4,3,2,1,0:T(8,128)(2,1)S(1)} %get-tuple-element.25.own), channel_id=1, source_target_pairs={{0,16},{8,24},{16,0},{24,8},{1,17},{9,25},{17,1},{25,9},{2,18},{10... | collective-permute-start | bytes 393224 | tf_op jit(solution)/shard_map/ppermute | solution.py:537
  28.8 5.0 %collective-permute-start.9 = (bf16[2,1,2,128,128]{4,3,2,1,0:T(8,128)(2,1)S(1)}, bf16[2,1,2,128,128]{4,3,2,1,0:T(8,128)(2,1)S(1)}, u32[]{:S(2)}, u32[]{:S(2)}) collective-permute-start(bf16[2,1,2,128,128]{4,3,2,1,0:T(8,128)(2,1)S(1)} %pad_maximum_fusion.own_edge), channel_id=1, source_target_pairs={{0,16},{8,24},{16,0},{24,8},{1,17},{9,25},{17,1},{25,9},{2,18},{10... | collective-permute-start | bytes 393224 | tf_op jit(solution)/shard_map/ppermute | solution.py:537
  30.4 5.5 %collective-permute-start.6 = (bf16[2,1,2,128,128]{4,3,2,1,0:T(8,128)(2,1)S(1)}, bf16[2,1,2,128,128]{4,3,2,1,0:T(8,128)(2,1)S(1)}, u32[]{:S(2)}, u32[]{:S(2)}) collective-permute-start(bf16[2,1,2,128,128]{4,3,2,1,0:T(8,128)(2,1)S(1)} %get-tuple-element.25.own), channel_id=1, source_target_pairs={{0,8},{8,0},{16,24},{24,16},{1,9},{9,1},{17,25},{25,17},{2,10},{10... | collective-permute-start | bytes 393224 | tf_op jit(solution)/shard_map/ppermute | solution.py:537
  30.4 6.9 %collective-permute-start.13 = (bf16[2,1,2,128,128]{4,3,2,1,0:T(8,128)(2,1)S(1)}, bf16[2,1,2,128,128]{4,3,2,1,0:T(8,128)(2,1)S(1)}, u32[]{:S(2)}, u32[]{:S(2)}) collective-permute-start(bf16[2,1,2,128,128]{4,3,2,1,0:T(8,128)(2,1)S(1)} %pad_maximum_fusion.own_edge), channel_id=1, source_target_pairs={{0,8},{8,0},{16,24},{24,16},{1,9},{9,1},{17,25},{25,17},{2,10},{10... | collective-permute-start | bytes 393224 | tf_op jit(solution)/shard_map/ppermute | solution.py:537
  31.5 7.0 %collective-permute-start.12 = (bf16[2,1,2,128,128]{4,3,2,1,0:T(8,128)(2,1)S(1)}, bf16[2,1,2,128,128]{4,3,2,1,0:T(8,128)(2,1)S(1)}, u32[]{:S(2)}, u32[]{:S(2)}) collective-permute-start(bf16[2,1,2,128,128]{4,3,2,1,0:T(8,128)(2,1)S(1)} %collective-permute-done.11.main), channel_id=1, source_target_pairs={{0,8},{8,0},{16,24},{24,16},{1,9},{9,1},{17,25},{25,17},{2,10},{10... | collective-permute-start | bytes 393224 | tf_op jit(solution)/shard_map/ppermute | solution.py:537
  33.8 5.9 %collective-permute-start.10 = (bf16[2,1,2,128,128]{4,3,2,1,0:T(8,128)(2,1)S(1)}, bf16[2,1,2,128,128]{4,3,2,1,0:T(8,128)(2,1)S(1)}, u32[]{:S(2)}, u32[]{:S(2)}) collective-permute-start(bf16[2,1,2,128,128]{4,3,2,1,0:T(8,128)(2,1)S(1)} %collective-permute-done.9.edge), channel_id=1, source_target_pairs={{0,8},{8,0},{16,24},{24,16},{1,9},{9,1},{17,25},{25,17},{2,10},{10... | collective-permute-start | bytes 393224 | tf_op jit(solution)/shard_map/ppermute | solution.py:537

commit v8 on v7

--- a/solution.py
+++ b/solution.py
@@ -93,7 +93,7 @@
     for c in range(cols):
         cosine = turn[c : c + 1, :]
         sine = turn[8 + c : 9 + c, :]
-        for s in order:
+        for i, s in enumerate(order):
             for copy in copies[c, s]:
                 copy.wait()
             rows = rows_of(facet, s, block)
@@ -108,8 +108,8 @@
             real, imag = turned(parts, cosine, sine)
             low = jnp.where(left, real, pltpu.roll(imag, HALF, 1))
             high = jnp.where(left, pltpu.roll(real, HALF, 1), imag)
-            target[0, s // 2, c] = low.astype(BF16)
-            target[1, s // 2, c] = high.astype(BF16)
+            target[0, i, c] = low.astype(BF16)
+            target[1, i, c] = high.astype(BF16)
 
 
 def edge_kernel(
@@ -126,7 +126,7 @@
     for copy in scalars:
         copy.start()
     copies = {}
-    order = range(1, facets, 2)
+    order = range(3, facets, 2)
     for c in range(cols):
         for s in order:
             rows = rows_of(facet, s, block)
@@ -169,7 +169,7 @@
     for copy in scalars:
         copy.start()
     copies = {}
-    order = range(0, facets, 2)
+    order = range(2, facets, 2)
     for c in range(cols):
         for s in order:
             rows = rows_of(facet, s, block)
@@ -191,12 +191,30 @@
     edges_of(keep, buf, copies, edge_turn, order, cols, block, facet)
 
 
-def main_kernel(cols, facets, spectra, turn, after, send, keep, buf, sems):
-    del after
+def main_kernel(
+    cols,
+    facets,
+    spectra,
+    turn,
+    edge_turn,
+    send,
+    keep,
+    near_send,
+    near_keep,
+    buf,
+    sems,
+    edge_buf,
+    edge_sems,
+):
     shard = spectra.shape[4]
     tiles = shard // LANES
     block = XM // facets
     facet = lax.axis_index("facet")
+    near = {}
+    for c in range(cols):
+        for s in range(2):
+            rows = rows_of(facet, s, block)
+            near[c, s] = fetched(spectra, edge_buf, edge_sems, c, s, rows, (0, shard - LANES))
     copies = {}
     first_tiles, _ = places_of(turn, cols)
     for c in range(cols):
@@ -206,6 +224,8 @@
         for s in range(facets):
             rows = rows_of(facet, s, block)
             copies[c, s] = fetched(spectra, buf, sems, c, s, rows, (low, high))
+    edges_of(near_send, edge_buf, near, edge_turn, (1,), cols, block, facet)
+    edges_of(near_keep, edge_buf, near, edge_turn, (0,), cols, block, facet)
     zero = jnp.zeros((1, LANES), F32)
     for c in range(cols):
         tile_at = turn[16 + c : 17 + c, :]
@@ -587,6 +607,8 @@
     )
 
     pieces = jax.ShapeDtypeStruct((2, facets // 2, cols, block, LANES), BF16)
+    fewer = jax.ShapeDtypeStruct((2, facets // 2 - 1, cols, block, LANES), BF16)
+    single = jax.ShapeDtypeStruct((2, 1, cols, block, LANES), BF16)
     tile_pair = pltpu.VMEM((cols, 2, 2, XM, LANES), BF16)
     pair_sems = pltpu.SemaphoreType.DMA((cols, 2, facets))
     whole_scalars = [
@@ -595,7 +617,7 @@
     ]
     edge_send, edge_turn = pl.pallas_call(
         functools.partial(edge_kernel, cols, facets, length),
-        out_shape=(pieces, jax.ShapeDtypeStruct((16, LANES), F32)),
+        out_shape=(fewer, jax.ShapeDtypeStruct((16, LANES), F32)),
         in_specs=[HBM, HBM, HBM],
         out_specs=(VMEM, VMEM),
         scratch_shapes=[tile_pair, pair_sems, *whole_scalars, pltpu.SemaphoreType.DMA((2,))],
@@ -604,7 +626,7 @@
     )(facet_offsets, column_index, facet_spectra)
     edge_keep, turn = pl.pallas_call(
         functools.partial(hold_kernel, cols, facets, length),
-        out_shape=(pieces, jax.ShapeDtypeStruct((32, LANES), F32)),
+        out_shape=(fewer, jax.ShapeDtypeStruct((32, LANES), F32)),
         in_specs=[HBM, HBM, HBM, HBM, VMEM],
         out_specs=(VMEM, VMEM),
         scratch_shapes=[
@@ -617,18 +639,30 @@
         compiler_params=params(12),
         name="hold",
     )(facet_offsets, column_index, places, facet_spectra, edge_turn)
-    pair = reduced(edge_keep, edge_send, facets)
-    edges = added(*pair)
-
-    main_send, main_keep = pl.pallas_call(
+    rest = added(edge_keep, swapped(edge_send, 1))
+    came = []
+    bit = 2
+    while bit < facets:
+        received = swapped(rest[:, 0::2], bit)
+        came.append(received[:, :1])
+        if rest.shape[1] > 1:
+            rest = added(rest[:, 1::2], received[:, 1:])
+        bit *= 2
+
+    main_send, main_keep, near_send, near_keep = pl.pallas_call(
         functools.partial(main_kernel, cols, facets),
-        out_shape=(pieces, pieces),
+        out_shape=(pieces, pieces, single, single),
         in_specs=[HBM, VMEM, VMEM],
-        out_specs=(VMEM, VMEM),
-        scratch_shapes=[tile_pair, pair_sems],
+        out_specs=(VMEM,) * 4,
+        scratch_shapes=[tile_pair, pair_sems, tile_pair, pair_sems],
         compiler_params=params(12),
         name="main",
     )(facet_spectra, turn, edge_turn)
+    came.append(swapped(near_send, 1))
+    total = near_keep.astype(F32)
+    for block_sum in came:
+        total = total + block_sum.astype(F32)
+    edges = total.astype(BF16)
     main_kept, main_received = reduced(main_keep, main_send, facets)
     from_prev = shifted(edges[1], 1)
     from_next = shifted(edges[0], -1)
@@ -678,11 +712,11 @@
     came_prev = shifted(to_next, 1)
     came_next = shifted(to_prev, -1)
     near = swapped(back, 1)
-    rest = gathered(back, facets)
-    far = swapped(rest, 1)
-    came = jnp.stack([came_prev, came_next])
-    near_edge = swapped(came, 1)
-    rest_edge = gathered(came, facets)
+    far_half = gathered(back, facets)
+    far = swapped(far_half, 1)
+    own_edge = jnp.stack([came_prev, came_next])
+    near_edge = swapped(own_edge, 1)
+    rest_edge = gathered(own_edge, facets)
     far_edge = swapped(rest_edge, 1)
     evens = tuple(range(2, facets, 2))
     odds = tuple(range(3, facets, 2))
@@ -694,14 +728,14 @@
         ]
 
     base = jax.ShapeDtypeStruct((2, len(evens), cols, block, LANES), F32)
-    single = jax.ShapeDtypeStruct((2, 1, cols, block, LANES), F32)
+    near_shape = jax.ShapeDtypeStruct((2, 1, cols, block, LANES), F32)
     updates, grids, near_base = pl.pallas_call(
         functools.partial(early_kernel, cols),
-        out_shape=(shape, grid_shape, single),
+        out_shape=(shape, grid_shape, near_shape),
         in_specs=[VMEM] * 6 + [HBM],
         out_specs=(HBM, HBM, VMEM),
         scratch_shapes=[
-            pltpu.VMEM(single.shape, F32),
+            pltpu.VMEM(near_shape.shape, F32),
             *tiles_for(2),
             *tiles_for(1),
             pltpu.SemaphoreType.DMA(()),
@@ -709,7 +743,7 @@
         input_output_aliases={6: 0},
         compiler_params=params(12),
         name="early",
-    )(turn, edge_turn, back, near, came, held, updates)
+    )(turn, edge_turn, back, near, own_edge, held, updates)
     updates, rest_base = pl.pallas_call(
         functools.partial(window_kernel, cols, evens),
         out_shape=(shape, base),
@@ -719,7 +753,7 @@
         input_output_aliases={5: 0},
         compiler_params=params(12),
         name="window",
-    )(turn, edge_turn, rest, near_edge, near_base, updates)
+    )(turn, edge_turn, far_half, near_edge, near_base, updates)
     updates, far_base = pl.pallas_call(
         functools.partial(middle_kernel, cols, odds, evens),
         out_shape=(shape, base),

time: 41 us -> 41 us (level)
    pallas_call x1, Pallas kernels: 1.58 us -> 2 us  [computed(): pl.pallas_call(functools.partial(main_kernel, cols, facets), out_shape=(p...]
    ppermute x10 -> x11, waiting for transfers between devices: 6.06 us -> 6.1 us  [swapped(): return lax.ppermute(block, 'facet', [(i, i ^ bit) for i in range(facets)])]
    ppermute x10 -> x11, starting transfers between devices: 8.49 us -> 8.53 us  [swapped(): return lax.ppermute(block, 'facet', [(i, i ^ bit) for i in range(facets)])]
  transfers between devices with their start and end apart: 14 -> 15, of which waited for: 5 -> 5; matrix products, arithmetic and copies ran while one was open for 1% -> 1% of each run, Pallas kernels for 23% -> 23%
where the time goes in v8:
time: 41 us; the launch traced here: 40.8 us
  starting transfers between devices  18.6 us (45%)
  Pallas kernels  12.7 us (31%)
  waiting for transfers between devices  8.45 us (21%)
  between operations  0.78 us (2%)
    ppermute x4, starting transfers between devices, shifted(): lax.ppermute(block, 'col', [(i, (i + distance) % count) for i in range(co...  10.1 us
    ppermute x11, starting transfers between devices, swapped(): return lax.ppermute(block, 'facet', [(i, i ^ bit) for i in range(facets)])  8.53 us
    ppermute x11, waiting for transfers between devices, swapped(): return lax.ppermute(block, 'facet', [(i, i ^ bit) for i in range(facets)])  6.1 us
    ppermute x4, waiting for transfers between devices, shifted(): lax.ppermute(block, 'col', [(i, (i + distance) % count) for i in range(co...  2.35 us
    pallas_call x1, Pallas kernels, computed(): pl.pallas_call(zero_kernel, out_shape=shape, in_specs=[VMEM], out_specs=H...  2.15 us
    pallas_call x1, Pallas kernels, computed(): pl.pallas_call(functools.partial(main_kernel, cols, facets), out_shape=(p...  2 us
    pallas_call x1, Pallas kernels, computed(): pl.pallas_call(functools.partial(early_kernel, cols), out_shape=(shape, g...  1.39 us
    pallas_call x1, Pallas kernels, computed(): pl.pallas_call(functools.partial(edge_kernel, cols, facets, length), out_...  1.26 us
  transfers between devices with their start and end apart: 15, of which 5 were waited for; matrix products, arithmetic and copies ran while one was open for 1% of the time, Pallas kernels for 23%

profile of v8, /device:TPU:0, one launch (start us, length us, event | category | flops | bytes accessed | tf_op | source)
XLA Modules:
  0.0 40.8 jit_solution(11708279580718547925)
XLA Ops:
  0.6 1.3 %edge.1 = (bf16[2,1,2,128,128]{4,3,2,1,0:T(8,128)(2,1)S(1)}, f32[16,128]{1,0:T(8,128)S(1)}) custom-call(s32[1,2]{1,0:T(1,128)} %offsets.3, s32[2]{0:T(128)} %column.3, bf16[2,1,2,512,1024]{4,3,2,1,0:T(8,128)(2,1)} %spectra.5), custom_call_target="tpu_custom_call" | custom-call | tf_op jit(solution)/shard_map/edge/pallas_call | solution.py:618
  1.9 0.6 %collective-permute-start.2 = (bf16[2,1,2,128,128]{4,3,2,1,0:T(8,128)(2,1)S(1)}, bf16[2,1,2,128,128]{4,3,2,1,0:T(8,128)(2,1)S(1)}, u32[]{:S(2)}, u32[]{:S(2)}) collective-permute-start(bf16[2,1,2,128,128]{4,3,2,1,0:T(8,128)(2,1)S(1)} %get-tuple-element.27), channel_id=1, source_target_pairs={{0,8},{8,0},{16,24},{24,16},{1,9},{9,1},{17,25},{25,17},{2,10},{10... | collective-permute-start | bytes 393224 | tf_op jit(solution)/shard_map/ppermute | solution.py:557
  2.5 1.3 %hold.1 = (bf16[2,1,2,128,128]{4,3,2,1,0:T(8,128)(2,1)S(1)}, f32[32,128]{1,0:T(8,128)S(1)}) custom-call(s32[1,2]{1,0:T(1,128)} %offsets.3, s32[2]{0:T(128)} %column.3, s32[1,2]{1,0:T(1,128)} %bitcast.9, bf16[2,1,2,512,1024]{4,3,2,1,0:T(8,128)(2,1)} %spectra.5, f32[16,128]{1,0:T(8,128)S(1)} %get-tuple-element.21.edge_turn.after), custom_call_target="tpu_custom_call" | custom-call | tf_op jit(solution)/shard_map/hold/pallas_call | solution.py:627
  3.7 2.0 %main.1 = (bf16[2,2,2,128,128]{4,3,2,1,0:T(8,128)(2,1)S(1)}, bf16[2,2,2,128,128]{4,3,2,1,0:T(8,128)(2,1)S(1)}, bf16[2,1,2,128,128]{4,3,2,1,0:T(8,128)(2,1)S(1)}, bf16[2,1,2,128,128]{4,3,2,1,0:T(8,128)(2,1)S(1)}) custom-call(bf16[2,1,2,512,1024]{4,3,2,1,0:T(8,128)(2,1)} %spectra.5, f32[32,128]{1,0:T(8,128)S(1)} %get-tuple-element.22.turn.after, ...), custom_call_target="tpu_custom_call" | custom-call | tf_op jit(solution)/shard_map/main/pallas_call | solution.py:652
  6.4 2.6 %collective-permute-start.3 = (bf16[2,1,2,128,128]{4,3,2,1,0:T(8,128)(2,1)S(1)}, bf16[2,1,2,128,128]{4,3,2,1,0:T(8,128)(2,1)S(1)}, u32[]{:S(2)}, u32[]{:S(2)}) collective-permute-start(bf16[2,1,2,128,128]{4,3,2,1,0:T(8,128)(2,1)S(1)} %add_convert_fusion.2), channel_id=1, source_target_pairs={{0,16},{8,24},{16,0},{24,8},{1,17},{9,25},{17,1},{25,9},{2,18},{10... | collective-permute-start | bytes 393224 | tf_op jit(solution)/shard_map/ppermute | solution.py:557
  9.1 1.0 %collective-permute-start.1 = (bf16[2,1,2,128,128]{4,3,2,1,0:T(8,128)(2,1)S(1)}, bf16[2,1,2,128,128]{4,3,2,1,0:T(8,128)(2,1)S(1)}, u32[]{:S(2)}, u32[]{:S(2)}) collective-permute-start(bf16[2,1,2,128,128]{4,3,2,1,0:T(8,128)(2,1)S(1)} %get-tuple-element.40), channel_id=1, source_target_pairs={{0,16},{8,24},{16,0},{24,8},{1,17},{9,25},{17,1},{25,9},{2,18},{10... | collective-permute-start | bytes 393224 | tf_op jit(solution)/shard_map/ppermute | solution.py:557
  10.1 3.2 %collective-permute-done.3 = bf16[2,1,2,128,128]{4,3,2,1,0:T(8,128)(2,1)S(1)} collective-permute-done((bf16[2,1,2,128,128]{4,3,2,1,0:T(8,128)(2,1)S(1)}, bf16[2,1,2,128,128]{4,3,2,1,0:T(8,128)(2,1)S(1)}, u32[]{:S(2)}, u32[]{:S(2)}) %collective-permute-start.3) | collective-permute-done | bytes 131104 | tf_op jit(solution)/shard_map/ppermute | solution.py:557
  13.4 2.1 %collective-permute-start.5 = (bf16[1,2,128,128]{3,2,1,0:T(8,128)(2,1)S(1)}, bf16[1,2,128,128]{3,2,1,0:T(8,128)(2,1)S(1)}, u32[]{:S(2)}, u32[]{:S(2)}) collective-permute-start(bf16[1,2,128,128]{3,2,1,0:T(8,128)(2,1)S(1)} %get-tuple-element.43), channel_id=1, source_target_pairs={{0,1},{1,2},{2,3},{3,4},{4,5},{5,6},{6,7},{7,0},{8,9},{9,10},{10,1... | collective-permute-start | bytes 196616 | tf_op jit(solution)/shard_map/ppermute | solution.py:562
  15.5 3.1 %collective-permute-start.6 = (bf16[1,2,128,128]{3,2,1,0:T(8,128)(2,1)S(1)}, bf16[1,2,128,128]{3,2,1,0:T(8,128)(2,1)S(1)}, u32[]{:S(2)}, u32[]{:S(2)}) collective-permute-start(bf16[1,2,128,128]{3,2,1,0:T(8,128)(2,1)S(1)} %get-tuple-element.42), channel_id=1, source_target_pairs={{0,7},{1,0},{2,1},{3,2},{4,3},{5,4},{6,5},{7,6},{8,15},{9,8},{10,9... | collective-permute-start | bytes 196616 | tf_op jit(solution)/shard_map/ppermute | solution.py:562
  19.0 1.7 %collective-permute-done.5.from_prev = bf16[1,2,128,128]{3,2,1,0:T(8,128)(2,1)S(1)} collective-permute-done((bf16[1,2,128,128]{3,2,1,0:T(8,128)(2,1)S(1)}, bf16[1,2,128,128]{3,2,1,0:T(8,128)(2,1)S(1)}, u32[]{:S(2)}, u32[]{:S(2)}) %collective-permute-start.5) | collective-permute-done | bytes 65568 | tf_op jit(solution)/shard_map/ppermute | solution.py:562
  20.8 0.9 %subgrid.1 = (bf16[2,1,2,128,512]{4,3,2,1,0:T(8,128)(2,1)S(1)}, bf16[2,1,2,128,128]{4,3,2,1,0:T(8,128)(2,1)S(1)}, bf16[1,2,128,128]{3,2,1,0:T(8,128)(2,1)S(1)}, bf16[1,2,128,128]{3,2,1,0:T(8,128)(2,1)S(1)}) custom-call(f32[32,128]{1,0:T(8,128)S(1)} %get-tuple-element.22.turn.after, bf16[2,1,2,128,128]{4,3,2,1,0:T(8,128)(2,1)S(1)} %get-tuple-element.41.kept, ...), custom_call_target="tpu_custom_call" | custom-call | tf_op jit(solution)/shard_map/subgrid/pallas_call | solution.py:694
  21.7 1.4 %collective-permute-start.8 = (bf16[1,2,128,128]{3,2,1,0:T(8,128)(2,1)S(1)}, bf16[1,2,128,128]{3,2,1,0:T(8,128)(2,1)S(1)}, u32[]{:S(2)}, u32[]{:S(2)}) collective-permute-start(bf16[1,2,128,128]{3,2,1,0:T(8,128)(2,1)S(1)} %get-tuple-element.30), channel_id=1, source_target_pairs={{0,1},{1,2},{2,3},{3,4},{4,5},{5,6},{6,7},{7,0},{8,9},{9,10},{10,1... | collective-permute-start | bytes 196616 | tf_op jit(solution)/shard_map/ppermute | solution.py:562
  23.2 3.5 %collective-permute-start.9 = (bf16[1,2,128,128]{3,2,1,0:T(8,128)(2,1)S(1)}, bf16[1,2,128,128]{3,2,1,0:T(8,128)(2,1)S(1)}, u32[]{:S(2)}, u32[]{:S(2)}) collective-permute-start(bf16[1,2,128,128]{3,2,1,0:T(8,128)(2,1)S(1)} %get-tuple-element.31), channel_id=1, source_target_pairs={{0,7},{1,0},{2,1},{3,2},{4,3},{5,4},{6,5},{7,6},{8,15},{9,8},{10,9... | collective-permute-start | bytes 196616 | tf_op jit(solution)/shard_map/ppermute | solution.py:562
  26.6 1.6 %collective-permute-start.12 = (bf16[2,1,2,128,128]{4,3,2,1,0:T(8,128)(2,1)S(1)}, bf16[2,1,2,128,128]{4,3,2,1,0:T(8,128)(2,1)S(1)}, u32[]{:S(2)}, u32[]{:S(2)}) collective-permute-start(bf16[2,1,2,128,128]{4,3,2,1,0:T(8,128)(2,1)S(1)} %get-tuple-element.29.own), channel_id=1, source_target_pairs={{0,16},{8,24},{16,0},{24,8},{1,17},{9,25},{17,1},{25,9},{2,18},{10... | collective-permute-start | bytes 393224 | tf_op jit(solution)/shard_map/ppermute | solution.py:557
  28.2 0.6 %collective-permute-done.8 = bf16[1,2,128,128]{3,2,1,0:T(8,128)(2,1)S(1)} collective-permute-done((bf16[1,2,128,128]{3,2,1,0:T(8,128)(2,1)S(1)}, bf16[1,2,128,128]{3,2,1,0:T(8,128)(2,1)S(1)}, u32[]{:S(2)}, u32[]{:S(2)}) %collective-permute-start.8) | collective-permute-done | bytes 65568 | tf_op jit(solution)/shard_map/ppermute | solution.py:562
  28.8 1.6 %collective-permute-start.10 = (bf16[2,1,2,128,128]{4,3,2,1,0:T(8,128)(2,1)S(1)}, bf16[2,1,2,128,128]{4,3,2,1,0:T(8,128)(2,1)S(1)}, u32[]{:S(2)}, u32[]{:S(2)}) collective-permute-start(bf16[2,1,2,128,128]{4,3,2,1,0:T(8,128)(2,1)S(1)} %pad_maximum_fusion.own_edge), channel_id=1, source_target_pairs={{0,16},{8,24},{16,0},{24,8},{1,17},{9,25},{17,1},{25,9},{2,18},{10... | collective-permute-start | bytes 393224 | tf_op jit(solution)/shard_map/ppermute | solution.py:557
  30.5 0.5 %collective-permute-start.14 = (bf16[2,1,2,128,128]{4,3,2,1,0:T(8,128)(2,1)S(1)}, bf16[2,1,2,128,128]{4,3,2,1,0:T(8,128)(2,1)S(1)}, u32[]{:S(2)}, u32[]{:S(2)}) collective-permute-start(bf16[2,1,2,128,128]{4,3,2,1,0:T(8,128)(2,1)S(1)} %pad_maximum_fusion.own_edge), channel_id=1, source_target_pairs={{0,8},{8,0},{16,24},{24,16},{1,9},{9,1},{17,25},{25,17},{2,10},{10... | collective-permute-start | bytes 393224 | tf_op jit(solution)/shard_map/ppermute | solution.py:557
  31.0 0.6 %collective-permute-done.12.main = bf16[2,1,2,128,128]{4,3,2,1,0:T(8,128)(2,1)S(1)} collective-permute-done((bf16[2,1,2,128,128]{4,3,2,1,0:T(8,128)(2,1)S(1)}, bf16[2,1,2,128,128]{4,3,2,1,0:T(8,128)(2,1)S(1)}, u32[]{:S(2)}, u32[]{:S(2)}) %collective-permute-start.12) | collective-permute-done | bytes 131104 | tf_op jit(solution)/shard_map/ppermute | solution.py:557
  31.6 2.3 %collective-permute-done.10.edge = bf16[2,1,2,128,128]{4,3,2,1,0:T(8,128)(2,1)S(1)} collective-permute-done((bf16[2,1,2,128,128]{4,3,2,1,0:T(8,128)(2,1)S(1)}, bf16[2,1,2,128,128]{4,3,2,1,0:T(8,128)(2,1)S(1)}, u32[]{:S(2)}, u32[]{:S(2)}) %collective-permute-start.10) | collective-permute-done | bytes 131104 | tf_op jit(solution)/shard_map/ppermute | solution.py:557
  33.9 2.1 %zero.1.whole = bf16[2,1,2,512,1024]{4,3,2,1,0:T(8,128)(2,1)} custom-call(f32[32,128]{1,0:T(8,128)S(1)} %get-tuple-element.22.turn.after), custom_call_target="tpu_custom_call" | custom-call | tf_op jit(solution)/shard_map/zero/pallas_call | solution.py:679
  36.0 1.4 %early.1 = (bf16[2,1,2,512,1024]{4,3,2,1,0:T(8,128)(2,1)}, bf16[2,1,2,128,512]{4,3,2,1,0:T(8,128)(2,1)}, f32[2,1,2,128,128]{4,3,2,1,0:T(8,128)S(1)}) custom-call(f32[32,128]{1,0:T(8,128)S(1)} %get-tuple-element.22.turn.after, f32[16,128]{1,0:T(8,128)S(1)} %get-tuple-element.21.edge_turn.after, ...), custom_call_target="tpu_custom_call", output_to_operand_aliasing={{0}: (6, {})} | custom-call | tf_op jit(solution)/shard_map/early/pallas_call | solution.py:732
  37.4 1.2 %window.1 = (bf16[2,1,2,512,1024]{4,3,2,1,0:T(8,128)(2,1)}, f32[2,1,2,128,128]{4,3,2,1,0:T(8,128)S(1)}) custom-call(f32[32,128]{1,0:T(8,128)S(1)} %get-tuple-element.22.turn.after, f32[16,128]{1,0:T(8,128)S(1)} %get-tuple-element.21.edge_turn.after, bf16[2,1,2,128,128]{4,3,2,1,0:T(8,128)(2,1)S(1)} %collective-permute-done.12.main, ...), custom_call_target="tpu_custom_call", output_to_operand_aliasing={{0}: (5, {})} | custom-call | tf_op jit(solution)/shard_map/window/pallas_call | solution.py:747
  38.6 1.2 %middle.1 = (bf16[2,1,2,512,1024]{4,3,2,1,0:T(8,128)(2,1)}, f32[2,1,2,128,128]{4,3,2,1,0:T(8,128)S(1)}) custom-call(f32[32,128]{1,0:T(8,128)S(1)} %get-tuple-element.22.turn.after, f32[16,128]{1,0:T(8,128)S(1)} %get-tuple-element.21.edge_turn.after, bf16[2,1,2,128,128]{4,3,2,1,0:T(8,128)(2,1)S(1)} %collective-permute-done.13.main, ...), custom_call_target="tpu_custom_call", output_to_operand_aliasing={{0}: (5, {})} | custom-call | tf_op jit(solution)/shard_map/middle/pallas_call | solution.py:757
  39.8 0.9 %end.1 = bf16[2,1,2,512,1024]{4,3,2,1,0:T(8,128)(2,1)} custom-call(f32[32,128]{1,0:T(8,128)S(1)} %get-tuple-element.22.turn.after, f32[16,128]{1,0:T(8,128)S(1)} %get-tuple-element.21.edge_turn.after, bf16[2,1,2,128,128]{4,3,2,1,0:T(8,128)(2,1)S(1)} %collective-permute-done.11.edge, ...), custom_call_target="tpu_custom_call", output_to_operand_aliasing={{}: (4, {})} | custom-call | tf_op jit(solution)/shard_map/end/pallas_call | solution.py:767
  (24 shorter events, 1.2 us)
Async XLA Ops:
  1.9 4.4 %collective-permute-start.2 = (bf16[2,1,2,128,128]{4,3,2,1,0:T(8,128)(2,1)S(1)}, bf16[2,1,2,128,128]{4,3,2,1,0:T(8,128)(2,1)S(1)}, u32[]{:S(2)}, u32[]{:S(2)}) collective-permute-start(bf16[2,1,2,128,128]{4,3,2,1,0:T(8,128)(2,1)S(1)} %get-tuple-element.27), channel_id=1, source_target_pairs={{0,8},{8,0},{16,24},{24,16},{1,9},{9,1},{17,25},{25,17},{2,10},{10... | collective-permute-start | bytes 393224 | tf_op jit(solution)/shard_map/ppermute | solution.py:557
  3.7 17.1 %copy-start = (bf16[2,1,128,512]{3,2,1,0:T(8,128)(2,1)S(1)}, bf16[2,1,128,512]{3,2,1,0:T(8,128)(2,1)}, u32[]{:S(2)}) copy-start(bf16[2,1,128,512]{3,2,1,0:T(8,128)(2,1)} %weights.1) | copy-start | bytes 786436
  5.7 3.2 %collective-permute-start = (bf16[2,2,2,128,128]{4,3,2,1,0:T(8,128)(2,1)S(1)}, bf16[2,2,2,128,128]{4,3,2,1,0:T(8,128)(2,1)S(1)}, u32[]{:S(2)}, u32[]{:S(2)}) collective-permute-start(bf16[2,2,2,128,128]{4,3,2,1,0:T(8,128)(2,1)S(1)} %get-tuple-element.24), channel_id=1, source_target_pairs={{0,8},{8,0},{16,24},{24,16},{1,9},{9,1},{17,25},{25,17},{2,10},{10... | collective-permute-start | bytes 786440 | tf_op jit(solution)/shard_map/ppermute | solution.py:557
  5.8 4.3 %collective-permute-start.4 = (bf16[2,1,2,128,128]{4,3,2,1,0:T(8,128)(2,1)S(1)}, bf16[2,1,2,128,128]{4,3,2,1,0:T(8,128)(2,1)S(1)}, u32[]{:S(2)}, u32[]{:S(2)}) collective-permute-start(bf16[2,1,2,128,128]{4,3,2,1,0:T(8,128)(2,1)S(1)} %get-tuple-element.28), channel_id=1, source_target_pairs={{0,8},{8,0},{16,24},{24,16},{1,9},{9,1},{17,25},{25,17},{2,10},{10... | collective-permute-start | bytes 393224 | tf_op jit(solution)/shard_map/ppermute | solution.py:557
  6.4 7.0 %collective-permute-start.3 = (bf16[2,1,2,128,128]{4,3,2,1,0:T(8,128)(2,1)S(1)}, bf16[2,1,2,128,128]{4,3,2,1,0:T(8,128)(2,1)S(1)}, u32[]{:S(2)}, u32[]{:S(2)}) collective-permute-start(bf16[2,1,2,128,128]{4,3,2,1,0:T(8,128)(2,1)S(1)} %add_convert_fusion.2), channel_id=1, source_target_pairs={{0,16},{8,24},{16,0},{24,8},{1,17},{9,25},{17,1},{25,9},{2,18},{10... | collective-permute-start | bytes 393224 | tf_op jit(solution)/shard_map/ppermute | solution.py:557
  9.1 11.7 %collective-permute-start.1 = (bf16[2,1,2,128,128]{4,3,2,1,0:T(8,128)(2,1)S(1)}, bf16[2,1,2,128,128]{4,3,2,1,0:T(8,128)(2,1)S(1)}, u32[]{:S(2)}, u32[]{:S(2)}) collective-permute-start(bf16[2,1,2,128,128]{4,3,2,1,0:T(8,128)(2,1)S(1)} %get-tuple-element.40), channel_id=1, source_target_pairs={{0,16},{8,24},{16,0},{24,8},{1,17},{9,25},{17,1},{25,9},{2,18},{10... | collective-permute-start | bytes 393224 | tf_op jit(solution)/shard_map/ppermute | solution.py:557
  13.4 7.4 %collective-permute-start.5 = (bf16[1,2,128,128]{3,2,1,0:T(8,128)(2,1)S(1)}, bf16[1,2,128,128]{3,2,1,0:T(8,128)(2,1)S(1)}, u32[]{:S(2)}, u32[]{:S(2)}) collective-permute-start(bf16[1,2,128,128]{3,2,1,0:T(8,128)(2,1)S(1)} %get-tuple-element.43), channel_id=1, source_target_pairs={{0,1},{1,2},{2,3},{3,4},{4,5},{5,6},{6,7},{7,0},{8,9},{9,10},{10,1... | collective-permute-start | bytes 196616 | tf_op jit(solution)/shard_map/ppermute | solution.py:562
  15.5 5.3 %collective-permute-start.6 = (bf16[1,2,128,128]{3,2,1,0:T(8,128)(2,1)S(1)}, bf16[1,2,128,128]{3,2,1,0:T(8,128)(2,1)S(1)}, u32[]{:S(2)}, u32[]{:S(2)}) collective-permute-start(bf16[1,2,128,128]{3,2,1,0:T(8,128)(2,1)S(1)} %get-tuple-element.42), channel_id=1, source_target_pairs={{0,7},{1,0},{2,1},{3,2},{4,3},{5,4},{6,5},{7,6},{8,15},{9,8},{10,9... | collective-permute-start | bytes 196616 | tf_op jit(solution)/shard_map/ppermute | solution.py:562
  21.7 7.1 %collective-permute-start.8 = (bf16[1,2,128,128]{3,2,1,0:T(8,128)(2,1)S(1)}, bf16[1,2,128,128]{3,2,1,0:T(8,128)(2,1)S(1)}, u32[]{:S(2)}, u32[]{:S(2)}) collective-permute-start(bf16[1,2,128,128]{3,2,1,0:T(8,128)(2,1)S(1)} %get-tuple-element.30), channel_id=1, source_target_pairs={{0,1},{1,2},{2,3},{3,4},{4,5},{5,6},{6,7},{7,0},{8,9},{9,10},{10,1... | collective-permute-start | bytes 196616 | tf_op jit(solution)/shard_map/ppermute | solution.py:562
  23.2 5.6 %collective-permute-start.9 = (bf16[1,2,128,128]{3,2,1,0:T(8,128)(2,1)S(1)}, bf16[1,2,128,128]{3,2,1,0:T(8,128)(2,1)S(1)}, u32[]{:S(2)}, u32[]{:S(2)}) collective-permute-start(bf16[1,2,128,128]{3,2,1,0:T(8,128)(2,1)S(1)} %get-tuple-element.31), channel_id=1, source_target_pairs={{0,7},{1,0},{2,1},{3,2},{4,3},{5,4},{6,5},{7,6},{8,15},{9,8},{10,9... | collective-permute-start | bytes 196616 | tf_op jit(solution)/shard_map/ppermute | solution.py:562
  26.6 5.0 %collective-permute-start.12 = (bf16[2,1,2,128,128]{4,3,2,1,0:T(8,128)(2,1)S(1)}, bf16[2,1,2,128,128]{4,3,2,1,0:T(8,128)(2,1)S(1)}, u32[]{:S(2)}, u32[]{:S(2)}) collective-permute-start(bf16[2,1,2,128,128]{4,3,2,1,0:T(8,128)(2,1)S(1)} %get-tuple-element.29.own), channel_id=1, source_target_pairs={{0,16},{8,24},{16,0},{24,8},{1,17},{9,25},{17,1},{25,9},{2,18},{10... | collective-permute-start | bytes 393224 | tf_op jit(solution)/shard_map/ppermute | solution.py:557
  28.8 5.0 %collective-permute-start.10 = (bf16[2,1,2,128,128]{4,3,2,1,0:T(8,128)(2,1)S(1)}, bf16[2,1,2,128,128]{4,3,2,1,0:T(8,128)(2,1)S(1)}, u32[]{:S(2)}, u32[]{:S(2)}) collective-permute-start(bf16[2,1,2,128,128]{4,3,2,1,0:T(8,128)(2,1)S(1)} %pad_maximum_fusion.own_edge), channel_id=1, source_target_pairs={{0,16},{8,24},{16,0},{24,8},{1,17},{9,25},{17,1},{25,9},{2,18},{10... | collective-permute-start | bytes 393224 | tf_op jit(solution)/shard_map/ppermute | solution.py:557
  30.5 5.5 %collective-permute-start.7 = (bf16[2,1,2,128,128]{4,3,2,1,0:T(8,128)(2,1)S(1)}, bf16[2,1,2,128,128]{4,3,2,1,0:T(8,128)(2,1)S(1)}, u32[]{:S(2)}, u32[]{:S(2)}) collective-permute-start(bf16[2,1,2,128,128]{4,3,2,1,0:T(8,128)(2,1)S(1)} %get-tuple-element.29.own), channel_id=1, source_target_pairs={{0,8},{8,0},{16,24},{24,16},{1,9},{9,1},{17,25},{25,17},{2,10},{10... | collective-permute-start | bytes 393224 | tf_op jit(solution)/shard_map/ppermute | solution.py:557
  30.5 6.9 %collective-permute-start.14 = (bf16[2,1,2,128,128]{4,3,2,1,0:T(8,128)(2,1)S(1)}, bf16[2,1,2,128,128]{4,3,2,1,0:T(8,128)(2,1)S(1)}, u32[]{:S(2)}, u32[]{:S(2)}) collective-permute-start(bf16[2,1,2,128,128]{4,3,2,1,0:T(8,128)(2,1)S(1)} %pad_maximum_fusion.own_edge), channel_id=1, source_target_pairs={{0,8},{8,0},{16,24},{24,16},{1,9},{9,1},{17,25},{25,17},{2,10},{10... | collective-permute-start | bytes 393224 | tf_op jit(solution)/shard_map/ppermute | solution.py:557
  31.6 7.0 %collective-permute-start.13 = (bf16[2,1,2,128,128]{4,3,2,1,0:T(8,128)(2,1)S(1)}, bf16[2,1,2,128,128]{4,3,2,1,0:T(8,128)(2,1)S(1)}, u32[]{:S(2)}, u32[]{:S(2)}) collective-permute-start(bf16[2,1,2,128,128]{4,3,2,1,0:T(8,128)(2,1)S(1)} %collective-permute-done.12.main), channel_id=1, source_target_pairs={{0,8},{8,0},{16,24},{24,16},{1,9},{9,1},{17,25},{25,17},{2,10},{10... | collective-permute-start | bytes 393224 | tf_op jit(solution)/shard_map/ppermute | solution.py:557
  33.9 5.9 %collective-permute-start.11 = (bf16[2,1,2,128,128]{4,3,2,1,0:T(8,128)(2,1)S(1)}, bf16[2,1,2,128,128]{4,3,2,1,0:T(8,128)(2,1)S(1)}, u32[]{:S(2)}, u32[]{:S(2)}) collective-permute-start(bf16[2,1,2,128,128]{4,3,2,1,0:T(8,128)(2,1)S(1)} %collective-permute-done.10.edge), channel_id=1, source_target_pairs={{0,8},{8,0},{16,24},{24,16},{1,9},{9,1},{17,25},{25,17},{2,10},{10... | collective-permute-start | bytes 393224 | tf_op jit(solution)/shard_map/ppermute | solution.py:557

commit v9 on v8

--- a/solution.py
+++ b/solution.py
@@ -199,6 +199,8 @@
     edge_turn,
     send,
     keep,
+    main_send,
+    main_keep,
     near_send,
     near_keep,
     buf,
@@ -237,7 +239,10 @@
             for copy in copies[c, s]:
                 copy.wait()
             rows = rows_of(facet, s, block)
-            target = send if s % 2 else keep
+            if s < 2:
+                target, at = (main_send if s else main_keep), 0
+            else:
+                target, at = (send if s % 2 else keep), s // 2 - 1
             parts = [
                 jnp.where(
                     is_low,
@@ -247,8 +252,8 @@
                 for part in range(2)
             ]
             real, imag = turned(parts, cosine, sine)
-            target[0, s // 2, c] = real.astype(BF16)
-            target[1, s // 2, c] = imag.astype(BF16)
+            target[0, at, c] = real.astype(BF16)
+            target[1, at, c] = imag.astype(BF16)
 
 
 def table_kernel(facets, after, table):
@@ -281,16 +286,14 @@
 def zero_kernel(after, out, buf, sems):
     del after
     cols, _, _, height, _ = out.shape
-    block = buf.shape[0]
+    block, width = buf.shape
     buf[...] = jnp.zeros(buf.shape, BF16)
     copies = []
     for c in range(cols):
         for part in range(2):
             for i in range(height // block):
-                rows = pl.ds(i * block, block)
-                copies.append(
-                    pltpu.make_async_copy(buf, out.at[c, 0, part, rows, :], sems.at[c, part, i])
-                )
+                place = out.at[c, 0, part, pl.ds(i * block, block), pl.ds(LANES, width)]
+                copies.append(pltpu.make_async_copy(buf, place, sems.at[c, part, i]))
     for copy in copies:
         copy.start()
     for copy in copies:
@@ -302,6 +305,7 @@
     shard,
     turn,
     kept,
+    near,
     received,
     from_prev,
     from_next,
@@ -325,9 +329,13 @@
         prev = from_prev[0, c].astype(F32)
         nxt = from_next[0, c].astype(F32)
         shift = remainder(LANES - begins[c], LANES)
-        real = kept[0, 0, c].astype(F32) + received[0, 0, c].astype(F32)
+        real, imag = (
+            kept[part, 0, c].astype(F32)
+            + near[part, 0, c].astype(F32)
+            + received[part, 0, c].astype(F32)
+            for part in range(2)
+        )
         real = real + jnp.where(low, pltpu.roll(prev, HALF, 1), jnp.where(high, nxt, zero))
-        imag = kept[1, 0, c].astype(F32) + received[1, 0, c].astype(F32)
         imag = imag + jnp.where(low, prev, jnp.where(high, pltpu.roll(nxt, HALF, 1), zero))
         rows = slice(c * block, (c + 1) * block)
         stack[rows, :WM] = pltpu.roll(real, shift, 1).astype(BF16)
@@ -567,14 +575,16 @@
 
 
 def reduced(kept, sent, facets):
-    received = swapped(sent, 1)
+    rest = added(kept, swapped(sent, 1))
+    came = []
     bit = 2
     while bit < facets:
-        blocks = added(kept, received)
-        kept, sent = blocks[:, 0::2], blocks[:, 1::2]
-        received = swapped(sent, bit)
+        received = swapped(rest[:, 0::2], bit)
+        came.append(received[:, :1])
+        if rest.shape[1] > 1:
+            rest = added(rest[:, 1::2], received[:, 1:])
         bit *= 2
-    return kept, received
+    return came
 
 
 def gathered(blocks, facets):
@@ -606,7 +616,6 @@
         for array in (facet_spectra, facet_offsets, column_index, subgrid_offsets.T)
     )
 
-    pieces = jax.ShapeDtypeStruct((2, facets // 2, cols, block, LANES), BF16)
     fewer = jax.ShapeDtypeStruct((2, facets // 2 - 1, cols, block, LANES), BF16)
     single = jax.ShapeDtypeStruct((2, 1, cols, block, LANES), BF16)
     tile_pair = pltpu.VMEM((cols, 2, 2, XM, LANES), BF16)
@@ -639,21 +648,13 @@
         compiler_params=params(12),
         name="hold",
     )(facet_offsets, column_index, places, facet_spectra, edge_turn)
-    rest = added(edge_keep, swapped(edge_send, 1))
-    came = []
-    bit = 2
-    while bit < facets:
-        received = swapped(rest[:, 0::2], bit)
-        came.append(received[:, :1])
-        if rest.shape[1] > 1:
-            rest = added(rest[:, 1::2], received[:, 1:])
-        bit *= 2
-
-    main_send, main_keep, near_send, near_keep = pl.pallas_call(
+    came = reduced(edge_keep, edge_send, facets)
+
+    main_far, main_rest, main_send, main_keep, near_send, near_keep = pl.pallas_call(
         functools.partial(main_kernel, cols, facets),
-        out_shape=(pieces, pieces, single, single),
+        out_shape=(fewer, fewer, single, single, single, single),
         in_specs=[HBM, VMEM, VMEM],
-        out_specs=(VMEM,) * 4,
+        out_specs=(VMEM,) * 6,
         scratch_shapes=[tile_pair, pair_sems, tile_pair, pair_sems],
         compiler_params=params(12),
         name="main",
@@ -663,7 +664,10 @@
     for block_sum in came:
         total = total + block_sum.astype(F32)
     edges = total.astype(BF16)
-    main_kept, main_received = reduced(main_keep, main_send, facets)
+    *more, main_received = reduced(main_rest, main_far, facets)
+    for block_sum in more:
+        main_keep = added(main_keep, block_sum)
+    main_near = swapped(main_send, 1)
     from_prev = shifted(edges[1], 1)
     from_next = shifted(edges[0], -1)
 
@@ -682,7 +686,7 @@
         in_specs=[VMEM],
         out_specs=HBM,
         scratch_shapes=[
-            pltpu.VMEM((LANES, shard), BF16),
+            pltpu.VMEM((LANES, shard - 2 * LANES), BF16),
             pltpu.SemaphoreType.DMA((cols, 2, XM // LANES)),
         ],
         compiler_params=params(12),
@@ -699,7 +703,7 @@
             edge,
             edge,
         ),
-        in_specs=[VMEM] * 7,
+        in_specs=[VMEM] * 8,
         out_specs=(VMEM, VMEM, VMEM, VMEM),
         scratch_shapes=[
             pltpu.VMEM((cols * block, 2 * WM), BF16),
@@ -707,7 +711,7 @@
         ],
         compiler_params=params(12),
         name="subgrid",
-    )(turn, main_kept, main_received, from_prev, from_next, table, weights)
+    )(turn, main_keep, main_near, main_received, from_prev, from_next, table, weights)
 
     came_prev = shifted(to_next, 1)
     came_next = shifted(to_prev, -1)

time: 41 us -> 41.1 us (level)
    ppermute x11 -> x12, waiting for transfers between devices: 6.1 us -> 6.4 us  [swapped(): return lax.ppermute(block, 'facet', [(i, i ^ bit) for i in range(facets)])]
    ppermute x11 -> x12, starting transfers between devices: 8.53 us -> 8.73 us  [swapped(): return lax.ppermute(block, 'facet', [(i, i ^ bit) for i in range(facets)])]
  transfers between devices with their start and end apart: 15 -> 16, of which waited for: 5 -> 5; matrix products, arithmetic and copies ran while one was open for 1% -> 0% of each run, Pallas kernels for 23% -> 23%
where the time goes in v9:
time: 41.1 us; the launch traced here: 40.8 us
  starting transfers between devices  18.8 us (46%)
  Pallas kernels  12.3 us (30%)
  waiting for transfers between devices  8.72 us (21%)
  between operations  0.79 us (2%)
    ppermute x4, starting transfers between devices, shifted(): lax.ppermute(block, 'col', [(i, (i + distance) % count) for i in range(co...  10.1 us
    ppermute x12, starting transfers between devices, swapped(): return lax.ppermute(block, 'facet', [(i, i ^ bit) for i in range(facets)])  8.73 us
    ppermute x12, waiting for transfers between devices, swapped(): return lax.ppermute(block, 'facet', [(i, i ^ bit) for i in range(facets)])  6.4 us
    ppermute x4, waiting for transfers between devices, shifted(): lax.ppermute(block, 'col', [(i, (i + distance) % count) for i in range(co...  2.32 us
    pallas_call x1, Pallas kernels, computed(): pl.pallas_call(functools.partial(main_kernel, cols, facets), out_shape=(f...  2 us
    pallas_call x1, Pallas kernels, computed(): pl.pallas_call(zero_kernel, out_shape=shape, in_specs=[VMEM], out_specs=H...  1.8 us
    pallas_call x1, Pallas kernels, computed(): pl.pallas_call(functools.partial(early_kernel, cols), out_shape=(shape, g...  1.38 us
    pallas_call x1, Pallas kernels, computed(): pl.pallas_call(functools.partial(edge_kernel, cols, facets, length), out_...  1.26 us
  transfers between devices with their start and end apart: 16, of which 5 were waited for; matrix products, arithmetic and copies ran while one was open for 0% of the time, Pallas kernels for 23%

profile of v9, /device:TPU:0, one launch (start us, length us, event | category | flops | bytes accessed | tf_op | source)
XLA Modules:
  0.0 40.8 jit_solution(8050990853729958016)
XLA Ops:
  0.6 1.3 %edge.1 = (bf16[2,1,2,128,128]{4,3,2,1,0:T(8,128)(2,1)S(1)}, f32[16,128]{1,0:T(8,128)S(1)}) custom-call(s32[1,2]{1,0:T(1,128)} %offsets.3, s32[2]{0:T(128)} %column.3, bf16[2,1,2,512,1024]{4,3,2,1,0:T(8,128)(2,1)} %spectra.5), custom_call_target="tpu_custom_call" | custom-call | tf_op jit(solution)/shard_map/edge/pallas_call | solution.py:627
  1.9 0.6 %collective-permute-start.3 = (bf16[2,1,2,128,128]{4,3,2,1,0:T(8,128)(2,1)S(1)}, bf16[2,1,2,128,128]{4,3,2,1,0:T(8,128)(2,1)S(1)}, u32[]{:S(2)}, u32[]{:S(2)}) collective-permute-start(bf16[2,1,2,128,128]{4,3,2,1,0:T(8,128)(2,1)S(1)} %get-tuple-element.31), channel_id=1, source_target_pairs={{0,8},{8,0},{16,24},{24,16},{1,9},{9,1},{17,25},{25,17},{2,10},{10... | collective-permute-start | bytes 393224 | tf_op jit(solution)/shard_map/ppermute | solution.py:565
  2.5 1.3 %hold.1 = (bf16[2,1,2,128,128]{4,3,2,1,0:T(8,128)(2,1)S(1)}, f32[32,128]{1,0:T(8,128)S(1)}) custom-call(s32[1,2]{1,0:T(1,128)} %offsets.3, s32[2]{0:T(128)} %column.3, s32[1,2]{1,0:T(1,128)} %bitcast.9, bf16[2,1,2,512,1024]{4,3,2,1,0:T(8,128)(2,1)} %spectra.5, f32[16,128]{1,0:T(8,128)S(1)} %get-tuple-element.23.edge_turn.after), custom_call_target="tpu_custom_call" | custom-call | tf_op jit(solution)/shard_map/hold/pallas_call | solution.py:636
  3.7 2.0 %main.1 = (bf16[2,1,2,128,128]{4,3,2,1,0:T(8,128)(2,1)S(1)}, bf16[2,1,2,128,128]{4,3,2,1,0:T(8,128)(2,1)S(1)}, bf16[2,1,2,128,128]{4,3,2,1,0:T(8,128)(2,1)S(1)},...) custom-call(bf16[2,1,2,512,1024]{4,3,2,1,0:T(8,128)(2,1)} %spectra.5, ...), custom_call_target="tpu_custom_call" | custom-call | tf_op jit(solution)/shard_map/main/pallas_call | solution.py:653
  6.4 3.0 %collective-permute-start.4 = (bf16[2,1,2,128,128]{4,3,2,1,0:T(8,128)(2,1)S(1)}, bf16[2,1,2,128,128]{4,3,2,1,0:T(8,128)(2,1)S(1)}, u32[]{:S(2)}, u32[]{:S(2)}) collective-permute-start(bf16[2,1,2,128,128]{4,3,2,1,0:T(8,128)(2,1)S(1)} %add_convert_fusion.1), channel_id=1, source_target_pairs={{0,16},{8,24},{16,0},{24,8},{1,17},{9,25},{17,1},{25,9},{2,18},{10... | collective-permute-start | bytes 393224 | tf_op jit(solution)/shard_map/ppermute | solution.py:565
  9.5 0.8 %collective-permute-start.2 = (bf16[2,1,2,128,128]{4,3,2,1,0:T(8,128)(2,1)S(1)}, bf16[2,1,2,128,128]{4,3,2,1,0:T(8,128)(2,1)S(1)}, u32[]{:S(2)}, u32[]{:S(2)}) collective-permute-start(bf16[2,1,2,128,128]{4,3,2,1,0:T(8,128)(2,1)S(1)} %add_convert_fusion.2), channel_id=1, source_target_pairs={{0,16},{8,24},{16,0},{24,8},{1,17},{9,25},{17,1},{25,9},{2,18},{10... | collective-permute-start | bytes 393224 | tf_op jit(solution)/shard_map/ppermute | solution.py:565
  10.3 3.5 %collective-permute-done.4 = bf16[2,1,2,128,128]{4,3,2,1,0:T(8,128)(2,1)S(1)} collective-permute-done((bf16[2,1,2,128,128]{4,3,2,1,0:T(8,128)(2,1)S(1)}, bf16[2,1,2,128,128]{4,3,2,1,0:T(8,128)(2,1)S(1)}, u32[]{:S(2)}, u32[]{:S(2)}) %collective-permute-start.4) | collective-permute-done | bytes 131104 | tf_op jit(solution)/shard_map/ppermute | solution.py:565
  13.8 2.1 %collective-permute-start.6 = (bf16[1,2,128,128]{3,2,1,0:T(8,128)(2,1)S(1)}, bf16[1,2,128,128]{3,2,1,0:T(8,128)(2,1)S(1)}, u32[]{:S(2)}, u32[]{:S(2)}) collective-permute-start(bf16[1,2,128,128]{3,2,1,0:T(8,128)(2,1)S(1)} %get-tuple-element.45), channel_id=1, source_target_pairs={{0,1},{1,2},{2,3},{3,4},{4,5},{5,6},{6,7},{7,0},{8,9},{9,10},{10,1... | collective-permute-start | bytes 196616 | tf_op jit(solution)/shard_map/ppermute | solution.py:570
  15.9 3.1 %collective-permute-start.7 = (bf16[1,2,128,128]{3,2,1,0:T(8,128)(2,1)S(1)}, bf16[1,2,128,128]{3,2,1,0:T(8,128)(2,1)S(1)}, u32[]{:S(2)}, u32[]{:S(2)}) collective-permute-start(bf16[1,2,128,128]{3,2,1,0:T(8,128)(2,1)S(1)} %get-tuple-element.44), channel_id=1, source_target_pairs={{0,7},{1,0},{2,1},{3,2},{4,3},{5,4},{6,5},{7,6},{8,15},{9,8},{10,9... | collective-permute-start | bytes 196616 | tf_op jit(solution)/shard_map/ppermute | solution.py:570
  19.5 1.7 %collective-permute-done.6.from_prev = bf16[1,2,128,128]{3,2,1,0:T(8,128)(2,1)S(1)} collective-permute-done((bf16[1,2,128,128]{3,2,1,0:T(8,128)(2,1)S(1)}, bf16[1,2,128,128]{3,2,1,0:T(8,128)(2,1)S(1)}, u32[]{:S(2)}, u32[]{:S(2)}) %collective-permute-start.6) | collective-permute-done | bytes 65568 | tf_op jit(solution)/shard_map/ppermute | solution.py:570
  21.2 0.9 %subgrid.1 = (bf16[2,1,2,128,512]{4,3,2,1,0:T(8,128)(2,1)S(1)}, bf16[2,1,2,128,128]{4,3,2,1,0:T(8,128)(2,1)S(1)}, bf16[1,2,128,128]{3,2,1,0:T(8,128)(2,1)S(1)}, bf16[1,2,128,128]{3,2,1,0:T(8,128)(2,1)S(1)}) custom-call(f32[32,128]{1,0:T(8,128)S(1)} %get-tuple-element.24.turn.after, bf16[2,1,2,128,128]{4,3,2,1,0:T(8,128)(2,1)S(1)} %get-tuple-element.25.kept, ...), custom_call_target="tpu_custom_call" | custom-call | tf_op jit(solution)/shard_map/subgrid/pallas_call | solution.py:698
  22.1 1.5 %collective-permute-start.9 = (bf16[1,2,128,128]{3,2,1,0:T(8,128)(2,1)S(1)}, bf16[1,2,128,128]{3,2,1,0:T(8,128)(2,1)S(1)}, u32[]{:S(2)}, u32[]{:S(2)}) collective-permute-start(bf16[1,2,128,128]{3,2,1,0:T(8,128)(2,1)S(1)} %get-tuple-element.34), channel_id=1, source_target_pairs={{0,1},{1,2},{2,3},{3,4},{4,5},{5,6},{6,7},{7,0},{8,9},{9,10},{10,1... | collective-permute-start | bytes 196616 | tf_op jit(solution)/shard_map/ppermute | solution.py:570
  23.6 3.4 %collective-permute-start.10 = (bf16[1,2,128,128]{3,2,1,0:T(8,128)(2,1)S(1)}, bf16[1,2,128,128]{3,2,1,0:T(8,128)(2,1)S(1)}, u32[]{:S(2)}, u32[]{:S(2)}) collective-permute-start(bf16[1,2,128,128]{3,2,1,0:T(8,128)(2,1)S(1)} %get-tuple-element.35), channel_id=1, source_target_pairs={{0,7},{1,0},{2,1},{3,2},{4,3},{5,4},{6,5},{7,6},{8,15},{9,8},{10,9... | collective-permute-start | bytes 196616 | tf_op jit(solution)/shard_map/ppermute | solution.py:570
  27.0 1.6 %collective-permute-start.13 = (bf16[2,1,2,128,128]{4,3,2,1,0:T(8,128)(2,1)S(1)}, bf16[2,1,2,128,128]{4,3,2,1,0:T(8,128)(2,1)S(1)}, u32[]{:S(2)}, u32[]{:S(2)}) collective-permute-start(bf16[2,1,2,128,128]{4,3,2,1,0:T(8,128)(2,1)S(1)} %get-tuple-element.33.own), channel_id=1, source_target_pairs={{0,16},{8,24},{16,0},{24,8},{1,17},{9,25},{17,1},{25,9},{2,18},{10... | collective-permute-start | bytes 393224 | tf_op jit(solution)/shard_map/ppermute | solution.py:565
  28.6 0.6 %collective-permute-done.9 = bf16[1,2,128,128]{3,2,1,0:T(8,128)(2,1)S(1)} collective-permute-done((bf16[1,2,128,128]{3,2,1,0:T(8,128)(2,1)S(1)}, bf16[1,2,128,128]{3,2,1,0:T(8,128)(2,1)S(1)}, u32[]{:S(2)}, u32[]{:S(2)}) %collective-permute-start.9) | collective-permute-done | bytes 65568 | tf_op jit(solution)/shard_map/ppermute | solution.py:570
  29.2 1.7 %collective-permute-start.11 = (bf16[2,1,2,128,128]{4,3,2,1,0:T(8,128)(2,1)S(1)}, bf16[2,1,2,128,128]{4,3,2,1,0:T(8,128)(2,1)S(1)}, u32[]{:S(2)}, u32[]{:S(2)}) collective-permute-start(bf16[2,1,2,128,128]{4,3,2,1,0:T(8,128)(2,1)S(1)} %pad_maximum_fusion.own_edge), channel_id=1, source_target_pairs={{0,16},{8,24},{16,0},{24,8},{1,17},{9,25},{17,1},{25,9},{2,18},{10... | collective-permute-start | bytes 393224 | tf_op jit(solution)/shard_map/ppermute | solution.py:565
  30.9 0.5 %collective-permute-start.15 = (bf16[2,1,2,128,128]{4,3,2,1,0:T(8,128)(2,1)S(1)}, bf16[2,1,2,128,128]{4,3,2,1,0:T(8,128)(2,1)S(1)}, u32[]{:S(2)}, u32[]{:S(2)}) collective-permute-start(bf16[2,1,2,128,128]{4,3,2,1,0:T(8,128)(2,1)S(1)} %pad_maximum_fusion.own_edge), channel_id=1, source_target_pairs={{0,8},{8,0},{16,24},{24,16},{1,9},{9,1},{17,25},{25,17},{2,10},{10... | collective-permute-start | bytes 393224 | tf_op jit(solution)/shard_map/ppermute | solution.py:565
  31.4 0.6 %collective-permute-done.13.main = bf16[2,1,2,128,128]{4,3,2,1,0:T(8,128)(2,1)S(1)} collective-permute-done((bf16[2,1,2,128,128]{4,3,2,1,0:T(8,128)(2,1)S(1)}, bf16[2,1,2,128,128]{4,3,2,1,0:T(8,128)(2,1)S(1)}, u32[]{:S(2)}, u32[]{:S(2)}) %collective-permute-start.13) | collective-permute-done | bytes 131104 | tf_op jit(solution)/shard_map/ppermute | solution.py:565
  32.0 2.3 %collective-permute-done.11.edge = bf16[2,1,2,128,128]{4,3,2,1,0:T(8,128)(2,1)S(1)} collective-permute-done((bf16[2,1,2,128,128]{4,3,2,1,0:T(8,128)(2,1)S(1)}, bf16[2,1,2,128,128]{4,3,2,1,0:T(8,128)(2,1)S(1)}, u32[]{:S(2)}, u32[]{:S(2)}) %collective-permute-start.11) | collective-permute-done | bytes 131104 | tf_op jit(solution)/shard_map/ppermute | solution.py:565
  34.3 1.8 %zero.1.whole = bf16[2,1,2,512,1024]{4,3,2,1,0:T(8,128)(2,1)} custom-call(f32[32,128]{1,0:T(8,128)S(1)} %get-tuple-element.24.turn.after), custom_call_target="tpu_custom_call" | custom-call | tf_op jit(solution)/shard_map/zero/pallas_call | solution.py:683
  36.1 1.4 %early.1 = (bf16[2,1,2,512,1024]{4,3,2,1,0:T(8,128)(2,1)}, bf16[2,1,2,128,512]{4,3,2,1,0:T(8,128)(2,1)}, f32[2,1,2,128,128]{4,3,2,1,0:T(8,128)S(1)}) custom-call(f32[32,128]{1,0:T(8,128)S(1)} %get-tuple-element.24.turn.after, f32[16,128]{1,0:T(8,128)S(1)} %get-tuple-element.23.edge_turn.after, ...), custom_call_target="tpu_custom_call", output_to_operand_aliasing={{0}: (6, {})} | custom-call | tf_op jit(solution)/shard_map/early/pallas_call | solution.py:736
  37.5 1.2 %window.1 = (bf16[2,1,2,512,1024]{4,3,2,1,0:T(8,128)(2,1)}, f32[2,1,2,128,128]{4,3,2,1,0:T(8,128)S(1)}) custom-call(f32[32,128]{1,0:T(8,128)S(1)} %get-tuple-element.24.turn.after, f32[16,128]{1,0:T(8,128)S(1)} %get-tuple-element.23.edge_turn.after, bf16[2,1,2,128,128]{4,3,2,1,0:T(8,128)(2,1)S(1)} %collective-permute-done.13.main, ...), custom_call_target="tpu_custom_call", output_to_operand_aliasing={{0}: (5, {})} | custom-call | tf_op jit(solution)/shard_map/window/pallas_call | solution.py:751
  38.7 1.2 %middle.1 = (bf16[2,1,2,512,1024]{4,3,2,1,0:T(8,128)(2,1)}, f32[2,1,2,128,128]{4,3,2,1,0:T(8,128)S(1)}) custom-call(f32[32,128]{1,0:T(8,128)S(1)} %get-tuple-element.24.turn.after, f32[16,128]{1,0:T(8,128)S(1)} %get-tuple-element.23.edge_turn.after, bf16[2,1,2,128,128]{4,3,2,1,0:T(8,128)(2,1)S(1)} %collective-permute-done.14.main, ...), custom_call_target="tpu_custom_call", output_to_operand_aliasing={{0}: (5, {})} | custom-call | tf_op jit(solution)/shard_map/middle/pallas_call | solution.py:761
  39.9 0.9 %end.1 = bf16[2,1,2,512,1024]{4,3,2,1,0:T(8,128)(2,1)} custom-call(f32[32,128]{1,0:T(8,128)S(1)} %get-tuple-element.24.turn.after, f32[16,128]{1,0:T(8,128)S(1)} %get-tuple-element.23.edge_turn.after, bf16[2,1,2,128,128]{4,3,2,1,0:T(8,128)(2,1)S(1)} %collective-permute-done.12.edge, ...), custom_call_target="tpu_custom_call", output_to_operand_aliasing={{}: (4, {})} | custom-call | tf_op jit(solution)/shard_map/end/pallas_call | solution.py:771
  (25 shorter events, 1.3 us)
Async XLA Ops:
  1.9 4.5 %collective-permute-start.3 = (bf16[2,1,2,128,128]{4,3,2,1,0:T(8,128)(2,1)S(1)}, bf16[2,1,2,128,128]{4,3,2,1,0:T(8,128)(2,1)S(1)}, u32[]{:S(2)}, u32[]{:S(2)}) collective-permute-start(bf16[2,1,2,128,128]{4,3,2,1,0:T(8,128)(2,1)S(1)} %get-tuple-element.31), channel_id=1, source_target_pairs={{0,8},{8,0},{16,24},{24,16},{1,9},{9,1},{17,25},{25,17},{2,10},{10... | collective-permute-start | bytes 393224 | tf_op jit(solution)/shard_map/ppermute | solution.py:565
  3.7 17.5 %copy-start = (bf16[2,1,128,512]{3,2,1,0:T(8,128)(2,1)S(1)}, bf16[2,1,128,512]{3,2,1,0:T(8,128)(2,1)}, u32[]{:S(2)}) copy-start(bf16[2,1,128,512]{3,2,1,0:T(8,128)(2,1)} %weights.1) | copy-start | bytes 786436
  5.7 4.5 %collective-permute-start.5 = (bf16[2,1,2,128,128]{4,3,2,1,0:T(8,128)(2,1)S(1)}, bf16[2,1,2,128,128]{4,3,2,1,0:T(8,128)(2,1)S(1)}, u32[]{:S(2)}, u32[]{:S(2)}) collective-permute-start(bf16[2,1,2,128,128]{4,3,2,1,0:T(8,128)(2,1)S(1)} %get-tuple-element.32), channel_id=1, source_target_pairs={{0,8},{8,0},{16,24},{24,16},{1,9},{9,1},{17,25},{25,17},{2,10},{10... | collective-permute-start | bytes 393224 | tf_op jit(solution)/shard_map/ppermute | solution.py:565
  5.8 3.6 %collective-permute-start.1 = (bf16[2,1,2,128,128]{4,3,2,1,0:T(8,128)(2,1)S(1)}, bf16[2,1,2,128,128]{4,3,2,1,0:T(8,128)(2,1)S(1)}, u32[]{:S(2)}, u32[]{:S(2)}) collective-permute-start(bf16[2,1,2,128,128]{4,3,2,1,0:T(8,128)(2,1)S(1)} %get-tuple-element.28), channel_id=1, source_target_pairs={{0,8},{8,0},{16,24},{24,16},{1,9},{9,1},{17,25},{25,17},{2,10},{10... | collective-permute-start | bytes 393224 | tf_op jit(solution)/shard_map/ppermute | solution.py:565
  6.3 13.2 %collective-permute-start = (bf16[2,1,2,128,128]{4,3,2,1,0:T(8,128)(2,1)S(1)}, bf16[2,1,2,128,128]{4,3,2,1,0:T(8,128)(2,1)S(1)}, u32[]{:S(2)}, u32[]{:S(2)}) collective-permute-start(bf16[2,1,2,128,128]{4,3,2,1,0:T(8,128)(2,1)S(1)} %get-tuple-element.26), channel_id=1, source_target_pairs={{0,8},{8,0},{16,24},{24,16},{1,9},{9,1},{17,25},{25,17},{2,10},{10... | collective-permute-start | bytes 393224 | tf_op jit(solution)/shard_map/ppermute | solution.py:565
  6.4 7.3 %collective-permute-start.4 = (bf16[2,1,2,128,128]{4,3,2,1,0:T(8,128)(2,1)S(1)}, bf16[2,1,2,128,128]{4,3,2,1,0:T(8,128)(2,1)S(1)}, u32[]{:S(2)}, u32[]{:S(2)}) collective-permute-start(bf16[2,1,2,128,128]{4,3,2,1,0:T(8,128)(2,1)S(1)} %add_convert_fusion.1), channel_id=1, source_target_pairs={{0,16},{8,24},{16,0},{24,8},{1,17},{9,25},{17,1},{25,9},{2,18},{10... | collective-permute-start | bytes 393224 | tf_op jit(solution)/shard_map/ppermute | solution.py:565
  9.5 10.0 %collective-permute-start.2 = (bf16[2,1,2,128,128]{4,3,2,1,0:T(8,128)(2,1)S(1)}, bf16[2,1,2,128,128]{4,3,2,1,0:T(8,128)(2,1)S(1)}, u32[]{:S(2)}, u32[]{:S(2)}) collective-permute-start(bf16[2,1,2,128,128]{4,3,2,1,0:T(8,128)(2,1)S(1)} %add_convert_fusion.2), channel_id=1, source_target_pairs={{0,16},{8,24},{16,0},{24,8},{1,17},{9,25},{17,1},{25,9},{2,18},{10... | collective-permute-start | bytes 393224 | tf_op jit(solution)/shard_map/ppermute | solution.py:565
  13.8 7.4 %collective-permute-start.6 = (bf16[1,2,128,128]{3,2,1,0:T(8,128)(2,1)S(1)}, bf16[1,2,128,128]{3,2,1,0:T(8,128)(2,1)S(1)}, u32[]{:S(2)}, u32[]{:S(2)}) collective-permute-start(bf16[1,2,128,128]{3,2,1,0:T(8,128)(2,1)S(1)} %get-tuple-element.45), channel_id=1, source_target_pairs={{0,1},{1,2},{2,3},{3,4},{4,5},{5,6},{6,7},{7,0},{8,9},{9,10},{10,1... | collective-permute-start | bytes 196616 | tf_op jit(solution)/shard_map/ppermute | solution.py:570
  15.9 5.3 %collective-permute-start.7 = (bf16[1,2,128,128]{3,2,1,0:T(8,128)(2,1)S(1)}, bf16[1,2,128,128]{3,2,1,0:T(8,128)(2,1)S(1)}, u32[]{:S(2)}, u32[]{:S(2)}) collective-permute-start(bf16[1,2,128,128]{3,2,1,0:T(8,128)(2,1)S(1)} %get-tuple-element.44), channel_id=1, source_target_pairs={{0,7},{1,0},{2,1},{3,2},{4,3},{5,4},{6,5},{7,6},{8,15},{9,8},{10,9... | collective-permute-start | bytes 196616 | tf_op jit(solution)/shard_map/ppermute | solution.py:570
  22.1 7.1 %collective-permute-start.9 = (bf16[1,2,128,128]{3,2,1,0:T(8,128)(2,1)S(1)}, bf16[1,2,128,128]{3,2,1,0:T(8,128)(2,1)S(1)}, u32[]{:S(2)}, u32[]{:S(2)}) collective-permute-start(bf16[1,2,128,128]{3,2,1,0:T(8,128)(2,1)S(1)} %get-tuple-element.34), channel_id=1, source_target_pairs={{0,1},{1,2},{2,3},{3,4},{4,5},{5,6},{6,7},{7,0},{8,9},{9,10},{10,1... | collective-permute-start | bytes 196616 | tf_op jit(solution)/shard_map/ppermute | solution.py:570
  23.6 5.6 %collective-permute-start.10 = (bf16[1,2,128,128]{3,2,1,0:T(8,128)(2,1)S(1)}, bf16[1,2,128,128]{3,2,1,0:T(8,128)(2,1)S(1)}, u32[]{:S(2)}, u32[]{:S(2)}) collective-permute-start(bf16[1,2,128,128]{3,2,1,0:T(8,128)(2,1)S(1)} %get-tuple-element.35), channel_id=1, source_target_pairs={{0,7},{1,0},{2,1},{3,2},{4,3},{5,4},{6,5},{7,6},{8,15},{9,8},{10,9... | collective-permute-start | bytes 196616 | tf_op jit(solution)/shard_map/ppermute | solution.py:570
  27.0 5.0 %collective-permute-start.13 = (bf16[2,1,2,128,128]{4,3,2,1,0:T(8,128)(2,1)S(1)}, bf16[2,1,2,128,128]{4,3,2,1,0:T(8,128)(2,1)S(1)}, u32[]{:S(2)}, u32[]{:S(2)}) collective-permute-start(bf16[2,1,2,128,128]{4,3,2,1,0:T(8,128)(2,1)S(1)} %get-tuple-element.33.own), channel_id=1, source_target_pairs={{0,16},{8,24},{16,0},{24,8},{1,17},{9,25},{17,1},{25,9},{2,18},{10... | collective-permute-start | bytes 393224 | tf_op jit(solution)/shard_map/ppermute | solution.py:565
  29.2 5.0 %collective-permute-start.11 = (bf16[2,1,2,128,128]{4,3,2,1,0:T(8,128)(2,1)S(1)}, bf16[2,1,2,128,128]{4,3,2,1,0:T(8,128)(2,1)S(1)}, u32[]{:S(2)}, u32[]{:S(2)}) collective-permute-start(bf16[2,1,2,128,128]{4,3,2,1,0:T(8,128)(2,1)S(1)} %pad_maximum_fusion.own_edge), channel_id=1, source_target_pairs={{0,16},{8,24},{16,0},{24,8},{1,17},{9,25},{17,1},{25,9},{2,18},{10... | collective-permute-start | bytes 393224 | tf_op jit(solution)/shard_map/ppermute | solution.py:565
  30.9 5.2 %collective-permute-start.8 = (bf16[2,1,2,128,128]{4,3,2,1,0:T(8,128)(2,1)S(1)}, bf16[2,1,2,128,128]{4,3,2,1,0:T(8,128)(2,1)S(1)}, u32[]{:S(2)}, u32[]{:S(2)}) collective-permute-start(bf16[2,1,2,128,128]{4,3,2,1,0:T(8,128)(2,1)S(1)} %get-tuple-element.33.own), channel_id=1, source_target_pairs={{0,8},{8,0},{16,24},{24,16},{1,9},{9,1},{17,25},{25,17},{2,10},{10... | collective-permute-start | bytes 393224 | tf_op jit(solution)/shard_map/ppermute | solution.py:565
  30.9 6.6 %collective-permute-start.15 = (bf16[2,1,2,128,128]{4,3,2,1,0:T(8,128)(2,1)S(1)}, bf16[2,1,2,128,128]{4,3,2,1,0:T(8,128)(2,1)S(1)}, u32[]{:S(2)}, u32[]{:S(2)}) collective-permute-start(bf16[2,1,2,128,128]{4,3,2,1,0:T(8,128)(2,1)S(1)} %pad_maximum_fusion.own_edge), channel_id=1, source_target_pairs={{0,8},{8,0},{16,24},{24,16},{1,9},{9,1},{17,25},{25,17},{2,10},{10... | collective-permute-start | bytes 393224 | tf_op jit(solution)/shard_map/ppermute | solution.py:565
  32.0 6.7 %collective-permute-start.14 = (bf16[2,1,2,128,128]{4,3,2,1,0:T(8,128)(2,1)S(1)}, bf16[2,1,2,128,128]{4,3,2,1,0:T(8,128)(2,1)S(1)}, u32[]{:S(2)}, u32[]{:S(2)}) collective-permute-start(bf16[2,1,2,128,128]{4,3,2,1,0:T(8,128)(2,1)S(1)} %collective-permute-done.13.main), channel_id=1, source_target_pairs={{0,8},{8,0},{16,24},{24,16},{1,9},{9,1},{17,25},{25,17},{2,10},{10... | collective-permute-start | bytes 393224 | tf_op jit(solution)/shard_map/ppermute | solution.py:565
  34.3 5.6 %collective-permute-start.12 = (bf16[2,1,2,128,128]{4,3,2,1,0:T(8,128)(2,1)S(1)}, bf16[2,1,2,128,128]{4,3,2,1,0:T(8,128)(2,1)S(1)}, u32[]{:S(2)}, u32[]{:S(2)}) collective-permute-start(bf16[2,1,2,128,128]{4,3,2,1,0:T(8,128)(2,1)S(1)} %collective-permute-done.11.edge), channel_id=1, source_target_pairs={{0,8},{8,0},{16,24},{24,16},{1,9},{9,1},{17,25},{25,17},{2,10},{10... | collective-permute-start | bytes 393224 | tf_op jit(solution)/shard_map/ppermute | solution.py:565

commit v10 on v9

--- a/solution.py
+++ b/solution.py
@@ -434,16 +434,14 @@
                 real * edge_cosine - imag * edge_sine,
                 imag * edge_cosine + real * edge_sine,
             )
-            for part in range(2):
-                value = base[part, i, c]
-                end = ends[part]
-                buf[c, 0, part, i] = (
-                    jnp.where(left, end, zero) + jnp.where(in_first, value, zero)
-                ).astype(BF16)
-                buf[c, 1, part, i] = (
-                    jnp.where(left, zero, end) + jnp.where(in_last, value, zero)
-                ).astype(BF16)
             for side, start in enumerate((0, shard - LANES)):
+                keep = left if side == 0 else jnp.logical_not(left)
+                inside = in_last if side else in_first
+                for part in range(2):
+                    buf[c, side, part, i] = (
+                        jnp.where(keep, ends[part], zero)
+                        + jnp.where(inside, base[part, i, c], zero)
+                    ).astype(BF16)
                 copy = pltpu.make_async_copy(
                     buf.at[c, side, :, i],
                     out.at[c, 0, :, rows, pl.ds(start, LANES)],

time: 41.1 us -> 41.1 us (level)
  no operation moved by 1% of the time
where the time goes in v10:
time: 41.1 us; the launch traced here: 40.8 us
  starting transfers between devices  18.8 us (46%)
  Pallas kernels  12.3 us (30%)
  waiting for transfers between devices  8.72 us (21%)
  between operations  0.79 us (2%)
    ppermute x4, starting transfers between devices, shifted(): lax.ppermute(block, 'col', [(i, (i + distance) % count) for i in range(co...  10.1 us
    ppermute x12, starting transfers between devices, swapped(): return lax.ppermute(block, 'facet', [(i, i ^ bit) for i in range(facets)])  8.73 us
    ppermute x12, waiting for transfers between devices, swapped(): return lax.ppermute(block, 'facet', [(i, i ^ bit) for i in range(facets)])  6.4 us
    ppermute x4, waiting for transfers between devices, shifted(): lax.ppermute(block, 'col', [(i, (i + distance) % count) for i in range(co...  2.32 us
    pallas_call x1, Pallas kernels, computed(): pl.pallas_call(functools.partial(main_kernel, cols, facets), out_shape=(f...  2 us
    pallas_call x1, Pallas kernels, computed(): pl.pallas_call(zero_kernel, out_shape=shape, in_specs=[VMEM], out_specs=H...  1.8 us
    pallas_call x1, Pallas kernels, computed(): pl.pallas_call(functools.partial(early_kernel, cols), out_shape=(shape, g...  1.4 us
    pallas_call x1, Pallas kernels, computed(): pl.pallas_call(functools.partial(edge_kernel, cols, facets, length), out_...  1.26 us
  transfers between devices with their start and end apart: 16, of which 5 were waited for; matrix products, arithmetic and copies ran while one was open for 0% of the time, Pallas kernels for 23%

profile of v10, /device:TPU:0, one launch (start us, length us, event | category | flops | bytes accessed | tf_op | source)
XLA Modules:
  0.0 40.8 jit_solution(3470594566198865961)
XLA Ops:
  0.6 1.3 %edge.1 = (bf16[2,1,2,128,128]{4,3,2,1,0:T(8,128)(2,1)S(1)}, f32[16,128]{1,0:T(8,128)S(1)}) custom-call(s32[1,2]{1,0:T(1,128)} %offsets.3, s32[2]{0:T(128)} %column.3, bf16[2,1,2,512,1024]{4,3,2,1,0:T(8,128)(2,1)} %spectra.5), custom_call_target="tpu_custom_call" | custom-call | tf_op jit(solution)/shard_map/edge/pallas_call | solution.py:625
  1.9 0.6 %collective-permute-start.3 = (bf16[2,1,2,128,128]{4,3,2,1,0:T(8,128)(2,1)S(1)}, bf16[2,1,2,128,128]{4,3,2,1,0:T(8,128)(2,1)S(1)}, u32[]{:S(2)}, u32[]{:S(2)}) collective-permute-start(bf16[2,1,2,128,128]{4,3,2,1,0:T(8,128)(2,1)S(1)} %get-tuple-element.31), channel_id=1, source_target_pairs={{0,8},{8,0},{16,24},{24,16},{1,9},{9,1},{17,25},{25,17},{2,10},{10... | collective-permute-start | bytes 393224 | tf_op jit(solution)/shard_map/ppermute | solution.py:563
  2.5 1.3 %hold.1 = (bf16[2,1,2,128,128]{4,3,2,1,0:T(8,128)(2,1)S(1)}, f32[32,128]{1,0:T(8,128)S(1)}) custom-call(s32[1,2]{1,0:T(1,128)} %offsets.3, s32[2]{0:T(128)} %column.3, s32[1,2]{1,0:T(1,128)} %bitcast.9, bf16[2,1,2,512,1024]{4,3,2,1,0:T(8,128)(2,1)} %spectra.5, f32[16,128]{1,0:T(8,128)S(1)} %get-tuple-element.23.edge_turn.after), custom_call_target="tpu_custom_call" | custom-call | tf_op jit(solution)/shard_map/hold/pallas_call | solution.py:634
  3.7 2.0 %main.1 = (bf16[2,1,2,128,128]{4,3,2,1,0:T(8,128)(2,1)S(1)}, bf16[2,1,2,128,128]{4,3,2,1,0:T(8,128)(2,1)S(1)}, bf16[2,1,2,128,128]{4,3,2,1,0:T(8,128)(2,1)S(1)},...) custom-call(bf16[2,1,2,512,1024]{4,3,2,1,0:T(8,128)(2,1)} %spectra.5, ...), custom_call_target="tpu_custom_call" | custom-call | tf_op jit(solution)/shard_map/main/pallas_call | solution.py:651
  6.4 3.0 %collective-permute-start.4 = (bf16[2,1,2,128,128]{4,3,2,1,0:T(8,128)(2,1)S(1)}, bf16[2,1,2,128,128]{4,3,2,1,0:T(8,128)(2,1)S(1)}, u32[]{:S(2)}, u32[]{:S(2)}) collective-permute-start(bf16[2,1,2,128,128]{4,3,2,1,0:T(8,128)(2,1)S(1)} %add_convert_fusion.1), channel_id=1, source_target_pairs={{0,16},{8,24},{16,0},{24,8},{1,17},{9,25},{17,1},{25,9},{2,18},{10... | collective-permute-start | bytes 393224 | tf_op jit(solution)/shard_map/ppermute | solution.py:563
  9.5 0.8 %collective-permute-start.2 = (bf16[2,1,2,128,128]{4,3,2,1,0:T(8,128)(2,1)S(1)}, bf16[2,1,2,128,128]{4,3,2,1,0:T(8,128)(2,1)S(1)}, u32[]{:S(2)}, u32[]{:S(2)}) collective-permute-start(bf16[2,1,2,128,128]{4,3,2,1,0:T(8,128)(2,1)S(1)} %add_convert_fusion.2), channel_id=1, source_target_pairs={{0,16},{8,24},{16,0},{24,8},{1,17},{9,25},{17,1},{25,9},{2,18},{10... | collective-permute-start | bytes 393224 | tf_op jit(solution)/shard_map/ppermute | solution.py:563
  10.3 3.5 %collective-permute-done.4 = bf16[2,1,2,128,128]{4,3,2,1,0:T(8,128)(2,1)S(1)} collective-permute-done((bf16[2,1,2,128,128]{4,3,2,1,0:T(8,128)(2,1)S(1)}, bf16[2,1,2,128,128]{4,3,2,1,0:T(8,128)(2,1)S(1)}, u32[]{:S(2)}, u32[]{:S(2)}) %collective-permute-start.4) | collective-permute-done | bytes 131104 | tf_op jit(solution)/shard_map/ppermute | solution.py:563
  13.8 2.1 %collective-permute-start.6 = (bf16[1,2,128,128]{3,2,1,0:T(8,128)(2,1)S(1)}, bf16[1,2,128,128]{3,2,1,0:T(8,128)(2,1)S(1)}, u32[]{:S(2)}, u32[]{:S(2)}) collective-permute-start(bf16[1,2,128,128]{3,2,1,0:T(8,128)(2,1)S(1)} %get-tuple-element.45), channel_id=1, source_target_pairs={{0,1},{1,2},{2,3},{3,4},{4,5},{5,6},{6,7},{7,0},{8,9},{9,10},{10,1... | collective-permute-start | bytes 196616 | tf_op jit(solution)/shard_map/ppermute | solution.py:568
  15.9 3.1 %collective-permute-start.7 = (bf16[1,2,128,128]{3,2,1,0:T(8,128)(2,1)S(1)}, bf16[1,2,128,128]{3,2,1,0:T(8,128)(2,1)S(1)}, u32[]{:S(2)}, u32[]{:S(2)}) collective-permute-start(bf16[1,2,128,128]{3,2,1,0:T(8,128)(2,1)S(1)} %get-tuple-element.44), channel_id=1, source_target_pairs={{0,7},{1,0},{2,1},{3,2},{4,3},{5,4},{6,5},{7,6},{8,15},{9,8},{10,9... | collective-permute-start | bytes 196616 | tf_op jit(solution)/shard_map/ppermute | solution.py:568
  19.5 1.7 %collective-permute-done.6.from_prev = bf16[1,2,128,128]{3,2,1,0:T(8,128)(2,1)S(1)} collective-permute-done((bf16[1,2,128,128]{3,2,1,0:T(8,128)(2,1)S(1)}, bf16[1,2,128,128]{3,2,1,0:T(8,128)(2,1)S(1)}, u32[]{:S(2)}, u32[]{:S(2)}) %collective-permute-start.6) | collective-permute-done | bytes 65568 | tf_op jit(solution)/shard_map/ppermute | solution.py:568
  21.2 0.9 %subgrid.1 = (bf16[2,1,2,128,512]{4,3,2,1,0:T(8,128)(2,1)S(1)}, bf16[2,1,2,128,128]{4,3,2,1,0:T(8,128)(2,1)S(1)}, bf16[1,2,128,128]{3,2,1,0:T(8,128)(2,1)S(1)}, bf16[1,2,128,128]{3,2,1,0:T(8,128)(2,1)S(1)}) custom-call(f32[32,128]{1,0:T(8,128)S(1)} %get-tuple-element.24.turn.after, bf16[2,1,2,128,128]{4,3,2,1,0:T(8,128)(2,1)S(1)} %get-tuple-element.25.kept, ...), custom_call_target="tpu_custom_call" | custom-call | tf_op jit(solution)/shard_map/subgrid/pallas_call | solution.py:696
  22.1 1.5 %collective-permute-start.9 = (bf16[1,2,128,128]{3,2,1,0:T(8,128)(2,1)S(1)}, bf16[1,2,128,128]{3,2,1,0:T(8,128)(2,1)S(1)}, u32[]{:S(2)}, u32[]{:S(2)}) collective-permute-start(bf16[1,2,128,128]{3,2,1,0:T(8,128)(2,1)S(1)} %get-tuple-element.34), channel_id=1, source_target_pairs={{0,1},{1,2},{2,3},{3,4},{4,5},{5,6},{6,7},{7,0},{8,9},{9,10},{10,1... | collective-permute-start | bytes 196616 | tf_op jit(solution)/shard_map/ppermute | solution.py:568
  23.6 3.4 %collective-permute-start.10 = (bf16[1,2,128,128]{3,2,1,0:T(8,128)(2,1)S(1)}, bf16[1,2,128,128]{3,2,1,0:T(8,128)(2,1)S(1)}, u32[]{:S(2)}, u32[]{:S(2)}) collective-permute-start(bf16[1,2,128,128]{3,2,1,0:T(8,128)(2,1)S(1)} %get-tuple-element.35), channel_id=1, source_target_pairs={{0,7},{1,0},{2,1},{3,2},{4,3},{5,4},{6,5},{7,6},{8,15},{9,8},{10,9... | collective-permute-start | bytes 196616 | tf_op jit(solution)/shard_map/ppermute | solution.py:568
  27.0 1.6 %collective-permute-start.13 = (bf16[2,1,2,128,128]{4,3,2,1,0:T(8,128)(2,1)S(1)}, bf16[2,1,2,128,128]{4,3,2,1,0:T(8,128)(2,1)S(1)}, u32[]{:S(2)}, u32[]{:S(2)}) collective-permute-start(bf16[2,1,2,128,128]{4,3,2,1,0:T(8,128)(2,1)S(1)} %get-tuple-element.33.own), channel_id=1, source_target_pairs={{0,16},{8,24},{16,0},{24,8},{1,17},{9,25},{17,1},{25,9},{2,18},{10... | collective-permute-start | bytes 393224 | tf_op jit(solution)/shard_map/ppermute | solution.py:563
  28.6 0.6 %collective-permute-done.9 = bf16[1,2,128,128]{3,2,1,0:T(8,128)(2,1)S(1)} collective-permute-done((bf16[1,2,128,128]{3,2,1,0:T(8,128)(2,1)S(1)}, bf16[1,2,128,128]{3,2,1,0:T(8,128)(2,1)S(1)}, u32[]{:S(2)}, u32[]{:S(2)}) %collective-permute-start.9) | collective-permute-done | bytes 65568 | tf_op jit(solution)/shard_map/ppermute | solution.py:568
  29.2 1.7 %collective-permute-start.11 = (bf16[2,1,2,128,128]{4,3,2,1,0:T(8,128)(2,1)S(1)}, bf16[2,1,2,128,128]{4,3,2,1,0:T(8,128)(2,1)S(1)}, u32[]{:S(2)}, u32[]{:S(2)}) collective-permute-start(bf16[2,1,2,128,128]{4,3,2,1,0:T(8,128)(2,1)S(1)} %pad_maximum_fusion.own_edge), channel_id=1, source_target_pairs={{0,16},{8,24},{16,0},{24,8},{1,17},{9,25},{17,1},{25,9},{2,18},{10... | collective-permute-start | bytes 393224 | tf_op jit(solution)/shard_map/ppermute | solution.py:563
  30.9 0.5 %collective-permute-start.15 = (bf16[2,1,2,128,128]{4,3,2,1,0:T(8,128)(2,1)S(1)}, bf16[2,1,2,128,128]{4,3,2,1,0:T(8,128)(2,1)S(1)}, u32[]{:S(2)}, u32[]{:S(2)}) collective-permute-start(bf16[2,1,2,128,128]{4,3,2,1,0:T(8,128)(2,1)S(1)} %pad_maximum_fusion.own_edge), channel_id=1, source_target_pairs={{0,8},{8,0},{16,24},{24,16},{1,9},{9,1},{17,25},{25,17},{2,10},{10... | collective-permute-start | bytes 393224 | tf_op jit(solution)/shard_map/ppermute | solution.py:563
  31.4 0.6 %collective-permute-done.13.main = bf16[2,1,2,128,128]{4,3,2,1,0:T(8,128)(2,1)S(1)} collective-permute-done((bf16[2,1,2,128,128]{4,3,2,1,0:T(8,128)(2,1)S(1)}, bf16[2,1,2,128,128]{4,3,2,1,0:T(8,128)(2,1)S(1)}, u32[]{:S(2)}, u32[]{:S(2)}) %collective-permute-start.13) | collective-permute-done | bytes 131104 | tf_op jit(solution)/shard_map/ppermute | solution.py:563
  32.0 2.3 %collective-permute-done.11.edge = bf16[2,1,2,128,128]{4,3,2,1,0:T(8,128)(2,1)S(1)} collective-permute-done((bf16[2,1,2,128,128]{4,3,2,1,0:T(8,128)(2,1)S(1)}, bf16[2,1,2,128,128]{4,3,2,1,0:T(8,128)(2,1)S(1)}, u32[]{:S(2)}, u32[]{:S(2)}) %collective-permute-start.11) | collective-permute-done | bytes 131104 | tf_op jit(solution)/shard_map/ppermute | solution.py:563
  34.3 1.8 %zero.1.whole = bf16[2,1,2,512,1024]{4,3,2,1,0:T(8,128)(2,1)} custom-call(f32[32,128]{1,0:T(8,128)S(1)} %get-tuple-element.24.turn.after), custom_call_target="tpu_custom_call" | custom-call | tf_op jit(solution)/shard_map/zero/pallas_call | solution.py:681
  36.1 1.4 %early.1 = (bf16[2,1,2,512,1024]{4,3,2,1,0:T(8,128)(2,1)}, bf16[2,1,2,128,512]{4,3,2,1,0:T(8,128)(2,1)}, f32[2,1,2,128,128]{4,3,2,1,0:T(8,128)S(1)}) custom-call(f32[32,128]{1,0:T(8,128)S(1)} %get-tuple-element.24.turn.after, f32[16,128]{1,0:T(8,128)S(1)} %get-tuple-element.23.edge_turn.after, ...), custom_call_target="tpu_custom_call", output_to_operand_aliasing={{0}: (6, {})} | custom-call | tf_op jit(solution)/shard_map/early/pallas_call | solution.py:734
  37.5 1.2 %window.1 = (bf16[2,1,2,512,1024]{4,3,2,1,0:T(8,128)(2,1)}, f32[2,1,2,128,128]{4,3,2,1,0:T(8,128)S(1)}) custom-call(f32[32,128]{1,0:T(8,128)S(1)} %get-tuple-element.24.turn.after, f32[16,128]{1,0:T(8,128)S(1)} %get-tuple-element.23.edge_turn.after, bf16[2,1,2,128,128]{4,3,2,1,0:T(8,128)(2,1)S(1)} %collective-permute-done.13.main, ...), custom_call_target="tpu_custom_call", output_to_operand_aliasing={{0}: (5, {})} | custom-call | tf_op jit(solution)/shard_map/window/pallas_call | solution.py:749
  38.7 1.2 %middle.1 = (bf16[2,1,2,512,1024]{4,3,2,1,0:T(8,128)(2,1)}, f32[2,1,2,128,128]{4,3,2,1,0:T(8,128)S(1)}) custom-call(f32[32,128]{1,0:T(8,128)S(1)} %get-tuple-element.24.turn.after, f32[16,128]{1,0:T(8,128)S(1)} %get-tuple-element.23.edge_turn.after, bf16[2,1,2,128,128]{4,3,2,1,0:T(8,128)(2,1)S(1)} %collective-permute-done.14.main, ...), custom_call_target="tpu_custom_call", output_to_operand_aliasing={{0}: (5, {})} | custom-call | tf_op jit(solution)/shard_map/middle/pallas_call | solution.py:759
  39.9 0.9 %end.1 = bf16[2,1,2,512,1024]{4,3,2,1,0:T(8,128)(2,1)} custom-call(f32[32,128]{1,0:T(8,128)S(1)} %get-tuple-element.24.turn.after, f32[16,128]{1,0:T(8,128)S(1)} %get-tuple-element.23.edge_turn.after, bf16[2,1,2,128,128]{4,3,2,1,0:T(8,128)(2,1)S(1)} %collective-permute-done.12.edge, ...), custom_call_target="tpu_custom_call", output_to_operand_aliasing={{}: (4, {})} | custom-call | tf_op jit(solution)/shard_map/end/pallas_call | solution.py:769
  (25 shorter events, 1.3 us)
Async XLA Ops:
  1.9 4.5 %collective-permute-start.3 = (bf16[2,1,2,128,128]{4,3,2,1,0:T(8,128)(2,1)S(1)}, bf16[2,1,2,128,128]{4,3,2,1,0:T(8,128)(2,1)S(1)}, u32[]{:S(2)}, u32[]{:S(2)}) collective-permute-start(bf16[2,1,2,128,128]{4,3,2,1,0:T(8,128)(2,1)S(1)} %get-tuple-element.31), channel_id=1, source_target_pairs={{0,8},{8,0},{16,24},{24,16},{1,9},{9,1},{17,25},{25,17},{2,10},{10... | collective-permute-start | bytes 393224 | tf_op jit(solution)/shard_map/ppermute | solution.py:563
  3.7 17.5 %copy-start = (bf16[2,1,128,512]{3,2,1,0:T(8,128)(2,1)S(1)}, bf16[2,1,128,512]{3,2,1,0:T(8,128)(2,1)}, u32[]{:S(2)}) copy-start(bf16[2,1,128,512]{3,2,1,0:T(8,128)(2,1)} %weights.1) | copy-start | bytes 786436
  5.7 4.5 %collective-permute-start.5 = (bf16[2,1,2,128,128]{4,3,2,1,0:T(8,128)(2,1)S(1)}, bf16[2,1,2,128,128]{4,3,2,1,0:T(8,128)(2,1)S(1)}, u32[]{:S(2)}, u32[]{:S(2)}) collective-permute-start(bf16[2,1,2,128,128]{4,3,2,1,0:T(8,128)(2,1)S(1)} %get-tuple-element.32), channel_id=1, source_target_pairs={{0,8},{8,0},{16,24},{24,16},{1,9},{9,1},{17,25},{25,17},{2,10},{10... | collective-permute-start | bytes 393224 | tf_op jit(solution)/shard_map/ppermute | solution.py:563
  5.8 3.6 %collective-permute-start.1 = (bf16[2,1,2,128,128]{4,3,2,1,0:T(8,128)(2,1)S(1)}, bf16[2,1,2,128,128]{4,3,2,1,0:T(8,128)(2,1)S(1)}, u32[]{:S(2)}, u32[]{:S(2)}) collective-permute-start(bf16[2,1,2,128,128]{4,3,2,1,0:T(8,128)(2,1)S(1)} %get-tuple-element.28), channel_id=1, source_target_pairs={{0,8},{8,0},{16,24},{24,16},{1,9},{9,1},{17,25},{25,17},{2,10},{10... | collective-permute-start | bytes 393224 | tf_op jit(solution)/shard_map/ppermute | solution.py:563
  6.3 13.2 %collective-permute-start = (bf16[2,1,2,128,128]{4,3,2,1,0:T(8,128)(2,1)S(1)}, bf16[2,1,2,128,128]{4,3,2,1,0:T(8,128)(2,1)S(1)}, u32[]{:S(2)}, u32[]{:S(2)}) collective-permute-start(bf16[2,1,2,128,128]{4,3,2,1,0:T(8,128)(2,1)S(1)} %get-tuple-element.26), channel_id=1, source_target_pairs={{0,8},{8,0},{16,24},{24,16},{1,9},{9,1},{17,25},{25,17},{2,10},{10... | collective-permute-start | bytes 393224 | tf_op jit(solution)/shard_map/ppermute | solution.py:563
  6.4 7.3 %collective-permute-start.4 = (bf16[2,1,2,128,128]{4,3,2,1,0:T(8,128)(2,1)S(1)}, bf16[2,1,2,128,128]{4,3,2,1,0:T(8,128)(2,1)S(1)}, u32[]{:S(2)}, u32[]{:S(2)}) collective-permute-start(bf16[2,1,2,128,128]{4,3,2,1,0:T(8,128)(2,1)S(1)} %add_convert_fusion.1), channel_id=1, source_target_pairs={{0,16},{8,24},{16,0},{24,8},{1,17},{9,25},{17,1},{25,9},{2,18},{10... | collective-permute-start | bytes 393224 | tf_op jit(solution)/shard_map/ppermute | solution.py:563
  9.5 10.0 %collective-permute-start.2 = (bf16[2,1,2,128,128]{4,3,2,1,0:T(8,128)(2,1)S(1)}, bf16[2,1,2,128,128]{4,3,2,1,0:T(8,128)(2,1)S(1)}, u32[]{:S(2)}, u32[]{:S(2)}) collective-permute-start(bf16[2,1,2,128,128]{4,3,2,1,0:T(8,128)(2,1)S(1)} %add_convert_fusion.2), channel_id=1, source_target_pairs={{0,16},{8,24},{16,0},{24,8},{1,17},{9,25},{17,1},{25,9},{2,18},{10... | collective-permute-start | bytes 393224 | tf_op jit(solution)/shard_map/ppermute | solution.py:563
  13.8 7.4 %collective-permute-start.6 = (bf16[1,2,128,128]{3,2,1,0:T(8,128)(2,1)S(1)}, bf16[1,2,128,128]{3,2,1,0:T(8,128)(2,1)S(1)}, u32[]{:S(2)}, u32[]{:S(2)}) collective-permute-start(bf16[1,2,128,128]{3,2,1,0:T(8,128)(2,1)S(1)} %get-tuple-element.45), channel_id=1, source_target_pairs={{0,1},{1,2},{2,3},{3,4},{4,5},{5,6},{6,7},{7,0},{8,9},{9,10},{10,1... | collective-permute-start | bytes 196616 | tf_op jit(solution)/shard_map/ppermute | solution.py:568
  15.9 5.3 %collective-permute-start.7 = (bf16[1,2,128,128]{3,2,1,0:T(8,128)(2,1)S(1)}, bf16[1,2,128,128]{3,2,1,0:T(8,128)(2,1)S(1)}, u32[]{:S(2)}, u32[]{:S(2)}) collective-permute-start(bf16[1,2,128,128]{3,2,1,0:T(8,128)(2,1)S(1)} %get-tuple-element.44), channel_id=1, source_target_pairs={{0,7},{1,0},{2,1},{3,2},{4,3},{5,4},{6,5},{7,6},{8,15},{9,8},{10,9... | collective-permute-start | bytes 196616 | tf_op jit(solution)/shard_map/ppermute | solution.py:568
  22.1 7.1 %collective-permute-start.9 = (bf16[1,2,128,128]{3,2,1,0:T(8,128)(2,1)S(1)}, bf16[1,2,128,128]{3,2,1,0:T(8,128)(2,1)S(1)}, u32[]{:S(2)}, u32[]{:S(2)}) collective-permute-start(bf16[1,2,128,128]{3,2,1,0:T(8,128)(2,1)S(1)} %get-tuple-element.34), channel_id=1, source_target_pairs={{0,1},{1,2},{2,3},{3,4},{4,5},{5,6},{6,7},{7,0},{8,9},{9,10},{10,1... | collective-permute-start | bytes 196616 | tf_op jit(solution)/shard_map/ppermute | solution.py:568
  23.6 5.6 %collective-permute-start.10 = (bf16[1,2,128,128]{3,2,1,0:T(8,128)(2,1)S(1)}, bf16[1,2,128,128]{3,2,1,0:T(8,128)(2,1)S(1)}, u32[]{:S(2)}, u32[]{:S(2)}) collective-permute-start(bf16[1,2,128,128]{3,2,1,0:T(8,128)(2,1)S(1)} %get-tuple-element.35), channel_id=1, source_target_pairs={{0,7},{1,0},{2,1},{3,2},{4,3},{5,4},{6,5},{7,6},{8,15},{9,8},{10,9... | collective-permute-start | bytes 196616 | tf_op jit(solution)/shard_map/ppermute | solution.py:568
  27.0 5.0 %collective-permute-start.13 = (bf16[2,1,2,128,128]{4,3,2,1,0:T(8,128)(2,1)S(1)}, bf16[2,1,2,128,128]{4,3,2,1,0:T(8,128)(2,1)S(1)}, u32[]{:S(2)}, u32[]{:S(2)}) collective-permute-start(bf16[2,1,2,128,128]{4,3,2,1,0:T(8,128)(2,1)S(1)} %get-tuple-element.33.own), channel_id=1, source_target_pairs={{0,16},{8,24},{16,0},{24,8},{1,17},{9,25},{17,1},{25,9},{2,18},{10... | collective-permute-start | bytes 393224 | tf_op jit(solution)/shard_map/ppermute | solution.py:563
  29.2 5.0 %collective-permute-start.11 = (bf16[2,1,2,128,128]{4,3,2,1,0:T(8,128)(2,1)S(1)}, bf16[2,1,2,128,128]{4,3,2,1,0:T(8,128)(2,1)S(1)}, u32[]{:S(2)}, u32[]{:S(2)}) collective-permute-start(bf16[2,1,2,128,128]{4,3,2,1,0:T(8,128)(2,1)S(1)} %pad_maximum_fusion.own_edge), channel_id=1, source_target_pairs={{0,16},{8,24},{16,0},{24,8},{1,17},{9,25},{17,1},{25,9},{2,18},{10... | collective-permute-start | bytes 393224 | tf_op jit(solution)/shard_map/ppermute | solution.py:563
  30.9 5.2 %collective-permute-start.8 = (bf16[2,1,2,128,128]{4,3,2,1,0:T(8,128)(2,1)S(1)}, bf16[2,1,2,128,128]{4,3,2,1,0:T(8,128)(2,1)S(1)}, u32[]{:S(2)}, u32[]{:S(2)}) collective-permute-start(bf16[2,1,2,128,128]{4,3,2,1,0:T(8,128)(2,1)S(1)} %get-tuple-element.33.own), channel_id=1, source_target_pairs={{0,8},{8,0},{16,24},{24,16},{1,9},{9,1},{17,25},{25,17},{2,10},{10... | collective-permute-start | bytes 393224 | tf_op jit(solution)/shard_map/ppermute | solution.py:563
  30.9 6.6 %collective-permute-start.15 = (bf16[2,1,2,128,128]{4,3,2,1,0:T(8,128)(2,1)S(1)}, bf16[2,1,2,128,128]{4,3,2,1,0:T(8,128)(2,1)S(1)}, u32[]{:S(2)}, u32[]{:S(2)}) collective-permute-start(bf16[2,1,2,128,128]{4,3,2,1,0:T(8,128)(2,1)S(1)} %pad_maximum_fusion.own_edge), channel_id=1, source_target_pairs={{0,8},{8,0},{16,24},{24,16},{1,9},{9,1},{17,25},{25,17},{2,10},{10... | collective-permute-start | bytes 393224 | tf_op jit(solution)/shard_map/ppermute | solution.py:563
  32.0 6.7 %collective-permute-start.14 = (bf16[2,1,2,128,128]{4,3,2,1,0:T(8,128)(2,1)S(1)}, bf16[2,1,2,128,128]{4,3,2,1,0:T(8,128)(2,1)S(1)}, u32[]{:S(2)}, u32[]{:S(2)}) collective-permute-start(bf16[2,1,2,128,128]{4,3,2,1,0:T(8,128)(2,1)S(1)} %collective-permute-done.13.main), channel_id=1, source_target_pairs={{0,8},{8,0},{16,24},{24,16},{1,9},{9,1},{17,25},{25,17},{2,10},{10... | collective-permute-start | bytes 393224 | tf_op jit(solution)/shard_map/ppermute | solution.py:563
  34.3 5.6 %collective-permute-start.12 = (bf16[2,1,2,128,128]{4,3,2,1,0:T(8,128)(2,1)S(1)}, bf16[2,1,2,128,128]{4,3,2,1,0:T(8,128)(2,1)S(1)}, u32[]{:S(2)}, u32[]{:S(2)}) collective-permute-start(bf16[2,1,2,128,128]{4,3,2,1,0:T(8,128)(2,1)S(1)} %collective-permute-done.11.edge), channel_id=1, source_target_pairs={{0,8},{8,0},{16,24},{24,16},{1,9},{9,1},{17,25},{25,17},{2,10},{10... | collective-permute-start | bytes 393224 | tf_op jit(solution)/shard_map/ppermute | solution.py:563
